TPU v7x, 32 devices: a whole 2x2x4 slice. The times are simulated.
32 devices in a mesh: dp: 2 (over x), sp: 16 (over z, y, core).
Axes of the slice: x: 2, y: 2, z: 4, core: 2. Of those that a mesh axis runs over, the one named last changes fastest.
Arguments:
- tokens: bfloat16 [2, 2, 4096, 768], P(None, 'dp', 'sp'), may hold values from -5 to 5
- doc_ids: int32 [2, 2, 4096], P(None, 'dp', 'sp'), may hold values from 0 to 1, as said below
- doc_bounds: int32 [2, 2, 3], P(None, 'dp'), may hold values from 0 to 4096, as said below
- landmark_ids: int32 [2, 2, 4096], P(None, 'dp', 'sp'), may hold values from 0 to 127, as said below
- query_weight: bfloat16 [2, 768, 768], P(None, ('dp', 'sp')), may hold values from -0.375 to 0.375
- key_weight: bfloat16 [2, 768, 768], P(None, ('dp', 'sp')), may hold values from -0.375 to 0.375
- value_weight: bfloat16 [2, 768, 768], P(None, ('dp', 'sp')), may hold values from -0.21875 to 0.21875
- out_weight: bfloat16 [2, 768, 768], P(None, ('dp', 'sp')), may hold values from -0.625 to 0.625
- conv_kernel: float32 [2, 12, 33], replicated, may hold values from -1 to 1
- up_weight: bfloat16 [2, 768, 3072], P(None, ('dp', 'sp')), may hold values from -0.21875 to 0.21875
- down_weight: bfloat16 [2, 3072, 768], P(None, ('dp', 'sp')), may hold values from -0.109375 to 0.109375
- norm_gain: float32 [2, 2, 768], replicated, may hold values from 0.25 to 1.75
- norm_bias: float32 [2, 2, 768], replicated, may hold values from -1.5 to 1.5
- cotangent: bfloat16 [2, 2, 4096, 768], P(None, 'dp', 'sp'), may hold values from -6 to 6
Outputs:
- output: bfloat16 [2, 2, 4096, 768], P(None, 'dp', 'sp')
- grad_tokens: float32 [2, 2, 4096, 768], P(None, 'dp', 'sp')
- grad_query: float32 [2, 768, 768], P(None, ('dp', 'sp'))
- grad_key: float32 [2, 768, 768], P(None, ('dp', 'sp'))
- grad_value: float32 [2, 768, 768], P(None, ('dp', 'sp'))
- grad_out: float32 [2, 768, 768], P(None, ('dp', 'sp'))
- grad_conv: float32 [2, 12, 33], replicated
- grad_up: float32 [2, 768, 3072], P(None, ('dp', 'sp'))
- grad_down: float32 [2, 3072, 768], P(None, ('dp', 'sp'))
- grad_gain: float32 [2, 2, 768], replicated
- grad_bias: float32 [2, 2, 768], replicated
Inputs may be any that keep to these rules, and one draw needn't show every extreme that they name: `doc_bounds`: each row holds 2 documents one after the other, each of 64 tokens or more. `doc_ids`: the document of each token as given by doc_bounds. `landmark_ids`: the token at position p of document d, which starts at s and has n tokens, has slot d * 64 + floor((p - s) * 64 / n).
All inputs are finite; a program needn't handle non-finite values.
Results may differ from a plain program's by a relative error of at most 0.024.
Values may be sent and summed in bfloat16 or wider, within the bound.
No kernel may reach another device: no remote copies, remote signals or barrier semaphores. Data moves between devices by JAX's collectives and lax.ppermute only.
A program may use at most 576 MiB of HBM per device.

v0:
```python
import functools

import jax
import jax.numpy as jnp
from jax import lax
from jax.sharding import PartitionSpec as P

HEADS = 12
HD = 64
LMK = 64
NS_ITERS = 6
KCONV = 33
SEQ = 4096
DOCS = 2
HALO = 16


highest = lax.Precision.HIGHEST
negative = -1e30
epsilon = 1e-05


def joined(value, axis, combine):
    everything = jax.tree.map(lambda part: lax.all_gather(part, axis), value)
    leading = jax.tree.map(lambda part: part[0], everything)

    def step(k, so_far):
        return combine(so_far, jax.tree.map(lambda part: part[k], everything))

    return lax.fori_loop(1, lax.axis_size(axis), step, leading)


def with_halo(block, sides, width):
    for axis, dim in sides:
        count = lax.axis_size(axis)
        forward = [(i, i + 1) for i in range(count - 1)]
        backward = [(target, source) for source, target in forward]
        low = lax.ppermute(
            lax.slice_in_dim(block, block.shape[dim] - width, None, axis=dim), axis, forward
        )
        high = lax.ppermute(lax.slice_in_dim(block, 0, width, axis=dim), axis, backward)
        block = jnp.concatenate([low, block, high], axis=dim)
    return block


def matmul_high(left_side, right_side):
    return jnp.dot(left_side, right_side, precision=highest)


def matmul_low(left_side, right_side):
    return jnp.dot(left_side, right_side, preferred_element_type=jnp.float32)


def rows_inner(left_side, right_side):
    return lax.dot_general(
        left_side, right_side, (((0,), (0,)), ((), ())), preferred_element_type=jnp.float32
    )


def back_product(grad_rows, weight_rows):
    return lax.dot_general(
        grad_rows, weight_rows, (((1,), (1,)), ((), ())), preferred_element_type=jnp.float32
    )


def norm_apply(summed, layer_gain, layer_bias):
    center = summed - jnp.mean(summed, axis=-1, keepdims=True)
    spread = jnp.mean(center * center, axis=-1, keepdims=True)
    return center * lax.rsqrt(spread + epsilon) * layer_gain + layer_bias


def gelu_tanh(values):
    return jax.nn.gelu(values, approximate=True)


def pseudo_inverse(kernel):
    identity = jnp.eye(LMK, dtype=jnp.float32)
    approx = jnp.swapaxes(kernel, -1, -2) / LMK
    for sweep_index in range(NS_ITERS):
        product = jnp.matmul(kernel, approx, precision=highest)
        nested = jnp.matmul(product, 7.0 * identity - product, precision=highest)
        nested = jnp.matmul(product, 15.0 * identity - nested, precision=highest)
        approx = 0.25 * jnp.matmul(approx, 13.0 * identity - nested, precision=highest)
    return approx


def marks_mix(query_marks, key_marks, marks_values):
    score_scale = HD ** (-0.5)
    query_docs = query_marks.reshape(DOCS, LMK, HEADS, HD)
    key_docs = key_marks.reshape(DOCS, LMK, HEADS, HD)
    scores = jnp.einsum("aihd,ajhd->ahij", query_docs, key_docs, precision=highest) * score_scale
    kernel = jax.nn.softmax(scores, axis=-1)
    pseudo = pseudo_inverse(kernel)
    value_docs = jnp.transpose(marks_values.reshape(HEADS, DOCS, LMK, HD), (1, 0, 2, 3))
    mixed = jnp.matmul(pseudo, value_docs, precision=highest)
    return jnp.transpose(mixed, (1, 0, 2, 3)).reshape(HEADS, DOCS * LMK, HD)


def token_mix(queries, key_marks, mixed_marks, row_docs, mark_docs):
    length = queries.shape[0]
    score_scale = HD ** (-0.5)
    query_heads = queries.reshape(length, HEADS, HD)
    key_heads = key_marks.reshape(DOCS * LMK, HEADS, HD)
    scores = jnp.einsum("thd,jhd->htj", query_heads, key_heads, precision=highest) * score_scale
    keep_mask = (row_docs[:, None] == mark_docs[None, :])[None]
    kernel = jax.nn.softmax(jnp.where(keep_mask, scores, negative), axis=-1)
    return jnp.einsum("htj,hjd->thd", kernel, mixed_marks, precision=highest).reshape(
        length, HEADS * HD
    )


def key_scores(query_marks, key_rows, row_docs, mark_docs):
    length = key_rows.shape[0]
    score_scale = HD ** (-0.5)
    mark_heads = query_marks.reshape(DOCS * LMK, HEADS, HD)
    key_heads = key_rows.reshape(length, HEADS, HD)
    scores = jnp.einsum("jhd,thd->hjt", mark_heads, key_heads, precision=highest) * score_scale
    keep_mask = (mark_docs[:, None] == row_docs[None, :])[None]
    return (jnp.where(keep_mask, scores, negative), keep_mask, mark_heads, key_heads)


def key_partial(query_marks, key_rows, value_rows, row_docs, mark_docs):
    length = key_rows.shape[0]
    scores, keep_mask, mark_heads, key_heads = key_scores(
        query_marks, key_rows, row_docs, mark_docs
    )
    top_score = jnp.max(scores, axis=-1)
    weights = jnp.where(keep_mask, jnp.exp(scores - top_score[..., None]), 0.0)
    numer_sum = jnp.einsum(
        "hjt,thd->hjd", weights, value_rows.reshape(length, HEADS, HD), precision=highest
    )
    return (top_score, jnp.sum(weights, axis=-1), numer_sum)


def merge_soft(first_part, second_part):
    top_first, total_first, numer_first = first_part
    top_second, total_second, numer_second = second_part
    top_score = jnp.maximum(top_first, top_second)
    scale_first = jnp.exp(top_first - top_score)
    scale_second = jnp.exp(top_second - top_score)
    return (
        top_score,
        total_first * scale_first + total_second * scale_second,
        numer_first * scale_first[..., None] + numer_second * scale_second[..., None],
    )


def key_back(
    query_marks,
    key_rows,
    value_rows,
    row_docs,
    mark_docs,
    top_score,
    total_sum,
    marks_values,
    grad_marks,
):
    length = key_rows.shape[0]
    score_scale = HD ** (-0.5)
    scores, keep_mask, mark_heads, key_heads = key_scores(
        query_marks, key_rows, row_docs, mark_docs
    )
    value_heads = value_rows.reshape(length, HEADS, HD)
    probs = jnp.where(keep_mask, jnp.exp(scores - top_score[..., None]), 0.0) / total_sum[..., None]
    grad_probs = jnp.einsum("hjd,thd->hjt", grad_marks, value_heads, precision=highest)
    row_dot = jnp.sum(grad_marks * marks_values, axis=-1)
    grad_scores = probs * (grad_probs - row_dot[..., None]) * score_scale
    grad_query = jnp.einsum("hjt,thd->jhd", grad_scores, key_heads, precision=highest).reshape(
        DOCS * LMK, HEADS * HD
    )
    grad_keys = jnp.einsum("hjt,jhd->thd", grad_scores, mark_heads, precision=highest).reshape(
        length, HEADS * HD
    )
    grad_values = jnp.einsum("hjt,hjd->thd", probs, grad_marks, precision=highest).reshape(
        length, HEADS * HD
    )
    return (grad_query, grad_keys, grad_values)


def doc_position(positions, row_bounds):
    return jnp.sum((positions[:, None] >= row_bounds[None, 1:DOCS]).astype(jnp.int32), axis=1)


def slot_counts(row_bounds):
    starts = row_bounds[:DOCS]
    sizes = row_bounds[1 : DOCS + 1] - starts
    index = jnp.arange(LMK, dtype=jnp.int32)
    upper = ((index[None, :] + 1) * sizes[:, None] + LMK - 1) // LMK
    lower = (index[None, :] * sizes[:, None] + LMK - 1) // LMK
    return (upper - lower).reshape(DOCS * LMK).astype(jnp.float32)


def band_table(pad_docs, pad_valid, center_docs):
    length = center_docs.shape[0]
    width = pad_docs.shape[0]
    offsets = jnp.arange(KCONV, dtype=jnp.int32)[:, None, None]
    rows = jnp.arange(length, dtype=jnp.int32)[None, :, None]
    cols = jnp.arange(width, dtype=jnp.int32)[None, None, :]
    keep_mask = jnp.logical_and(
        cols == rows + offsets,
        jnp.logical_and(
            pad_valid[None, None, :], pad_docs[None, None, :] == center_docs[None, :, None]
        ),
    )
    return keep_mask.astype(jnp.float32)


def conv_apply(padded, kernel, band, flipped):
    length = band.shape[1]
    width = band.shape[2]
    taps = kernel[:, ::-1] if flipped else kernel
    mixing = jnp.einsum("ho,otp->htp", taps, band, precision=highest)
    heads = padded.reshape(width, HEADS, HD)
    return jnp.einsum("htp,phd->thd", mixing, heads, precision=highest).reshape(length, HEADS * HD)


def conv_kernel_grad(grad_conv, padded, band):
    length = band.shape[1]
    width = band.shape[2]
    pairs = jnp.einsum(
        "thd,phd->htp",
        grad_conv.reshape(length, HEADS, HD),
        padded.reshape(width, HEADS, HD),
        precision=highest,
    )
    return jnp.einsum("htp,otp->ho", pairs, band, precision=highest)


def layer_forward(hidden, fetched, kernel, layer_gain, layer_bias, context):
    query_weight, key_weight, value_weight, out_weight, up_weight, down_weight = fetched
    onehot, onehot_low, counts, row_docs, mark_docs, band = context
    hidden_low = hidden.astype(jnp.bfloat16)
    query_low = matmul_low(hidden_low, query_weight).astype(jnp.bfloat16)
    key_low = matmul_low(hidden_low, key_weight).astype(jnp.bfloat16)
    value_low = matmul_low(hidden_low, value_weight).astype(jnp.bfloat16)
    query_share, key_share = (
        lax.psum_scatter(rows_inner(onehot_low, query_low), "sp", scatter_dimension=1, tiled=True),
        lax.psum_scatter(rows_inner(onehot_low, key_low), "sp", scatter_dimension=1, tiled=True),
    )
    query_sums, key_sums = (
        lax.all_gather(query_share, "sp", axis=1, tiled=True),
        lax.all_gather(key_share, "sp", axis=1, tiled=True),
    )
    query_marks = query_sums / counts[:, None]
    key_marks = key_sums / counts[:, None]
    queries = query_low.astype(jnp.float32)
    key_rows = key_low.astype(jnp.float32)
    value_rows = value_low.astype(jnp.float32)
    partial_soft = key_partial(query_marks, key_rows, value_rows, row_docs, mark_docs)
    top_score, total_sum, numer_sum = joined(
        (partial_soft[0], partial_soft[1], partial_soft[2]), "sp", merge_soft
    )
    marks_values = numer_sum / total_sum[..., None]
    mixed_marks, marks_pull = jax.vjp(marks_mix, query_marks, key_marks, marks_values)
    attended, token_pull = jax.vjp(
        functools.partial(token_mix, row_docs=row_docs, mark_docs=mark_docs),
        queries,
        key_marks,
        mixed_marks,
    )
    padded = with_halo(value_low, (("sp", 0),), HALO).astype(jnp.float32)
    branch_low = (attended + conv_apply(padded, kernel, band, False)).astype(jnp.bfloat16)
    projected = matmul_low(branch_low, out_weight)
    normed, first_pull = jax.vjp(norm_apply, hidden + projected, layer_gain[0], layer_bias[0])
    normed_low = normed.astype(jnp.bfloat16)
    expanded = matmul_low(normed_low, up_weight)
    activated, gelu_pull = jax.vjp(gelu_tanh, expanded)
    activated_low = activated.astype(jnp.bfloat16)
    result, second_pull = jax.vjp(
        norm_apply, normed + matmul_low(activated_low, down_weight), layer_gain[1], layer_bias[1]
    )
    saved_state = (
        hidden_low,
        query_marks,
        key_rows,
        value_rows,
        top_score,
        total_sum,
        marks_values,
        marks_pull,
        token_pull,
        padded,
        branch_low,
        first_pull,
        normed_low,
        gelu_pull,
        activated_low,
        second_pull,
    )
    return (result, saved_state)


def layer_backward(grad_result, saved_state, fetched, kernel, context):
    query_weight, key_weight, value_weight, out_weight, up_weight, down_weight = fetched
    onehot, onehot_low, counts, row_docs, mark_docs, band = context
    (
        hidden_low,
        query_marks,
        key_rows,
        value_rows,
        top_score,
        total_sum,
        marks_values,
        marks_pull,
        token_pull,
        padded,
        branch_low,
        first_pull,
        normed_low,
        gelu_pull,
        activated_low,
        second_pull,
    ) = saved_state
    marks_total = query_marks.shape[0]
    grad_second, gain_second, bias_second = second_pull(grad_result)
    dense_grad = grad_second.astype(jnp.bfloat16)
    grad_down = rows_inner(activated_low, dense_grad)
    (grad_expanded,) = gelu_pull(back_product(dense_grad, down_weight))
    expanded_grad = grad_expanded.astype(jnp.bfloat16)
    grad_up = rows_inner(normed_low, expanded_grad)
    grad_first, gain_first, bias_first = first_pull(
        grad_second + back_product(expanded_grad, up_weight)
    )
    projected_grad = grad_first.astype(jnp.bfloat16)
    grad_out = rows_inner(branch_low, projected_grad)
    branch_grad = back_product(projected_grad, out_weight)
    query_token_grad, key_marks_part, mixed_part = token_pull(branch_grad)
    mixed_flat = jnp.transpose(mixed_part, (1, 0, 2)).reshape(marks_total, HEADS * HD)
    key_share, mixed_share = (
        lax.psum_scatter(
            key_marks_part.astype(jnp.bfloat16), "sp", scatter_dimension=1, tiled=True
        ).astype(jnp.float32),
        lax.psum_scatter(
            mixed_flat.astype(jnp.bfloat16), "sp", scatter_dimension=1, tiled=True
        ).astype(jnp.float32),
    )
    key_marks_first, mixed_whole = (
        lax.all_gather(key_share, "sp", axis=1, tiled=True),
        lax.all_gather(mixed_share, "sp", axis=1, tiled=True),
    )
    mixed_grad = jnp.transpose(mixed_whole.reshape(marks_total, HEADS, HD), (1, 0, 2))
    query_marks_grad, key_marks_second, marks_values_grad = marks_pull(mixed_grad)
    query_part, key_soft_grad, value_soft_grad = key_back(
        query_marks,
        key_rows,
        value_rows,
        row_docs,
        mark_docs,
        top_score,
        total_sum,
        marks_values,
        marks_values_grad,
    )
    query_share = lax.psum_scatter(
        query_part.astype(jnp.bfloat16), "sp", scatter_dimension=1, tiled=True
    ).astype(jnp.float32)
    query_marks_grad = query_marks_grad + lax.all_gather(query_share, "sp", axis=1, tiled=True)
    key_marks_grad = key_marks_first + key_marks_second
    padded_grad = with_halo(branch_grad.astype(jnp.bfloat16), (("sp", 0),), HALO).astype(
        branch_grad.dtype
    )
    conv_grad = conv_kernel_grad(branch_grad, padded, band)
    query_grad = (
        query_token_grad + matmul_high(onehot, query_marks_grad / counts[:, None])
    ).astype(jnp.bfloat16)
    key_grad = (key_soft_grad + matmul_high(onehot, key_marks_grad / counts[:, None])).astype(
        jnp.bfloat16
    )
    value_grad = (value_soft_grad + conv_apply(padded_grad, kernel, band, True)).astype(
        jnp.bfloat16
    )
    grad_hidden = (
        grad_first
        + back_product(query_grad, query_weight)
        + back_product(key_grad, key_weight)
        + back_product(value_grad, value_weight)
    )
    weight_grads = (
        rows_inner(hidden_low, query_grad),
        rows_inner(hidden_low, key_grad),
        rows_inner(hidden_low, value_grad),
        grad_out,
        grad_up,
        grad_down,
    )
    return (
        grad_hidden,
        weight_grads,
        conv_grad,
        jnp.stack([gain_first, gain_second]),
        jnp.stack([bias_first, bias_second]),
    )


def local(
    tokens,
    doc_ids,
    doc_bounds,
    landmark_ids,
    query_weight,
    key_weight,
    value_weight,
    out_weight,
    conv_kernel,
    up_weight,
    down_weight,
    norm_gain,
    norm_bias,
    cotangent,
):
    block_index = lax.axis_index("sp")
    batches = tokens.shape[0]
    layers = query_weight.shape[0]
    length = tokens.shape[2]
    marks_total = DOCS * LMK
    mark_docs = jnp.arange(marks_total, dtype=jnp.int32) // LMK
    owned = (query_weight, key_weight, value_weight, out_weight, up_weight, down_weight)
    shard_sums = tuple((jnp.zeros(tensor.shape, jnp.float32) for tensor in owned))
    full_sums = None
    conv_parts = [jnp.zeros(conv_kernel.shape[1:], jnp.float32) for layer_index in range(layers)]
    gain_parts = [jnp.zeros(norm_gain.shape[1:], jnp.float32) for layer_index in range(layers)]
    bias_parts = [jnp.zeros(norm_bias.shape[1:], jnp.float32) for layer_index in range(layers)]
    outputs = []
    input_grads = []
    gathered = None
    gathered = (
        lax.all_gather(owned[0], ("dp", "sp"), axis=1, tiled=True),
        lax.all_gather(owned[1], ("dp", "sp"), axis=1, tiled=True),
        lax.all_gather(owned[2], ("dp", "sp"), axis=1, tiled=True),
        lax.all_gather(owned[3], ("dp", "sp"), axis=1, tiled=True),
        lax.all_gather(owned[4], ("dp", "sp"), axis=1, tiled=True),
        lax.all_gather(owned[5], ("dp", "sp"), axis=1, tiled=True),
    )
    for batch_index in range(batches):
        row_docs = doc_ids[batch_index, 0]
        row_bounds = doc_bounds[batch_index, 0]
        row_marks = landmark_ids[batch_index, 0]
        onehot = (row_marks[:, None] == jnp.arange(marks_total, dtype=jnp.int32)[None, :]).astype(
            jnp.float32
        )
        first_token = block_index * length
        positions = first_token - HALO + jnp.arange(length + 2 * HALO, dtype=jnp.int32)
        pad_docs = doc_position(positions, row_bounds)
        pad_valid = jnp.logical_and(positions >= 0, positions < SEQ)
        center_docs = doc_position(first_token + jnp.arange(length, dtype=jnp.int32), row_bounds)
        band = band_table(pad_docs, pad_valid, center_docs)
        context = (
            onehot,
            onehot.astype(jnp.bfloat16),
            slot_counts(row_bounds),
            row_docs,
            mark_docs,
            band,
        )
        hidden = tokens[batch_index, 0].astype(jnp.float32)
        saved_layers = []
        for layer_index in range(layers):
            fetched = tuple((tensor[layer_index] for tensor in gathered))
            hidden, saved_state = layer_forward(
                hidden,
                fetched,
                conv_kernel[layer_index],
                norm_gain[layer_index],
                norm_bias[layer_index],
                context,
            )
            saved_layers.append(saved_state)
        outputs.append(hidden.astype(jnp.bfloat16))
        grad_hidden = cotangent[batch_index, 0].astype(jnp.float32)
        batch_layers = [None] * layers
        for layer_index in reversed(range(layers)):
            fetched = tuple((tensor[layer_index] for tensor in gathered))
            grad_hidden, weight_grads, conv_grad, gain_grad, bias_grad = layer_backward(
                grad_hidden, saved_layers[layer_index], fetched, conv_kernel[layer_index], context
            )
            conv_parts[layer_index] = conv_parts[layer_index] + conv_grad
            gain_parts[layer_index] = gain_parts[layer_index] + gain_grad
            bias_parts[layer_index] = bias_parts[layer_index] + bias_grad
            batch_layers[layer_index] = weight_grads
        stacked_batch = tuple(
            (
                jnp.stack([batch_layers[layer_index][member] for layer_index in range(layers)])
                for member in range(6)
            )
        )
        if full_sums is None:
            full_sums = stacked_batch
        else:
            full_sums = tuple(
                (running + fresh_grad for running, fresh_grad in zip(full_sums, stacked_batch))
            )
        input_grads.append(grad_hidden)
    shard_sums = (
        lax.psum_scatter(full_sums[0], ("dp", "sp"), scatter_dimension=1, tiled=True),
        lax.psum_scatter(full_sums[1], ("dp", "sp"), scatter_dimension=1, tiled=True),
        lax.psum_scatter(full_sums[2], ("dp", "sp"), scatter_dimension=1, tiled=True),
        lax.psum_scatter(full_sums[3], ("dp", "sp"), scatter_dimension=1, tiled=True),
        lax.psum_scatter(full_sums[4], ("dp", "sp"), scatter_dimension=1, tiled=True),
        lax.psum_scatter(full_sums[5], ("dp", "sp"), scatter_dimension=1, tiled=True),
    )
    small_sums = lax.psum(
        (jnp.stack(conv_parts), jnp.stack(gain_parts), jnp.stack(bias_parts)), ("dp", "sp")
    )
    return (
        jnp.stack(outputs)[:, None],
        jnp.stack(input_grads)[:, None],
        shard_sums[0],
        shard_sums[1],
        shard_sums[2],
        shard_sums[3],
        small_sums[0],
        shard_sums[4],
        shard_sums[5],
        small_sums[1],
        small_sums[2],
    )


def solution(mesh):
    placed = (
        P(None, "dp", "sp", None),
        P(None, "dp", "sp"),
        P(None, "dp", None),
        P(None, "dp", "sp"),
        P(None, ("dp", "sp"), None),
        P(None, ("dp", "sp"), None),
        P(None, ("dp", "sp"), None),
        P(None, ("dp", "sp"), None),
        P(),
        P(None, ("dp", "sp"), None),
        P(None, ("dp", "sp"), None),
        P(),
        P(),
        P(None, "dp", "sp", None),
    )
    return jax.shard_map(
        local,
        mesh=mesh,
        in_specs=placed,
        out_specs=(
            P(None, "dp", "sp", None),
            P(None, "dp", "sp", None),
            P(None, ("dp", "sp"), None),
            P(None, ("dp", "sp"), None),
            P(None, ("dp", "sp"), None),
            P(None, ("dp", "sp"), None),
            P(),
            P(None, ("dp", "sp"), None),
            P(None, ("dp", "sp"), None),
            P(),
            P(),
        ),
        check_vma=False,
    )
```

profile of v0, /device:TPU:0, one launch (start us, length us, event | category | flops | bytes accessed | tf_op | source)
XLA Modules:
  0.0 3148.9 jit_solution(15136820689575044595)
XLA Ops:
  13.0 58.1 %all-gather.33.cloned.1.call-done = bf16[2,768,768]{2,1,0:T(8,128)(2,1)} async-done(((bf16[2,24,768]{2,1,0:T(8,128)(2,1)}), bf16[2,768,768]{2,1,0:T(8,128)(2,1)}) %all-gather.33.cloned.1.call-update) | async-done | bytes 2359312 | tf_op jit(solution)/shard_map/all_gather | solution.py:429
  75.9 54.3 %all-gather.31.cloned.1.call-done = bf16[2,768,768]{2,1,0:T(8,128)(2,1)} async-done(((bf16[2,24,768]{2,1,0:T(8,128)(2,1)}), bf16[2,768,768]{2,1,0:T(8,128)(2,1)}) %all-gather.31.cloned.1.call-update) | async-done | bytes 2359312 | tf_op jit(solution)/shard_map/all_gather | solution.py:428
  138.3 51.2 %all-gather.35.cloned.1.call-done = bf16[2,768,768]{2,1,0:T(8,128)(2,1)} async-done(((bf16[2,24,768]{2,1,0:T(8,128)(2,1)}), bf16[2,768,768]{2,1,0:T(8,128)(2,1)}) %all-gather.35.cloned.1.call-update) | async-done | bytes 2359312 | tf_op jit(solution)/shard_map/all_gather | solution.py:430
  199.0 48.9 %reduce-scatter.26.cloned.1.call-done = f32[128,48]{0,1:T(8,128)} async-done(((f32[128,768]{0,1:T(8,128)}), f32[128,48]{0,1:T(8,128)}) %reduce-scatter.26.cloned.1.call-update) | async-done | bytes 24592 | tf_op jit(solution)/shard_map/reduce_scatter | solution.py:239
  247.9 20.7 all_gather.153
  268.6 38.3 %reduce-scatter.24.cloned.1.call-done = f32[128,48]{0,1:T(8,128)} async-done(((f32[128,768]{0,1:T(8,128)}), f32[128,48]{0,1:T(8,128)}) %reduce-scatter.24.cloned.1.call-update) | async-done | bytes 24592 | tf_op jit(solution)/shard_map/reduce_scatter | solution.py:238
  306.8 20.7 all_gather.151
  338.6 26.2 reduce-scatter.34.cloned.1.call-done
  364.8 22.1 all_gather.173
  386.9 37.0 %reduce-scatter.32.cloned.1.call-done = f32[128,48]{0,1:T(8,128)} async-done(((f32[128,768]{0,1:T(8,128)}), f32[128,48]{0,1:T(8,128)}) %reduce-scatter.32.cloned.1.call-update) | async-done | bytes 24592 | tf_op jit(solution)/shard_map/reduce_scatter | solution.py:238
  423.9 21.8 all_gather.172
  721.3 41.9 %while.76 = (s32[]{:T(128)}, f32[12,128]{1,0:T(8,128)S(1)}, f32[12,128]{1,0:T(8,128)S(1)}, f32[12,128,64]{2,1,0:T(8,128)S(1)}, f32[16,12,128]{2,1,0:T(8,128)}, /...) while((s32[]{:T(128)}, f32[12,128]{1,0:T(8,128)S(1)}, ...), condition=%wide.region_7.8_spmd, body=%wide.region_6.7_spmd.sunk | while | flops 304133 | bytes 2814103 | solution.py:30
  770.8 41.6 %while.78 = (s32[]{:T(128)}, f32[12,128]{1,0:T(8,128)S(1)}, f32[12,128]{1,0:T(8,128)S(1)}, f32[12,128,64]{2,1,0:T(8,128)S(1)}, f32[16,12,128]{2,1,0:T(8,128)S(1)...) while((s32[]{:T(128)}, f32[12,128]{1,0:T(8,128)S(1)}, ...), condition=%wide.region_35.36_spmd, body=%wide.region_34.35_spmd.sunk | while | flops 304133 | bytes 2814103 | solution.py:30
  921.3 20.7 all_gather.165
  942.1 38.2 %reduce-scatter.28.cloned.1.call-done = f32[128,48]{0,1:T(8,128)} async-done(((f32[128,768]{0,1:T(8,128)}), f32[128,48]{0,1:T(8,128)}) %reduce-scatter.28.cloned.1.call-update) | async-done | bytes 24592 | tf_op jit(solution)/shard_map/reduce_scatter | solution.py:238
  980.3 21.1 all_gather.164
  1096.8 21.7 all_gather.180
  1231.8 41.9 %while.77 = (s32[]{:T(128)}, f32[12,128]{1,0:T(8,128)S(1)}, f32[12,128]{1,0:T(8,128)S(1)}, f32[12,128,64]{2,1,0:T(8,128)S(1)}, f32[16,12,128]{2,1,0:T(8,128)}, /...) while((s32[]{:T(128)}, f32[12,128]{1,0:T(8,128)S(1)}, ...), condition=%wide.region_21.22_spmd, body=%wide.region_20.21_spmd.sunk | while | flops 304133 | bytes 2814103 | solution.py:30
  1304.4 41.8 %while.79 = (s32[]{:T(128)}, f32[12,128]{1,0:T(8,128)S(1)}, f32[12,128]{1,0:T(8,128)S(1)}, f32[12,128,64]{2,1,0:T(8,128)S(1)}, f32[16,12,128]{2,1,0:T(8,128)S(1)...) while((s32[]{:T(128)}, f32[12,128]{1,0:T(8,128)S(1)}, ...), condition=%wide.region_49.50_spmd, body=%wide.region_48.49_spmd.sunk | while | flops 304133 | bytes 2814103 | solution.py:30
  1450.3 21.9 all_gather.194
  1662.9 21.2 all_gather.196
  1775.6 21.4 all_gather.195
  1796.9 30.9 reduce-scatter.42.cloned.1.call-done
  1828.5 20.7 all_gather.189
  1941.3 20.5 all_gather.197
  2165.8 21.2 all_gather.199
  2323.5 20.5 all_gather.192
  2463.0 38.2 %all-reduce.3 = (f32[2,12,33]{2,1,0:T(8,128)S(1)}, f32[2,2,768]{2,1,0:T(2,128)}, f32[2,2,768]{2,1,0:T(2,128)}) all-reduce(f32[2,12,33]{2,1,0:T(8,128)S(1)} %pad_maximum_fusion.8, f32[2,2,768]{2,1,0:T(2,128)S(1)} %pad_maximum_fusion.9, f32[2,2,768]{2,1,0:T(2,128)S(1)} %pad_maximum_fusion.10), channel_id=1, replica_groups=mesh['dp'=2,'sp'=16] {'dp','sp'}, use_global_device_ids=true, to_apply=%region_100.101 | all-reduce | flops 6936 | bytes 55488 | tf_op jit(solution)/shard_map/psum | solution.py:502
  2511.2 94.3 %all-reduce.7.cloned.1.call-done = (f32[2,768,768]{2,0,1:T(2,128)}, f32[2,768,768]{2,0,1:T(2,128)}, f32[2,768,768]{2,0,1:T(2,128)}) async-done(((f32[2,768,768]{2,0,1:T(2,128)}, f32[2,768,768]{2,0,1:T(2,128)}, f32[2,768,768]{2,0,1:T(2,128)}), (f32[2,768,768]{2,0,1:T(2,128)}, f32[2,768,768]{2,0,1:T(2,128)}, f32[2,768,768]{2,0,1:T(2,128)})) %all-reduce.7.cloned.1.call-update) | async-done | bytes 14155792
  2610.3 108.1 %reduce-scatter.64.cloned.1.call-done = f32[2,24,768]{2,1,0:T(8,128)} async-done(((f32[2,768,768]{2,1,0:T(8,128)}), f32[2,24,768]{2,1,0:T(8,128)}) %reduce-scatter.64.cloned.1.call-update) | async-done | bytes 147472 | tf_op jit(solution)/shard_map/reduce_scatter | solution.py:498
  2718.4 211.7 %reduce-scatter.66.cloned.1.call-done = f32[2,24,3072]{2,1,0:T(8,128)} async-done(((f32[2,768,3072]{2,1,0:T(8,128)}), f32[2,24,3072]{2,1,0:T(8,128)}) %reduce-scatter.66.cloned.1.call-update) | async-done | bytes 589840 | tf_op jit(solution)/shard_map/reduce_scatter | solution.py:499
  2930.1 211.8 %reduce-scatter.68.cloned.1.call-done = f32[2,96,768]{2,1,0:T(8,128)} async-done(((f32[2,3072,768]{2,1,0:T(8,128)}), f32[2,96,768]{2,1,0:T(8,128)}) %reduce-scatter.68.cloned.1.call-update) | async-done | bytes 589840 | tf_op jit(solution)/shard_map/reduce_scatter | solution.py:500
  (2434 shorter events, 1777.3 us)
Async XLA Ops:
  7.9 122.3 %all-gather.31.cloned.1.call-start = ((), (), s32[]{:S(2)}) async-start(), calls=%async_computation.23 | async-start | bytes 2433024 | tf_op jit(solution)/shard_map/all_gather | solution.py:428
  8.7 180.8 %all-gather.35.cloned.1.call-start = ((), (), s32[]{:S(2)}) async-start(), calls=%async_computation.27 | async-start | bytes 2433024 | tf_op jit(solution)/shard_map/all_gather | solution.py:430
  9.4 238.5 %reduce-scatter.26.cloned.1.call-start = ((), (), s32[]{:S(2)}) async-start(), calls=%async_computation.26 | async-start | bytes 417792 | tf_op jit(solution)/shard_map/reduce_scatter | solution.py:239
  75.6 231.2 %reduce-scatter.24.cloned.1.call-start = ((), (), s32[]{:S(2)}) async-start(), calls=%async_computation.24 | async-start | bytes 417792 | tf_op jit(solution)/shard_map/reduce_scatter | solution.py:238
  134.6 230.2 %reduce-scatter.34.cloned.1.call-start = ((), (), s32[]{:S(2)}) async-start(), calls=%async_computation.34 | async-start | bytes 417792 | tf_op jit(solution)/shard_map/reduce_scatter | solution.py:239
  138.2 285.7 %reduce-scatter.32.cloned.1.call-start = ((), (), s32[]{:S(2)}) async-start(), calls=%async_computation.33 | async-start | bytes 417792 | tf_op jit(solution)/shard_map/reduce_scatter | solution.py:238
  198.9 521.1 %all-gather.43.cloned.1.call-start = ((), (), s32[]{:S(2)}) async-start(), calls=%async_computation.52 | async-start | bytes 6684672 | tf_op jit(solution)/shard_map/all_gather | solution.py:24
  334.3 435.2 %all-gather.47.cloned.1.call-start = ((), (), s32[]{:S(2)}) async-start(), calls=%async_computation.54 | async-start | bytes 6684672 | tf_op jit(solution)/shard_map/all_gather | solution.py:24
  453.0 377.6 %all-gather.37.cloned.1.call-start = ((), (), s32[]{:S(2)}) async-start(), calls=%async_computation.28 | async-start | bytes 2433024 | tf_op jit(solution)/shard_map/all_gather | solution.py:431
  453.6 387.7 %all-gather.39.cloned.1.call-start = ((), (), s32[]{:S(2)}) async-start(), calls=%async_computation.29 | async-start | bytes 9732096 | tf_op jit(solution)/shard_map/all_gather | solution.py:432
  454.3 392.6 %all-gather.41.cloned.1.call-start = ((), (), s32[]{:S(2)}) async-start(), calls=%async_computation.30 | async-start | bytes 9732096 | tf_op jit(solution)/shard_map/all_gather | solution.py:433
  454.9 466.4 %reduce-scatter.30.cloned.1.call-start = ((), (), s32[]{:S(2)}) async-start(), calls=%async_computation.32 | async-start | bytes 417792 | tf_op jit(solution)/shard_map/reduce_scatter | solution.py:239
  867.0 113.3 %reduce-scatter.28.cloned.1.call-start = ((), (), s32[]{:S(2)}) async-start(), calls=%async_computation.31 | async-start | bytes 417792 | tf_op jit(solution)/shard_map/reduce_scatter | solution.py:238
  872.7 188.6 %reduce-scatter.38.cloned.1.call-start = ((), (), s32[]{:S(2)}) async-start(), calls=%async_computation.36 | async-start | bytes 417792 | tf_op jit(solution)/shard_map/reduce_scatter | solution.py:239
  881.4 215.4 %reduce-scatter.36.cloned.1.call-start = ((), (), s32[]{:S(2)}) async-start(), calls=%async_computation.35 | async-start | bytes 417792 | tf_op jit(solution)/shard_map/reduce_scatter | solution.py:238
  898.8 331.7 %all-gather.45.cloned.1.call-start = ((), (), s32[]{:S(2)}) async-start(), calls=%async_computation.53 | async-start | bytes 6684672 | tf_op jit(solution)/shard_map/all_gather | solution.py:24
  1061.3 241.8 %all-gather.49.cloned.1.call-start = ((), (), s32[]{:S(2)}) async-start(), calls=%async_computation.55 | async-start | bytes 6684672 | tf_op jit(solution)/shard_map/all_gather | solution.py:24
  1230.4 219.2 %reduce-scatter.52.cloned.1.call-start = ((), (), s32[]{:S(2)}) async-start(), calls=%async_computation.43 | async-start | bytes 208896 | tf_op jit(solution)/shard_map/reduce_scatter | solution.py:334
  1398.6 176.9 %reduce-scatter.40.cloned.1.call-start = ((), (), s32[]{:S(2)}) async-start(), calls=%async_computation.37 | async-start | bytes 208896 | tf_op jit(solution)/shard_map/reduce_scatter | solution.py:334
  1416.9 245.3 %reduce-scatter.56.cloned.1.call-start = ((), (), s32[]{:S(2)}) async-start(), calls=%async_computation.45 | async-start | bytes 208896 | tf_op jit(solution)/shard_map/reduce_scatter | solution.py:331
  1421.6 299.2 %reduce-scatter.44.cloned.1.call-start = ((), (), s32[]{:S(2)}) async-start(), calls=%async_computation.39 | async-start | bytes 208896 | tf_op jit(solution)/shard_map/reduce_scatter | solution.py:331
  1436.6 338.3 %reduce-scatter.54.cloned.1.call-start = ((), (), s32[]{:S(2)}) async-start(), calls=%async_computation.44 | async-start | bytes 208896 | tf_op jit(solution)/shard_map/reduce_scatter | solution.py:355
  1766.0 174.6 %reduce-scatter.58.cloned.1.call-start = ((), (), s32[]{:S(2)}) async-start(), calls=%async_computation.46 | async-start | bytes 208896 | tf_op jit(solution)/shard_map/reduce_scatter | solution.py:334
  1889.6 151.8 %reduce-scatter.46.cloned.1.call-start = ((), (), s32[]{:S(2)}) async-start(), calls=%async_computation.40 | async-start | bytes 208896 | tf_op jit(solution)/shard_map/reduce_scatter | solution.py:334
  1913.6 251.5 %reduce-scatter.62.cloned.1.call-start = ((), (), s32[]{:S(2)}) async-start(), calls=%async_computation.48 | async-start | bytes 208896 | tf_op jit(solution)/shard_map/reduce_scatter | solution.py:331
  1916.9 298.9 %reduce-scatter.50.cloned.1.call-start = ((), (), s32[]{:S(2)}) async-start(), calls=%async_computation.42 | async-start | bytes 208896 | tf_op jit(solution)/shard_map/reduce_scatter | solution.py:331
  1928.5 366.3 %reduce-scatter.60.cloned.1.call-start = ((), (), s32[]{:S(2)}) async-start(), calls=%async_computation.47 | async-start | bytes 208896 | tf_op jit(solution)/shard_map/reduce_scatter | solution.py:355
  2215.7 107.2 %reduce-scatter.48.cloned.1.call-start = ((), (), s32[]{:S(2)}) async-start(), calls=%async_computation.41 | async-start | bytes 208896 | tf_op jit(solution)/shard_map/reduce_scatter | solution.py:355
  2265.1 340.4 %all-reduce.7.cloned.1.call-start = ((), (), s32[]{:S(2)}) async-start(), calls=%async_computation.56 | async-start | bytes 28311552
  2359.6 358.8 %reduce-scatter.64.cloned.1.call-start = ((), (), s32[]{:S(2)}) async-start(), calls=%async_computation.49 | async-start | bytes 4866048 | tf_op jit(solution)/shard_map/reduce_scatter | solution.py:498
  2367.5 562.7 %reduce-scatter.66.cloned.1.call-start = ((), (), s32[]{:S(2)}) async-start(), calls=%async_computation.50 | async-start | bytes 19464192 | tf_op jit(solution)/shard_map/reduce_scatter | solution.py:499
  2393.4 748.5 %reduce-scatter.68.cloned.1.call-start = ((), (), s32[]{:S(2)}) async-start(), calls=%async_computation.51 | async-start | bytes 19464192 | tf_op jit(solution)/shard_map/reduce_scatter | solution.py:500
  (665 other events, 7482.3 us)
Sparse Core Ops, SparseCore 0:
  11.0 60.0 all-gather.32
  74.0 56.2 all-gather.30
  133.2 56.2 all-gather.34
  193.4 54.4 reduce-scatter.25
  252.2 54.5 reduce-scatter.23
  310.2 54.5 reduce-scatter.33
  369.3 54.5 reduce-scatter.31
  426.8 61.5 all-gather.42
  490.7 61.0 all-gather.46
  554.6 56.1 all-gather.36
  613.8 81.6 all-gather.38
  698.3 80.9 all-gather.40
  867.2 54.1 reduce-scatter.29
  925.7 54.5 reduce-scatter.27
  983.6 54.6 reduce-scatter.37
  1042.1 54.6 reduce-scatter.35
  1099.5 62.5 all-gather.44
  1230.5 59.0 all-gather.48
  1452.9 52.6 reduce-scatter.39
  1509.1 52.6 reduce-scatter.55
  1565.3 52.6 reduce-scatter.43
  1720.9 50.8 reduce-scatter.53
  1775.1 52.6 reduce-scatter.41
  1944.0 52.6 reduce-scatter.45
  2000.0 52.6 reduce-scatter.61
  2056.2 52.6 reduce-scatter.49
  2215.8 50.8 reduce-scatter.59
  2270.0 52.7 reduce-scatter.47
  2359.7 245.7 all-reduce.6
  2611.6 106.8 reduce-scatter.63
  2726.4 203.6 reduce-scatter.65
  2938.2 203.6 reduce-scatter.67
  (2 shorter events, 101.5 us)
where the time goes:
time: 3170 us; the launch traced here: 3150 us
  waiting for transfers between devices  1080 us (34%)
  matrix products  920 us (29%)
  blocking collectives  600 us (19%)
  local copies, waits for them, and re-layouts  290 us (9%)
  other arithmetic  192 us (6%)
  starting transfers between devices  41.7 us (1%)
    reduce_scatter x1, waiting for transfers between devices, local(): lax.psum_scatter(full_sums[5], ('dp', 'sp'), scatter_dimension=1, tiled=T...  212 us
    reduce_scatter x1, waiting for transfers between devices, local(): lax.psum_scatter(full_sums[4], ('dp', 'sp'), scatter_dimension=1, tiled=T...  212 us
    all_gather x8, blocking collectives, joined(): everything = jax.tree.map(lambda part: lax.all_gather(part, axis), value)  150 us
    dot_general x72, matrix products, pseudo_inverse(): product = jnp.matmul(kernel, approx, precision=highest)  136 us
    reduce_scatter x4, waiting for transfers between devices, layer_forward(): lax.psum_scatter(rows_inner(onehot_low, query_low), 'sp', scatter_dimensi...  130 us
    reduce_scatter x1, waiting for transfers between devices, local(): lax.psum_scatter(full_sums[3], ('dp', 'sp'), scatter_dimension=1, tiled=T...  108 us
    dot_general x72, matrix products, pseudo_inverse(): jnp.matmul(approx, 13.0 * identity - nested, precision=highest)  104 us
    unnamed x35, waiting for transfers between devices  98.5 us
  transfers between devices with their start and end apart: 50, of which 18 were waited for; matrix products, arithmetic and copies ran while one was open for 38% of the time, Pallas kernels for 0%

commit v1 on v0

v1 whole, which is shorter than its diff:
```python
import functools

import jax
import jax.numpy as jnp
from jax import lax
from jax.experimental import pallas as pl
from jax.experimental.pallas import tpu as pltpu
from jax.sharding import PartitionSpec as P

HEADS = 12
HD = 64
LMK = 64
NS_ITERS = 6
KCONV = 33
DOCS = 2
HALO = 16
SLOTS = DOCS * LMK
PAIRS = HEADS // 2
WIDE = 2 * HD
WINDOW = 40
TAPS = 40

highest = lax.Precision.HIGHEST
negative = -1e30
epsilon = 1e-05
score_scale = HD ** (-0.5)
bf16 = jnp.bfloat16
f32 = jnp.float32


def nn(left, right):
    return lax.dot_general(left, right, (((1,), (0,)), ((), ())), preferred_element_type=f32)


def nt(left, right):
    return lax.dot_general(left, right, (((1,), (1,)), ((), ())), preferred_element_type=f32)


def tn(left, right):
    return lax.dot_general(left, right, (((0,), (0,)), ((), ())), preferred_element_type=f32)


def hnn(left, right):
    return lax.dot_general(
        left, right, (((1,), (0,)), ((), ())), precision=highest, preferred_element_type=f32
    )


def hnt(left, right):
    return lax.dot_general(
        left, right, (((1,), (1,)), ((), ())), precision=highest, preferred_element_type=f32
    )


def htn(left, right):
    return lax.dot_general(
        left, right, (((0,), (0,)), ((), ())), precision=highest, preferred_element_type=f32
    )


def iota(shape, dim):
    return lax.broadcasted_iota(jnp.int32, shape, dim)


def sums_kernel(ids_ref, qk_ref, out_ref):
    length = qk_ref.shape[0]
    onehot = (iota((SLOTS, length), 0) == ids_ref[0]).astype(f32).astype(bf16)
    for side in range(2):
        sums = nn(onehot, qk_ref[:, side * WIDE : (side + 1) * WIDE])
        for doc in range(DOCS):
            out_ref[0, doc, side] = sums[doc * LMK : (doc + 1) * LMK]


def marks_block(ref, side):
    return ref[0, :, side].astype(f32).reshape(SLOTS, WIDE)


def pair_lanes(length, first):
    return pl.BlockSpec((length, 2 * WIDE), lambda b, p: (b, first + p))


def one_lanes(length, first):
    return pl.BlockSpec((length, WIDE), lambda b, p: (b, first + p))


def task_spec():
    return pl.BlockSpec((1, DOCS, 2, LMK, WIDE), lambda b, p: (b, 0, p, 0, 0))


def task_shape(batches, dtype):
    return jax.ShapeDtypeStruct((batches, DOCS, HEADS, LMK, WIDE), dtype)


def local_sums(row_ids, qkv):
    batches, _, length = row_ids.shape
    return pl.pallas_call(
        sums_kernel,
        grid=(batches, PAIRS),
        in_specs=[
            pl.BlockSpec((1, 1, length), lambda b, p: (b, 0, 0)),
            pair_lanes(length, 0),
        ],
        out_specs=task_spec(),
        out_shape=task_shape(batches, f32),
        name="local_sums",
    )(row_ids, qkv)


def key_partial_kernel(ids_ref, qk_ref, v_ref, marks_ref, out_ref):
    length = qk_ref.shape[0]
    keep = (ids_ref[0] >> 6) == (iota((SLOTS, length), 0) >> 6)
    lane = iota((SLOTS, WIDE), 1)
    values = v_ref[...]
    for side in range(2):
        query_marks = jnp.where(lane >= HD, marks_block(marks_ref, side), 0.0).astype(bf16)
        scores = nt(query_marks, qk_ref[:, side * WIDE : (side + 1) * WIDE]) * score_scale
        scores = jnp.where(keep, scores, negative)
        top = jnp.max(scores, axis=1, keepdims=True)
        weights = jnp.where(keep, jnp.exp(scores - top), 0.0)
        total = jnp.sum(weights, axis=1, keepdims=True)
        numer = nn(weights.astype(bf16), values)
        if side:
            numer = pltpu.roll(numer, HD, 1)
        packed = jnp.where(lane < HD, numer, jnp.where(lane < HD + 32, top, total))
        for doc in range(DOCS):
            out_ref[0, doc, side] = packed[doc * LMK : (doc + 1) * LMK]


def key_partial(row_ids, qkv, marks):
    batches, _, length = row_ids.shape
    return pl.pallas_call(
        key_partial_kernel,
        grid=(batches, PAIRS),
        in_specs=[
            pl.BlockSpec((1, 1, length), lambda b, p: (b, 0, 0)),
            pair_lanes(length, 0),
            one_lanes(length, HEADS),
            task_spec(),
        ],
        out_specs=task_spec(),
        out_shape=task_shape(batches, f32),
        name="key_partial",
    )(row_ids, qkv, qkv, marks)


def identity():
    return (iota((LMK, LMK), 0) == iota((LMK, LMK), 1)).astype(f32)


def mark_softmax(query_marks, key_marks):
    scores = hnt(query_marks, key_marks) * score_scale
    weights = jnp.exp(scores - jnp.max(scores, axis=1, keepdims=True))
    return weights / jnp.sum(weights, axis=1, keepdims=True)


def newton(kernels, steps_ref=None):
    eye = identity()

    def sweep(index, approx):
        product = [hnn(k, x) for k, x in zip(kernels, approx)]
        middle = [15.0 * eye - hnn(p, 7.0 * eye - p) for p in product]
        outer = [13.0 * eye - hnn(p, c) for p, c in zip(product, middle)]
        if steps_ref is not None:
            for task, step in enumerate(zip(approx, product, middle, outer)):
                for slot, value in enumerate(step):
                    steps_ref[index, task, slot] = value
        return tuple(0.25 * hnn(x, e) for x, e in zip(approx, outer))

    start = tuple(jnp.swapaxes(kernel, 0, 1) / LMK for kernel in kernels)
    return lax.fori_loop(0, NS_ITERS, sweep, start)


def owner_kernel(sums_ref, inverse_ref, marks_ref, swapped_ref, pseudo_ref):
    count = marks_ref.shape[0]
    kernels = []
    for task in range(count):
        total = sums_ref[0, task]
        for part in range(1, sums_ref.shape[0]):
            total = total + sums_ref[part, task]
        marks = total * inverse_ref[task]
        marks_ref[task] = marks
        swapped_ref[task] = pltpu.roll(marks, HD, 1).astype(bf16)
        kernels.append(mark_softmax(marks[:, :HD], marks[:, HD:]))
    for task, pseudo in enumerate(newton(kernels)):
        pseudo_ref[task] = pseudo


def owner_marks(sums, inverse):
    count = sums.shape[1]
    return pl.pallas_call(
        owner_kernel,
        out_shape=(
            jax.ShapeDtypeStruct((count, LMK, WIDE), f32),
            jax.ShapeDtypeStruct((count, LMK, WIDE), bf16),
            jax.ShapeDtypeStruct((count, LMK, LMK), f32),
        ),
        name="owner_marks",
    )(sums, inverse)


def with_exact(left, column, lane):
    first = column.astype(bf16).astype(f32)
    second = (column - first).astype(bf16).astype(f32)
    third = column - first - second
    right = jnp.where(
        lane == HD, first, jnp.where(lane == HD + 1, second, jnp.where(lane == HD + 2, third, 0.0))
    )
    return jnp.where(lane < HD, left, right).astype(bf16)


def exact_column(block):
    return block[:, HD : HD + 1] + block[:, HD + 1 : HD + 2] + block[:, HD + 2 : HD + 3]


def merge_kernel(parts_ref, pseudo_ref, values_ref, payload_ref):
    count = values_ref.shape[0]
    lane = iota((LMK, WIDE), 1)
    for task in range(count):
        parts = [parts_ref[part, task] for part in range(parts_ref.shape[0])]
        tops = [part[:, HD : HD + 1] for part in parts]
        top = functools.reduce(jnp.maximum, tops)
        joined = sum(part * jnp.exp(t - top) for part, t in zip(parts, tops))
        total = joined[:, HD + 32 : HD + 33]
        values = joined / total
        values_ref[task] = values
        mixed = hnn(pseudo_ref[task], values)
        payload_ref[task] = with_exact(mixed, top + jnp.log(total), lane)


def owner_merge(parts, pseudo):
    count = parts.shape[1]
    return pl.pallas_call(
        merge_kernel,
        out_shape=(
            jax.ShapeDtypeStruct((count, LMK, WIDE), f32),
            jax.ShapeDtypeStruct((count, LMK, WIDE), bf16),
        ),
        name="owner_merge",
    )(parts, pseudo)


def fill_padded(pad_ref, low, center, high):
    length = center.shape[0]
    pad_ref[0:HALO] = low.astype(f32)
    pad_ref[HALO : HALO + length] = center.astype(f32)
    pad_ref[HALO + length : 2 * HALO + length] = high.astype(f32)


def same_side(start, bound, offset):
    rows = start + iota((WINDOW, WIDE), 0)
    return (rows < bound) == (rows + (offset - HALO) < bound)


def window_start(bound, length):
    start = jnp.clip(((bound - HALO) >> 3) << 3, 0, length - WINDOW)
    return pl.multiple_of(start, 8)


def convolve(pad_ref, taps_ref, bound, out_ref):
    length = out_ref.shape[0]
    block = 64
    for first in range(0, length, block):
        total = jnp.zeros((block, WIDE), f32)
        for offset in range(KCONV):
            total = total + pad_ref[first + offset : first + offset + block] * taps_ref[offset : offset + 1]
        out_ref[first : first + block] = total
    start = window_start(bound, length)
    total = jnp.zeros((WINDOW, WIDE), f32)
    for offset in range(KCONV):
        nearby = pad_ref[pl.ds(start + offset, WINDOW)]
        total = total + jnp.where(same_side(start, bound, offset), nearby, 0.0) * taps_ref[offset : offset + 1]
    out_ref[pl.ds(start, WINDOW)] = total


def taps_gradient(grad_ref, pad_ref, bound, out_ref):
    length = grad_ref.shape[0]
    start = window_start(bound, length)
    out_ref[0, KCONV:] = jnp.zeros((TAPS - KCONV, WIDE), f32)
    window = grad_ref[pl.ds(start, WINDOW)]
    for offset in range(KCONV):
        total = jnp.sum(grad_ref[...] * pad_ref[offset : offset + length], axis=0, keepdims=True)
        crossing = window * pad_ref[pl.ds(start + offset, WINDOW)]
        crossing = jnp.where(same_side(start, bound, offset), 0.0, crossing)
        out_ref[0, offset : offset + 1] = total - jnp.sum(crossing, axis=0, keepdims=True)


def token_weights(qk, marks, keep, lane):
    key_marks = jnp.where(lane < HD, marks, 0.0).astype(bf16)
    scores = jnp.where(keep, nt(qk, key_marks) * score_scale, negative)
    weights = jnp.exp(scores - jnp.max(scores, axis=1, keepdims=True))
    return key_marks, weights / jnp.sum(weights, axis=1, keepdims=True)


def half_values(ref, side, lane):
    block = jnp.where(lane < HD, marks_block(ref, side), 0.0)
    if side:
        block = pltpu.roll(block, HD, 1)
    return block.astype(bf16)


def token_kernel(
    bound_ref, ids_ref, qk_ref, v_ref, low_ref, high_ref, marks_ref, mixed_ref, taps_ref,
    out_ref, pad_ref, conv_ref,
):
    length = qk_ref.shape[0]
    fill_padded(pad_ref, low_ref[0], v_ref[...], high_ref[0])
    convolve(pad_ref, taps_ref, bound_ref[pl.program_id(0)], conv_ref)
    keep = (ids_ref[0] >> 6) == (iota((length, SLOTS), 1) >> 6)
    lane = iota((SLOTS, WIDE), 1)
    total = conv_ref[...]
    for side in range(2):
        _, weights = token_weights(
            qk_ref[:, side * WIDE : (side + 1) * WIDE], marks_block(marks_ref, side), keep, lane
        )
        total = total + nn(weights.astype(bf16), half_values(mixed_ref, side, lane))
    out_ref[...] = total.astype(bf16)


def halo_spec():
    return pl.BlockSpec((1, HALO, WIDE), lambda b, p, s: (b, 0, p))


def with_scalar(spec):
    return pl.BlockSpec(spec.block_shape, lambda b, p, s: spec.index_map(b, p))


def token_mix(bounds, col_ids, qkv, low, high, marks, mixed, taps):
    batches, length, _ = col_ids.shape
    return pl.pallas_call(
        token_kernel,
        grid_spec=pltpu.PrefetchScalarGridSpec(
            num_scalar_prefetch=1,
            grid=(batches, PAIRS),
            in_specs=[
                pl.BlockSpec((1, length, 1), lambda b, p, s: (b, 0, 0)),
                with_scalar(pair_lanes(length, 0)),
                with_scalar(one_lanes(length, HEADS)),
                halo_spec(),
                halo_spec(),
                with_scalar(task_spec()),
                with_scalar(task_spec()),
                pl.BlockSpec((TAPS, WIDE), lambda b, p, s: (0, p)),
            ],
            out_specs=with_scalar(one_lanes(length, 0)),
            scratch_shapes=[
                pltpu.VMEM((length + 2 * HALO, WIDE), f32),
                pltpu.VMEM((length, WIDE), f32),
            ],
        ),
        out_shape=jax.ShapeDtypeStruct((batches * length, HEADS * HD), bf16),
        name="token_mix",
    )(bounds, col_ids, qkv, qkv, low, high, marks, mixed, taps)


def token_back_kernel(
    bound_ref, ids_ref, qk_ref, v_ref, low_ref, high_ref, grad_ref, grad_low_ref, grad_high_ref,
    marks_ref, mixed_ref, taps_ref,
    dq_ref, task_ref, dv_ref, dtaps_ref, pad_ref, conv_ref,
):
    length = qk_ref.shape[0]
    bound = bound_ref[pl.program_id(0)]
    grad = grad_ref[...]
    fill_padded(pad_ref, grad_low_ref[0], grad, grad_high_ref[0])
    convolve(pad_ref, taps_ref, bound, conv_ref)
    dv_ref[...] = conv_ref[...]
    fill_padded(pad_ref, low_ref[0], v_ref[...], high_ref[0])
    taps_gradient(grad_ref, pad_ref, bound, dtaps_ref)
    keep = (ids_ref[0] >> 6) == (iota((length, SLOTS), 1) >> 6)
    lane = iota((SLOTS, WIDE), 1)
    grad_low = grad.astype(bf16)
    for side in range(2):
        qk = qk_ref[:, side * WIDE : (side + 1) * WIDE]
        key_marks, weights = token_weights(qk, marks_block(marks_ref, side), keep, lane)
        grad_weights = nt(grad_low, half_values(mixed_ref, side, lane))
        inner = jnp.sum(weights * grad_weights, axis=1, keepdims=True)
        grad_scores = (weights * (grad_weights - inner) * score_scale).astype(bf16)
        dq_ref[:, side * WIDE : (side + 1) * WIDE] = nn(grad_scores, key_marks)
        grad_keys = tn(grad_scores, qk)
        grad_mixed = tn(weights.astype(bf16), grad_low)
        if not side:
            grad_mixed = pltpu.roll(grad_mixed, HD, 1)
        packed = jnp.where(lane < HD, grad_keys, grad_mixed).astype(bf16)
        for doc in range(DOCS):
            task_ref[0, doc, side] = packed[doc * LMK : (doc + 1) * LMK]


def token_back(bounds, col_ids, qkv, low, high, grad, grad_low, grad_high, marks, mixed, taps):
    batches, length, _ = col_ids.shape
    rows = batches * length
    return pl.pallas_call(
        token_back_kernel,
        grid_spec=pltpu.PrefetchScalarGridSpec(
            num_scalar_prefetch=1,
            grid=(batches, PAIRS),
            in_specs=[
                pl.BlockSpec((1, length, 1), lambda b, p, s: (b, 0, 0)),
                with_scalar(pair_lanes(length, 0)),
                with_scalar(one_lanes(length, HEADS)),
                halo_spec(),
                halo_spec(),
                with_scalar(one_lanes(length, 0)),
                halo_spec(),
                halo_spec(),
                with_scalar(task_spec()),
                with_scalar(task_spec()),
                pl.BlockSpec((TAPS, WIDE), lambda b, p, s: (0, p)),
            ],
            out_specs=[
                with_scalar(pair_lanes(length, 0)),
                with_scalar(task_spec()),
                with_scalar(one_lanes(length, 0)),
                pl.BlockSpec((1, TAPS, WIDE), lambda b, p, s: (b, 0, p)),
            ],
            scratch_shapes=[
                pltpu.VMEM((length + 2 * HALO, WIDE), f32),
                pltpu.VMEM((length, WIDE), f32),
            ],
        ),
        out_shape=(
            jax.ShapeDtypeStruct((rows, HEADS * WIDE), f32),
            task_shape(batches, bf16),
            jax.ShapeDtypeStruct((rows, HEADS * HD), f32),
            jax.ShapeDtypeStruct((batches, TAPS, HEADS * HD), f32),
        ),
        name="token_back",
    )(bounds, col_ids, qkv, qkv, low, high, grad, grad_low, grad_high, marks, mixed, taps)


def owner_back_kernel(parts_ref, pseudo_ref, values_ref, total_ref, payload_ref):
    count = values_ref.shape[0]
    lane = iota((LMK, WIDE), 1)
    for task in range(count):
        total = parts_ref[0, task].astype(f32)
        for part in range(1, parts_ref.shape[0]):
            total = total + parts_ref[part, task].astype(f32)
        total_ref[task] = total
        grad_values = htn(pseudo_ref[task], pltpu.roll(total, HD, 1))
        inner = jnp.sum(
            jnp.where(lane < HD, grad_values * values_ref[task], 0.0), axis=1, keepdims=True
        )
        payload_ref[task] = with_exact(grad_values, inner, lane)


def owner_back(parts, pseudo, values):
    count = parts.shape[1]
    return pl.pallas_call(
        owner_back_kernel,
        out_shape=(
            jax.ShapeDtypeStruct((count, LMK, WIDE), f32),
            jax.ShapeDtypeStruct((count, LMK, WIDE), bf16),
        ),
        name="owner_back",
    )(parts, pseudo, values)


def newton_back_kernel(marks_ref, values_ref, total_ref, out_ref, steps_ref):
    count = marks_ref.shape[0]
    tasks = range(count)
    marks = [marks_ref[task] for task in tasks]
    queries = [m[:, :HD] for m in marks]
    keys = [m[:, HD:] for m in marks]
    kernels = [mark_softmax(q, k) for q, k in zip(queries, keys)]
    newton(kernels, steps_ref)
    eye = identity()

    def sweep(index, carry):
        results = []
        for task in tasks:
            grad, grad_kernel = carry[task]
            approx, product, middle, outer = (
                steps_ref[NS_ITERS - 1 - index, task, slot] for slot in range(4)
            )
            grad_outer = 0.25 * htn(approx, grad)
            grad_middle = -htn(product, grad_outer)
            grad_inner = -htn(product, grad_middle)
            grad_product = (
                -hnt(grad_outer, middle) - hnt(grad_middle, 7.0 * eye - product) - grad_inner
            )
            grad_kernel = grad_kernel + hnt(grad_product, approx)
            grad = 0.25 * hnt(grad, outer) + htn(kernels[task], grad_product)
            results.append((grad, grad_kernel))
        return tuple(results)

    start = tuple(
        (hnt(total_ref[task][:, HD:], values_ref[task][:, :HD]), jnp.zeros((LMK, LMK), f32))
        for task in tasks
    )
    ends = lax.fori_loop(0, NS_ITERS, sweep, start)
    for task in tasks:
        grad, grad_kernel = ends[task]
        grad_kernel = grad_kernel + jnp.swapaxes(grad, 0, 1) / LMK
        kernel = kernels[task]
        inner = jnp.sum(kernel * grad_kernel, axis=1, keepdims=True)
        grad_scores = kernel * (grad_kernel - inner) * score_scale
        grad_queries = hnn(grad_scores, keys[task])
        grad_keys = htn(grad_scores, queries[task]) + total_ref[task][:, :HD]
        out_ref[task] = jnp.concatenate([grad_queries, grad_keys], axis=1)


def newton_back(marks, values, total):
    return pl.pallas_call(
        newton_back_kernel,
        out_shape=jax.ShapeDtypeStruct(marks.shape, f32),
        scratch_shapes=[pltpu.VMEM((NS_ITERS, marks.shape[0], 4, LMK, LMK), f32)],
        name="newton_back",
    )(marks, values, total)


def key_back_kernel(
    ids_ref, qk_ref, v_ref, marks_ref, mixed_ref, grads_ref, dq_ref, dconv_ref,
    dqk_ref, dv_ref, part_ref,
):
    length = qk_ref.shape[0]
    keep = (ids_ref[0] >> 6) == (iota((SLOTS, length), 0) >> 6)
    lane = iota((SLOTS, WIDE), 1)
    half = iota((LMK // 2, WIDE), 1)
    values = v_ref[...]
    grad_values = dconv_ref[...]
    for side in range(2):
        qk = qk_ref[:, side * WIDE : (side + 1) * WIDE]
        query_marks = jnp.where(lane >= HD, marks_block(marks_ref, side), 0.0).astype(bf16)
        scores = nt(query_marks, qk) * score_scale
        level = exact_column(marks_block(mixed_ref, side))
        probs = jnp.where(keep, jnp.exp(scores - level), 0.0)
        inner = exact_column(marks_block(grads_ref, side))
        grad_marks = half_values(grads_ref, side, lane)
        grad_probs = nt(grad_marks, values)
        grad_scores = (probs * (grad_probs - inner) * score_scale).astype(bf16)
        dqk_ref[:, side * WIDE : (side + 1) * WIDE] = dq_ref[
            :, side * WIDE : (side + 1) * WIDE
        ] + tn(grad_scores, query_marks)
        grad_values = grad_values + tn(probs.astype(bf16), grad_marks)
        part = nn(grad_scores, qk)
        for doc in range(DOCS):
            upper = part[doc * LMK : doc * LMK + LMK // 2]
            lower = part[doc * LMK + LMK // 2 : (doc + 1) * LMK]
            part_ref[0, doc, side] = jnp.where(half < HD, pltpu.roll(upper, HD, 1), lower).astype(
                bf16
            )
    dv_ref[...] = grad_values.astype(bf16)


def key_back(row_ids, qkv, marks, mixed, grads, dq, dconv):
    batches, _, length = row_ids.shape
    rows = batches * length
    return pl.pallas_call(
        key_back_kernel,
        grid=(batches, PAIRS),
        in_specs=[
            pl.BlockSpec((1, 1, length), lambda b, p: (b, 0, 0)),
            pair_lanes(length, 0),
            one_lanes(length, HEADS),
            task_spec(),
            task_spec(),
            task_spec(),
            pair_lanes(length, 0),
            one_lanes(length, 0),
        ],
        out_specs=[
            pair_lanes(length, 0),
            one_lanes(length, 0),
            pl.BlockSpec((1, DOCS, 2, LMK // 2, WIDE), lambda b, p: (b, 0, p, 0, 0)),
        ],
        out_shape=(
            jax.ShapeDtypeStruct((rows, HEADS * WIDE), f32),
            jax.ShapeDtypeStruct((rows, HEADS * HD), bf16),
            jax.ShapeDtypeStruct((batches, DOCS, HEADS, LMK // 2, WIDE), bf16),
        ),
        name="key_back",
    )(row_ids, qkv, qkv, marks, mixed, grads, dq, dconv)


def spread_kernel(ids_ref, marks_ref, dqk_ref, out_ref):
    length = dqk_ref.shape[0]
    onehot = (iota((length, SLOTS), 1) == ids_ref[0]).astype(f32).astype(bf16)
    for side in range(2):
        marks = marks_block(marks_ref, side).astype(bf16)
        lanes = slice(side * WIDE, (side + 1) * WIDE)
        out_ref[:, lanes] = (dqk_ref[:, lanes] + nn(onehot, marks)).astype(bf16)


def spread(col_ids, marks, dqk):
    batches, length, _ = col_ids.shape
    return pl.pallas_call(
        spread_kernel,
        grid=(batches, PAIRS),
        in_specs=[
            pl.BlockSpec((1, length, 1), lambda b, p: (b, 0, 0)),
            task_spec(),
            pair_lanes(length, 0),
        ],
        out_specs=pair_lanes(length, 0),
        out_shape=jax.ShapeDtypeStruct(dqk.shape, bf16),
        name="spread",
    )(col_ids, marks, dqk)


def norm_apply(summed, layer_gain, layer_bias):
    center = summed - jnp.mean(summed, axis=-1, keepdims=True)
    spread_of = jnp.mean(center * center, axis=-1, keepdims=True)
    return center * lax.rsqrt(spread_of + epsilon) * layer_gain + layer_bias


def gelu_tanh(values):
    return jax.nn.gelu(values, approximate=True)


def to_owners(tasks, axis):
    count = lax.axis_size(axis)
    flat = tasks.reshape((-1,) + tasks.shape[3:])
    each = -(-flat.shape[0] // count)
    short = each * count - flat.shape[0]
    if short:
        flat = jnp.pad(flat, ((0, short),) + ((0, 0),) * (flat.ndim - 1))
    flat = flat.reshape((count, each) + flat.shape[1:])
    return lax.all_to_all(flat, axis, 0, 0)


def from_owners(owned, axis, batches):
    whole = lax.all_gather(owned, axis, axis=0, tiled=True)
    tasks = batches * DOCS * HEADS
    return whole[:tasks].reshape((batches, DOCS, HEADS) + owned.shape[1:])


def halo_of(block, axis, batches):
    count = lax.axis_size(axis)
    rows = block.reshape(batches, -1, block.shape[-1])
    forward = [(i, i + 1) for i in range(count - 1)]
    backward = [(i + 1, i) for i in range(count - 1)]
    low = lax.ppermute(rows[:, rows.shape[1] - HALO :], axis, forward)
    high = lax.ppermute(rows[:, :HALO], axis, backward)
    return low, high


def slot_counts(row_bounds):
    starts = row_bounds[:, :DOCS]
    sizes = row_bounds[:, 1 : DOCS + 1] - starts
    index = jnp.arange(LMK, dtype=jnp.int32)
    upper = ((index + 1) * sizes[..., None] + LMK - 1) // LMK
    lower = (index * sizes[..., None] + LMK - 1) // LMK
    return (upper - lower).astype(f32)


def interleave(query, key):
    rows = query.shape[0]
    pair = jnp.stack([query.reshape(rows, HEADS, HD), key.reshape(rows, HEADS, HD)], axis=2)
    return pair.reshape(rows, HEADS * WIDE)


def local(
    tokens,
    doc_ids,
    doc_bounds,
    landmark_ids,
    query_weight,
    key_weight,
    value_weight,
    out_weight,
    conv_kernel,
    up_weight,
    down_weight,
    norm_gain,
    norm_bias,
    cotangent,
):
    batches, _, length, width = tokens.shape
    layers = query_weight.shape[0]
    rows = batches * length
    shard = query_weight.shape[1]
    hidden_units = up_weight.shape[2]
    folds = hidden_units // width
    every = ("dp", "sp")
    position = lax.axis_index("sp")
    devices = lax.axis_size("sp")

    row_ids = landmark_ids.reshape(batches, 1, length)
    col_ids = landmark_ids.reshape(batches, length, 1)
    bounds = doc_bounds[:, 0]
    local_bound = bounds[:, 1] - position * length
    counts = slot_counts(bounds)
    tasks = batches * DOCS * HEADS
    each = -(-tasks // devices)
    inverse = jnp.broadcast_to((1.0 / counts)[:, :, None, :], (batches, DOCS, HEADS, LMK))
    inverse = jnp.pad(
        inverse.reshape(tasks, LMK, 1), ((0, each * devices - tasks), (0, 0), (0, 0)), constant_values=1.0
    )
    inverse = lax.dynamic_slice_in_dim(inverse, position * each, each, 0)

    first = []
    second = []
    for layer in range(layers):
        first.append(
            jnp.concatenate(
                [interleave(query_weight[layer], key_weight[layer]), value_weight[layer]], axis=1
            )
        )
        up_folded = jnp.swapaxes(up_weight[layer].reshape(shard, width, folds), 1, 2)
        second.append(
            jnp.concatenate(
                [
                    out_weight[layer],
                    up_folded.reshape(shard, hidden_units),
                    down_weight[layer].reshape(shard, hidden_units),
                ],
                axis=1,
            )
        )
    gathered = []
    for layer in range(layers):
        if layer == 0:
            head = lax.all_gather(first[0], every, axis=0, tiled=True)
            tail = lax.all_gather(second[0], every, axis=0, tiled=True)
        else:
            both = lax.all_gather(
                jnp.concatenate([first[layer], second[layer]], axis=1), every, axis=0, tiled=True
            )
            head, tail = both[:, : 3 * width], both[:, 3 * width :]
        gathered.append(
            (
                head,
                tail[:, :width],
                tail[:, width : width + hidden_units],
                tail[:, width + hidden_units :],
            )
        )

    taps = [
        jnp.pad(jnp.repeat(conv_kernel[layer].T, HD, axis=1), ((0, TAPS - KCONV), (0, 0)))
        for layer in range(layers)
    ]
    flipped = [
        jnp.pad(jnp.repeat(conv_kernel[layer].T[::-1], HD, axis=1), ((0, TAPS - KCONV), (0, 0)))
        for layer in range(layers)
    ]

    hidden = tokens.reshape(rows, width).astype(f32)
    saved = []
    for layer in range(layers):
        qkv_weight, out_w, up_w, down_w = gathered[layer]
        hidden_low = hidden.astype(bf16)
        qkv = nn(hidden_low, qkv_weight).astype(bf16)
        low, high = halo_of(qkv[:, 2 * width :], "sp", batches)
        sums = to_owners(local_sums(row_ids, qkv), "sp")
        marks, swapped, pseudo = owner_marks(sums, inverse)
        all_marks = from_owners(swapped, "sp", batches)
        parts = to_owners(key_partial(row_ids, qkv, all_marks), "sp")
        values, payload = owner_merge(parts, pseudo)
        all_mixed = from_owners(payload, "sp", batches)
        branch = token_mix(
            local_bound, col_ids, qkv, low, high, all_marks, all_mixed, taps[layer]
        )
        gain, bias = norm_gain[layer], norm_bias[layer]
        normed, first_pull = jax.vjp(norm_apply, hidden + nn(branch, out_w), gain[0], bias[0])
        normed_low = normed.astype(bf16)
        expanded = nn(normed_low, up_w)
        activated, gelu_pull = jax.vjp(gelu_tanh, expanded)
        activated_low = activated.astype(bf16)
        dense = sum(
            nn(activated_low[:, s * width : (s + 1) * width], down_w[:, s * width : (s + 1) * width])
            for s in range(folds)
        )
        hidden, second_pull = jax.vjp(norm_apply, normed + dense, gain[1], bias[1])
        saved.append(
            (hidden_low, qkv, low, high, marks, pseudo, all_marks, values, all_mixed, branch,
             first_pull, normed_low, gelu_pull, activated_low, second_pull)
        )
    output = hidden.astype(bf16).reshape(batches, 1, length, width)

    grad = cotangent.reshape(rows, width).astype(f32)
    shards = [None] * layers
    small = [None] * layers
    for layer in reversed(range(layers)):
        qkv_weight, out_w, up_w, down_w = gathered[layer]
        (hidden_low, qkv, low, high, marks, pseudo, all_marks, values, all_mixed, branch,
         first_pull, normed_low, gelu_pull, activated_low, second_pull) = saved[layer]
        grad_second, gain_second, bias_second = second_pull(grad)
        dense_grad = grad_second.astype(bf16)
        grad_active = nt(
            dense_grad,
            jnp.swapaxes(down_w.reshape(width, folds, width), 0, 1).reshape(hidden_units, width),
        )
        (grad_expanded,) = gelu_pull(grad_active)
        expanded_grad = grad_expanded.astype(bf16)
        grad_first, gain_first, bias_first = first_pull(grad_second + nt(expanded_grad, up_w))
        projected_grad = grad_first.astype(bf16)
        branch_grad = nt(projected_grad, out_w)
        grad_low, grad_high = halo_of(branch_grad.astype(bf16), "sp", batches)
        dq, task_grads, dconv, dtaps = token_back(
            local_bound, col_ids, qkv, low, high, branch_grad, grad_low, grad_high,
            all_marks, all_mixed, flipped[layer],
        )
        total, payload = owner_back(to_owners(task_grads, "sp"), pseudo, values)
        all_grads = from_owners(payload, "sp", batches)
        own_grads = newton_back(marks, values, total)
        dqk, dv, query_part = key_back(row_ids, qkv, all_marks, all_mixed, all_grads, dq, dconv)
        query_sum = jnp.sum(to_owners(query_part, "sp").astype(f32), axis=0)
        query_sum = jnp.swapaxes(query_sum.reshape(each, LMK // 2, 2, HD), 1, 2).reshape(
            each, LMK, HD
        )
        own_grads = (own_grads + jnp.pad(query_sum, ((0, 0), (0, 0), (0, HD)))) * inverse
        mark_grads = from_owners(own_grads.astype(bf16), "sp", batches)
        dqk = spread(col_ids, mark_grads, dqk)
        grad = (
            grad_first
            + nt(dqk, qkv_weight[:, : 2 * width])
            + nt(dv, qkv_weight[:, 2 * width :])
        )
        pieces = [
            tn(hidden_low, dqk),
            tn(hidden_low, dv),
            tn(branch, projected_grad),
            tn(normed_low, expanded_grad),
        ] + [tn(activated_low[:, s * width : (s + 1) * width], dense_grad) for s in range(folds)]
        stacked = jnp.concatenate([piece.astype(bf16) for piece in pieces], axis=1)
        shards[layer] = lax.psum_scatter(stacked, every, scatter_dimension=0, tiled=True)
        conv_grad = jnp.sum(dtaps, axis=0)[:KCONV].reshape(KCONV, HEADS, HD).sum(axis=-1).T
        small[layer] = (
            conv_grad,
            jnp.stack([gain_first, gain_second]),
            jnp.stack([bias_first, bias_second]),
        )
    grad_tokens = grad.reshape(batches, 1, length, width)
    conv_sum, gain_sum, bias_sum = lax.psum(
        tuple(jnp.stack([small[layer][k] for layer in range(layers)]) for k in range(3)), every
    )
    results = [[] for _ in range(6)]
    for layer in range(layers):
        whole = shards[layer].astype(f32)
        pair = whole[:, : 2 * width].reshape(shard, HEADS, 2, HD)
        results[0].append(pair[:, :, 0].reshape(shard, width))
        results[1].append(pair[:, :, 1].reshape(shard, width))
        results[2].append(whole[:, 2 * width : 3 * width])
        results[3].append(whole[:, 3 * width : 4 * width])
        up_grad = whole[:, 4 * width : 4 * width + hidden_units].reshape(shard, folds, width)
        results[4].append(jnp.swapaxes(up_grad, 1, 2).reshape(shard, hidden_units))
        results[5].append(whole[:, 4 * width + hidden_units :].reshape(shard * folds, width))
    grads = [jnp.stack(parts) for parts in results]
    return (
        output,
        grad_tokens,
        grads[0],
        grads[1],
        grads[2],
        grads[3],
        conv_sum,
        grads[4],
        grads[5],
        gain_sum,
        bias_sum,
    )


def solution(mesh):
    tokens_spec = P(None, "dp", "sp", None)
    ids_spec = P(None, "dp", "sp")
    weight_spec = P(None, ("dp", "sp"), None)
    return jax.shard_map(
        local,
        mesh=mesh,
        in_specs=(
            tokens_spec,
            ids_spec,
            P(None, "dp", None),
            ids_spec,
            weight_spec,
            weight_spec,
            weight_spec,
            weight_spec,
            P(),
            weight_spec,
            weight_spec,
            P(),
            P(),
            tokens_spec,
        ),
        out_specs=(
            tokens_spec,
            tokens_spec,
            weight_spec,
            weight_spec,
            weight_spec,
            weight_spec,
            P(),
            weight_spec,
            weight_spec,
            P(),
            P(),
        ),
        check_vma=False,
    )
```

time: 3170 us -> 1160 us (0.37)
  waiting for transfers between devices: 1080 us -> 252 us
  matrix products: 920 us -> 133 us
  Pallas kernels: 0 us -> 246 us
  blocking collectives: 600 us -> 358 us
  local copies, waits for them, and re-layouts: 290 us -> 83.9 us
  other arithmetic: 192 us -> 21.4 us
    dot_general x472 -> x40, matrix products: 920 us -> 133 us  [the longest x14 48.2 us: nn(): lax.dot_general(left, right, (((1,), (0,)), ((), ())), preferred_element_...]
    reduce_scatter x23 -> x2, waiting for transfers between devices: 816 us -> 104 us  [local(): lax.psum_scatter(stacked, every, scatter_dimension=0, tiled=True)]
    all_gather x28 -> x8, blocking collectives: 561 us -> 222 us  [from_owners(): whole = lax.all_gather(owned, axis, axis=0, tiled=True)]
    pallas_call x0 -> x20, Pallas kernels: none -> 246 us  [the longest x2 58.4 us: token_back(): pl.pallas_call(token_back_kernel, grid_spec=pltpu.PrefetchScalarGridSpec(...]
    add x132 -> x1, other arithmetic: 124 us -> 0.01 us  [slot_counts(): upper = ((index + 1) * sizes[..., None] + LMK - 1) // LMK]
    all_gather x10 -> x3, waiting for transfers between devices: 164 us -> 58.8 us  [the longest x1 58.8 us: local(): head = lax.all_gather(first[0], every, axis=0, tiled=True)]
    unnamed x35 -> x5, waiting for transfers between devices: 98.5 us -> 0.08 us
    all_to_all x0 -> x3, blocking collectives: none -> 97.9 us  [to_owners(): return lax.all_to_all(flat, axis, 0, 0)]
  transfers between devices with their start and end apart: 50 -> 18, of which waited for: 18 -> 7; matrix products, arithmetic and copies ran while one was open for 38% -> 14% of each run, Pallas kernels for 0% -> 13%
where the time goes in v1:
time: 1160 us; the launch traced here: 1140 us
  blocking collectives  358 us (31%)
  waiting for transfers between devices  252 us (22%)
  Pallas kernels  246 us (21%)
  matrix products  133 us (11%)
  local copies, waits for them, and re-layouts  83.9 us (7%)
  starting transfers between devices  35.1 us (3%)
  other arithmetic  21.4 us (2%)
  between operations  15.5 us (1%)
    all_gather x8, blocking collectives, from_owners(): whole = lax.all_gather(owned, axis, axis=0, tiled=True)  222 us
    reduce_scatter x2, waiting for transfers between devices, local(): lax.psum_scatter(stacked, every, scatter_dimension=0, tiled=True)  104 us
    all_to_all x3, blocking collectives, to_owners(): return lax.all_to_all(flat, axis, 0, 0)  97.9 us
    all_to_all x5, waiting for transfers between devices, to_owners(): return lax.all_to_all(flat, axis, 0, 0)  87.4 us
    all_gather x1, waiting for transfers between devices, local(): head = lax.all_gather(first[0], every, axis=0, tiled=True)  58.8 us
    pallas_call x2, Pallas kernels, token_back(): pl.pallas_call(token_back_kernel, grid_spec=pltpu.PrefetchScalarGridSpec(...  58.4 us
    dot_general x14, matrix products, nn(): lax.dot_general(left, right, (((1,), (0,)), ((), ())), preferred_element_...  48.2 us
    dot_general x16, matrix products, tn(): lax.dot_general(left, right, (((0,), (0,)), ((), ())), preferred_element_...  44.1 us
  transfers between devices with their start and end apart: 18, of which 7 were waited for; matrix products, arithmetic and copies ran while one was open for 14% of the time, Pallas kernels for 13%

profile of v1, /device:TPU:0, one launch (start us, length us, event | category | flops | bytes accessed | tf_op | source)
XLA Modules:
  0.0 1144.5 jit_solution(16923313581788989438)
XLA Ops:
  15.6 58.8 %all-gather.4.cloned.1.call-done = bf16[768,2304]{1,0:T(8,128)(2,1)} async-done(((bf16[24,2304]{1,0:T(8,128)(2,1)}), bf16[768,2304]{1,0:T(8,128)(2,1)}) %all-gather.4.cloned.1.call-update) | async-done | bytes 3538960 | tf_op jit(solution)/shard_map/all_gather | solution.py:711
  79.9 8.2 local_sums.2
  95.0 43.0 %all-to-all-done.sums_ref = f32[16,3,64,128]{3,2,1,0:T(8,128)S(1)} async-done(((f32[16,3,64,128]{3,2,1,0:T(8,128)}), f32[16,3,64,128]{3,2,1,0:T(8,128)S(1)}, u32[]{:S(2)}, u32[]{:S(2)}) %all-to-all-start) | async-done | bytes 1572896 | tf_op jit(solution)/shard_map/all_to_all | solution.py:616
  146.8 34.1 %all_gather.34 = bf16[48,64,128]{2,1,0:T(8,128)(2,1)} all-gather(bf16[3,64,128]{2,1,0:T(8,128)(2,1)} %get-tuple-element.39), channel_id=1, replica_groups=mesh['dp'=2,'sp'=16] {'sp'}, dimensions={0}, use_global_device_ids=true | all-gather | bytes 835584 | tf_op jit(solution)/shard_map/all_gather | solution.py:620
  180.9 11.8 %key_partial.2 = f32[2,2,12,64,128]{4,3,2,1,0:T(8,128)} custom-call(s32[2,1,256]{2,1,0:T(1,128)} %ids_ref.11, bf16[512,2304]{1,0:T(8,128)(2,1)} %fusion.24.qk_ref.v_ref, bf16[512,2304]{1,0:T(8,128)(2,1)} %fusion.24.qk_ref.v_ref, bf16[2,2,12,64,128]{4,3,2,1,0:T(8,128)(2,1)} %bitcast.150), custom_call_target="tpu_custom_call" | custom-call | tf_op jit(solution)/shard_map/key_partial/pallas_call | solution.py:131
  202.9 35.1 %all-to-all-done.1.parts_ref = f32[16,3,64,128]{3,2,1,0:T(8,128)S(1)} async-done(((f32[16,3,64,128]{3,2,1,0:T(8,128)}), f32[16,3,64,128]{3,2,1,0:T(8,128)S(1)}, u32[]{:S(2)}, u32[]{:S(2)}) %all-to-all-start.1) | async-done | bytes 1572896 | tf_op jit(solution)/shard_map/all_to_all | solution.py:616
  242.4 35.1 %all_gather.35 = bf16[48,64,128]{2,1,0:T(8,128)(2,1)} all-gather(bf16[3,64,128]{2,1,0:T(8,128)(2,1)} %get-tuple-element.41), channel_id=1, replica_groups=mesh['dp'=2,'sp'=16] {'sp'}, dimensions={0}, use_global_device_ids=true | all-gather | bytes 835584 | tf_op jit(solution)/shard_map/all_gather | solution.py:620
  278.1 17.4 %token_mix.2 = bf16[512,768]{1,0:T(8,128)(2,1)} custom-call(s32[2]{0:T(128)} %subtract_reduce_fusion.bound_ref, s32[2,256,1]{2,1,0:T(8,128)} %reshape.389.ids_ref, bf16[512,2304]{1,0:T(8,128)(2,1)} %fusion.24.qk_ref.v_ref, bf16[512,2304]{1,0:T(8,128)(2,1)} %fusion.24.qk_ref.v_ref, bf16[2,16,768]{2,1,0:T(8,128)(2,1)} %copy-done.25, ...), custom_call_target="tpu_custom_call" | custom-call | tf_op jit(solution)/shard_map/token_mix/pallas_call | solution.py:329
  298.2 9.3 multiply_convert_fusion.1
  331.6 40.5 %all_to_all.40.sums_ref = f32[16,3,64,128]{3,2,1,0:T(8,128)} all-to-all(f32[16,3,64,128]{3,2,1,0:T(8,128)} %bitcast.169), channel_id=1, replica_groups=mesh['dp'=2,'sp'=16] {'sp'}, dimensions={0} | all-to-all | bytes 3145728 | tf_op jit(solution)/shard_map/all_to_all | solution.py:616
  379.7 24.5 %all_gather.38 = bf16[48,64,128]{2,1,0:T(8,128)(2,1)} all-gather(bf16[3,64,128]{2,1,0:T(8,128)(2,1)} %get-tuple-element.42), channel_id=1, replica_groups=mesh['dp'=2,'sp'=16] {'sp'}, dimensions={0}, use_global_device_ids=true | all-gather | bytes 835584 | tf_op jit(solution)/shard_map/all_gather | solution.py:620
  404.2 11.7 %key_partial.3 = f32[2,2,12,64,128]{4,3,2,1,0:T(8,128)} custom-call(s32[2,1,256]{2,1,0:T(1,128)} %ids_ref.11, bf16[512,2304]{1,0:T(8,128)(2,1)} %convolution_convert_fusion.3.qk_ref.v_ref, bf16[512,2304]{1,0:T(8,128)(2,1)} %convolution_convert_fusion.3.qk_ref.v_ref, bf16[2,2,12,64,128]{4,3,2,1,0:T(8,128)(2,1)} %bitcast.154), custom_call_target="tpu_custom_call" | custom-call | tf_op jit(solution)/shard_map/key_partial/pallas_call | solution.py:131
  443.4 9.3 all-to-all-done.3.parts_ref
  455.8 28.7 %all_gather.39 = bf16[48,64,128]{2,1,0:T(8,128)(2,1)} all-gather(bf16[3,64,128]{2,1,0:T(8,128)(2,1)} %get-tuple-element.44), channel_id=1, replica_groups=mesh['dp'=2,'sp'=16] {'sp'}, dimensions={0}, use_global_device_ids=true | all-gather | bytes 835584 | tf_op jit(solution)/shard_map/all_gather | solution.py:620
  485.1 17.2 %token_mix.3 = bf16[512,768]{1,0:T(8,128)(2,1)} custom-call(s32[2]{0:T(128)} %subtract_reduce_fusion.bound_ref, s32[2,256,1]{2,1,0:T(8,128)} %reshape.389.ids_ref, bf16[512,2304]{1,0:T(8,128)(2,1)} %convolution_convert_fusion.3.qk_ref.v_ref, bf16[512,2304]{1,0:T(8,128)(2,1)} %convolution_convert_fusion.3.qk_ref.v_ref, bf16[2,16,768]{2,1,0:T(8,128)(2,1)} %copy-done.27, ...), custom_call_target="tpu_custom_call" | custom-call | tf_op jit(solution)/shard_map/token_mix/pallas_call | solution.py:329
  505.1 9.6 multiply_convert_fusion
  542.9 29.2 %token_back.2 = (f32[512,1536]{1,0:T(8,128)}, bf16[2,2,12,64,128]{4,3,2,1,0:T(8,128)(2,1)}, f32[512,768]{1,0:T(8,128)}, f32[2,40,768]{2,1,0:T(8,128)}) custom-call(s32[2]{0:T(128)} %subtract_reduce_fusion.bound_ref, s32[2,256,1]{2,1,0:T(8,128)} %reshape.389.ids_ref, bf16[512,2304]{1,0:T(8,128)(2,1)} %convolution_convert_fusion.3.qk_ref.v_ref, ...), custom_call_target="tpu_custom_call" | custom-call | tf_op jit(solution)/shard_map/token_back/pallas_call | solution.py:390
  572.1 25.0 %all_to_all.41.parts_ref = bf16[16,3,64,128]{3,2,1,0:T(8,128)(2,1)} all-to-all(bf16[16,3,64,128]{3,2,1,0:T(8,128)(2,1)} %bitcast.193), channel_id=1, replica_groups=mesh['dp'=2,'sp'=16] {'sp'}, dimensions={0} | all-to-all | bytes 1572864 | tf_op jit(solution)/shard_map/all_to_all | solution.py:616
  599.4 23.4 %all_gather.40 = bf16[48,64,128]{2,1,0:T(8,128)(2,1)} all-gather(bf16[3,64,128]{2,1,0:T(8,128)(2,1)} %get-tuple-element.49), channel_id=1, replica_groups=mesh['dp'=2,'sp'=16] {'sp'}, dimensions={0}, use_global_device_ids=true | all-gather | bytes 835584 | tf_op jit(solution)/shard_map/all_gather | solution.py:620
  622.8 13.4 %key_back.2 = (f32[512,1536]{1,0:T(8,128)}, bf16[512,768]{1,0:T(8,128)(2,1)}, bf16[2,2,12,32,128]{4,3,2,1,0:T(8,128)(2,1)}) custom-call(s32[2,1,256]{2,1,0:T(1,128)} %ids_ref.11, bf16[512,2304]{1,0:T(8,128)(2,1)} %convolution_convert_fusion.3.qk_ref.v_ref, bf16[512,2304]{1,0:T(8,128)(2,1)} %convolution_convert_fusion.3.qk_ref.v_ref, ...), custom_call_target="tpu_custom_call" | custom-call | tf_op jit(solution)/shard_map/key_back/pallas_call | solution.py:546
  639.9 20.8 %newton_back.2 = f32[3,64,128]{2,1,0:T(8,128)} custom-call(f32[3,64,128]{2,1,0:T(8,128)} %get-tuple-element.45.marks_ref, f32[3,64,128]{2,1,0:T(8,128)} %get-tuple-element.46.values_ref, f32[3,64,128]{2,1,0:T(8,128)} %get-tuple-element.48.total_ref), custom_call_target="tpu_custom_call" | custom-call | tf_op jit(solution)/shard_map/newton_back/pallas_call | solution.py:501
  661.9 25.3 %all_gather.41 = bf16[48,64,128]{2,1,0:T(8,128)(2,1)} all-gather(bf16[3,64,128]{2,1,0:T(8,128)(2,1)S(1)} %multiply_convert_fusion.3), channel_id=1, replica_groups=mesh['dp'=2,'sp'=16] {'sp'}, dimensions={0}, use_global_device_ids=true | all-gather | bytes 835584 | tf_op jit(solution)/shard_map/all_gather | solution.py:620
  687.2 9.3 spread.2
  766.5 29.2 %token_back.3 = (f32[512,1536]{1,0:T(8,128)}, bf16[2,2,12,64,128]{4,3,2,1,0:T(8,128)(2,1)}, f32[512,768]{1,0:T(8,128)}, f32[2,40,768]{2,1,0:T(8,128)}) custom-call(s32[2]{0:T(128)} %subtract_reduce_fusion.bound_ref, s32[2,256,1]{2,1,0:T(8,128)} %reshape.389.ids_ref, bf16[512,2304]{1,0:T(8,128)(2,1)} %fusion.24.qk_ref.v_ref, ...), custom_call_target="tpu_custom_call" | custom-call | tf_op jit(solution)/shard_map/token_back/pallas_call | solution.py:390
  795.7 32.5 %all_to_all.42.parts_ref = bf16[16,3,64,128]{3,2,1,0:T(8,128)(2,1)} all-to-all(bf16[16,3,64,128]{3,2,1,0:T(8,128)(2,1)} %bitcast.192), channel_id=1, replica_groups=mesh['dp'=2,'sp'=16] {'sp'}, dimensions={0} | all-to-all | bytes 1572864 | tf_op jit(solution)/shard_map/all_to_all | solution.py:616
  830.5 25.2 %all_gather.42 = bf16[48,64,128]{2,1,0:T(8,128)(2,1)} all-gather(bf16[3,64,128]{2,1,0:T(8,128)(2,1)} %get-tuple-element.59), channel_id=1, replica_groups=mesh['dp'=2,'sp'=16] {'sp'}, dimensions={0}, use_global_device_ids=true | all-gather | bytes 835584 | tf_op jit(solution)/shard_map/all_gather | solution.py:620
  855.7 13.5 %key_back.3 = (f32[512,1536]{1,0:T(8,128)}, bf16[512,768]{1,0:T(8,128)(2,1)}, bf16[2,2,12,32,128]{4,3,2,1,0:T(8,128)(2,1)}) custom-call(s32[2,1,256]{2,1,0:T(1,128)} %ids_ref.11, bf16[512,2304]{1,0:T(8,128)(2,1)} %fusion.24.qk_ref.v_ref, bf16[512,2304]{1,0:T(8,128)(2,1)} %fusion.24.qk_ref.v_ref, bf16[2,2,12,64,128]{4,3,2,1,0:T(8,128)(2,1)} %bitcast.153, ...), custom_call_target="tpu_custom_call" | custom-call | tf_op jit(solution)/shard_map/key_back/pallas_call | solution.py:546
  883.9 20.8 %newton_back.3 = f32[3,64,128]{2,1,0:T(8,128)} custom-call(f32[3,64,128]{2,1,0:T(8,128)} %get-tuple-element.55.marks_ref, f32[3,64,128]{2,1,0:T(8,128)} %get-tuple-element.56.values_ref, f32[3,64,128]{2,1,0:T(8,128)} %get-tuple-element.58.total_ref), custom_call_target="tpu_custom_call" | custom-call | tf_op jit(solution)/shard_map/newton_back/pallas_call | solution.py:501
  907.4 25.3 %all_gather.43 = bf16[48,64,128]{2,1,0:T(8,128)(2,1)} all-gather(bf16[3,64,128]{2,1,0:T(8,128)(2,1)S(1)} %multiply_convert_fusion.2), channel_id=1, replica_groups=mesh['dp'=2,'sp'=16] {'sp'}, dimensions={0}, use_global_device_ids=true | all-gather | bytes 835584 | tf_op jit(solution)/shard_map/all_gather | solution.py:620
  932.7 9.1 spread.3
  976.8 38.1 %all-reduce.6 = (f32[2,12,33]{2,1,0:T(8,128)S(1)}, f32[2,2,768]{2,1,0:T(2,128)}, f32[2,2,768]{2,1,0:T(2,128)}) all-reduce(f32[2,12,33]{2,1,0:T(8,128)S(1)} %pad_maximum_fusion.10, f32[2,2,768]{2,1,0:T(2,128)S(1)} %pad_maximum_fusion.11, f32[2,2,768]{2,1,0:T(2,128)} %pad_maximum_fusion.12), channel_id=1, replica_groups=mesh['dp'=2,'sp'=16] {'dp','sp'}, use_global_device_ids=true, to_apply=%region_24.25 | all-reduce | flops 6936 | bytes 55488 | tf_op jit(solution)/shard_map/psum | solution.py:823
  1025.7 103.9 %reduce-scatter.3.cloned.1.call-done = bf16[24,9216]{1,0:T(8,128)(2,1)} async-done(((bf16[768,9216]{1,0:T(8,128)(2,1)}), bf16[24,9216]{1,0:T(8,128)(2,1)}) %reduce-scatter.3.cloned.1.call-update) | async-done | bytes 442384 | tf_op jit(solution)/shard_map/reduce_scatter | solution.py:815
  (401 shorter events, 290.7 us)
Async XLA Ops:
  7.2 67.2 %all-gather.4.cloned.1.call-start = ((), (), s32[]{:S(2)}) async-start(), calls=%async_computation.10 | async-start | bytes 3649536 | tf_op jit(solution)/shard_map/all_gather | solution.py:711
  11.0 284.5 %all-gather.6.cloned.1.call-start = ((), (), s32[]{:S(2)}) async-start(), calls=%async_computation.11 | async-start | bytes 10948608 | tf_op jit(solution)/shard_map/all_gather | solution.py:712
  12.9 304.9 %all-gather.8.cloned.1.call-start = ((), (), s32[]{:S(2)}) async-start(), calls=%async_computation.12 | async-start | bytes 14598144 | tf_op jit(solution)/shard_map/all_gather | solution.py:714
  14.0 60.4 %copy-start.53 = (bf16[2,1,256,768]{3,2,1,0:T(8,128)(2,1)S(1)}, bf16[2,1,256,768]{3,2,1,0:T(8,128)(2,1)}, u32[]{:S(2)}) copy-start(bf16[2,1,256,768]{3,2,1,0:T(8,128)(2,1)} %param.14) | copy-start | bytes 2359300
  88.0 49.9 %all-to-all-start = ((f32[16,3,64,128]{3,2,1,0:T(8,128)}), f32[16,3,64,128]{3,2,1,0:T(8,128)S(1)}, u32[]{:S(2)}, u32[]{:S(2)}) async-start(f32[16,3,64,128]{3,2,1,0:T(8,128)} %bitcast.166), calls=%async_computation | async-start | bytes 3145728 | tf_op jit(solution)/shard_map/all_to_all | solution.py:616
  192.8 45.2 %all-to-all-start.1 = ((f32[16,3,64,128]{3,2,1,0:T(8,128)}), f32[16,3,64,128]{3,2,1,0:T(8,128)S(1)}, u32[]{:S(2)}, u32[]{:S(2)}) async-start(f32[16,3,64,128]{3,2,1,0:T(8,128)} %bitcast.170), calls=%async_computation.1 | async-start | bytes 3145728 | tf_op jit(solution)/shard_map/all_to_all | solution.py:616
  199.3 115.4 %copy-start.42 = (f32[768]{0:T(1024)}, f32[768]{0:T(1024)S(1)}, u32[]{:S(2)}) copy-start(f32[768]{0:T(1024)S(1)} %get-tuple-element.132) | copy-start | bytes 9220
  199.4 78.1 %collective-permute-start = (bf16[2,16,768]{2,1,0:T(8,128)(2,1)S(1)}, bf16[2,16,768]{2,1,0:T(8,128)(2,1)S(1)}, u32[]{:S(2)}, u32[]{:S(2)}) collective-permute-start(bf16[2,16,768]{2,1,0:T(8,128)(2,1)S(1)} %get-tuple-element.159), channel_id=1, source_target_pairs={{0,1},{1,2},{2,3},{3,4},{4,5},{5,6},{6,7},{7,8},{8,9},{9,10},{10,1... | collective-permute-start | bytes 147464 | tf_op jit(solution)/shard_map/ppermute | solution.py:630
  201.6 75.9 %collective-permute-start.1 = (bf16[2,16,768]{2,1,0:T(8,128)(2,1)S(1)}, bf16[2,16,768]{2,1,0:T(8,128)(2,1)S(1)}, u32[]{:S(2)}, u32[]{:S(2)}) collective-permute-start(bf16[2,16,768]{2,1,0:T(8,128)(2,1)S(1)} %get-tuple-element.158), channel_id=1, source_target_pairs={{1,0},{2,1},{3,2},{4,3},{5,4},{6,5},{7,6},{8,7},{9,8},{10,9},{11,1... | collective-permute-start | bytes 147464 | tf_op jit(solution)/shard_map/ppermute | solution.py:631
  278.1 17.4 %copy-start.54 = (bf16[2,1,256,768]{3,2,1,0:T(8,128)(2,1)S(1)}, bf16[2,1,256,768]{3,2,1,0:T(8,128)(2,1)}, u32[]{:S(2)}) copy-start(bf16[2,1,256,768]{3,2,1,0:T(8,128)(2,1)} %param.14) | copy-start | bytes 2359300
  297.9 16.9 %copy-start.3 = (f32[512,768]{1,0:T(8,128)}, f32[512,768]{1,0:T(8,128)S(1)}, u32[]{:S(2)}) copy-start(f32[512,768]{1,0:T(8,128)S(1)} %get-tuple-element.175) | copy-start | bytes 4718596
  307.5 7.2 copy-start.29
  415.9 36.8 %all-to-all-start.3 = ((f32[16,3,64,128]{3,2,1,0:T(8,128)}), f32[16,3,64,128]{3,2,1,0:T(8,128)}, u32[]{:S(2)}, u32[]{:S(2)}) async-start(f32[16,3,64,128]{3,2,1,0:T(8,128)} %bitcast.171), calls=%async_computation.3 | async-start | bytes 3145728 | tf_op jit(solution)/shard_map/all_to_all | solution.py:616
  421.9 62.6 %collective-permute-start.2 = (bf16[2,16,768]{2,1,0:T(8,128)(2,1)S(1)}, bf16[2,16,768]{2,1,0:T(8,128)(2,1)S(1)}, u32[]{:S(2)}, u32[]{:S(2)}) collective-permute-start(bf16[2,16,768]{2,1,0:T(8,128)(2,1)S(1)} %get-tuple-element.157), channel_id=1, source_target_pairs={{0,1},{1,2},{2,3},{3,4},{4,5},{5,6},{6,7},{7,8},{8,9},{9,10},{10,1... | collective-permute-start | bytes 147464 | tf_op jit(solution)/shard_map/ppermute | solution.py:630
  424.0 60.4 %collective-permute-start.3 = (bf16[2,16,768]{2,1,0:T(8,128)(2,1)S(1)}, bf16[2,16,768]{2,1,0:T(8,128)(2,1)S(1)}, u32[]{:S(2)}, u32[]{:S(2)}) collective-permute-start(bf16[2,16,768]{2,1,0:T(8,128)(2,1)S(1)} %get-tuple-element.156), channel_id=1, source_target_pairs={{1,0},{2,1},{3,2},{4,3},{5,4},{6,5},{7,6},{8,7},{9,8},{10,9},{11,1... | collective-permute-start | bytes 147464 | tf_op jit(solution)/shard_map/ppermute | solution.py:631
  504.7 29.5 %copy-start.5 = (f32[512,768]{1,0:T(8,128)}, f32[512,768]{1,0:T(8,128)S(1)}, u32[]{:S(2)}) copy-start(f32[512,768]{1,0:T(8,128)S(1)} %get-tuple-element.181) | copy-start | bytes 4718596
  504.8 9.9 slice-start.2
  505.1 9.6 slice-start.3
  505.1 9.6 slice-start.4
  505.1 9.6 slice-start.5
  536.9 4.7 collective-permute-start.4
  539.2 3.1 collective-permute-start.5
  636.2 24.5 %all-to-all-start.5 = ((bf16[16,3,32,128]{3,2,1,0:T(8,128)(2,1)}), bf16[16,3,32,128]{3,2,1,0:T(8,128)(2,1)S(1)}, u32[]{:S(2)}, u32[]{:S(2)}) async-start(bf16[16,3,32,128]{3,2,1,0:T(8,128)(2,1)} %bitcast.201), calls=%async_computation.5 | async-start | bytes 786432 | tf_op jit(solution)/shard_map/all_to_all | solution.py:616
  639.8 382.1 %reduce-scatter.5.cloned.1.call-start = ((), (), s32[]{:S(2)}) async-start(), calls=%async_computation.14 | async-start | bytes 14598144 | tf_op jit(solution)/shard_map/reduce_scatter | solution.py:815
  736.6 10.0 slice-start.8
  736.6 10.0 slice-start.13
  744.8 8.4 slice-start.10
  760.2 5.2 collective-permute-start.6
  763.0 3.5 collective-permute-start.7
  869.2 35.6 %all-to-all-start.7 = ((bf16[16,3,32,128]{3,2,1,0:T(8,128)(2,1)}), bf16[16,3,32,128]{3,2,1,0:T(8,128)(2,1)S(1)}, u32[]{:S(2)}, u32[]{:S(2)}) async-start(bf16[16,3,32,128]{3,2,1,0:T(8,128)(2,1)} %bitcast.200), calls=%async_computation.7 | async-start | bytes 786432 | tf_op jit(solution)/shard_map/all_to_all | solution.py:616
  872.7 256.9 %reduce-scatter.3.cloned.1.call-start = ((), (), s32[]{:S(2)}) async-start(), calls=%async_computation.13 | async-start | bytes 14598144 | tf_op jit(solution)/shard_map/reduce_scatter | solution.py:815
  970.4 45.1 %copy-start.15 = (bf16[512,1536]{1,0:T(8,128)(2,1)S(1)}, bf16[512,1536]{1,0:T(8,128)(2,1)}, u32[]{:S(2)}) copy-start(bf16[512,1536]{1,0:T(8,128)(2,1)} %spread.3) | copy-start | bytes 4718596
  (60 other events, 175.5 us)
Sparse Core Ops, SparseCore 0:
  11.5 62.8 all-gather.3
  77.8 113.0 all-gather.5
  194.4 122.5 all-gather.7
  717.8 178.0 reduce-scatter.4
  969.3 160.2 reduce-scatter.2

commit v2 on v1

v2 whole, which is shorter than its diff:
```python
import functools

import jax
import jax.numpy as jnp
from jax import lax
from jax.experimental import pallas as pl
from jax.experimental.pallas import tpu as pltpu
from jax.sharding import PartitionSpec as P

HEADS = 12
HD = 64
LMK = 64
NS_ITERS = 6
KCONV = 33
DOCS = 2
HALO = 16
SLOTS = DOCS * LMK
PAIRS = HEADS // 2
WIDE = 2 * HD
WINDOW = 40
TAPS = 40

negative = -1e30
epsilon = 1e-05
score_scale = HD ** (-0.5)
bf16 = jnp.bfloat16
f32 = jnp.float32


def nn(left, right):
    return lax.dot_general(left, right, (((1,), (0,)), ((), ())), preferred_element_type=f32)


def nt(left, right):
    return lax.dot_general(left, right, (((1,), (1,)), ((), ())), preferred_element_type=f32)


def tn(left, right):
    return lax.dot_general(left, right, (((0,), (0,)), ((), ())), preferred_element_type=f32)


def split_two(value):
    first = value.astype(bf16)
    return first, (value - first.astype(f32)).astype(bf16)


def three_pass(product, left, right):
    left_first, left_second = split_two(left)
    right_first, right_second = split_two(right)
    small = product(left_first, right_second) + product(left_second, right_first)
    return product(left_first, right_first) + small


def hnn(left, right):
    return three_pass(nn, left, right)


def hnt(left, right):
    return three_pass(nt, left, right)


def htn(left, right):
    return three_pass(tn, left, right)


def iota(shape, dim):
    return lax.broadcasted_iota(jnp.int32, shape, dim)


def task_rows(place_ref, doc, head):
    return place_ref[doc * HEADS + head]


def read_marks(ref, place_ref, head):
    parts = [ref[task_rows(place_ref, doc, head)] for doc in range(DOCS)]
    return jnp.concatenate(parts, axis=0).astype(f32)


def write_marks(ref, place_ref, head, value):
    rows = value.shape[0] // DOCS
    for doc in range(DOCS):
        ref[task_rows(place_ref, doc, head)] = value[doc * rows : (doc + 1) * rows].astype(
            ref.dtype
        )


def whole(shape):
    zeros = (0,) * len(shape)
    return pl.BlockSpec(shape, lambda p, *scalars: zeros)


def lanes(rows, width):
    return pl.BlockSpec((rows, width), lambda p, *scalars: (0, p))


def lanes3(batches, rows, width):
    return pl.BlockSpec((batches, rows, width), lambda p, *scalars: (0, 0, p))


def over_pairs(body, name, scalars, in_specs, out_specs, out_shape, args, flops, scratch=()):
    moved = sum(a.size * a.dtype.itemsize for a in args)
    moved += sum(
        functools.reduce(lambda x, y: x * y, o.shape) * o.dtype.itemsize
        for o in jax.tree.leaves(out_shape)
    )
    return pl.pallas_call(
        body,
        grid_spec=pltpu.PrefetchScalarGridSpec(
            num_scalar_prefetch=len(scalars),
            grid=(PAIRS,),
            in_specs=in_specs,
            out_specs=out_specs,
            scratch_shapes=scratch,
        ),
        out_shape=out_shape,
        cost_estimate=pl.CostEstimate(flops=flops, bytes_accessed=moved, transcendentals=0),
        compiler_params=pltpu.CompilerParams(vmem_limit_bytes=48 * 1024 * 1024),
        name=name,
    )(*scalars, *args)


def project_kernel(place_ref, ids_ref, hidden_ref, qk_weight_ref, v_weight_ref, qk_ref, v_ref, sums_ref):
    pair = pl.program_id(0)
    qk_ref[...] = nn(hidden_ref[...], qk_weight_ref[...]).astype(bf16)
    v_ref[...] = nn(hidden_ref[...], v_weight_ref[...]).astype(bf16)
    onehot = (iota((SLOTS, ids_ref.shape[1]), 0) == ids_ref[...]).astype(f32).astype(bf16)
    sums = nn(onehot, qk_ref[...])
    for side in range(2):
        write_marks(sums_ref, place_ref, 2 * pair + side, sums[:, side * WIDE : (side + 1) * WIDE])


def project(place, row_ids, hidden_low, weight, room, layer):
    rows, width = hidden_low.shape
    first = layer * 3 * PAIRS
    return over_pairs(
        project_kernel,
        "project",
        (place,),
        [
            whole(row_ids.shape),
            whole(hidden_low.shape),
            pl.BlockSpec((width, 2 * WIDE), lambda p, *s: (0, first // 2 + p)),
            pl.BlockSpec((width, WIDE), lambda p, *s: (0, first + HEADS + p)),
        ],
        [lanes(rows, 2 * WIDE), lanes(rows, WIDE), whole((room, LMK, WIDE))],
        (
            jax.ShapeDtypeStruct((rows, HEADS * WIDE), bf16),
            jax.ShapeDtypeStruct((rows, HEADS * HD), bf16),
            jax.ShapeDtypeStruct((room, LMK, WIDE), f32),
        ),
        (row_ids, hidden_low, weight, weight),
        2 * rows * width * 3 * width,
    )


def key_partial_kernel(place_ref, ids_ref, qk_ref, v_ref, marks_ref, out_ref):
    pair = pl.program_id(0)
    lane = iota((SLOTS, WIDE), 1)
    keep = (ids_ref[...] >> 6) == (iota((SLOTS, ids_ref.shape[1]), 0) >> 6)
    values = v_ref[...]
    for side in range(2):
        marks = read_marks(marks_ref, place_ref, 2 * pair + side)
        query_marks = jnp.where(lane >= HD, marks, 0.0).astype(bf16)
        scores = nt(query_marks, qk_ref[:, side * WIDE : (side + 1) * WIDE]) * score_scale
        scores = jnp.where(keep, scores, negative)
        top = jnp.max(scores, axis=1, keepdims=True)
        weights = jnp.where(keep, jnp.exp(scores - top), 0.0)
        total = jnp.sum(weights, axis=1, keepdims=True)
        numer = nn(weights.astype(bf16), values)
        if side:
            numer = pltpu.roll(numer, HD, 1)
        packed = jnp.where(lane < HD, numer, jnp.where(lane < HD + 32, top, total))
        write_marks(out_ref, place_ref, 2 * pair + side, packed)


def key_partial(place, row_ids, qk, v, marks):
    rows = qk.shape[0]
    return over_pairs(
        key_partial_kernel,
        "key_partial",
        (place,),
        [whole(row_ids.shape), lanes(rows, 2 * WIDE), lanes(rows, WIDE), whole(marks.shape)],
        whole(marks.shape),
        jax.ShapeDtypeStruct(marks.shape, f32),
        (row_ids, qk, v, marks),
        4 * rows * SLOTS * WIDE * HEADS,
    )


def exact_three(column):
    first = column.astype(bf16).astype(f32)
    second = (column - first).astype(bf16).astype(f32)
    return first, second, column - first - second


def join_kernel(mine_ref, other_ref, out_ref):
    lane = iota((LMK, WIDE), 1)
    half = mine_ref.shape[0]

    def one(task, carry):
        mine, other = mine_ref[task], other_ref[task]
        top_mine, top_other = mine[:, HD : HD + 1], other[:, HD : HD + 1]
        top = jnp.maximum(top_mine, top_other)
        joined = mine * jnp.exp(top_mine - top) + other * jnp.exp(top_other - top)
        parts = exact_three(top) + exact_three(joined[:, HD + 32 : HD + 33])
        for index, part in enumerate(parts):
            joined = jnp.where(lane == HD + index, part, joined)
        out_ref[task] = joined.astype(bf16)
        return carry

    lax.fori_loop(0, half, one, 0, unroll=4)


def join_pair(parts, other):
    return pl.pallas_call(
        join_kernel,
        grid=(1,),
        in_specs=[
            pl.BlockSpec(other.shape, lambda g: (0, 0, 0)),
            pl.BlockSpec(other.shape, lambda g: (0, 0, 0)),
        ],
        out_specs=pl.BlockSpec(other.shape, lambda g: (0, 0, 0)),
        out_shape=jax.ShapeDtypeStruct(other.shape, bf16),
        name="join_pair",
    )(parts, other)


def identity():
    return (iota((LMK, LMK), 0) == iota((LMK, LMK), 1)).astype(f32)


def mark_softmax(query_marks, key_marks):
    scores = hnt(query_marks, key_marks) * score_scale
    weights = jnp.exp(scores - jnp.max(scores, axis=1, keepdims=True))
    return weights / jnp.sum(weights, axis=1, keepdims=True)


def newton(kernels, steps_ref=None):
    eye = identity()

    def sweep(index, approx):
        product = [hnn(k, x) for k, x in zip(kernels, approx)]
        middle = [15.0 * eye - hnn(p, 7.0 * eye - p) for p in product]
        outer = [13.0 * eye - hnn(p, c) for p, c in zip(product, middle)]
        if steps_ref is not None:
            for task, step in enumerate(zip(approx, product, middle, outer)):
                for slot, value in enumerate(step):
                    steps_ref[index, task, slot] = value
        return tuple(0.25 * hnn(x, e) for x, e in zip(approx, outer))

    start = tuple(jnp.swapaxes(kernel, 0, 1) / LMK for kernel in kernels)
    return lax.fori_loop(0, NS_ITERS, sweep, start)


def small_call(body, name, out_shape, args, scratch=(), flops=10**8):
    return pl.pallas_call(
        body,
        out_shape=out_shape,
        scratch_shapes=scratch,
        cost_estimate=pl.CostEstimate(flops=flops, bytes_accessed=10**6, transcendentals=0),
        name=name,
    )(*args)


def add_parts(refs, task):
    total = refs[0][task].astype(f32)
    for ref in refs[1:]:
        total = total + ref[task].astype(f32)
    return total


def owner_kernel(*refs):
    *part_refs, inverse_ref, marks_ref, swapped_ref = refs
    for task in range(marks_ref.shape[0]):
        marks = add_parts(part_refs, task) * inverse_ref[task]
        marks_ref[task] = marks
        swapped_ref[task] = pltpu.roll(marks, HD, 1).astype(bf16)


def owner_marks(parts, inverse):
    shape = parts[0].shape
    return small_call(
        owner_kernel,
        "owner_marks",
        (jax.ShapeDtypeStruct(shape, f32), jax.ShapeDtypeStruct(shape, bf16)),
        (*parts, inverse),
    )


def pseudo_kernel(marks_ref, pseudo_ref):
    count = marks_ref.shape[0]
    kernels = [mark_softmax(marks_ref[t][:, :HD], marks_ref[t][:, HD:]) for t in range(count)]
    for task, pseudo in enumerate(newton(kernels)):
        pseudo_ref[task] = pseudo


def owner_pseudo(marks):
    return small_call(
        pseudo_kernel,
        "owner_pseudo",
        jax.ShapeDtypeStruct((marks.shape[0], LMK, LMK), f32),
        (marks,),
        flops=5 * 10**9,
    )


def with_exact(left, column, lane):
    result = jnp.where(lane < HD, left, 0.0)
    for index, part in enumerate(exact_three(column)):
        result = jnp.where(lane == HD + index, part, result)
    return result.astype(bf16)


def exact_column(block, start=HD):
    return block[:, start : start + 1] + block[:, start + 1 : start + 2] + block[:, start + 2 : start + 3]


def merge_kernel(*refs):
    *part_refs, pseudo_ref, values_ref, payload_ref = refs
    lane = iota((LMK, WIDE), 1)
    for task in range(values_ref.shape[0]):
        parts = [ref[task].astype(f32) for ref in part_refs]
        tops = [exact_column(part) for part in parts]
        top = functools.reduce(jnp.maximum, tops)
        scales = [jnp.exp(t - top) for t in tops]
        total = sum(exact_column(part, HD + 3) * scale for part, scale in zip(parts, scales))
        values = sum(part * scale for part, scale in zip(parts, scales)) / total
        values_ref[task] = values
        mixed = hnn(pseudo_ref[task], values)
        payload_ref[task] = with_exact(mixed, top + jnp.log(total), lane)


def owner_merge(parts, pseudo):
    shape = parts[0].shape
    return small_call(
        merge_kernel,
        "owner_merge",
        (jax.ShapeDtypeStruct(shape, f32), jax.ShapeDtypeStruct(shape, bf16)),
        (*parts, pseudo),
    )


def fill_padded(pad_ref, low, center, high):
    length = center.shape[0]
    pad_ref[0:HALO] = low.astype(f32)
    pad_ref[HALO : HALO + length] = center.astype(f32)
    pad_ref[HALO + length : 2 * HALO + length] = high.astype(f32)


def same_side(start, bound, offset):
    rows = start + iota((WINDOW, WIDE), 0)
    return (rows < bound) == (rows + (offset - HALO) < bound)


def window_start(bound, length):
    start = jnp.clip(((bound - HALO) >> 3) << 3, 0, length - WINDOW)
    return pl.multiple_of(start, 8)


def convolve(pad_ref, taps_ref, bound, out_ref):
    length = out_ref.shape[0]
    block = 64
    for first in range(0, length, block):
        total = jnp.zeros((block, WIDE), f32)
        for offset in range(KCONV):
            total = total + pad_ref[first + offset : first + offset + block] * taps_ref[offset : offset + 1]
        out_ref[first : first + block] = total
    start = window_start(bound, length)
    total = jnp.zeros((WINDOW, WIDE), f32)
    for offset in range(KCONV):
        nearby = pad_ref[pl.ds(start + offset, WINDOW)]
        total = total + jnp.where(same_side(start, bound, offset), nearby, 0.0) * taps_ref[offset : offset + 1]
    out_ref[pl.ds(start, WINDOW)] = total


def taps_gradient(grad_ref, pad_ref, bound, length):
    start = window_start(bound, length)
    window = grad_ref[pl.ds(start, WINDOW)]
    rows = []
    for offset in range(KCONV):
        total = jnp.sum(grad_ref[0:length] * pad_ref[offset : offset + length], axis=0, keepdims=True)
        crossing = window * pad_ref[pl.ds(start + offset, WINDOW)]
        crossing = jnp.where(same_side(start, bound, offset), 0.0, crossing)
        rows.append(total - jnp.sum(crossing, axis=0, keepdims=True))
    return rows


def half_values(block, side, lane):
    block = jnp.where(lane < HD, block, 0.0)
    if side:
        block = pltpu.roll(block, HD, 1)
    return block.astype(bf16)


def token_prep_kernel(
    place_ref, bound_ref, ids_ref, qk_ref, v_ref, low_ref, high_ref, marks_ref, taps_ref,
    weights_ref, conv_ref, pad_ref, acc_ref,
):
    segments = low_ref.shape[0]
    length = v_ref.shape[0] // segments
    pair = pl.program_id(0)
    lane = iota((SLOTS, WIDE), 1)
    for segment in range(segments):
        rows = slice(segment * length, (segment + 1) * length)
        fill_padded(pad_ref, low_ref[segment], v_ref[rows], high_ref[segment])
        convolve(pad_ref, taps_ref, bound_ref[segment], acc_ref)
        conv_ref[rows] = acc_ref[...]
    keep = (ids_ref[...] >> 6) == (iota((ids_ref.shape[0], SLOTS), 1) >> 6)
    for side in range(2):
        columns = slice(side * WIDE, (side + 1) * WIDE)
        marks = read_marks(marks_ref, place_ref, 2 * pair + side)
        key_marks = jnp.where(lane < HD, marks, 0.0).astype(bf16)
        scores = jnp.where(keep, nt(qk_ref[:, columns], key_marks) * score_scale, negative)
        weights = jnp.exp(scores - jnp.max(scores, axis=1, keepdims=True))
        weights = weights / jnp.sum(weights, axis=1, keepdims=True)
        weights_ref[:, columns] = weights.astype(bf16)


def token_prep(place, bounds, col_ids, qk, v, low, high, marks, taps):
    rows = v.shape[0]
    segments = low.shape[0]
    length = rows // segments
    return over_pairs(
        token_prep_kernel,
        "token_prep",
        (place, bounds),
        [
            whole(col_ids.shape),
            lanes(rows, 2 * WIDE),
            lanes(rows, WIDE),
            lanes3(segments, HALO, WIDE),
            lanes3(segments, HALO, WIDE),
            whole(marks.shape),
            lanes(TAPS, WIDE),
        ],
        [lanes(rows, 2 * WIDE), lanes(rows, WIDE)],
        (
            jax.ShapeDtypeStruct((rows, HEADS * WIDE), bf16),
            jax.ShapeDtypeStruct((rows, HEADS * HD), f32),
        ),
        (col_ids, qk, v, low, high, marks, taps),
        10**10,
        [pltpu.VMEM((length + 2 * HALO, WIDE), f32), pltpu.VMEM((length, WIDE), f32)],
    )


def token_mix_kernel(place_ref, weights_ref, conv_ref, mixed_ref, out_ref):
    pair = pl.program_id(0)
    lane = iota((SLOTS, WIDE), 1)
    mixed = [
        half_values(read_marks(mixed_ref, place_ref, 2 * pair + side), side, lane)
        for side in range(2)
    ]
    attended = nn(weights_ref[...], jnp.concatenate(mixed, axis=0))
    out_ref[...] = (attended + conv_ref[...]).astype(bf16)


def token_mix(place, weights, conv, mixed):
    rows = weights.shape[0]
    return over_pairs(
        token_mix_kernel,
        "token_mix",
        (place,),
        [lanes(rows, 2 * WIDE), lanes(rows, WIDE), whole(mixed.shape)],
        lanes(rows, WIDE),
        jax.ShapeDtypeStruct((rows, HEADS * HD), bf16),
        (weights, conv, mixed),
        2 * rows * SLOTS * WIDE * HEADS,
    )


def token_back_kernel(
    place_ref, qk_ref, grad_ref, weights_ref, marks_ref, mixed_ref, dq_ref, task_ref
):
    pair = pl.program_id(0)
    lane = iota((SLOTS, WIDE), 1)
    grad = grad_ref[...]
    for side in range(2):
        columns = slice(side * WIDE, (side + 1) * WIDE)
        head = 2 * pair + side
        qk = qk_ref[:, columns]
        marks = read_marks(marks_ref, place_ref, head)
        key_marks = jnp.where(lane < HD, marks, 0.0).astype(bf16)
        weights_low = weights_ref[:, columns]
        weights = weights_low.astype(f32)
        mixed = half_values(read_marks(mixed_ref, place_ref, head), side, lane)
        grad_weights = nt(grad, mixed)
        inner = jnp.sum(weights * grad_weights, axis=1, keepdims=True)
        grad_scores = (weights * (grad_weights - inner) * score_scale).astype(bf16)
        dq_ref[:, columns] = nn(grad_scores, key_marks)
        grad_keys = tn(grad_scores, qk)
        grad_mixed = tn(weights_low, grad)
        if not side:
            grad_mixed = pltpu.roll(grad_mixed, HD, 1)
        write_marks(task_ref, place_ref, head, jnp.where(lane < HD, grad_keys, grad_mixed))


def token_back(place, qk, grad, weights, marks, mixed):
    rows = qk.shape[0]
    return over_pairs(
        token_back_kernel,
        "token_back",
        (place,),
        [
            lanes(rows, 2 * WIDE),
            lanes(rows, WIDE),
            lanes(rows, 2 * WIDE),
            whole(marks.shape),
            whole(mixed.shape),
        ],
        [lanes(rows, 2 * WIDE), whole(marks.shape)],
        (
            jax.ShapeDtypeStruct((rows, HEADS * WIDE), f32),
            jax.ShapeDtypeStruct(marks.shape, bf16),
        ),
        (qk, grad, weights, marks, mixed),
        8 * rows * SLOTS * WIDE * HEADS,
    )


def conv_back_kernel(
    bound_ref, v_ref, low_ref, high_ref, grad_ref, grad_low_ref, grad_high_ref, taps_ref,
    dv_ref, dtaps_ref, pad_ref, acc_ref,
):
    batches = low_ref.shape[0]
    length = v_ref.shape[0] // batches
    dtaps_ref[KCONV:] = jnp.zeros((TAPS - KCONV, WIDE), f32)
    for batch in range(batches):
        rows = slice(batch * length, (batch + 1) * length)
        bound = bound_ref[batch]
        grad = grad_ref[rows].astype(f32)
        fill_padded(pad_ref, grad_low_ref[batch], grad, grad_high_ref[batch])
        convolve(pad_ref, taps_ref, bound, acc_ref)
        dv_ref[rows] = acc_ref[...]
        fill_padded(pad_ref, low_ref[batch], v_ref[rows], high_ref[batch])
        acc_ref[...] = grad
        for offset, row in enumerate(taps_gradient(acc_ref, pad_ref, bound, length)):
            if batch:
                row = row + dtaps_ref[offset : offset + 1]
            dtaps_ref[offset : offset + 1] = row


def conv_back(bounds, v, low, high, grad, grad_low, grad_high, taps):
    batches = low.shape[0]
    rows = v.shape[0]
    length = rows // batches
    return over_pairs(
        conv_back_kernel,
        "conv_back",
        (bounds,),
        [
            lanes(rows, WIDE),
            lanes3(batches, HALO, WIDE),
            lanes3(batches, HALO, WIDE),
            lanes(rows, WIDE),
            lanes3(batches, HALO, WIDE),
            lanes3(batches, HALO, WIDE),
            lanes(TAPS, WIDE),
        ],
        [lanes(rows, WIDE), lanes(TAPS, WIDE)],
        (
            jax.ShapeDtypeStruct((rows, HEADS * HD), f32),
            jax.ShapeDtypeStruct((TAPS, HEADS * HD), f32),
        ),
        (v, low, high, grad, grad_low, grad_high, taps),
        10**10,
        [pltpu.VMEM((length + 2 * HALO, WIDE), f32), pltpu.VMEM((length, WIDE), f32)],
    )


def owner_back_kernel(*refs):
    *part_refs, pseudo_ref, values_ref, total_ref, payload_ref = refs
    lane = iota((LMK, WIDE), 1)
    for task in range(values_ref.shape[0]):
        total = add_parts(part_refs, task)
        total_ref[task] = total
        grad_values = htn(pseudo_ref[task], pltpu.roll(total, HD, 1))
        inner = jnp.sum(
            jnp.where(lane < HD, grad_values * values_ref[task], 0.0), axis=1, keepdims=True
        )
        payload_ref[task] = with_exact(grad_values, inner, lane)


def owner_back(parts, pseudo, values):
    shape = values.shape
    return small_call(
        owner_back_kernel,
        "owner_back",
        (jax.ShapeDtypeStruct(shape, f32), jax.ShapeDtypeStruct(shape, bf16)),
        (*parts, pseudo, values),
    )


def newton_back_kernel(marks_ref, values_ref, total_ref, out_ref, steps_ref):
    count = marks_ref.shape[0]
    tasks = range(count)
    marks = [marks_ref[task] for task in tasks]
    queries = [m[:, :HD] for m in marks]
    keys = [m[:, HD:] for m in marks]
    kernels = [mark_softmax(q, k) for q, k in zip(queries, keys)]
    newton(kernels, steps_ref)
    eye = identity()

    def sweep(index, carry):
        results = []
        for task in tasks:
            grad, grad_kernel = carry[task]
            approx, product, middle, outer = (
                steps_ref[NS_ITERS - 1 - index, task, slot] for slot in range(4)
            )
            grad_outer = 0.25 * htn(approx, grad)
            grad_middle = -htn(product, grad_outer)
            grad_inner = -htn(product, grad_middle)
            grad_product = (
                -hnt(grad_outer, middle) - hnt(grad_middle, 7.0 * eye - product) - grad_inner
            )
            grad_kernel = grad_kernel + hnt(grad_product, approx)
            grad = 0.25 * hnt(grad, outer) + htn(kernels[task], grad_product)
            results.append((grad, grad_kernel))
        return tuple(results)

    start = tuple(
        (hnt(total_ref[task][:, HD:], values_ref[task][:, :HD]), jnp.zeros((LMK, LMK), f32))
        for task in tasks
    )
    ends = lax.fori_loop(0, NS_ITERS, sweep, start)
    for task in tasks:
        grad, grad_kernel = ends[task]
        grad_kernel = grad_kernel + jnp.swapaxes(grad, 0, 1) / LMK
        kernel = kernels[task]
        inner = jnp.sum(kernel * grad_kernel, axis=1, keepdims=True)
        grad_scores = kernel * (grad_kernel - inner) * score_scale
        grad_queries = hnn(grad_scores, keys[task])
        grad_keys = htn(grad_scores, queries[task]) + total_ref[task][:, :HD]
        out_ref[task] = jnp.concatenate([grad_queries, grad_keys], axis=1)


def newton_back(marks, values, total):
    return small_call(
        newton_back_kernel,
        "newton_back",
        jax.ShapeDtypeStruct(marks.shape, f32),
        (marks, values, total),
        [pltpu.VMEM((NS_ITERS, marks.shape[0], 4, LMK, LMK), f32)],
        15 * 10**9,
    )


def last_kernel(*refs):
    *part_refs, own_ref, inverse_ref, out_ref = refs
    half = LMK // 2
    lane = iota((half, WIDE), 1)
    for task in range(out_ref.shape[0]):
        total = add_parts(part_refs, task)
        for index, rows in enumerate((total, pltpu.roll(total, HD, 1))):
            where = slice(index * half, (index + 1) * half)
            value = own_ref[task, where] + jnp.where(lane < HD, rows, 0.0)
            out_ref[task, where] = (value * inverse_ref[task, where]).astype(bf16)


def owner_last(parts, own, inverse):
    return small_call(
        last_kernel,
        "owner_last",
        jax.ShapeDtypeStruct(own.shape, bf16),
        (*parts, own, inverse),
    )


def key_back_kernel(
    place_ref, ids_ref, qk_ref, v_ref, marks_ref, mixed_ref, grads_ref, dq_ref, dconv_ref,
    dqk_ref, dv_ref, part_ref,
):
    pair = pl.program_id(0)
    lane = iota((SLOTS, WIDE), 1)
    half = iota((LMK // 2, WIDE), 1)
    keep = (ids_ref[...] >> 6) == (iota((SLOTS, ids_ref.shape[1]), 0) >> 6)
    values = v_ref[...]
    grad_values = dconv_ref[...]
    for side in range(2):
        columns = slice(side * WIDE, (side + 1) * WIDE)
        head = 2 * pair + side
        qk = qk_ref[:, columns]
        marks = read_marks(marks_ref, place_ref, head)
        query_marks = jnp.where(lane >= HD, marks, 0.0).astype(bf16)
        scores = nt(query_marks, qk) * score_scale
        level = exact_column(read_marks(mixed_ref, place_ref, head))
        probs = jnp.where(keep, jnp.exp(scores - level), 0.0)
        grads = read_marks(grads_ref, place_ref, head)
        inner = exact_column(grads)
        grad_marks = half_values(grads, side, lane)
        grad_probs = nt(grad_marks, values)
        grad_scores = (probs * (grad_probs - inner) * score_scale).astype(bf16)
        dqk_ref[:, columns] = dq_ref[:, columns] + tn(grad_scores, query_marks)
        grad_values = grad_values + tn(probs.astype(bf16), grad_marks)
        part = nn(grad_scores, qk)
        for doc in range(DOCS):
            upper = part[doc * LMK : doc * LMK + LMK // 2]
            lower = part[doc * LMK + LMK // 2 : (doc + 1) * LMK]
            part_ref[task_rows(place_ref, doc, head)] = jnp.where(
                half < HD, pltpu.roll(upper, HD, 1), lower
            ).astype(bf16)
    dv_ref[...] = grad_values.astype(bf16)


def key_back(place, row_ids, qk, v, marks, mixed, grads, dq, dconv):
    rows = qk.shape[0]
    part_shape = (marks.shape[0], LMK // 2, WIDE)
    return over_pairs(
        key_back_kernel,
        "key_back",
        (place,),
        [
            whole(row_ids.shape),
            lanes(rows, 2 * WIDE),
            lanes(rows, WIDE),
            whole(marks.shape),
            whole(mixed.shape),
            whole(grads.shape),
            lanes(rows, 2 * WIDE),
            lanes(rows, WIDE),
        ],
        [lanes(rows, 2 * WIDE), lanes(rows, WIDE), whole(part_shape)],
        (
            jax.ShapeDtypeStruct((rows, HEADS * WIDE), f32),
            jax.ShapeDtypeStruct((rows, HEADS * HD), bf16),
            jax.ShapeDtypeStruct(part_shape, bf16),
        ),
        (row_ids, qk, v, marks, mixed, grads, dq, dconv),
        10 * rows * SLOTS * WIDE * HEADS,
    )


def spread_kernel(place_ref, ids_ref, marks_ref, dqk_ref, out_ref):
    pair = pl.program_id(0)
    onehot = (iota((ids_ref.shape[0], SLOTS), 1) == ids_ref[...]).astype(f32).astype(bf16)
    marks = [read_marks(marks_ref, place_ref, 2 * pair + side).astype(bf16) for side in range(2)]
    out_ref[...] = (dqk_ref[...] + nn(onehot, jnp.concatenate(marks, axis=1))).astype(bf16)


def spread(place, col_ids, marks, dqk):
    rows = dqk.shape[0]
    return over_pairs(
        spread_kernel,
        "spread",
        (place,),
        [whole(col_ids.shape), whole(marks.shape), lanes(rows, 2 * WIDE)],
        lanes(rows, 2 * WIDE),
        jax.ShapeDtypeStruct(dqk.shape, bf16),
        (col_ids, marks, dqk),
        2 * rows * SLOTS * WIDE * HEADS,
    )


def norm_apply(summed, layer_gain, layer_bias):
    center = summed - jnp.mean(summed, axis=-1, keepdims=True)
    spread_of = jnp.mean(center * center, axis=-1, keepdims=True)
    return center * lax.rsqrt(spread_of + epsilon) * layer_gain + layer_bias


def gelu_tanh(values):
    return jax.nn.gelu(values, approximate=True)


def bits_of(axis):
    return lax.axis_size(axis).bit_length() - 1


def flip(value, axis, mask):
    count = lax.axis_size(axis)
    return lax.ppermute(value, axis, [(i, i ^ mask) for i in range(count)])


def reverse_bits(index, bits):
    return sum(((index >> b) & 1) << (bits - 1 - b) for b in range(bits))


def row_bits():
    return bits_of("sp") - 1


def places(tasks, each):
    bits = row_bits()
    index = jnp.arange(tasks, dtype=jnp.int32)
    relative = (index // each) ^ (lax.axis_index("sp") & ((1 << bits) - 1))
    return reverse_bits(relative, bits) * each + index % each


def send_direct(near, each):
    bits = row_bits()
    parts = [near[:each]]
    for index in range(1, near.shape[0] // each):
        parts.append(
            flip(near[index * each : (index + 1) * each], "sp", reverse_bits(index, bits))
        )
    return parts


def to_owners(tasks, each):
    half = tasks.shape[0] // 2
    other = flip(tasks[half:], "sp", 1)
    near = (tasks[:half].astype(f32) + other.astype(f32)).astype(bf16)
    return send_direct(near, each)


def from_owners(owned):
    gathered = owned
    for bit in reversed(range(row_bits())):
        gathered = jnp.concatenate([gathered, flip(gathered, "sp", 1 << bit)], axis=0)
    return gathered


def all_sum(value):
    for axis in ("sp", "dp"):
        for bit in range(bits_of(axis)):
            value = value + flip(value, axis, 1 << bit)
    return value


class Shares:
    def __init__(self, matrix, lead=1):
        self.names = [("dp", bit) for bit in reversed(range(bits_of("dp")))]
        self.names += [("sp", bit) for bit in reversed(range(bits_of("sp")))]
        shards = lax.axis_size("dp") * lax.axis_size("sp")
        rows = matrix.shape[0] // (lead * shards)
        self.values = matrix.reshape((lead,) + (2,) * len(self.names) + (rows, matrix.shape[1]))

    def halve(self, *order):
        for name in order:
            axis = self.names.index(name)
            self.names.pop(axis)
            bit = (lax.axis_index(name[0]) >> name[1]) & 1
            send = lax.dynamic_index_in_dim(self.values, 1 - bit, axis + 1, keepdims=False)
            keep = lax.dynamic_index_in_dim(self.values, bit, axis + 1, keepdims=False)
            other = flip(send, name[0], 1 << name[1])
            self.values = (keep.astype(f32) + other.astype(f32)).astype(bf16)
        return self

    def columns(self, first, last):
        part = object.__new__(Shares)
        part.names = list(self.names)
        part.values = self.values[..., first:last]
        return part

    def result(self):
        return jnp.concatenate(list(self.values), axis=-1)


def near_and_far():
    far = ("sp", bits_of("sp") - 1)
    near = [("sp", bit) for bit in range(1, bits_of("sp") - 1)]
    return [("dp", bit) for bit in range(bits_of("dp"))] + near, far


def swap_rows(mine):
    top = lax.axis_index("sp") >> row_bits()
    send = lax.dynamic_index_in_dim(mine, 1 - top, 0, keepdims=False)
    keep = lax.dynamic_index_in_dim(mine, top, 0, keepdims=False)
    return keep, send, 1 << row_bits(), top


def in_order(keep, other, top):
    return jnp.where(top == 0, jnp.stack([keep, other]), jnp.stack([other, keep]))


def halo_of(block, segments):
    count = 1 << row_bits()
    index = lax.axis_index("sp") & (count - 1)
    rows = block.reshape(segments, -1, block.shape[-1])
    ahead = [(i, i - count + 1 if i % count == count - 1 else i + 1) for i in range(2 * count)]
    back = [(target, source) for source, target in ahead]
    low = lax.ppermute(rows[:, rows.shape[1] - HALO :], "sp", ahead)
    high = lax.ppermute(rows[:, :HALO], "sp", back)
    none = jnp.zeros_like(low[:1])
    low = jnp.where(index == 0, jnp.concatenate([none, low[:1]]), low)
    high = jnp.where(index == count - 1, jnp.concatenate([high[1:], none]), high)
    return low, high


def slot_counts(bounds):
    starts = bounds[:DOCS]
    sizes = bounds[1 : DOCS + 1] - starts
    index = jnp.arange(LMK, dtype=jnp.int32)
    upper = ((index + 1) * sizes[:, None] + LMK - 1) // LMK
    lower = (index * sizes[:, None] + LMK - 1) // LMK
    return (upper - lower).astype(f32)


def interleave(query, key):
    rows = query.shape[0]
    pair = jnp.stack([query.reshape(rows, HEADS, HD), key.reshape(rows, HEADS, HD)], axis=2)
    return pair.reshape(rows, HEADS * WIDE)


def local(
    tokens,
    doc_ids,
    doc_bounds,
    landmark_ids,
    query_weight,
    key_weight,
    value_weight,
    out_weight,
    conv_kernel,
    up_weight,
    down_weight,
    norm_gain,
    norm_bias,
    cotangent,
):
    segments, _, length, width = tokens.shape
    layers = query_weight.shape[0]
    rows = segments * length
    shard = query_weight.shape[1]
    hidden_units = up_weight.shape[2]
    folds = hidden_units // width
    every = ("dp", "sp")
    position = lax.axis_index("sp")
    group = 1 << row_bits()
    index = position & (group - 1)

    keep, send, mask, top = swap_rows(tokens[:, 0])
    token_rows = in_order(keep, flip(send, "sp", mask), top).reshape(rows, width)
    bounds = lax.dynamic_index_in_dim(doc_bounds[:, 0], top, 0, keepdims=False)
    starts = (index + group * jnp.arange(segments, dtype=jnp.int32)) * length
    positions = (starts[:, None] + jnp.arange(length, dtype=jnp.int32)).reshape(rows)
    later = positions >= bounds[1]
    begin = jnp.where(later, bounds[1], bounds[0])
    size = jnp.where(later, bounds[2], bounds[1]) - begin
    ids = later.astype(jnp.int32) * LMK + (positions - begin) * LMK // size
    row_ids, col_ids = ids[None, :], ids[:, None]
    local_bound = bounds[1] - starts
    counts = slot_counts(bounds)
    tasks = DOCS * HEADS
    each = -(-tasks // group)
    room = each * group
    place = places(tasks, each)
    inverse = jnp.broadcast_to((1.0 / counts)[:, None, :], (DOCS, HEADS, LMK))
    inverse = jnp.pad(
        inverse.reshape(tasks, LMK, 1), ((0, room - tasks), (0, 0), (0, 0)), constant_values=1.0
    )
    inverse = lax.dynamic_slice_in_dim(inverse, index * each, each, 0)

    first = []
    second = []
    for layer in range(layers):
        first.append(
            jnp.concatenate(
                [interleave(query_weight[layer], key_weight[layer]), value_weight[layer]], axis=1
            )
        )
        up_folded = jnp.swapaxes(up_weight[layer].reshape(shard, width, folds), 1, 2)
        second.append(
            jnp.concatenate(
                [
                    out_weight[layer],
                    up_folded.reshape(shard, hidden_units),
                    down_weight[layer].reshape(shard, hidden_units),
                ],
                axis=1,
            )
        )
    heads = lax.all_gather(jnp.concatenate(first, axis=1), every, axis=0, tiled=True)
    tails = [lax.all_gather(part, every, axis=0, tiled=True) for part in second]
    gathered = [
        (
            layer * 3 * width,
            tails[layer][:, :width],
            tails[layer][:, width : width + hidden_units],
            [
                tails[layer][:, width + hidden_units + s * width : width + hidden_units + (s + 1) * width]
                for s in range(folds)
            ],
        )
        for layer in range(layers)
    ]

    taps = [
        jnp.pad(jnp.repeat(conv_kernel[layer].T, HD, axis=1), ((0, TAPS - KCONV), (0, 0)))
        for layer in range(layers)
    ]
    flipped = [
        jnp.pad(jnp.repeat(conv_kernel[layer].T[::-1], HD, axis=1), ((0, TAPS - KCONV), (0, 0)))
        for layer in range(layers)
    ]

    hidden = token_rows.astype(f32)
    saved = []
    for layer in range(layers):
        _, out_w, up_w, down_w = gathered[layer]
        hidden_low = hidden.astype(bf16)
        qk, v, sums = project(place, row_ids, hidden_low, heads, room, layer)
        low, high = halo_of(v, segments)
        marks, swapped = owner_marks(to_owners(sums, each), inverse)
        all_marks = from_owners(swapped)
        pseudo = owner_pseudo(marks)
        partial = key_partial(place, row_ids, qk, v, all_marks)
        near = join_pair(partial, flip(partial[room // 2 :], "sp", 1))
        values, payload = owner_merge(send_direct(near, each), pseudo)
        all_mixed = from_owners(payload)
        weights, conv = token_prep(
            place, local_bound, col_ids, qk, v, low, high, all_marks, taps[layer]
        )
        branch = token_mix(place, weights, conv, all_mixed)
        gain, bias = norm_gain[layer], norm_bias[layer]
        normed, first_pull = jax.vjp(norm_apply, hidden + nn(branch, out_w), gain[0], bias[0])
        normed_low = normed.astype(bf16)
        expanded = nn(normed_low, up_w)
        activated, gelu_pull = jax.vjp(gelu_tanh, expanded)
        activated_low = activated.astype(bf16)
        dense = sum(
            nn(activated_low[:, s * width : (s + 1) * width], down_w[s]) for s in range(folds)
        )
        hidden, second_pull = jax.vjp(norm_apply, normed + dense, gain[1], bias[1])
        saved.append(
            (hidden_low, qk, v, low, high, marks, pseudo, all_marks, values, all_mixed, weights, branch,
             first_pull, normed_low, gelu_pull, activated_low, second_pull)
        )
    def back_home(value, send_as):
        keep, send, mask, top = swap_rows(value.reshape(segments, length, width))
        other = flip(send.astype(send_as), "sp", mask).astype(value.dtype)
        return in_order(keep, other, top)[:, None]

    output = back_home(hidden.astype(bf16), bf16)

    keep, send, mask, top = swap_rows(cotangent[:, 0])
    grad = in_order(keep, flip(send, "sp", mask), top).reshape(rows, width).astype(f32)
    early_shares = [None] * layers
    late_shares = [None] * layers
    waiting = []
    small = [None] * layers
    for layer in reversed(range(layers)):
        at, out_w, up_w, down_w = gathered[layer]
        (hidden_low, qk, v, low, high, marks, pseudo, all_marks, values, all_mixed, weights, branch,
         first_pull, normed_low, gelu_pull, activated_low, second_pull) = saved[layer]
        grad_second, gain_second, bias_second = second_pull(grad)
        dense_grad = grad_second.astype(bf16)
        grad_active = jnp.concatenate([nt(dense_grad, down_w[s]) for s in range(folds)], axis=1)
        (grad_expanded,) = gelu_pull(grad_active)
        expanded_grad = grad_expanded.astype(bf16)
        grad_first, gain_first, bias_first = first_pull(grad_second + nt(expanded_grad, up_w))
        projected_grad = grad_first.astype(bf16)
        branch_grad = nt(projected_grad, out_w).astype(bf16)
        waiting += [
            tn(normed_low, expanded_grad[:, s * width : (s + 1) * width]) for s in range(folds)
        ]
        waiting += [
            tn(activated_low[:, s * width : (s + 1) * width], dense_grad) for s in range(folds)
        ]
        waiting.append(tn(branch, projected_grad))
        shares = lax.psum_scatter(
            jnp.stack([part.astype(bf16) for part in waiting]), every, scatter_dimension=1, tiled=True
        )
        early = 2 * folds + 1
        if len(waiting) > early:
            late_shares[layer + 1] = shares[: len(waiting) - early]
        early_shares[layer] = shares[len(waiting) - early :]
        grad_low, grad_high = halo_of(branch_grad, segments)
        dq, task_grads = token_back(place, qk, branch_grad, weights, all_marks, all_mixed)
        total, payload = owner_back(to_owners(task_grads, each), pseudo, values)
        all_grads = from_owners(payload)
        own_grads = newton_back(marks, values, total)
        dconv, dtaps = conv_back(
            local_bound, v, low, high, branch_grad, grad_low, grad_high, flipped[layer]
        )
        dqk, dv, query_part = key_back(
            place, row_ids, qk, v, all_marks, all_mixed, all_grads, dq, dconv
        )
        mark_grads = from_owners(owner_last(to_owners(query_part, each), own_grads, inverse))
        dqk = spread(place, col_ids, mark_grads, dqk)
        grad = (
            grad_first
            + nt(dqk, heads[:, at : at + 2 * width])
            + nt(dv, heads[:, at + 2 * width : at + 3 * width])
        )
        waiting = [
            tn(hidden_low, dqk[:, :width]),
            tn(hidden_low, dqk[:, width:]),
            tn(hidden_low, dv),
        ]
        conv_grad = dtaps[:KCONV].reshape(KCONV, HEADS, HD).sum(axis=-1).T
        small[layer] = (
            conv_grad,
            jnp.stack([gain_first, gain_second]),
            jnp.stack([bias_first, bias_second]),
        )
    near, far = near_and_far()
    turns = []
    for turn, part in enumerate(waiting):
        shift = turn * len(near) // 3
        order = [("sp", 0)] + near[shift:] + near[:shift] + [far]
        turns.append(Shares(part.astype(bf16)).halve(*order).result())
    late_shares[0] = jnp.stack(turns)
    grad_tokens = back_home(grad, bf16)
    conv_rows = jnp.stack([small[layer][0] for layer in range(layers)]).reshape(-1)
    conv_rows = jnp.pad(conv_rows, (0, -conv_rows.shape[0] % width)).reshape(-1, width)
    scales = [small[layer][k] for k in (1, 2) for layer in range(layers)]
    packed = all_sum(jnp.concatenate(scales + [conv_rows], axis=0))
    gain_sum = packed[: 2 * layers].reshape(layers, 2, width)
    bias_sum = packed[2 * layers : 4 * layers].reshape(layers, 2, width)
    conv_sum = packed[4 * layers :].reshape(-1)[: layers * HEADS * KCONV]
    conv_sum = conv_sum.reshape(layers, HEADS, KCONV)
    results = [[] for _ in range(6)]
    for layer in range(layers):
        late = late_shares[layer].astype(f32)
        early = early_shares[layer].astype(f32)
        pair = jnp.concatenate([late[0], late[1]], axis=1).reshape(shard, HEADS, 2, HD)
        results[0].append(pair[:, :, 0].reshape(shard, width))
        results[1].append(pair[:, :, 1].reshape(shard, width))
        results[2].append(late[2])
        results[3].append(early[2 * folds])
        results[4].append(jnp.transpose(early[:folds], (1, 2, 0)).reshape(shard, hidden_units))
        results[5].append(
            jnp.swapaxes(early[folds : 2 * folds], 0, 1).reshape(shard * folds, width)
        )
    grads = [jnp.stack(parts) for parts in results]
    return (
        output,
        grad_tokens,
        grads[0],
        grads[1],
        grads[2],
        grads[3],
        conv_sum,
        grads[4],
        grads[5],
        gain_sum,
        bias_sum,
    )


def solution(mesh):
    tokens_spec = P(None, "dp", "sp", None)
    ids_spec = P(None, "dp", "sp")
    weight_spec = P(None, ("dp", "sp"), None)
    return jax.shard_map(
        local,
        mesh=mesh,
        in_specs=(
            tokens_spec,
            ids_spec,
            P(None, "dp", None),
            ids_spec,
            weight_spec,
            weight_spec,
            weight_spec,
            weight_spec,
            P(),
            weight_spec,
            weight_spec,
            P(),
            P(),
            tokens_spec,
        ),
        out_specs=(
            tokens_spec,
            tokens_spec,
            weight_spec,
            weight_spec,
            weight_spec,
            weight_spec,
            P(),
            weight_spec,
            weight_spec,
            P(),
            P(),
        ),
        check_vma=False,
    )
```

time: 1160 us -> 771 us (0.66)
  blocking collectives: 358 us -> 0 us
  Pallas kernels: 246 us -> 184 us
  starting transfers between devices: 35.1 us -> 82.6 us
  other arithmetic: 21.4 us -> 59.7 us
  matrix products: 133 us -> 98.4 us
  waiting for transfers between devices: 252 us -> 223 us
    all_gather x8 -> x0, blocking collectives: 222 us -> none  [from_owners(): whole = lax.all_gather(owned, axis, axis=0, tiled=True)]
    ppermute x8 -> x88, waiting for transfers between devices: 1.83 us -> 173 us  [the longest x80 170 us: flip(): return lax.ppermute(value, axis, [(i, i ^ mask) for i in range(count)])]
    reduce_scatter x2 -> x0, waiting for transfers between devices: 104 us -> none  [local(): lax.psum_scatter(stacked, every, scatter_dimension=0, tiled=True)]
    all_to_all x3 -> x0, blocking collectives: 97.9 us -> none  [to_owners(): return lax.all_to_all(flat, axis, 0, 0)]
    all_to_all x5 -> x0, waiting for transfers between devices: 87.4 us -> none  [to_owners(): return lax.all_to_all(flat, axis, 0, 0)]
    ppermute x8 -> x88, starting transfers between devices: 14.6 us -> 82 us  [the longest x80 77.5 us: flip(): return lax.ppermute(value, axis, [(i, i ^ mask) for i in range(count)])]
    pallas_call x20 -> x30, Pallas kernels: 246 us -> 184 us  [the longest x16 116 us: over_pairs(): pl.pallas_call(body, grid_spec=pltpu.PrefetchScalarGridSpec(num_scalar_pr...]
    psum x1 -> x0, blocking collectives: 38.1 us -> none  [local(): lax.psum(tuple((jnp.stack([small[layer][k] for layer in range(layers)]) f...]
  transfers between devices with their start and end apart: 18 -> 93, of which waited for: 7 -> 47; matrix products, arithmetic and copies ran while one was open for 14% -> 24% of each run, Pallas kernels for 13% -> 23%
where the time goes in v2:
time: 771 us; the launch traced here: 761 us
  waiting for transfers between devices  223 us (29%)
  Pallas kernels  184 us (24%)
  matrix products  98.4 us (13%)
  local copies, waits for them, and re-layouts  94.9 us (12%)
  starting transfers between devices  82.6 us (11%)
  other arithmetic  59.7 us (8%)
  between operations  17.8 us (2%)
    ppermute x80, waiting for transfers between devices, flip(): return lax.ppermute(value, axis, [(i, i ^ mask) for i in range(count)])  170 us
    pallas_call x16, Pallas kernels, over_pairs(): pl.pallas_call(body, grid_spec=pltpu.PrefetchScalarGridSpec(num_scalar_pr...  116 us
    ppermute x80, starting transfers between devices, flip(): return lax.ppermute(value, axis, [(i, i ^ mask) for i in range(count)])  77.5 us
    pallas_call x12, Pallas kernels, small_call(): pl.pallas_call(body, out_shape=out_shape, scratch_shapes=scratch, cost_es...  61.7 us
    all_gather x1, waiting for transfers between devices, local(): lax.all_gather(jnp.concatenate(first, axis=1), every, axis=0, tiled=True)  50.8 us
    unnamed x395, local copies, waits for them, and re-layouts  45.4 us
    dot_general x16, matrix products, nt(): lax.dot_general(left, right, (((1,), (1,)), ((), ())), preferred_element_...  44.3 us
    dot_general x12, matrix products, nn(): lax.dot_general(left, right, (((1,), (0,)), ((), ())), preferred_element_...  33.3 us
  transfers between devices with their start and end apart: 93, of which 47 were waited for; matrix products, arithmetic and copies ran while one was open for 24% of the time, Pallas kernels for 23%

profile of v2, /device:TPU:0, one launch (start us, length us, event | category | flops | bytes accessed | tf_op | source)
XLA Modules:
  0.0 760.9 jit_solution(7076439364160043600)
XLA Ops:
  23.3 18.0 %collective-permute-done = bf16[256,768]{1,0:T(8,128)(2,1)S(1)} collective-permute-done((bf16[256,768]{1,0:T(8,128)(2,1)S(1)}, bf16[256,768]{1,0:T(8,128)(2,1)S(1)}, u32[]{:S(2)}, u32[]{:S(2)}) %collective-permute-start) | collective-permute-done | bytes 393248 | tf_op jit(solution)/shard_map/ppermute | solution.py:771
  41.5 50.8 %all-gather.4.cloned.1.call-done.qk_weight_ref.v_weight_ref = bf16[768,4608]{1,0:T(8,128)(2,1)} async-done(((bf16[24,4608]{1,0:T(8,128)(2,1)}), bf16[768,4608]{1,0:T(8,128)(2,1)}) %all-gather.4.cloned.1.call-update) | async-done | bytes 7077904 | tf_op jit(solution)/shard_map/all_gather | solution.py:963
  92.3 6.9 project.2
  105.2 5.4 fusion.160.ids_ref
  123.9 4.9 collective-permute-done.7
  136.7 5.5 key_partial.2.mine_ref
  152.9 6.1 owner_pseudo.2.refs_4_
  165.6 10.5 %token_prep.2 = (bf16[512,1536]{1,0:T(8,128)(2,1)S(1)}, f32[512,768]{1,0:T(8,128)S(1)}) custom-call(s32[24]{0:T(128)S(1)} %fusion.173.place_ref, s32[2]{0:T(128)S(1)} %broadcast_subtract_fusion.bound_ref, s32[512,1]{1,0:T(8,128)S(1)} %copy-done.29, bf16[512,1536]{1,0:T(8,128)(2,1)} %copy-done.2, bf16[512,768]{1,0:T(8,128)(2,1)S(1)} %get-tuple-element.48.v_ref, ...), custom_call_target="tpu_custom_call" | custom-call | flops 10000000000 | bytes 6121472 | tf_op jit(solution)/shard_map/token_prep/pallas_call | solution.py:106
  191.0 9.0 %multiply_convert_fusion.1 = (bf16[512,3072]{1,0:T(8,128)(2,1)S(1)}, f32[512,3072]{1,0:T(8,128)}) fusion(bf16[512,768]{1,0:T(8,128)(2,1)S(1)} %fusion.76, bf16[768,6912]{1,0:T(8,128)(2,1)} %all-gather.6.cloned.1.call-done), kind=kOutput, calls=%fused_computation.21 | convolution fusion | flops 2430074880 | bytes 14942208 | tf_op jit(solution)/shard_map/dot_general | solution.py:31
  210.8 6.9 project.3
  226.0 12.0 %collective-permute-done.22.refs_3_ = bf16[3,64,128]{2,1,0:T(8,128)(2,1)S(1)} collective-permute-done((bf16[3,64,128]{2,1,0:T(8,128)(2,1)S(1)}, bf16[3,64,128]{2,1,0:T(8,128)(2,1)S(1)}, u32[]{:S(2)}, u32[]{:S(2)}) %collective-permute-start.22) | collective-permute-done | bytes 49184 | tf_op jit(solution)/shard_map/ppermute | solution.py:771
  250.1 6.6 collective-permute-done.24
  258.3 6.0 key_partial.3.mine_ref
  274.9 6.2 owner_pseudo.3.refs_4_
  286.4 10.5 %token_prep.3 = (bf16[512,1536]{1,0:T(8,128)(2,1)S(1)}, f32[512,768]{1,0:T(8,128)S(1)}) custom-call(s32[24]{0:T(128)S(1)} %fusion.173.place_ref, s32[2]{0:T(128)S(1)} %broadcast_subtract_fusion.bound_ref, s32[512,1]{1,0:T(8,128)S(1)} %copy-done.30, bf16[512,1536]{1,0:T(8,128)(2,1)} %copy-done.4, bf16[512,768]{1,0:T(8,128)(2,1)S(1)} %copy-done.20, ...), custom_call_target="tpu_custom_call" | custom-call | flops 10000000000 | bytes 6121472 | tf_op jit(solution)/shard_map/token_prep/pallas_call | solution.py:106
  310.7 5.8 multiply_convert_fusion
  339.8 6.1 multiply_reduce_fusion
  350.0 7.0 token_back.2
  392.2 13.7 %conv_back.2 = (f32[512,768]{1,0:T(8,128)S(1)}, f32[40,768]{1,0:T(8,128)S(1)}) custom-call(s32[2]{0:T(128)S(1)} %broadcast_subtract_fusion.bound_ref, bf16[512,768]{1,0:T(8,128)(2,1)S(1)} %copy-done.21, bf16[2,16,768]{2,1,0:T(8,128)(2,1)S(1)} %copy-done.64, bf16[2,16,768]{2,1,0:T(8,128)(2,1)S(1)} %copy-done.62, bf16[512,768]{1,0:T(8,128)(2,1)S(1)} %copy-done.35, ...), custom_call_target="tpu_custom_call" | custom-call | flops 10000000000 | bytes 3588096 | tf_op jit(solution)/shard_map/conv_back/pallas_call | solution.py:106
  406.0 8.8 %key_back.2 = (f32[512,1536]{1,0:T(8,128)}, bf16[512,768]{1,0:T(8,128)(2,1)S(1)}, bf16[24,32,128]{2,1,0:T(8,128)(2,1)S(1)}) custom-call(s32[24]{0:T(128)S(1)} %fusion.173.place_ref, s32[1,512]{1,0:T(1,128)S(1)} %fusion.168.ids_ref, bf16[512,1536]{1,0:T(8,128)(2,1)S(1)} %copy-done.5, bf16[512,768]{1,0:T(8,128)(2,1)S(1)} %copy-done.21, ...), custom_call_target="tpu_custom_call" | custom-call | flops 1006632960 | bytes 12388352 | tf_op jit(solution)/shard_map/key_back/pallas_call | solution.py:106
  421.2 16.6 %newton_back.2.refs_4_ = f32[3,64,128]{2,1,0:T(8,128)} custom-call(f32[3,64,128]{2,1,0:T(8,128)} %get-tuple-element.61.marks_ref, f32[3,64,128]{2,1,0:T(8,128)} %get-tuple-element.64.refs_5_.values_ref, f32[3,64,128]{2,1,0:T(8,128)} %get-tuple-element.69.total_ref), custom_call_target="tpu_custom_call" | custom-call | flops 15000000512 | bytes 1000000 | tf_op jit(solution)/shard_map/newton_back/pallas_call | solution.py:256
  442.0 7.2 collective-permute-done.48
  480.7 6.1 multiply_reduce_fusion.2
  499.6 6.4 copy.198
  510.7 7.0 token_back.3
  552.6 13.7 %conv_back.3 = (f32[512,768]{1,0:T(8,128)S(1)}, f32[40,768]{1,0:T(8,128)S(1)}) custom-call(s32[2]{0:T(128)S(1)} %broadcast_subtract_fusion.bound_ref, bf16[512,768]{1,0:T(8,128)(2,1)S(1)} %copy-done.18, bf16[2,16,768]{2,1,0:T(8,128)(2,1)S(1)} %copy-done.60, bf16[2,16,768]{2,1,0:T(8,128)(2,1)S(1)} %copy-done.58, bf16[512,768]{1,0:T(8,128)(2,1)S(1)} %copy-done.37, ...), custom_call_target="tpu_custom_call" | custom-call | flops 10000000000 | bytes 3588096 | tf_op jit(solution)/shard_map/conv_back/pallas_call | solution.py:106
  584.6 7.1 collective-permute-done.85
  595.2 8.7 %key_back.3 = (f32[512,1536]{1,0:T(8,128)}, bf16[512,768]{1,0:T(8,128)(2,1)S(1)}, bf16[24,32,128]{2,1,0:T(8,128)(2,1)S(1)}) custom-call(s32[24]{0:T(128)S(1)} %fusion.173.place_ref, s32[1,512]{1,0:T(1,128)S(1)} %fusion.168.ids_ref, bf16[512,1536]{1,0:T(8,128)(2,1)S(1)} %copy-done.3, bf16[512,768]{1,0:T(8,128)(2,1)S(1)} %copy-done.18, ...), custom_call_target="tpu_custom_call" | custom-call | flops 1006632960 | bytes 12388352 | tf_op jit(solution)/shard_map/key_back/pallas_call | solution.py:106
  613.4 16.4 %newton_back.3.refs_4_ = f32[3,64,128]{2,1,0:T(8,128)} custom-call(f32[3,64,128]{2,1,0:T(8,128)} %get-tuple-element.53.marks_ref, f32[3,64,128]{2,1,0:T(8,128)} %get-tuple-element.73.refs_5_.values_ref, f32[3,64,128]{2,1,0:T(8,128)} %get-tuple-element.78.total_ref), custom_call_target="tpu_custom_call" | custom-call | flops 15000000512 | bytes 1000000 | tf_op jit(solution)/shard_map/newton_back/pallas_call | solution.py:256
  632.7 9.4 %collective-permute-done.33 = bf16[256,768]{1,0:T(8,128)(2,1)S(1)} collective-permute-done((bf16[256,768]{1,0:T(8,128)(2,1)S(1)}, bf16[256,768]{1,0:T(8,128)(2,1)S(1)}, u32[]{:S(2)}, u32[]{:S(2)}) %collective-permute-start.33) | collective-permute-done | bytes 393248 | tf_op jit(solution)/shard_map/ppermute | solution.py:771
  666.0 33.8 %collective-permute-done.67 = bf16[256,768]{1,0:T(8,128)(2,1)S(1)} collective-permute-done((bf16[256,768]{1,0:T(8,128)(2,1)S(1)}, bf16[256,768]{1,0:T(8,128)(2,1)S(1)}, u32[]{:S(2)}, u32[]{:S(2)}) %collective-permute-start.67) | collective-permute-done | bytes 393248 | tf_op jit(solution)/shard_map/ppermute | solution.py:771
  720.5 4.6 collective-permute-done.75
  (914 shorter events, 399.8 us)
Async XLA Ops:
  7.2 85.0 %all-gather.4.cloned.1.call-start = ((), (), s32[]{:S(2)}) async-start(), calls=%async_computation.2 | async-start | bytes 7299072 | tf_op jit(solution)/shard_map/all_gather | solution.py:963
  10.9 176.7 %all-gather.6.cloned.1.call-start = ((), (), s32[]{:S(2)}) async-start(), calls=%async_computation.3 | async-start | bytes 10948608 | tf_op jit(solution)/shard_map/all_gather | solution.py:964
  12.9 293.8 %all-gather.8.cloned.1.call-start = ((), (), s32[]{:S(2)}) async-start(), calls=%async_computation.4 | async-start | bytes 10948608 | tf_op jit(solution)/shard_map/all_gather | solution.py:964
  14.8 725.4 %reduce-scatter.9.cloned.1.call-start = ((), (), s32[]{:S(2)}) async-start(), calls=%async_computation.6 | async-start | bytes 10948608
  14.9 26.4 %collective-permute-start = (bf16[256,768]{1,0:T(8,128)(2,1)S(1)}, bf16[256,768]{1,0:T(8,128)(2,1)S(1)}, u32[]{:S(2)}, u32[]{:S(2)}) collective-permute-start(bf16[256,768]{1,0:T(8,128)(2,1)S(1)} %get-tuple-element.189), channel_id=1, source_target_pairs={{0,8},{1,9},{2,10},{3,11},{4,12},{5,13},{6,14},{7,15},{8,0},{9,1},... | collective-permute-start | bytes 1179656 | tf_op jit(solution)/shard_map/ppermute | solution.py:771
  219.1 101.4 %collective-permute-start.34 = (bf16[256,768]{1,0:T(8,128)(2,1)}, bf16[256,768]{1,0:T(8,128)(2,1)}, u32[]{:S(2)}, u32[]{:S(2)}) collective-permute-start(bf16[256,768]{1,0:T(8,128)(2,1)} %get-tuple-element.180), channel_id=1, source_target_pairs={{0,8},{1,9},{2,10},{3,11},{4,12},{5,13},{6,14},{7,15},{8,0},{9,1},... | collective-permute-start | bytes 1179656 | tf_op jit(solution)/shard_map/ppermute | solution.py:771
  222.2 15.9 %collective-permute-start.22 = (bf16[3,64,128]{2,1,0:T(8,128)(2,1)S(1)}, bf16[3,64,128]{2,1,0:T(8,128)(2,1)S(1)}, u32[]{:S(2)}, u32[]{:S(2)}) collective-permute-start(bf16[3,64,128]{2,1,0:T(8,128)(2,1)S(1)} %get-tuple-element.216), channel_id=1, source_target_pairs={{0,6},{1,7},{2,4},{3,5},{4,2},{5,3},{6,0},{7,1},{8,14},{9,15},{10,... | collective-permute-start | bytes 147464 | tf_op jit(solution)/shard_map/ppermute | solution.py:771
  223.7 14.3 %collective-permute-start.21 = (bf16[3,64,128]{2,1,0:T(8,128)(2,1)S(1)}, bf16[3,64,128]{2,1,0:T(8,128)(2,1)S(1)}, u32[]{:S(2)}, u32[]{:S(2)}) collective-permute-start(bf16[3,64,128]{2,1,0:T(8,128)(2,1)S(1)} %get-tuple-element.217), channel_id=1, source_target_pairs={{0,2},{1,3},{2,0},{3,1},{4,6},{5,7},{6,4},{7,5},{8,10},{9,11},{10,... | collective-permute-start | bytes 147464 | tf_op jit(solution)/shard_map/ppermute | solution.py:771
  223.9 14.7 %collective-permute-start.20 = (bf16[3,64,128]{2,1,0:T(8,128)(2,1)S(1)}, bf16[3,64,128]{2,1,0:T(8,128)(2,1)S(1)}, u32[]{:S(2)}, u32[]{:S(2)}) collective-permute-start(bf16[3,64,128]{2,1,0:T(8,128)(2,1)S(1)} %get-tuple-element.218), channel_id=1, source_target_pairs={{0,4},{1,5},{2,6},{3,7},{4,0},{5,1},{6,2},{7,3},{8,12},{9,13},{10,... | collective-permute-start | bytes 147464 | tf_op jit(solution)/shard_map/ppermute | solution.py:771
  225.7 21.1 %collective-permute-start.18 = (bf16[2,16,768]{2,1,0:T(8,128)(2,1)S(1)}, bf16[2,16,768]{2,1,0:T(8,128)(2,1)S(1)}, u32[]{:S(2)}, u32[]{:S(2)}) collective-permute-start(bf16[2,16,768]{2,1,0:T(8,128)(2,1)S(1)} %get-tuple-element.184), channel_id=1, source_target_pairs={{1,0},{2,1},{3,2},{4,3},{5,4},{6,5},{7,6},{0,7},{9,8},{10,9},{11,1... | collective-permute-start | bytes 147464 | tf_op jit(solution)/shard_map/ppermute | solution.py:873
  357.1 20.5 %collective-permute-start.43 = (bf16[2,16,768]{2,1,0:T(8,128)(2,1)S(1)}, bf16[2,16,768]{2,1,0:T(8,128)(2,1)S(1)}, u32[]{:S(2)}, u32[]{:S(2)}) collective-permute-start(bf16[2,16,768]{2,1,0:T(8,128)(2,1)S(1)} %get-tuple-element.178), channel_id=1, source_target_pairs={{1,0},{2,1},{3,2},{4,3},{5,4},{6,5},{7,6},{0,7},{9,8},{10,9},{11,1... | collective-permute-start | bytes 147464 | tf_op jit(solution)/shard_map/ppermute | solution.py:873
  359.0 23.0 %collective-permute-start.42 = (bf16[2,16,768]{2,1,0:T(8,128)(2,1)S(1)}, bf16[2,16,768]{2,1,0:T(8,128)(2,1)S(1)}, u32[]{:S(2)}, u32[]{:S(2)}) collective-permute-start(bf16[2,16,768]{2,1,0:T(8,128)(2,1)S(1)} %get-tuple-element.179), channel_id=1, source_target_pairs={{0,1},{1,2},{2,3},{3,4},{4,5},{5,6},{6,7},{7,0},{8,9},{9,10},{10,1... | collective-permute-start | bytes 147464 | tf_op jit(solution)/shard_map/ppermute | solution.py:872
  377.1 365.9 %reduce-scatter.7.cloned.1.call-start = ((), (), s32[]{:S(2)}) async-start(), calls=%async_computation.5 | async-start | bytes 14598144
  390.9 15.1 %collective-permute-start.41 = (bf16[12,64,128]{2,1,0:T(8,128)(2,1)S(1)}, bf16[12,64,128]{2,1,0:T(8,128)(2,1)S(1)}, u32[]{:S(2)}, u32[]{:S(2)}) collective-permute-start(bf16[12,64,128]{2,1,0:T(8,128)(2,1)S(1)} %pad_maximum_fusion.17), channel_id=1, source_target_pairs={{0,1},{1,0},{2,3},{3,2},{4,5},{5,4},{6,7},{7,6},{8,9},{9,8},{10,11... | collective-permute-start | bytes 589832 | tf_op jit(solution)/shard_map/ppermute | solution.py:771
  417.8 20.1 %collective-permute-start.47 = (bf16[3,32,128]{2,1,0:T(8,128)(2,1)S(1)}, bf16[3,32,128]{2,1,0:T(8,128)(2,1)S(1)}, u32[]{:S(2)}, u32[]{:S(2)}) collective-permute-start(bf16[3,32,128]{2,1,0:T(8,128)(2,1)S(1)} %get-tuple-element.232), channel_id=1, source_target_pairs={{0,6},{1,7},{2,4},{3,5},{4,2},{5,3},{6,0},{7,1},{8,14},{9,15},{10,... | collective-permute-start | bytes 73736 | tf_op jit(solution)/shard_map/ppermute | solution.py:771
  420.7 17.2 %collective-permute-start.46 = (bf16[3,32,128]{2,1,0:T(8,128)(2,1)S(1)}, bf16[3,32,128]{2,1,0:T(8,128)(2,1)S(1)}, u32[]{:S(2)}, u32[]{:S(2)}) collective-permute-start(bf16[3,32,128]{2,1,0:T(8,128)(2,1)S(1)} %get-tuple-element.233), channel_id=1, source_target_pairs={{0,2},{1,3},{2,0},{3,1},{4,6},{5,7},{6,4},{7,5},{8,10},{9,11},{10,... | collective-permute-start | bytes 73736 | tf_op jit(solution)/shard_map/ppermute | solution.py:771
  421.0 16.8 %collective-permute-start.45 = (bf16[3,32,128]{2,1,0:T(8,128)(2,1)S(1)}, bf16[3,32,128]{2,1,0:T(8,128)(2,1)}, u32[]{:S(2)}, u32[]{:S(2)}) collective-permute-start(bf16[3,32,128]{2,1,0:T(8,128)(2,1)S(1)} %get-tuple-element.234), channel_id=1, source_target_pairs={{0,4},{1,5},{2,6},{3,7},{4,0},{5,1},{6,2},{7,3},{8,12},{9,13},{10,... | collective-permute-start | bytes 73736 | tf_op jit(solution)/shard_map/ppermute | solution.py:771
  518.5 11.4 %collective-permute-start.51 = (bf16[12,64,128]{2,1,0:T(8,128)(2,1)}, bf16[12,64,128]{2,1,0:T(8,128)(2,1)}, u32[]{:S(2)}, u32[]{:S(2)}) collective-permute-start(bf16[12,64,128]{2,1,0:T(8,128)(2,1)} %slice.581), channel_id=1, source_target_pairs={{0,1},{1,0},{2,3},{3,2},{4,5},{5,4},{6,7},{7,6},{8,9},{9,8},{10,11... | collective-permute-start | bytes 589832 | tf_op jit(solution)/shard_map/ppermute | solution.py:771
  548.2 22.7 %collective-permute-start.56 = (bf16[6,64,128]{2,1,0:T(8,128)(2,1)}, bf16[6,64,128]{2,1,0:T(8,128)(2,1)}, u32[]{:S(2)}, u32[]{:S(2)}) collective-permute-start(bf16[6,64,128]{2,1,0:T(8,128)(2,1)} %pad_maximum_fusion.31), channel_id=1, source_target_pairs={{0,2},{1,3},{2,0},{3,1},{4,6},{5,7},{6,4},{7,5},{8,10},{9,11},{10,... | collective-permute-start | bytes 294920 | tf_op jit(solution)/shard_map/ppermute | solution.py:771
  572.5 20.2 %collective-permute-start.57 = (bf16[12,64,128]{2,1,0:T(8,128)(2,1)}, bf16[12,64,128]{2,1,0:T(8,128)(2,1)}, u32[]{:S(2)}, u32[]{:S(2)}) collective-permute-start(bf16[12,64,128]{2,1,0:T(8,128)(2,1)} %pad_maximum_fusion.19), channel_id=1, source_target_pairs={{0,1},{1,0},{2,3},{3,2},{4,5},{5,4},{6,7},{7,6},{8,9},{9,8},{10,11... | collective-permute-start | bytes 589832 | tf_op jit(solution)/shard_map/ppermute | solution.py:771
  592.6 15.1 %collective-permute-start.86 = (f32[10,768]{1,0:T(8,128)S(1)}, f32[10,768]{1,0:T(8,128)S(1)}, u32[]{:S(2)}, u32[]{:S(2)}) collective-permute-start(f32[10,768]{1,0:T(8,128)S(1)} %add.553), channel_id=1, source_target_pairs={{0,8},{1,9},{2,10},{3,11},{4,12},{5,13},{6,14},{7,15},{8,0},{9,1},... | collective-permute-start | bytes 92168 | tf_op jit(solution)/shard_map/ppermute | solution.py:771
  604.9 37.2 %collective-permute-start.33 = (bf16[256,768]{1,0:T(8,128)(2,1)S(1)}, bf16[256,768]{1,0:T(8,128)(2,1)S(1)}, u32[]{:S(2)}, u32[]{:S(2)}) collective-permute-start(bf16[256,768]{1,0:T(8,128)(2,1)S(1)} %get-tuple-element.183), channel_id=1, source_target_pairs={{0,8},{1,9},{2,10},{3,11},{4,12},{5,13},{6,14},{7,15},{8,0},{9,1},... | collective-permute-start | bytes 1179656 | tf_op jit(solution)/shard_map/ppermute | solution.py:771
  607.7 35.4 %collective-permute-start.87 = (f32[10,768]{1,0:T(8,128)S(1)}, f32[10,768]{1,0:T(8,128)S(1)}, u32[]{:S(2)}, u32[]{:S(2)}) collective-permute-start(f32[10,768]{1,0:T(8,128)S(1)} %add.554), channel_id=1, source_target_pairs={{0,16},{16,0},{1,17},{17,1},{2,18},{18,2},{3,19},{19,3},{4,20},{20... | collective-permute-start | bytes 92168 | tf_op jit(solution)/shard_map/ppermute | solution.py:771
  609.9 19.9 %collective-permute-start.63 = (bf16[3,32,128]{2,1,0:T(8,128)(2,1)S(1)}, bf16[3,32,128]{2,1,0:T(8,128)(2,1)S(1)}, u32[]{:S(2)}, u32[]{:S(2)}) collective-permute-start(bf16[3,32,128]{2,1,0:T(8,128)(2,1)S(1)} %get-tuple-element.228), channel_id=1, source_target_pairs={{0,6},{1,7},{2,4},{3,5},{4,2},{5,3},{6,0},{7,1},{8,14},{9,15},{10,... | collective-permute-start | bytes 73736 | tf_op jit(solution)/shard_map/ppermute | solution.py:771
  610.6 19.2 %collective-permute-start.62 = (bf16[3,32,128]{2,1,0:T(8,128)(2,1)S(1)}, bf16[3,32,128]{2,1,0:T(8,128)(2,1)S(1)}, u32[]{:S(2)}, u32[]{:S(2)}) collective-permute-start(bf16[3,32,128]{2,1,0:T(8,128)(2,1)S(1)} %get-tuple-element.229), channel_id=1, source_target_pairs={{0,2},{1,3},{2,0},{3,1},{4,6},{5,7},{6,4},{7,5},{8,10},{9,11},{10,... | collective-permute-start | bytes 73736 | tf_op jit(solution)/shard_map/ppermute | solution.py:771
  611.3 18.5 %collective-permute-start.61 = (bf16[3,32,128]{2,1,0:T(8,128)(2,1)S(1)}, bf16[3,32,128]{2,1,0:T(8,128)(2,1)S(1)}, u32[]{:S(2)}, u32[]{:S(2)}) collective-permute-start(bf16[3,32,128]{2,1,0:T(8,128)(2,1)S(1)} %get-tuple-element.230), channel_id=1, source_target_pairs={{0,4},{1,5},{2,6},{3,7},{4,0},{5,1},{6,2},{7,3},{8,12},{9,13},{10,... | collective-permute-start | bytes 73736 | tf_op jit(solution)/shard_map/ppermute | solution.py:771
  650.6 12.6 %collective-permute-start.78 = (bf16[1,2,2,2,2,24,768]{6,5,2,4,1,3,0:T(8,128)(2,1)S(1)}, bf16[1,2,2,2,2,24,768]{6,5,2,4,1,3,0:T(8,128)(2,1)S(1)}, u32[]{:S(2)}, u32[]{:S(2)}) collective-permute-start(bf16[1,2,2,2,2,24,768]{6,5,2,4,1,3,0:T(8,128)(2,1)S(1)} %bitcast.369), channel_id=1, source_target_pairs={{0,1},{1,0},{2,3},{3,2},{4,5},{5,4},{6,7},{7,6},{8,9},{9,8},{10,11... | collective-permute-start | bytes 1769480 | tf_op jit(solution)/shard_map/ppermute | solution.py:771
  656.2 50.4 %collective-permute-start.73 = (bf16[1,2,2,2,2,24,768]{6,5,2,1,3,4,0:T(8,128)(2,1)S(1)}, bf16[1,2,2,2,2,24,768]{6,5,2,1,3,4,0:T(8,128)(2,1)S(1)}, u32[]{:S(2)}, u32[]{:S(2)}) collective-permute-start(bf16[1,2,2,2,2,24,768]{6,5,2,1,3,4,0:T(8,128)(2,1)S(1)} %bitcast.367), channel_id=1, source_target_pairs={{0,1},{1,0},{2,3},{3,2},{4,5},{5,4},{6,7},{7,6},{8,9},{9,8},{10,11... | collective-permute-start | bytes 1769480 | tf_op jit(solution)/shard_map/ppermute | solution.py:771
  662.2 37.6 %collective-permute-start.67 = (bf16[256,768]{1,0:T(8,128)(2,1)S(1)}, bf16[256,768]{1,0:T(8,128)(2,1)S(1)}, u32[]{:S(2)}, u32[]{:S(2)}) collective-permute-start(bf16[256,768]{1,0:T(8,128)(2,1)S(1)} %fusion.155), channel_id=1, source_target_pairs={{0,8},{1,9},{2,10},{3,11},{4,12},{5,13},{6,14},{7,15},{8,0},{9,1},... | collective-permute-start | bytes 1179656 | tf_op jit(solution)/shard_map/ppermute | solution.py:771
  663.3 36.5 %collective-permute-start.79 = (bf16[1,2,2,2,24,768]{5,4,2,3,1,0:T(8,128)(2,1)S(1)}, bf16[1,2,2,2,24,768]{5,4,2,3,1,0:T(8,128)(2,1)S(1)}, u32[]{:S(2)}, u32[]{:S(2)}) collective-permute-start(bf16[1,2,2,2,24,768]{5,4,2,3,1,0:T(8,128)(2,1)S(1)} %dynamic-slice_bitcast_fusion.7), channel_id=1, source_target_pairs={{0,4},{1,5},{2,6},{3,7},{4,0},{5,1},{6,2},{7,3},{8,12},{9,13},{10,... | collective-permute-start | bytes 884744 | tf_op jit(solution)/shard_map/ppermute | solution.py:771
  665.9 42.5 %collective-permute-start.68 = (bf16[1,2,2,2,2,24,768]{6,5,2,3,4,1,0:T(8,128)(2,1)S(1)}, bf16[1,2,2,2,2,24,768]{6,5,2,3,4,1,0:T(8,128)(2,1)S(1)}, u32[]{:S(2)}, u32[]{:S(2)}) collective-permute-start(bf16[1,2,2,2,2,24,768]{6,5,2,3,4,1,0:T(8,128)(2,1)S(1)} %bitcast.368), channel_id=1, source_target_pairs={{0,1},{1,0},{2,3},{3,2},{4,5},{5,4},{6,7},{7,6},{8,9},{9,8},{10,11... | collective-permute-start | bytes 1769480 | tf_op jit(solution)/shard_map/ppermute | solution.py:771
  706.8 12.3 %collective-permute-start.74 = (bf16[1,2,2,2,24,768]{5,4,2,1,3,0:T(8,128)(2,1)S(1)}, bf16[1,2,2,2,24,768]{5,4,2,1,3,0:T(8,128)(2,1)S(1)}, u32[]{:S(2)}, u32[]{:S(2)}) collective-permute-start(bf16[1,2,2,2,24,768]{5,4,2,1,3,0:T(8,128)(2,1)S(1)} %dynamic-slice_bitcast_fusion.8), channel_id=1, source_target_pairs={{0,2},{1,3},{2,0},{3,1},{4,6},{5,7},{6,4},{7,5},{8,10},{9,11},{10,... | collective-permute-start | bytes 884744 | tf_op jit(solution)/shard_map/ppermute | solution.py:771
  (253 other events, 1957.2 us)
Sparse Core Ops, SparseCore 0:
  11.5 80.6 all-gather.3
  95.7 88.2 all-gather.5
  186.9 100.1 all-gather.7
  377.2 143.5 reduce-scatter.8
  526.6 197.8 reduce-scatter.6

commit v3 on v2

--- a/solution.py
+++ b/solution.py
@@ -19,6 +19,7 @@
 WIDE = 2 * HD
 WINDOW = 40
 TAPS = 40
+CHUNK = 128
 
 negative = -1e30
 epsilon = 1e-05
@@ -61,6 +62,14 @@
 
 def htn(left, right):
     return three_pass(tn, left, right)
+
+
+def lnt(left, right):
+    return nt(left.astype(bf16), right.astype(bf16))
+
+
+def ltn(left, right):
+    return tn(left.astype(bf16), right.astype(bf16))
 
 
 def iota(shape, dim):
@@ -95,6 +104,10 @@
 
 def lanes3(batches, rows, width):
     return pl.BlockSpec((batches, rows, width), lambda p, *scalars: (0, 0, p))
+
+
+def in_hbm(array):
+    return pltpu.with_memory_space_constraint(array, pltpu.HBM)
 
 
 def over_pairs(body, name, scalars, in_specs, out_specs, out_shape, args, flops, scratch=()):
@@ -114,33 +127,45 @@
         ),
         out_shape=out_shape,
         cost_estimate=pl.CostEstimate(flops=flops, bytes_accessed=moved, transcendentals=0),
-        compiler_params=pltpu.CompilerParams(vmem_limit_bytes=48 * 1024 * 1024),
+        compiler_params=pltpu.CompilerParams(vmem_limit_bytes=16 * 1024 * 1024),
         name=name,
-    )(*scalars, *args)
-
-
-def project_kernel(place_ref, ids_ref, hidden_ref, qk_weight_ref, v_weight_ref, qk_ref, v_ref, sums_ref):
+    )(*scalars, *[in_hbm(a) for a in args])
+
+
+def project_kernel(
+    place_ref, ids_ref, hidden_qk_ref, hidden_v_ref, qk_weight_ref, v_weight_ref,
+    qk_ref, v_ref, sums_ref,
+):
     pair = pl.program_id(0)
-    qk_ref[...] = nn(hidden_ref[...], qk_weight_ref[...]).astype(bf16)
-    v_ref[...] = nn(hidden_ref[...], v_weight_ref[...]).astype(bf16)
+    qk_ref[...] = nn(hidden_qk_ref[0], qk_weight_ref[0]).astype(bf16)
+    v_ref[...] = nn(hidden_v_ref[0], v_weight_ref[0]).astype(bf16)
     onehot = (iota((SLOTS, ids_ref.shape[1]), 0) == ids_ref[...]).astype(f32).astype(bf16)
     sums = nn(onehot, qk_ref[...])
     for side in range(2):
         write_marks(sums_ref, place_ref, 2 * pair + side, sums[:, side * WIDE : (side + 1) * WIDE])
 
 
-def project(place, row_ids, hidden_low, weight, room, layer):
-    rows, width = hidden_low.shape
-    first = layer * 3 * PAIRS
+def project(place, row_ids, hidden, weight, room, first):
+    count, rows, width = hidden.shape
+    per = PAIRS // 2
+    if count > 1:
+        hidden_qk = lambda p, *s: (p // per, 0, 0)
+        weight_qk = lambda p, *s: (p // per, 0, p % per)
+        weight_v = lambda p, *s: (2, 0, p)
+    else:
+        hidden_qk = lambda p, *s: (0, 0, 0)
+        weight_qk = lambda p, *s: (0, 0, first // (2 * WIDE) + p)
+        weight_v = lambda p, *s: (0, 0, first // WIDE + HEADS + p)
     return over_pairs(
         project_kernel,
         "project",
         (place,),
         [
             whole(row_ids.shape),
-            whole(hidden_low.shape),
-            pl.BlockSpec((width, 2 * WIDE), lambda p, *s: (0, first // 2 + p)),
-            pl.BlockSpec((width, WIDE), lambda p, *s: (0, first + HEADS + p)),
+            pl.BlockSpec((1, rows, width), hidden_qk),
+            pl.BlockSpec((1, rows, width), lambda p, *s: (count - 1, 0, 0)),
+            pl.BlockSpec((1, width, 2 * WIDE), weight_qk),
+            pl.BlockSpec((1, width, WIDE), weight_v),
         ],
         [lanes(rows, 2 * WIDE), lanes(rows, WIDE), whole((room, LMK, WIDE))],
         (
@@ -148,7 +173,7 @@
             jax.ShapeDtypeStruct((rows, HEADS * HD), bf16),
             jax.ShapeDtypeStruct((room, LMK, WIDE), f32),
         ),
-        (row_ids, hidden_low, weight, weight),
+        (row_ids, hidden, hidden, weight, weight),
         2 * rows * width * 3 * width,
     )
 
@@ -287,18 +312,21 @@
     )
 
 
-def pseudo_kernel(marks_ref, pseudo_ref):
+def pseudo_kernel(marks_ref, pseudo_ref, kernel_ref, steps_ref):
     count = marks_ref.shape[0]
     kernels = [mark_softmax(marks_ref[t][:, :HD], marks_ref[t][:, HD:]) for t in range(count)]
-    for task, pseudo in enumerate(newton(kernels)):
+    for task, pseudo in enumerate(newton(kernels, steps_ref)):
         pseudo_ref[task] = pseudo
+        kernel_ref[task] = kernels[task]
 
 
 def owner_pseudo(marks):
+    count = marks.shape[0]
+    square = jax.ShapeDtypeStruct((count, LMK, LMK), f32)
     return small_call(
         pseudo_kernel,
         "owner_pseudo",
-        jax.ShapeDtypeStruct((marks.shape[0], LMK, LMK), f32),
+        (square, square, jax.ShapeDtypeStruct((NS_ITERS, count, 4, LMK, LMK), f32)),
         (marks,),
         flops=5 * 10**9,
     )
@@ -340,6 +368,16 @@
     )
 
 
+def tap_rows(scalar_ref, flipped):
+    first = 2 * pl.program_id(0) * KCONV
+    left = iota((1, WIDE), 1) < HD
+    rows = []
+    for offset in range(KCONV):
+        tap = KCONV - 1 - offset if flipped else offset
+        rows.append(jnp.where(left, scalar_ref[first + tap], scalar_ref[first + KCONV + tap]))
+    return rows
+
+
 def fill_padded(pad_ref, low, center, high):
     length = center.shape[0]
     pad_ref[0:HALO] = low.astype(f32)
@@ -357,19 +395,19 @@
     return pl.multiple_of(start, 8)
 
 
-def convolve(pad_ref, taps_ref, bound, out_ref):
+def convolve(pad_ref, taps, bound, out_ref):
     length = out_ref.shape[0]
     block = 64
     for first in range(0, length, block):
         total = jnp.zeros((block, WIDE), f32)
         for offset in range(KCONV):
-            total = total + pad_ref[first + offset : first + offset + block] * taps_ref[offset : offset + 1]
+            total = total + pad_ref[first + offset : first + offset + block] * taps[offset]
         out_ref[first : first + block] = total
     start = window_start(bound, length)
     total = jnp.zeros((WINDOW, WIDE), f32)
     for offset in range(KCONV):
         nearby = pad_ref[pl.ds(start + offset, WINDOW)]
-        total = total + jnp.where(same_side(start, bound, offset), nearby, 0.0) * taps_ref[offset : offset + 1]
+        total = total + jnp.where(same_side(start, bound, offset), nearby, 0.0) * taps[offset]
     out_ref[pl.ds(start, WINDOW)] = total
 
 
@@ -392,19 +430,43 @@
     return block.astype(bf16)
 
 
-def token_prep_kernel(
-    place_ref, bound_ref, ids_ref, qk_ref, v_ref, low_ref, high_ref, marks_ref, taps_ref,
-    weights_ref, conv_ref, pad_ref, acc_ref,
+def conv_kernel_body(
+    bound_ref, scalar_ref, v_ref, low_ref, high_ref, conv_ref, pad_ref, acc_ref
 ):
+    taps = tap_rows(scalar_ref, False)
     segments = low_ref.shape[0]
     length = v_ref.shape[0] // segments
-    pair = pl.program_id(0)
-    lane = iota((SLOTS, WIDE), 1)
     for segment in range(segments):
         rows = slice(segment * length, (segment + 1) * length)
         fill_padded(pad_ref, low_ref[segment], v_ref[rows], high_ref[segment])
-        convolve(pad_ref, taps_ref, bound_ref[segment], acc_ref)
+        convolve(pad_ref, taps, bound_ref[segment], acc_ref)
         conv_ref[rows] = acc_ref[...]
+
+
+def conv_forward(bounds, v, low, high, taps):
+    rows = v.shape[0]
+    segments = low.shape[0]
+    length = rows // segments
+    return over_pairs(
+        conv_kernel_body,
+        "conv_forward",
+        (bounds, taps),
+        [
+            lanes(rows, WIDE),
+            lanes3(segments, HALO, WIDE),
+            lanes3(segments, HALO, WIDE),
+        ],
+        lanes(rows, WIDE),
+        jax.ShapeDtypeStruct((rows, HEADS * HD), f32),
+        (v, low, high),
+        5 * 10**9,
+        [pltpu.VMEM((length + 2 * HALO, WIDE), f32), pltpu.VMEM((length, WIDE), f32)],
+    )
+
+
+def token_prep_kernel(place_ref, ids_ref, qk_ref, marks_ref, weights_ref):
+    pair = pl.program_id(0)
+    lane = iota((SLOTS, WIDE), 1)
     keep = (ids_ref[...] >> 6) == (iota((ids_ref.shape[0], SLOTS), 1) >> 6)
     for side in range(2):
         columns = slice(side * WIDE, (side + 1) * WIDE)
@@ -416,31 +478,17 @@
         weights_ref[:, columns] = weights.astype(bf16)
 
 
-def token_prep(place, bounds, col_ids, qk, v, low, high, marks, taps):
-    rows = v.shape[0]
-    segments = low.shape[0]
-    length = rows // segments
+def token_prep(place, col_ids, qk, marks):
+    rows = qk.shape[0]
     return over_pairs(
         token_prep_kernel,
         "token_prep",
-        (place, bounds),
-        [
-            whole(col_ids.shape),
-            lanes(rows, 2 * WIDE),
-            lanes(rows, WIDE),
-            lanes3(segments, HALO, WIDE),
-            lanes3(segments, HALO, WIDE),
-            whole(marks.shape),
-            lanes(TAPS, WIDE),
-        ],
-        [lanes(rows, 2 * WIDE), lanes(rows, WIDE)],
-        (
-            jax.ShapeDtypeStruct((rows, HEADS * WIDE), bf16),
-            jax.ShapeDtypeStruct((rows, HEADS * HD), f32),
-        ),
-        (col_ids, qk, v, low, high, marks, taps),
-        10**10,
-        [pltpu.VMEM((length + 2 * HALO, WIDE), f32), pltpu.VMEM((length, WIDE), f32)],
+        (place,),
+        [whole(col_ids.shape), lanes(rows, 2 * WIDE), whole(marks.shape)],
+        lanes(rows, 2 * WIDE),
+        jax.ShapeDtypeStruct((rows, HEADS * WIDE), bf16),
+        (col_ids, qk, marks),
+        5 * 10**9,
     )
 
 
@@ -519,18 +567,19 @@
 
 
 def conv_back_kernel(
-    bound_ref, v_ref, low_ref, high_ref, grad_ref, grad_low_ref, grad_high_ref, taps_ref,
+    bound_ref, scalar_ref, v_ref, low_ref, high_ref, grad_ref, grad_low_ref, grad_high_ref,
     dv_ref, dtaps_ref, pad_ref, acc_ref,
 ):
     batches = low_ref.shape[0]
     length = v_ref.shape[0] // batches
     dtaps_ref[KCONV:] = jnp.zeros((TAPS - KCONV, WIDE), f32)
+    taps = tap_rows(scalar_ref, True)
     for batch in range(batches):
         rows = slice(batch * length, (batch + 1) * length)
         bound = bound_ref[batch]
         grad = grad_ref[rows].astype(f32)
         fill_padded(pad_ref, grad_low_ref[batch], grad, grad_high_ref[batch])
-        convolve(pad_ref, taps_ref, bound, acc_ref)
+        convolve(pad_ref, taps, bound, acc_ref)
         dv_ref[rows] = acc_ref[...]
         fill_padded(pad_ref, low_ref[batch], v_ref[rows], high_ref[batch])
         acc_ref[...] = grad
@@ -547,7 +596,7 @@
     return over_pairs(
         conv_back_kernel,
         "conv_back",
-        (bounds,),
+        (bounds, taps),
         [
             lanes(rows, WIDE),
             lanes3(batches, HALO, WIDE),
@@ -555,14 +604,13 @@
             lanes(rows, WIDE),
             lanes3(batches, HALO, WIDE),
             lanes3(batches, HALO, WIDE),
-            lanes(TAPS, WIDE),
         ],
         [lanes(rows, WIDE), lanes(TAPS, WIDE)],
         (
             jax.ShapeDtypeStruct((rows, HEADS * HD), f32),
             jax.ShapeDtypeStruct((TAPS, HEADS * HD), f32),
         ),
-        (v, low, high, grad, grad_low, grad_high, taps),
+        (v, low, high, grad, grad_low, grad_high),
         10**10,
         [pltpu.VMEM((length + 2 * HALO, WIDE), f32), pltpu.VMEM((length, WIDE), f32)],
     )
@@ -591,14 +639,13 @@
     )
 
 
-def newton_back_kernel(marks_ref, values_ref, total_ref, out_ref, steps_ref):
+def newton_back_kernel(marks_ref, kernel_ref, steps_ref, values_ref, total_ref, out_ref):
     count = marks_ref.shape[0]
     tasks = range(count)
     marks = [marks_ref[task] for task in tasks]
     queries = [m[:, :HD] for m in marks]
     keys = [m[:, HD:] for m in marks]
-    kernels = [mark_softmax(q, k) for q, k in zip(queries, keys)]
-    newton(kernels, steps_ref)
+    kernels = [kernel_ref[task] for task in tasks]
     eye = identity()
 
     def sweep(index, carry):
@@ -608,19 +655,19 @@
             approx, product, middle, outer = (
                 steps_ref[NS_ITERS - 1 - index, task, slot] for slot in range(4)
             )
-            grad_outer = 0.25 * htn(approx, grad)
-            grad_middle = -htn(product, grad_outer)
-            grad_inner = -htn(product, grad_middle)
+            grad_outer = 0.25 * ltn(approx, grad)
+            grad_middle = -ltn(product, grad_outer)
+            grad_inner = -ltn(product, grad_middle)
             grad_product = (
-                -hnt(grad_outer, middle) - hnt(grad_middle, 7.0 * eye - product) - grad_inner
+                -lnt(grad_outer, middle) - lnt(grad_middle, 7.0 * eye - product) - grad_inner
             )
-            grad_kernel = grad_kernel + hnt(grad_product, approx)
-            grad = 0.25 * hnt(grad, outer) + htn(kernels[task], grad_product)
+            grad_kernel = grad_kernel + lnt(grad_product, approx)
+            grad = 0.25 * lnt(grad, outer) + ltn(kernels[task], grad_product)
             results.append((grad, grad_kernel))
         return tuple(results)
 
     start = tuple(
-        (hnt(total_ref[task][:, HD:], values_ref[task][:, :HD]), jnp.zeros((LMK, LMK), f32))
+        (lnt(total_ref[task][:, HD:], values_ref[task][:, :HD]), jnp.zeros((LMK, LMK), f32))
         for task in tasks
     )
     ends = lax.fori_loop(0, NS_ITERS, sweep, start)
@@ -631,18 +678,17 @@
         inner = jnp.sum(kernel * grad_kernel, axis=1, keepdims=True)
         grad_scores = kernel * (grad_kernel - inner) * score_scale
         grad_queries = hnn(grad_scores, keys[task])
-        grad_keys = htn(grad_scores, queries[task]) + total_ref[task][:, :HD]
+        grad_keys = ltn(grad_scores, queries[task]) + total_ref[task][:, :HD]
         out_ref[task] = jnp.concatenate([grad_queries, grad_keys], axis=1)
 
 
-def newton_back(marks, values, total):
+def newton_back(marks, kernel, steps, values, total):
     return small_call(
         newton_back_kernel,
         "newton_back",
         jax.ShapeDtypeStruct(marks.shape, f32),
-        (marks, values, total),
-        [pltpu.VMEM((NS_ITERS, marks.shape[0], 4, LMK, LMK), f32)],
-        15 * 10**9,
+        (marks, kernel, steps, values, total),
+        flops=10**10,
     )
 
 
@@ -668,7 +714,7 @@
 
 
 def key_back_kernel(
-    place_ref, ids_ref, qk_ref, v_ref, marks_ref, mixed_ref, grads_ref, dq_ref, dconv_ref,
+    place_ref, ids_ref, qk_ref, v_ref, marks_ref, mixed_ref, grads_ref, dq_ref,
     dqk_ref, dv_ref, part_ref,
 ):
     pair = pl.program_id(0)
@@ -676,7 +722,7 @@
     half = iota((LMK // 2, WIDE), 1)
     keep = (ids_ref[...] >> 6) == (iota((SLOTS, ids_ref.shape[1]), 0) >> 6)
     values = v_ref[...]
-    grad_values = dconv_ref[...]
+    grad_values = 0.0
     for side in range(2):
         columns = slice(side * WIDE, (side + 1) * WIDE)
         head = 2 * pair + side
@@ -700,10 +746,10 @@
             part_ref[task_rows(place_ref, doc, head)] = jnp.where(
                 half < HD, pltpu.roll(upper, HD, 1), lower
             ).astype(bf16)
-    dv_ref[...] = grad_values.astype(bf16)
-
-
-def key_back(place, row_ids, qk, v, marks, mixed, grads, dq, dconv):
+    dv_ref[...] = grad_values
+
+
+def key_back(place, row_ids, qk, v, marks, mixed, grads, dq):
     rows = qk.shape[0]
     part_shape = (marks.shape[0], LMK // 2, WIDE)
     return over_pairs(
@@ -718,48 +764,242 @@
             whole(mixed.shape),
             whole(grads.shape),
             lanes(rows, 2 * WIDE),
-            lanes(rows, WIDE),
         ],
         [lanes(rows, 2 * WIDE), lanes(rows, WIDE), whole(part_shape)],
         (
             jax.ShapeDtypeStruct((rows, HEADS * WIDE), f32),
-            jax.ShapeDtypeStruct((rows, HEADS * HD), bf16),
+            jax.ShapeDtypeStruct((rows, HEADS * HD), f32),
             jax.ShapeDtypeStruct(part_shape, bf16),
         ),
-        (row_ids, qk, v, marks, mixed, grads, dq, dconv),
+        (row_ids, qk, v, marks, mixed, grads, dq),
         10 * rows * SLOTS * WIDE * HEADS,
     )
 
 
-def spread_kernel(place_ref, ids_ref, marks_ref, dqk_ref, out_ref):
+def spread_kernel(
+    place_ref, ids_ref, marks_ref, dqk_in_ref, dv_in_ref, dconv_ref, first_ref, qk_weight_ref, v_weight_ref,
+    dqk_ref, dv_ref, grad_ref,
+):
     pair = pl.program_id(0)
     onehot = (iota((ids_ref.shape[0], SLOTS), 1) == ids_ref[...]).astype(f32).astype(bf16)
     marks = [read_marks(marks_ref, place_ref, 2 * pair + side).astype(bf16) for side in range(2)]
-    out_ref[...] = (dqk_ref[...] + nn(onehot, jnp.concatenate(marks, axis=1))).astype(bf16)
-
-
-def spread(place, col_ids, marks, dqk):
-    rows = dqk.shape[0]
+    dqk = (dqk_in_ref[...] + nn(onehot, jnp.concatenate(marks, axis=1))).astype(bf16)
+    dv = (dv_in_ref[...] + dconv_ref[...]).astype(bf16)
+    dqk_ref[...] = dqk
+    dv_ref[...] = dv
+
+    @pl.when(pair == 0)
+    def _():
+        grad_ref[...] = first_ref[...]
+
+    grad_ref[...] += nt(dqk, qk_weight_ref[...]) + nt(dv, v_weight_ref[...])
+
+
+def spread(place, col_ids, marks, dqk, dv, dconv, grad_first, weight, first):
+    rows, width = grad_first.shape
     return over_pairs(
         spread_kernel,
         "spread",
         (place,),
-        [whole(col_ids.shape), whole(marks.shape), lanes(rows, 2 * WIDE)],
-        lanes(rows, 2 * WIDE),
-        jax.ShapeDtypeStruct(dqk.shape, bf16),
-        (col_ids, marks, dqk),
-        2 * rows * SLOTS * WIDE * HEADS,
-    )
-
-
-def norm_apply(summed, layer_gain, layer_bias):
+        [
+            whole(col_ids.shape),
+            whole(marks.shape),
+            lanes(rows, 2 * WIDE),
+            lanes(rows, WIDE),
+            lanes(rows, WIDE),
+            whole(grad_first.shape),
+            pl.BlockSpec((width, 2 * WIDE), lambda p, *s: (0, first // (2 * WIDE) + p)),
+            pl.BlockSpec((width, WIDE), lambda p, *s: (0, first // WIDE + HEADS + p)),
+        ],
+        [lanes(rows, 2 * WIDE), lanes(rows, WIDE), whole(grad_first.shape)],
+        (
+            jax.ShapeDtypeStruct(dqk.shape, bf16),
+            jax.ShapeDtypeStruct(dv.shape, bf16),
+            jax.ShapeDtypeStruct(grad_first.shape, f32),
+        ),
+        (col_ids, marks, dqk, dv, dconv, grad_first, weight, weight),
+        8 * rows * width * width,
+    )
+
+
+gelu_scale = (2.0 / jnp.pi) ** 0.5
+gelu_cubic = 0.044715
+
+
+def normalize(summed):
     center = summed - jnp.mean(summed, axis=-1, keepdims=True)
-    spread_of = jnp.mean(center * center, axis=-1, keepdims=True)
-    return center * lax.rsqrt(spread_of + epsilon) * layer_gain + layer_bias
-
-
-def gelu_tanh(values):
-    return jax.nn.gelu(values, approximate=True)
+    inverse = lax.rsqrt(jnp.mean(center * center, axis=-1, keepdims=True) + epsilon)
+    return center * inverse, inverse
+
+
+def normalize_back(grad, gain, unit, inverse):
+    scaled = grad * gain
+    mean = jnp.mean(scaled, axis=-1, keepdims=True)
+    along = jnp.mean(scaled * unit, axis=-1, keepdims=True)
+    return inverse * (scaled - mean - unit * along)
+
+
+def row_chunks(ref):
+    size = min(CHUNK, ref.shape[0])
+    return [slice(first, first + size) for first in range(0, ref.shape[0], size)]
+
+
+def dense_kernel(
+    hidden_ref, branch_ref, out_ref, up_ref, down_ref, gain_ref, bias_ref,
+    unit_first_ref, inverse_first_ref, normed_low_ref, expanded_ref, active_ref,
+    unit_second_ref, inverse_second_ref, result_ref, result_low_ref, normed_ref, total_ref,
+):
+    step = pl.program_id(0)
+
+    @pl.when(step == 0)
+    def _():
+        unit, inverse = normalize(hidden_ref[...] + nn(branch_ref[...], out_ref[...]))
+        unit_first_ref[...] = unit
+        inverse_first_ref[...] = jnp.broadcast_to(inverse, inverse_first_ref.shape)
+        normed = unit * gain_ref[0:1] + bias_ref[0:1]
+        normed_ref[...] = normed
+        normed_low_ref[...] = normed.astype(bf16)
+        total_ref[...] = normed
+
+    for rows in row_chunks(normed_low_ref):
+        expanded = nn(normed_low_ref[rows], up_ref[...])
+        expanded_ref[rows] = expanded
+        bent = jnp.tanh(gelu_scale * (expanded + gelu_cubic * (expanded * expanded * expanded)))
+        active = (0.5 * expanded * (1.0 + bent)).astype(bf16)
+        active_ref[rows] = active
+        total_ref[rows] += nn(active, down_ref[...])
+
+    @pl.when(step == pl.num_programs(0) - 1)
+    def _():
+        unit, inverse = normalize(total_ref[...])
+        unit_second_ref[...] = unit
+        inverse_second_ref[...] = jnp.broadcast_to(inverse, inverse_second_ref.shape)
+        result = unit * gain_ref[1:2] + bias_ref[1:2]
+        result_ref[...] = result
+        result_low_ref[...] = result.astype(bf16)
+
+
+def dense_call(body, name, folds, in_specs, out_specs, out_shape, args, flops, scratch):
+    return pl.pallas_call(
+        body,
+        grid=(folds,),
+        in_specs=in_specs,
+        out_specs=out_specs,
+        out_shape=out_shape,
+        scratch_shapes=scratch,
+        cost_estimate=pl.CostEstimate(flops=flops, bytes_accessed=3 * 10**7, transcendentals=0),
+        compiler_params=pltpu.CompilerParams(vmem_limit_bytes=44 * 1024 * 1024),
+        name=name,
+    )(*[in_hbm(a) for a in args])
+
+
+def weight_specs(width, folds):
+    return [
+        pl.BlockSpec((width, width), lambda k: (0, 0)),
+        pl.BlockSpec((width, width), lambda k: (0, 1 + k)),
+        pl.BlockSpec((width, width), lambda k: (0, 1 + folds + k)),
+    ]
+
+
+def fixed(shape):
+    return pl.BlockSpec(shape, lambda k: (0,) * len(shape))
+
+
+def dense_forward(hidden, branch, weights, gain, bias, folds):
+    rows, width = hidden.shape
+    wide, thin = (rows, width), (rows, WIDE)
+    moving = pl.BlockSpec(wide, lambda k: (0, k))
+    return dense_call(
+        dense_kernel,
+        "dense_forward",
+        folds,
+        [fixed(wide), fixed(wide)] + weight_specs(width, folds) + [fixed(gain.shape), fixed(bias.shape)],
+        [
+            fixed(wide), fixed(thin), fixed(wide), moving, moving,
+            fixed(wide), fixed(thin), fixed(wide), fixed(wide),
+        ],
+        (
+            jax.ShapeDtypeStruct(wide, f32),
+            jax.ShapeDtypeStruct(thin, f32),
+            jax.ShapeDtypeStruct(wide, bf16),
+            jax.ShapeDtypeStruct((rows, folds * width), f32),
+            jax.ShapeDtypeStruct((rows, folds * width), bf16),
+            jax.ShapeDtypeStruct(wide, f32),
+            jax.ShapeDtypeStruct(thin, f32),
+            jax.ShapeDtypeStruct(wide, f32),
+            jax.ShapeDtypeStruct(wide, bf16),
+        ),
+        (hidden, branch, weights, weights, weights, gain, bias),
+        2 * rows * width * width * (1 + 2 * folds),
+        [pltpu.VMEM(wide, f32), pltpu.VMEM(wide, f32)],
+    )
+
+
+def dense_back_kernel(
+    grad_ref, unit_first_ref, inverse_first_ref, expanded_ref, unit_second_ref, inverse_second_ref,
+    out_ref, up_ref, down_ref, gain_ref,
+    dense_ref, expanded_grad_ref, first_ref, projected_ref, branch_ref, scales_ref, total_ref,
+):
+    step = pl.program_id(0)
+
+    @pl.when(step == 0)
+    def _():
+        grad, unit = grad_ref[...], unit_second_ref[...]
+        second = normalize_back(grad, gain_ref[1:2], unit, inverse_second_ref[:, 0:1])
+        total_ref[...] = second
+        dense_ref[...] = second.astype(bf16)
+        scales_ref[1:2] = jnp.sum(grad * unit, axis=0, keepdims=True)
+        scales_ref[3:4] = jnp.sum(grad, axis=0, keepdims=True)
+
+    for rows in row_chunks(dense_ref):
+        expanded = expanded_ref[rows]
+        square = expanded * expanded
+        bent = jnp.tanh(gelu_scale * (expanded + gelu_cubic * (square * expanded)))
+        slope = 0.5 * (1.0 + bent) + 0.5 * expanded * (1.0 - bent * bent) * (
+            gelu_scale * (1.0 + 3.0 * gelu_cubic * square)
+        )
+        expanded_grad = (nt(dense_ref[rows], down_ref[...]) * slope).astype(bf16)
+        expanded_grad_ref[rows] = expanded_grad
+        total_ref[rows] += nt(expanded_grad, up_ref[...])
+
+    @pl.when(step == pl.num_programs(0) - 1)
+    def _():
+        grad, unit = total_ref[...], unit_first_ref[...]
+        first = normalize_back(grad, gain_ref[0:1], unit, inverse_first_ref[:, 0:1])
+        first_ref[...] = first
+        projected = first.astype(bf16)
+        projected_ref[...] = projected
+        branch_ref[...] = nt(projected, out_ref[...]).astype(bf16)
+        scales_ref[0:1] = jnp.sum(grad * unit, axis=0, keepdims=True)
+        scales_ref[2:3] = jnp.sum(grad, axis=0, keepdims=True)
+
+
+def dense_backward(grad, kept, weights, gain, folds):
+    unit_first, inverse_first, expanded, unit_second, inverse_second = kept
+    rows, width = grad.shape
+    wide, thin = (rows, width), (rows, WIDE)
+    moving = pl.BlockSpec(wide, lambda k: (0, k))
+    return dense_call(
+        dense_back_kernel,
+        "dense_backward",
+        folds,
+        [fixed(wide), fixed(wide), fixed(thin), moving, fixed(wide), fixed(thin)]
+        + weight_specs(width, folds)
+        + [fixed(gain.shape)],
+        [fixed(wide), moving, fixed(wide), fixed(wide), fixed(wide), fixed((4, width))],
+        (
+            jax.ShapeDtypeStruct(wide, bf16),
+            jax.ShapeDtypeStruct((rows, folds * width), bf16),
+            jax.ShapeDtypeStruct(wide, f32),
+            jax.ShapeDtypeStruct(wide, bf16),
+            jax.ShapeDtypeStruct(wide, bf16),
+            jax.ShapeDtypeStruct((4, width), f32),
+        ),
+        (grad, unit_first, inverse_first, expanded, unit_second, inverse_second,
+         weights, weights, weights, gain),
+        2 * rows * width * width * (1 + 2 * folds),
+        [pltpu.VMEM(wide, f32)],
+    )
 
 
 def bits_of(axis):
@@ -803,11 +1043,13 @@
     return send_direct(near, each)
 
 
-def from_owners(owned):
+def from_owners(owned, beside=None):
     gathered = owned
-    for bit in reversed(range(row_bits())):
+    for number, bit in enumerate(reversed(range(row_bits()))):
+        if beside is not None and number == 1:
+            gathered, beside = lax.optimization_barrier((gathered, beside))
         gathered = jnp.concatenate([gathered, flip(gathered, "sp", 1 << bit)], axis=0)
-    return gathered
+    return gathered if beside is None else (gathered, beside)
 
 
 def all_sum(value):
@@ -846,10 +1088,24 @@
         return jnp.concatenate(list(self.values), axis=-1)
 
 
-def near_and_far():
-    far = ("sp", bits_of("sp") - 1)
-    near = [("sp", bit) for bit in range(1, bits_of("sp") - 1)]
-    return [("dp", bit) for bit in range(bits_of("dp"))] + near, far
+def turn_order(turn):
+    near = [("dp", bit) for bit in range(bits_of("dp"))]
+    near += [("sp", bit) for bit in range(1, bits_of("sp") - 1)]
+    shift = turn * len(near) // 3
+    return [("sp", 0)] + near[shift:] + near[:shift] + [("sp", bits_of("sp") - 1)]
+
+
+def turned(width, turn):
+    shard = width // (lax.axis_size("dp") * lax.axis_size("sp"))
+    column = jnp.arange(width, dtype=jnp.int32)
+    order = turn_order(turn)
+    away = column // shard
+    owner = lax.axis_index("dp") * lax.axis_size("sp") + lax.axis_index("sp")
+    for number, (axis, bit) in enumerate(order):
+        weight = (lax.axis_size("sp") if axis == "dp" else 1) << bit
+        owner = owner ^ (((away >> (len(order) - 1 - number)) & 1) * weight)
+    source = owner * shard + column % shard
+    return (iota((width, width), 0) == source[None, :]).astype(bf16)
 
 
 def swap_rows(mine):
@@ -884,6 +1140,26 @@
     upper = ((index + 1) * sizes[:, None] + LMK - 1) // LMK
     lower = (index * sizes[:, None] + LMK - 1) // LMK
     return (upper - lower).astype(f32)
+
+
+def fold_matrix(folds):
+    size = folds * WIDE
+    row, column = iota((size, size), 0), iota((size, size), 1)
+    return (row == (column % WIDE) * folds + column // WIDE).astype(bf16)
+
+
+def folded(matrix, fold, folds):
+    rows, columns = matrix.shape
+    blocks = columns // (folds * WIDE)
+    parts = nn(matrix.reshape(rows * blocks, folds * WIDE), fold).astype(bf16)
+    return jnp.swapaxes(parts.reshape(rows, blocks, folds, WIDE), 1, 2).reshape(rows, columns)
+
+
+def unfolded(matrix, fold, folds):
+    rows, columns = matrix.shape
+    blocks = columns // (folds * WIDE)
+    parts = jnp.swapaxes(matrix.reshape(rows, folds, blocks, WIDE), 1, 2)
+    return nt(parts.reshape(rows * blocks, folds * WIDE), fold).reshape(rows, columns)
 
 
 def interleave(query, key):
@@ -924,11 +1200,12 @@
     bounds = lax.dynamic_index_in_dim(doc_bounds[:, 0], top, 0, keepdims=False)
     starts = (index + group * jnp.arange(segments, dtype=jnp.int32)) * length
     positions = (starts[:, None] + jnp.arange(length, dtype=jnp.int32)).reshape(rows)
-    later = positions >= bounds[1]
+    later = positions[None, :] >= bounds[1]
     begin = jnp.where(later, bounds[1], bounds[0])
     size = jnp.where(later, bounds[2], bounds[1]) - begin
-    ids = later.astype(jnp.int32) * LMK + (positions - begin) * LMK // size
-    row_ids, col_ids = ids[None, :], ids[:, None]
+    ids = later.astype(jnp.int32) * LMK + (positions[None, :] - begin) * LMK // size
+    row_ids = lax.optimization_barrier(ids)
+    col_ids = row_ids.reshape(rows, 1)
     local_bound = bounds[1] - starts
     counts = slot_counts(bounds)
     tasks = DOCS * HEADS
@@ -941,157 +1218,157 @@
     )
     inverse = lax.dynamic_slice_in_dim(inverse, index * each, each, 0)
 
-    first = []
-    second = []
-    for layer in range(layers):
-        first.append(
-            jnp.concatenate(
-                [interleave(query_weight[layer], key_weight[layer]), value_weight[layer]], axis=1
-            )
-        )
-        up_folded = jnp.swapaxes(up_weight[layer].reshape(shard, width, folds), 1, 2)
-        second.append(
-            jnp.concatenate(
-                [
-                    out_weight[layer],
-                    up_folded.reshape(shard, hidden_units),
-                    down_weight[layer].reshape(shard, hidden_units),
-                ],
-                axis=1,
-            )
-        )
-    heads = lax.all_gather(jnp.concatenate(first, axis=1), every, axis=0, tiled=True)
-    tails = [lax.all_gather(part, every, axis=0, tiled=True) for part in second]
-    gathered = [
-        (
-            layer * 3 * width,
-            tails[layer][:, :width],
-            tails[layer][:, width : width + hidden_units],
-            [
-                tails[layer][:, width + hidden_units + s * width : width + hidden_units + (s + 1) * width]
-                for s in range(folds)
-            ],
+    first = [
+        jnp.concatenate(
+            [interleave(query_weight[layer], key_weight[layer]), value_weight[layer]], axis=1
         )
         for layer in range(layers)
     ]
-
-    taps = [
-        jnp.pad(jnp.repeat(conv_kernel[layer].T, HD, axis=1), ((0, TAPS - KCONV), (0, 0)))
-        for layer in range(layers)
-    ]
-    flipped = [
-        jnp.pad(jnp.repeat(conv_kernel[layer].T[::-1], HD, axis=1), ((0, TAPS - KCONV), (0, 0)))
-        for layer in range(layers)
-    ]
-
+    turns = [first[0][:, t * width : (t + 1) * width] for t in range(3)]
+    orders = [list(reversed(turn_order(t))) for t in range(3)]
+    fold = fold_matrix(folds)
+    tails = [None] * layers
+    for number in range(len(orders[0])):
+        if number == 2:
+            turns, held = lax.optimization_barrier(
+                (turns, (first[1:], out_weight, up_weight, down_weight))
+            )
+            later_first = held[0] + [first[0]]
+            up_folded = folded(held[2].reshape(layers * shard, hidden_units), fold, folds)
+            up_folded = up_folded.reshape(layers, shard, hidden_units)
+            later_blocks = [
+                jnp.concatenate(
+                    [
+                        held[1][layer],
+                        up_folded[layer],
+                        held[3][layer].reshape(shard, hidden_units),
+                        later_first[layer],
+                    ],
+                    axis=1,
+                )
+                for layer in range(layers)
+            ]
+        if number == 3:
+            turns, token_rows = lax.optimization_barrier((turns, token_rows))
+        if number == len(orders[0]) - 1:
+            turns, later_blocks[0] = lax.optimization_barrier((turns, later_blocks[0]))
+        turns = [
+            jnp.concatenate([turn, flip(turn, order[number][0], 1 << order[number][1])], axis=0)
+            for turn, order in zip(turns, orders)
+        ]
+    start = jnp.stack(turns)
+    start_hidden = jnp.stack([nn(token_rows, turned(width, t)).astype(bf16) for t in range(3)])
+    tails = [lax.all_gather(part, every, axis=0, tiled=True) for part in later_blocks]
+    place_of_heads = width + 2 * hidden_units
+
+    taps = [conv_kernel[layer].reshape(-1) for layer in range(layers)]
     hidden = token_rows.astype(f32)
+    hidden_low = token_rows
+    cotangent_keep, cotangent_send, mask, top = swap_rows(cotangent[:, 0])
     saved = []
     for layer in range(layers):
-        _, out_w, up_w, down_w = gathered[layer]
-        hidden_low = hidden.astype(bf16)
-        qk, v, sums = project(place, row_ids, hidden_low, heads, room, layer)
+        weights = tails[layer]
+        if layer:
+            qk, v, sums = project(
+                place, row_ids, hidden_low[None], tails[layer - 1][None], room, place_of_heads
+            )
+        else:
+            qk, v, sums = project(place, row_ids, start_hidden, start, room, 0)
         low, high = halo_of(v, segments)
         marks, swapped = owner_marks(to_owners(sums, each), inverse)
-        all_marks = from_owners(swapped)
-        pseudo = owner_pseudo(marks)
+        swapped, v_conv = lax.optimization_barrier((swapped, v))
+        conv = conv_forward(local_bound, v_conv, low, high, taps[layer])
+        all_marks, conv = from_owners(swapped, conv)
+        pseudo, mark_kernel, steps = owner_pseudo(marks)
         partial = key_partial(place, row_ids, qk, v, all_marks)
         near = join_pair(partial, flip(partial[room // 2 :], "sp", 1))
         values, payload = owner_merge(send_direct(near, each), pseudo)
-        all_mixed = from_owners(payload)
-        weights, conv = token_prep(
-            place, local_bound, col_ids, qk, v, low, high, all_marks, taps[layer]
+        payload, qk_held = lax.optimization_barrier((payload, qk))
+        token_weights = token_prep(place, col_ids, qk_held, all_marks)
+        all_mixed, token_weights = from_owners(payload, token_weights)
+        branch = token_mix(place, token_weights, conv, all_mixed)
+        (unit_first, inverse_first, normed_low, expanded, activated_low,
+         unit_second, inverse_second, next_hidden, next_low) = dense_forward(
+            hidden, branch, weights, norm_gain[layer], norm_bias[layer], folds
         )
-        branch = token_mix(place, weights, conv, all_mixed)
-        gain, bias = norm_gain[layer], norm_bias[layer]
-        normed, first_pull = jax.vjp(norm_apply, hidden + nn(branch, out_w), gain[0], bias[0])
-        normed_low = normed.astype(bf16)
-        expanded = nn(normed_low, up_w)
-        activated, gelu_pull = jax.vjp(gelu_tanh, expanded)
-        activated_low = activated.astype(bf16)
-        dense = sum(
-            nn(activated_low[:, s * width : (s + 1) * width], down_w[s]) for s in range(folds)
+        kept = (unit_first, inverse_first, expanded, unit_second, inverse_second)
+        saved.append(
+            (hidden_low, qk, v, low, high, marks, pseudo, mark_kernel, steps, all_marks, values,
+             all_mixed, token_weights, branch, normed_low, activated_low, kept)
         )
-        hidden, second_pull = jax.vjp(norm_apply, normed + dense, gain[1], bias[1])
-        saved.append(
-            (hidden_low, qk, v, low, high, marks, pseudo, all_marks, values, all_mixed, weights, branch,
-             first_pull, normed_low, gelu_pull, activated_low, second_pull)
-        )
-    def back_home(value, send_as):
-        keep, send, mask, top = swap_rows(value.reshape(segments, length, width))
-        other = flip(send.astype(send_as), "sp", mask).astype(value.dtype)
-        return in_order(keep, other, top)[:, None]
-
-    output = back_home(hidden.astype(bf16), bf16)
-
-    keep, send, mask, top = swap_rows(cotangent[:, 0])
-    grad = in_order(keep, flip(send, "sp", mask), top).reshape(rows, width).astype(f32)
+        hidden, hidden_low = next_hidden, next_low
+        if layer == 0:
+            hidden_low, cotangent_send = lax.optimization_barrier((hidden_low, cotangent_send))
+            cotangent_other = flip(cotangent_send, "sp", mask)
+
+    cotangent_other, hidden_low = lax.optimization_barrier((cotangent_other, hidden_low))
+    grad = in_order(cotangent_keep, cotangent_other, top).reshape(rows, width).astype(f32)
+    keep, send, mask, top = swap_rows(hidden_low.reshape(segments, length, width))
+    output = in_order(keep, flip(send, "sp", mask), top)[:, None]
     early_shares = [None] * layers
     late_shares = [None] * layers
     waiting = []
     small = [None] * layers
     for layer in reversed(range(layers)):
-        at, out_w, up_w, down_w = gathered[layer]
-        (hidden_low, qk, v, low, high, marks, pseudo, all_marks, values, all_mixed, weights, branch,
-         first_pull, normed_low, gelu_pull, activated_low, second_pull) = saved[layer]
-        grad_second, gain_second, bias_second = second_pull(grad)
-        dense_grad = grad_second.astype(bf16)
-        grad_active = jnp.concatenate([nt(dense_grad, down_w[s]) for s in range(folds)], axis=1)
-        (grad_expanded,) = gelu_pull(grad_active)
-        expanded_grad = grad_expanded.astype(bf16)
-        grad_first, gain_first, bias_first = first_pull(grad_second + nt(expanded_grad, up_w))
-        projected_grad = grad_first.astype(bf16)
-        branch_grad = nt(projected_grad, out_w).astype(bf16)
-        waiting += [
-            tn(normed_low, expanded_grad[:, s * width : (s + 1) * width]) for s in range(folds)
-        ]
+        (hidden_low, qk, v, low, high, marks, pseudo, mark_kernel, steps, all_marks, values,
+         all_mixed, token_weights, branch, normed_low, activated_low, kept) = saved[layer]
+        dense_grad, expanded_grad, grad_first, projected_grad, branch_grad, scales = dense_backward(
+            grad, kept, tails[layer], norm_gain[layer], folds
+        )
+        grad_low, grad_high = halo_of(branch_grad, segments)
+        dq, task_grads = token_back(place, qk, branch_grad, token_weights, all_marks, all_mixed)
+        task_grads, held = lax.optimization_barrier(
+            (task_grads, (normed_low, expanded_grad, activated_low, dense_grad, branch, projected_grad))
+        )
+        normed_low, expanded_grad, activated_low, dense_grad, branch, projected_grad = held
+        waiting += [tn(normed_low, expanded_grad)]
         waiting += [
             tn(activated_low[:, s * width : (s + 1) * width], dense_grad) for s in range(folds)
         ]
         waiting.append(tn(branch, projected_grad))
         shares = lax.psum_scatter(
-            jnp.stack([part.astype(bf16) for part in waiting]), every, scatter_dimension=1, tiled=True
+            jnp.concatenate([part.astype(bf16) for part in waiting], axis=1),
+            every,
+            scatter_dimension=0,
+            tiled=True,
         )
-        early = 2 * folds + 1
-        if len(waiting) > early:
-            late_shares[layer + 1] = shares[: len(waiting) - early]
-        early_shares[layer] = shares[len(waiting) - early :]
-        grad_low, grad_high = halo_of(branch_grad, segments)
-        dq, task_grads = token_back(place, qk, branch_grad, weights, all_marks, all_mixed)
+        late = shares.shape[1] - (2 * hidden_units + width)
+        if late:
+            late_shares[layer + 1] = shares[:, :late]
+        early_shares[layer] = shares[:, late:]
         total, payload = owner_back(to_owners(task_grads, each), pseudo, values)
-        all_grads = from_owners(payload)
-        own_grads = newton_back(marks, values, total)
+        own_grads = newton_back(marks, mark_kernel, steps, values, total)
+        all_grads, own_grads = from_owners(payload, own_grads)
+        dqk, dv, query_part = key_back(
+            place, row_ids, qk, v, all_marks, all_mixed, all_grads, dq
+        )
+        query_part, conv_grad_in = lax.optimization_barrier((query_part, branch_grad))
         dconv, dtaps = conv_back(
-            local_bound, v, low, high, branch_grad, grad_low, grad_high, flipped[layer]
+            local_bound, v, low, high, conv_grad_in, grad_low, grad_high, taps[layer]
         )
-        dqk, dv, query_part = key_back(
-            place, row_ids, qk, v, all_marks, all_mixed, all_grads, dq, dconv
+        last = owner_last(to_owners(query_part, each), own_grads, inverse)
+        mark_grads, (dconv, dtaps) = from_owners(last, (dconv, dtaps))
+        dqk, dv, grad = spread(
+            place, col_ids, mark_grads, dqk, dv, dconv, grad_first,
+            tails[(layer - 1) % layers], place_of_heads,
         )
-        mark_grads = from_owners(owner_last(to_owners(query_part, each), own_grads, inverse))
-        dqk = spread(place, col_ids, mark_grads, dqk)
-        grad = (
-            grad_first
-            + nt(dqk, heads[:, at : at + 2 * width])
-            + nt(dv, heads[:, at + 2 * width : at + 3 * width])
-        )
-        waiting = [
-            tn(hidden_low, dqk[:, :width]),
-            tn(hidden_low, dqk[:, width:]),
-            tn(hidden_low, dv),
-        ]
+        waiting = [tn(hidden_low, dqk), tn(hidden_low, dv)]
         conv_grad = dtaps[:KCONV].reshape(KCONV, HEADS, HD).sum(axis=-1).T
-        small[layer] = (
-            conv_grad,
-            jnp.stack([gain_first, gain_second]),
-            jnp.stack([bias_first, bias_second]),
-        )
-    near, far = near_and_far()
-    turns = []
-    for turn, part in enumerate(waiting):
-        shift = turn * len(near) // 3
-        order = [("sp", 0)] + near[shift:] + near[:shift] + [far]
-        turns.append(Shares(part.astype(bf16)).halve(*order).result())
-    late_shares[0] = jnp.stack(turns)
-    grad_tokens = back_home(grad, bf16)
+        small[layer] = (conv_grad, scales[:2], scales[2:])
+    final = [
+        Shares(part.astype(bf16)) for part in (waiting[0][:, :width], waiting[0][:, width:], waiting[1])
+    ]
+    for turn, part in enumerate(final):
+        part.halve(turn_order(turn)[0])
+    keep, send, mask, top = swap_rows(grad.reshape(segments, length, width))
+    values, send = lax.optimization_barrier(([part.values for part in final], send.astype(bf16)))
+    other = flip(send, "sp", mask)
+    for turn, part in enumerate(final):
+        part.values = values[turn]
+        part.halve(*turn_order(turn)[1:])
+    last, other = lax.optimization_barrier(([part.result() for part in final], other))
+    late_shares[0] = jnp.concatenate(last, axis=1)
+    grad_tokens = in_order(keep, other.astype(f32), top)[:, None]
     conv_rows = jnp.stack([small[layer][0] for layer in range(layers)]).reshape(-1)
     conv_rows = jnp.pad(conv_rows, (0, -conv_rows.shape[0] % width)).reshape(-1, width)
     scales = [small[layer][k] for k in (1, 2) for layer in range(layers)]
@@ -1102,17 +1379,15 @@
     conv_sum = conv_sum.reshape(layers, HEADS, KCONV)
     results = [[] for _ in range(6)]
     for layer in range(layers):
-        late = late_shares[layer].astype(f32)
-        early = early_shares[layer].astype(f32)
-        pair = jnp.concatenate([late[0], late[1]], axis=1).reshape(shard, HEADS, 2, HD)
+        late, early = late_shares[layer], early_shares[layer]
+        pair = late[:, : 2 * width].astype(f32).reshape(shard, HEADS, 2, HD)
         results[0].append(pair[:, :, 0].reshape(shard, width))
         results[1].append(pair[:, :, 1].reshape(shard, width))
-        results[2].append(late[2])
-        results[3].append(early[2 * folds])
-        results[4].append(jnp.transpose(early[:folds], (1, 2, 0)).reshape(shard, hidden_units))
-        results[5].append(
-            jnp.swapaxes(early[folds : 2 * folds], 0, 1).reshape(shard * folds, width)
-        )
+        results[2].append(late[:, 2 * width :].astype(f32))
+        results[3].append(early[:, 2 * hidden_units :].astype(f32))
+        results[4].append(unfolded(early[:, :hidden_units], fold, folds))
+        down_grad = early[:, hidden_units : 2 * hidden_units].astype(f32)
+        results[5].append(down_grad.reshape(shard * folds, width))
     grads = [jnp.stack(parts) for parts in results]
     return (
         output,

time: 771 us -> 702 us (0.911)
  Pallas kernels: 184 us -> 276 us
  waiting for transfers between devices: 223 us -> 140 us
  matrix products: 98.4 us -> 39.7 us
  starting transfers between devices: 82.6 us -> 112 us
  other arithmetic: 59.7 us -> 34.3 us
  local copies, waits for them, and re-layouts: 94.9 us -> 72.9 us
    pallas_call x0 -> x4, Pallas kernels: none -> 65.8 us  [dense_call(): pl.pallas_call(body, grid=(folds,), in_specs=in_specs, out_specs=out_spec...]
    all_gather x3 -> x2, waiting for transfers between devices: 50.8 us -> 0.01 us  [local(): lax.all_gather(part, every, axis=0, tiled=True)]
    ppermute x80 -> x95, waiting for transfers between devices: 170 us -> 124 us  [flip(): return lax.ppermute(value, axis, [(i, i ^ mask) for i in range(count)])]
    dot_general x16 -> x2, matrix products: 44.3 us -> 0.75 us  [nt(): lax.dot_general(left, right, (((1,), (1,)), ((), ())), preferred_element_...]
    pallas_call x16 -> x18, Pallas kernels: 116 us -> 153 us  [over_pairs(): pl.pallas_call(body, grid_spec=pltpu.PrefetchScalarGridSpec(num_scalar_pr...]
    dot_general x12 -> x4, matrix products: 33.3 us -> 2.94 us  [nn(): lax.dot_general(left, right, (((1,), (0,)), ((), ())), preferred_element_...]
    ppermute x80 -> x95, starting transfers between devices: 77.5 us -> 101 us  [flip(): return lax.ppermute(value, axis, [(i, i ^ mask) for i in range(count)])]
    dot_general x24 -> x16, matrix products: 20.8 us -> 36.1 us  [tn(): lax.dot_general(left, right, (((0,), (0,)), ((), ())), preferred_element_...]
  transfers between devices with their start and end apart: 93 -> 107, of which waited for: 47 -> 58; matrix products, arithmetic and copies ran while one was open for 24% -> 12% of each run, Pallas kernels for 23% -> 36%
where the time goes in v3:
time: 702 us; the launch traced here: 692 us
  Pallas kernels  276 us (39%)
  waiting for transfers between devices  140 us (20%)
  starting transfers between devices  112 us (16%)
  local copies, waits for them, and re-layouts  72.9 us (10%)
  matrix products  39.7 us (6%)
  other arithmetic  34.3 us (5%)
  between operations  16.3 us (2%)
    pallas_call x18, Pallas kernels, over_pairs(): pl.pallas_call(body, grid_spec=pltpu.PrefetchScalarGridSpec(num_scalar_pr...  153 us
    ppermute x95, waiting for transfers between devices, flip(): return lax.ppermute(value, axis, [(i, i ^ mask) for i in range(count)])  124 us
    ppermute x95, starting transfers between devices, flip(): return lax.ppermute(value, axis, [(i, i ^ mask) for i in range(count)])  101 us
    pallas_call x4, Pallas kernels, dense_call(): pl.pallas_call(body, grid=(folds,), in_specs=in_specs, out_specs=out_spec...  65.8 us
    pallas_call x12, Pallas kernels, small_call(): pl.pallas_call(body, out_shape=out_shape, scratch_shapes=scratch, cost_es...  51.3 us
    unnamed x247, local copies, waits for them, and re-layouts  38 us
    dot_general x16, matrix products, tn(): lax.dot_general(left, right, (((0,), (0,)), ((), ())), preferred_element_...  36.1 us
  transfers between devices with their start and end apart: 107, of which 58 were waited for; matrix products, arithmetic and copies ran while one was open for 12% of the time, Pallas kernels for 36%

profile of v3, /device:TPU:0, one launch (start us, length us, event | category | flops | bytes accessed | tf_op | source)
XLA Modules:
  0.0 691.6 jit_solution(10660945252487416544)
XLA Ops:
  45.7 5.7 collective-permute-done.10
  70.4 7.8 %project.2 = (bf16[512,1536]{1,0:T(8,128)(2,1)S(1)}, bf16[512,768]{1,0:T(8,128)(2,1)S(1)}, f32[24,64,128]{2,1,0:T(8,128)S(1)}) custom-call(s32[24]{0:T(128)S(1)} %fusion.75.place_ref, s32[1,512]{1,0:T(1,128)} %fusion.72.ids_ref, bf16[3,512,768]{2,1,0:T(8,128)(2,1)} %pad_maximum_fusion.1.hidden_qk_ref.hidden_v_ref, ...), custom_call_target="tpu_custom_call" | custom-call | flops 1811939328 | bytes 14944256 | tf_op jit(solution)/shard_map/project/pallas_call | solution.py:119
  99.3 7.8 %conv_forward.2.conv_ref = f32[512,768]{1,0:T(8,128)S(1)} custom-call(s32[2]{0:T(128)S(1)} %broadcast_subtract_fusion.bound_ref, f32[396]{0:T(512)S(1)} %reshape_squeeze.13.scalar_ref, bf16[512,768]{1,0:T(8,128)(2,1)} %copy-done.8, bf16[2,16,768]{2,1,0:T(8,128)(2,1)} %pad_select_fusion.7.low_ref, bf16[2,16,768]{2,1,0:T(8,128)(2,1)} %pad_select_fusion.6.high_ref), custom_call_target="tpu_custom_call" | custom-call | flops 5000000000 | bytes 2457600 | tf_op jit(solution)/shard_map/conv_forward/pallas_call | solution.py:119
  115.1 6.9 key_partial.2.mine_ref
  132.9 6.8 owner_pseudo.2
  145.1 5.9 token_prep.2.weights_ref
  166.1 13.9 %dense_forward.2 = (f32[512,768]{1,0:T(8,128)S(1)}, f32[512,128]{1,0:T(8,128)S(1)}, bf16[512,768]{1,0:T(8,128)(2,1)S(1)}, f32[512,3072]{1,0:T(8,128)}, bf16[512,...) custom-call(f32[512,768]{1,0:T(8,128)} %convert_element_type.441.hid, ...), custom_call_target="tpu_custom_call" | custom-call | flops 5435817984 | bytes 30000000 | tf_op jit(solution)/shard_map/dense_forward/pallas_call | solution.py:883
  180.9 9.2 %project.3 = (bf16[512,1536]{1,0:T(8,128)(2,1)S(1)}, bf16[512,768]{1,0:T(8,128)(2,1)S(1)}, f32[24,64,128]{2,1,0:T(8,128)S(1)}) custom-call(s32[24]{0:T(128)S(1)} %fusion.75.place_ref, s32[1,512]{1,0:T(1,128)} %fusion.72.ids_ref, bf16[1,512,768]{2,1,0:T(8,128)(2,1)} %bitcast.227, bf16[1,512,768]{2,1,0:T(8,128)(2,1)} %bitcast.228, ...), custom_call_target="tpu_custom_call" | custom-call | flops 1811939328 | bytes 33032192 | tf_op jit(solution)/shard_map/project/pallas_call | solution.py:119
  212.5 7.8 %conv_forward.3.conv_ref = f32[512,768]{1,0:T(8,128)S(1)} custom-call(s32[2]{0:T(128)S(1)} %broadcast_subtract_fusion.bound_ref, f32[396]{0:T(512)S(1)} %reshape_squeeze.14.scalar_ref, bf16[512,768]{1,0:T(8,128)(2,1)} %copy-done.9, bf16[2,16,768]{2,1,0:T(8,128)(2,1)} %pad_select_fusion.5.low_ref, bf16[2,16,768]{2,1,0:T(8,128)(2,1)} %pad_select_fusion.4.high_ref), custom_call_target="tpu_custom_call" | custom-call | flops 5000000000 | bytes 2457600 | tf_op jit(solution)/shard_map/conv_forward/pallas_call | solution.py:119
  230.4 6.9 key_partial.3.mine_ref
  248.0 6.9 owner_pseudo.3
  259.5 6.1 token_prep.3.weights_ref
  279.8 14.4 %dense_forward.3 = (f32[512,768]{1,0:T(8,128)S(1)}, f32[512,128]{1,0:T(8,128)S(1)}, bf16[512,768]{1,0:T(8,128)(2,1)S(1)}, f32[512,3072]{1,0:T(8,128)}, bf16[512,...) custom-call(f32[512,768]{1,0:T(8,128)} %copy-done.25, ...), custom_call_target="tpu_custom_call" | custom-call | flops 5435817984 | bytes 30000000 | tf_op jit(solution)/shard_map/dense_forward/pallas_call | solution.py:883
  296.5 18.8 %dense_backward.2 = (bf16[512,768]{1,0:T(8,128)(2,1)S(1)}, bf16[512,3072]{1,0:T(8,128)(2,1)S(1)}, f32[512,768]{1,0:T(8,128)S(1)}, bf16[512,768]{1,0:T(8,128)(2,1...) custom-call(f32[512,768]{1,0:T(8,128)} %bitcast_convert_fusion.grad_ref, f32[512,768]{1,0:T(8,128)} %copy-done.29, ...), custom_call_target="tpu_custom_call" | custom-call | flops 5435817984 | bytes 30000000 | tf_op jit(solution)/shard_map/dense_backward/pallas_call | solution.py:883
  316.1 7.9 %token_back.2 = (f32[512,1536]{1,0:T(8,128)S(1)}, bf16[24,64,128]{2,1,0:T(8,128)(2,1)S(1)}) custom-call(s32[24]{0:T(128)S(1)} %fusion.75.place_ref, bf16[512,1536]{1,0:T(8,128)(2,1)} %copy-done.3, bf16[512,768]{1,0:T(8,128)(2,1)} %copy-done.35, bf16[512,1536]{1,0:T(8,128)(2,1)} %copy-done.5, bf16[24,64,128]{2,1,0:T(8,128)(2,1)} %copy-done.54, ...), custom_call_target="tpu_custom_call" | custom-call | flops 805306368 | bytes 8257536 | tf_op jit(solution)/shard_map/token_back/pallas_call | solution.py:119
  353.2 10.4 %newton_back.2.refs_4_ = f32[3,64,128]{2,1,0:T(8,128)} custom-call(f32[3,64,128]{2,1,0:T(8,128)} %get-tuple-element.196.marks_ref, f32[3,64,64]{2,1,0:T(8,128)} %get-tuple-element.222.kernel_ref, f32[6,3,4,64,64]{4,3,2,1,0:T(8,128)} %get-tuple-element.223.steps_ref, f32[3,64,128]{2,1,0:T(8,128)} %get-tuple-element.220.refs_5_.values_ref, ...), custom_call_target="tpu_custom_call" | custom-call | flops 10000000000 | bytes 1000000 | tf_op jit(solution)/shard_map/newton_back/pallas_call | solution.py:281
  374.6 9.2 %key_back.2 = (f32[512,1536]{1,0:T(8,128)S(1)}, f32[512,768]{1,0:T(8,128)S(1)}, bf16[24,32,128]{2,1,0:T(8,128)(2,1)S(1)}) custom-call(s32[24]{0:T(128)S(1)} %fusion.75.place_ref, s32[1,512]{1,0:T(1,128)} %fusion.72.ids_ref, bf16[512,1536]{1,0:T(8,128)(2,1)} %copy-done.3, bf16[512,768]{1,0:T(8,128)(2,1)} %copy-done.9, bf16[24,64,128]{2,1,0:T(8,128)(2,1)} %copy-done.54, ...), custom_call_target="tpu_custom_call" | custom-call | flops 1006632960 | bytes 11601920 | tf_op jit(solution)/shard_map/key_back/pallas_call | solution.py:119
  397.9 14.3 %conv_back.2 = (f32[512,768]{1,0:T(8,128)S(1)}, f32[40,768]{1,0:T(8,128)S(1)}) custom-call(s32[2]{0:T(128)S(1)} %broadcast_subtract_fusion.bound_ref, f32[396]{0:T(512)S(1)} %reshape_squeeze.14.scalar_ref, bf16[512,768]{1,0:T(8,128)(2,1)} %copy-done.9, bf16[2,16,768]{2,1,0:T(8,128)(2,1)} %pad_select_fusion.5.low_ref, ...), custom_call_target="tpu_custom_call" | custom-call | flops 10000000000 | bytes 3465216 | tf_op jit(solution)/shard_map/conv_back/pallas_call | solution.py:119
  420.5 10.3 %spread.2 = (bf16[512,1536]{1,0:T(8,128)(2,1)S(1)}, bf16[512,768]{1,0:T(8,128)(2,1)S(1)}, f32[512,768]{1,0:T(8,128)S(1)}) custom-call(s32[24]{0:T(128)S(1)} %fusion.75.place_ref, s32[512,1]{1,0:T(8,128)} %copy.159.ids_ref, bf16[24,64,128]{2,1,0:T(8,128)(2,1)} %pad_maximum_fusion.8.marks_ref, f32[512,1536]{1,0:T(8,128)} %copy-done.11, f32[512,768]{1,0:T(8,128)} %copy-done.27, ...), custom_call_target="tpu_custom_call" | custom-call | flops 2415919104 | bytes 40503296 | tf_op jit(solution)/shard_map/spread/pallas_call | solution.py:119
  433.1 18.8 %dense_backward.3 = (bf16[512,768]{1,0:T(8,128)(2,1)S(1)}, bf16[512,3072]{1,0:T(8,128)(2,1)S(1)}, f32[512,768]{1,0:T(8,128)S(1)}, bf16[512,768]{1,0:T(8,128)(2,1...) custom-call(f32[512,768]{1,0:T(8,128)} %copy-done.31, f32[512,768]{1,0:T(8,128)} %copy-done.20, ...), custom_call_target="tpu_custom_call" | custom-call | flops 5435817984 | bytes 30000000 | tf_op jit(solution)/shard_map/dense_backward/pallas_call | solution.py:883
  454.7 9.3 %token_back.3 = (f32[512,1536]{1,0:T(8,128)S(1)}, bf16[24,64,128]{2,1,0:T(8,128)(2,1)S(1)}) custom-call(s32[24]{0:T(128)S(1)} %fusion.75.place_ref, bf16[512,1536]{1,0:T(8,128)(2,1)} %copy-done.2, bf16[512,768]{1,0:T(8,128)(2,1)} %copy-done.34, bf16[512,1536]{1,0:T(8,128)(2,1)} %copy-done.4, bf16[24,64,128]{2,1,0:T(8,128)(2,1)} %copy-done.52, ...), custom_call_target="tpu_custom_call" | custom-call | flops 805306368 | bytes 8257536 | tf_op jit(solution)/shard_map/token_back/pallas_call | solution.py:119
  495.9 5.8 collective-permute-done.67.refs_1_
  508.9 10.4 %newton_back.3.refs_4_ = f32[3,64,128]{2,1,0:T(8,128)} custom-call(f32[3,64,128]{2,1,0:T(8,128)} %get-tuple-element.176.marks_ref, f32[3,64,64]{2,1,0:T(8,128)} %get-tuple-element.254.kernel_ref, f32[6,3,4,64,64]{4,3,2,1,0:T(8,128)} %get-tuple-element.255.steps_ref, f32[3,64,128]{2,1,0:T(8,128)} %get-tuple-element.252.refs_5_.values_ref, ...), custom_call_target="tpu_custom_call" | custom-call | flops 10000000000 | bytes 1000000 | tf_op jit(solution)/shard_map/newton_back/pallas_call | solution.py:281
  526.4 8.8 %key_back.3 = (f32[512,1536]{1,0:T(8,128)S(1)}, f32[512,768]{1,0:T(8,128)S(1)}, bf16[24,32,128]{2,1,0:T(8,128)(2,1)S(1)}) custom-call(s32[24]{0:T(128)S(1)} %fusion.75.place_ref, s32[1,512]{1,0:T(1,128)} %fusion.72.ids_ref, bf16[512,1536]{1,0:T(8,128)(2,1)} %copy-done.2, bf16[512,768]{1,0:T(8,128)(2,1)} %copy-done.8, bf16[24,64,128]{2,1,0:T(8,128)(2,1)} %copy-done.52, ...), custom_call_target="tpu_custom_call" | custom-call | flops 1006632960 | bytes 11601920 | tf_op jit(solution)/shard_map/key_back/pallas_call | solution.py:119
  549.2 14.3 %conv_back.3 = (f32[512,768]{1,0:T(8,128)S(1)}, f32[40,768]{1,0:T(8,128)S(1)}) custom-call(s32[2]{0:T(128)S(1)} %broadcast_subtract_fusion.bound_ref, f32[396]{0:T(512)S(1)} %copy-done.41, bf16[512,768]{1,0:T(8,128)(2,1)} %copy-done.8, bf16[2,16,768]{2,1,0:T(8,128)(2,1)} %pad_select_fusion.7.low_ref, bf16[2,16,768]{2,1,0:T(8,128)(2,1)} %pad_select_fusion.6.high_ref, ...), custom_call_target="tpu_custom_call" | custom-call | flops 10000000000 | bytes 3465216 | tf_op jit(solution)/shard_map/conv_back/pallas_call | solution.py:119
  573.0 6.7 collective-permute-done.100
  580.8 7.9 %collective-permute-done.101 = f32[10,768]{1,0:T(8,128)S(1)} collective-permute-done((f32[10,768]{1,0:T(8,128)S(1)}, f32[10,768]{1,0:T(8,128)S(1)}, u32[]{:S(2)}, u32[]{:S(2)}) %collective-permute-start.101) | collective-permute-done | bytes 30752 | tf_op jit(solution)/shard_map/ppermute | solution.py:1011
  597.1 10.4 %spread.3 = (bf16[512,1536]{1,0:T(8,128)(2,1)S(1)}, bf16[512,768]{1,0:T(8,128)(2,1)S(1)}, f32[512,768]{1,0:T(8,128)S(1)}) custom-call(s32[24]{0:T(128)S(1)} %fusion.75.place_ref, s32[512,1]{1,0:T(8,128)} %copy.159.ids_ref, bf16[24,64,128]{2,1,0:T(8,128)(2,1)} %pad_maximum_fusion.10.marks_ref, f32[512,1536]{1,0:T(8,128)} %copy-done.10, ...), custom_call_target="tpu_custom_call" | custom-call | flops 2415919104 | bytes 40503296 | tf_op jit(solution)/shard_map/spread/pallas_call | solution.py:119
  618.6 8.5 %collective-permute-done.85 = bf16[1,2,2,2,24,768]{5,4,1,2,3,0:T(8,128)(2,1)S(1)} collective-permute-done((bf16[1,2,2,2,24,768]{5,4,1,2,3,0:T(8,128)(2,1)S(1)}, bf16[1,2,2,2,24,768]{5,4,1,2,3,0:T(8,128)(2,1)S(1)}, u32[]{:S(2)}, u32[]{:S(2)}) %collective-permute-start.85) | collective-permute-done | bytes 294944 | tf_op jit(solution)/shard_map/ppermute | solution.py:1011
  631.8 6.9 collective-permute-done.93
  641.1 8.8 %collective-permute-done.90 = bf16[1,2,2,24,768]{4,3,2,1,0:T(8,128)(2,1)S(1)} collective-permute-done((bf16[1,2,2,24,768]{4,3,2,1,0:T(8,128)(2,1)S(1)}, bf16[1,2,2,24,768]{4,3,2,1,0:T(8,128)(2,1)S(1)}, u32[]{:S(2)}, u32[]{:S(2)}) %collective-permute-start.90) | collective-permute-done | bytes 147488 | tf_op jit(solution)/shard_map/ppermute | solution.py:1011
  668.1 7.4 %reduce-scatter.3.cloned.1.call-done = bf16[24,9216]{1,0:T(8,128)(2,1)} async-done(((bf16[768,9216]{1,0:T(8,128)(2,1)}), bf16[24,9216]{1,0:T(8,128)(2,1)}) %reduce-scatter.3.cloned.1.call-update) | async-done | bytes 442384 | tf_op jit(solution)/shard_map/reduce_scatter | solution.py:1329
  (724 shorter events, 374.2 us)
Async XLA Ops:
  7.2 158.9 %all-gather.3.cloned.1.call-start = ((), (), s32[]{:S(2)}) async-start(), calls=%async_computation.2 | async-start | bytes 14598144 | tf_op jit(solution)/shard_map/all_gather | solution.py:1261
  9.6 9.4 %collective-permute-start = (bf16[24,768]{1,0:T(8,128)(2,1)S(1)}, bf16[24,768]{1,0:T(8,128)(2,1)S(1)}, u32[]{:S(2)}, u32[]{:S(2)}) collective-permute-start(bf16[24,768]{1,0:T(8,128)(2,1)S(1)} %get-tuple-element.431), channel_id=1, source_target_pairs={{0,8},{1,9},{2,10},{3,11},{4,12},{5,13},{6,14},{7,15},{8,0},{9,1},... | collective-permute-start | bytes 110600 | tf_op jit(solution)/shard_map/ppermute | solution.py:1011
  18.2 22.8 %collective-permute-start.9 = (bf16[256,768]{1,0:T(8,128)(2,1)}, bf16[256,768]{1,0:T(8,128)(2,1)}, u32[]{:S(2)}, u32[]{:S(2)}) collective-permute-start(bf16[256,768]{1,0:T(8,128)(2,1)} %get-tuple-element.381), channel_id=1, source_target_pairs={{0,8},{1,9},{2,10},{3,11},{4,12},{5,13},{6,14},{7,15},{8,0},{9,1},... | collective-permute-start | bytes 1179656 | tf_op jit(solution)/shard_map/ppermute | solution.py:1011
  19.0 9.3 %collective-permute-start.1 = (bf16[48,768]{1,0:T(8,128)(2,1)S(1)}, bf16[48,768]{1,0:T(8,128)(2,1)S(1)}, u32[]{:S(2)}, u32[]{:S(2)}) collective-permute-start(bf16[48,768]{1,0:T(8,128)(2,1)S(1)} %pad_maximum_fusion.38), channel_id=1, source_target_pairs={{0,4},{1,5},{2,6},{3,7},{4,0},{5,1},{6,2},{7,3},{8,12},{9,13},{10,... | collective-permute-start | bytes 221192 | tf_op jit(solution)/shard_map/ppermute | solution.py:1011
  30.0 11.0 %collective-permute-start.7 = (bf16[96,768]{1,0:T(8,128)(2,1)S(1)}, bf16[96,768]{1,0:T(8,128)(2,1)S(1)}, u32[]{:S(2)}, u32[]{:S(2)}) collective-permute-start(bf16[96,768]{1,0:T(8,128)(2,1)S(1)} %pad_maximum_fusion.25), channel_id=1, source_target_pairs={{0,4},{1,5},{2,6},{3,7},{4,0},{5,1},{6,2},{7,3},{8,12},{9,13},{10,... | collective-permute-start | bytes 442376 | tf_op jit(solution)/shard_map/ppermute | solution.py:1011
  42.3 9.1 %collective-permute-start.10 = (bf16[192,768]{1,0:T(8,128)(2,1)S(1)}, bf16[192,768]{1,0:T(8,128)(2,1)}, u32[]{:S(2)}, u32[]{:S(2)}) collective-permute-start(bf16[192,768]{1,0:T(8,128)(2,1)S(1)} %pad_maximum_fusion.11), channel_id=1, source_target_pairs={{0,16},{16,0},{1,17},{17,1},{2,18},{18,2},{3,19},{19,3},{4,20},{20... | collective-permute-start | bytes 884744 | tf_op jit(solution)/shard_map/ppermute | solution.py:1011
  53.8 226.0 %all-gather.5.cloned.1.call-start = ((), (), s32[]{:S(2)}) async-start(), calls=%async_computation.3 | async-start | bytes 14598144 | tf_op jit(solution)/shard_map/all_gather | solution.py:1261
  57.4 608.0 %reduce-scatter.5.cloned.1.call-start = ((), (), s32[]{:S(2)}) async-start(), calls=%async_computation.5 | async-start | bytes 10948608 | tf_op jit(solution)/shard_map/reduce_scatter | solution.py:1329
  129.2 10.6 %collective-permute-start.26 = (bf16[3,64,128]{2,1,0:T(8,128)(2,1)S(1)}, bf16[3,64,128]{2,1,0:T(8,128)(2,1)S(1)}, u32[]{:S(2)}, u32[]{:S(2)}) collective-permute-start(bf16[3,64,128]{2,1,0:T(8,128)(2,1)S(1)} %get-tuple-element.410), channel_id=1, source_target_pairs={{0,4},{1,5},{2,6},{3,7},{4,0},{5,1},{6,2},{7,3},{8,12},{9,13},{10,... | collective-permute-start | bytes 147464 | tf_op jit(solution)/shard_map/ppermute | solution.py:1011
  191.4 10.7 %collective-permute-start.33 = (f32[12,64,128]{2,1,0:T(8,128)S(1)}, f32[12,64,128]{2,1,0:T(8,128)S(1)}, u32[]{:S(2)}, u32[]{:S(2)}) collective-permute-start(f32[12,64,128]{2,1,0:T(8,128)S(1)} %slice.413), channel_id=1, source_target_pairs={{0,1},{1,0},{2,3},{3,2},{4,5},{5,4},{6,7},{7,6},{8,9},{9,8},{10,11... | collective-permute-start | bytes 1179656 | tf_op jit(solution)/shard_map/ppermute | solution.py:1011
  244.5 10.4 %collective-permute-start.43 = (bf16[3,64,128]{2,1,0:T(8,128)(2,1)S(1)}, bf16[3,64,128]{2,1,0:T(8,128)(2,1)S(1)}, u32[]{:S(2)}, u32[]{:S(2)}) collective-permute-start(bf16[3,64,128]{2,1,0:T(8,128)(2,1)S(1)} %get-tuple-element.402), channel_id=1, source_target_pairs={{0,4},{1,5},{2,6},{3,7},{4,0},{5,1},{6,2},{7,3},{8,12},{9,13},{10,... | collective-permute-start | bytes 147464 | tf_op jit(solution)/shard_map/ppermute | solution.py:1011
  245.8 9.1 %collective-permute-start.44 = (bf16[3,64,128]{2,1,0:T(8,128)(2,1)S(1)}, bf16[3,64,128]{2,1,0:T(8,128)(2,1)S(1)}, u32[]{:S(2)}, u32[]{:S(2)}) collective-permute-start(bf16[3,64,128]{2,1,0:T(8,128)(2,1)S(1)} %get-tuple-element.401), channel_id=1, source_target_pairs={{0,2},{1,3},{2,0},{3,1},{4,6},{5,7},{6,4},{7,5},{8,10},{9,11},{10,... | collective-permute-start | bytes 147464 | tf_op jit(solution)/shard_map/ppermute | solution.py:1011
  268.4 25.8 %collective-permute-start.32 = (bf16[256,768]{1,0:T(8,128)(2,1)S(1)}, bf16[256,768]{1,0:T(8,128)(2,1)S(1)}, u32[]{:S(2)}, u32[]{:S(2)}) collective-permute-start(bf16[256,768]{1,0:T(8,128)(2,1)S(1)} %get-tuple-element.186), channel_id=1, source_target_pairs={{0,8},{1,9},{2,10},{3,11},{4,12},{5,13},{6,14},{7,15},{8,0},{9,1},... | collective-permute-start | bytes 1179656 | tf_op jit(solution)/shard_map/ppermute | solution.py:1011
  339.6 335.9 %reduce-scatter.3.cloned.1.call-start = ((), (), s32[]{:S(2)}) async-start(), calls=%async_computation.4 | async-start | bytes 14598144 | tf_op jit(solution)/shard_map/reduce_scatter | solution.py:1329
  351.6 12.0 %collective-permute-start.54 = (bf16[3,64,128]{2,1,0:T(8,128)(2,1)}, bf16[3,64,128]{2,1,0:T(8,128)(2,1)S(1)}, u32[]{:S(2)}, u32[]{:S(2)}) collective-permute-start(bf16[3,64,128]{2,1,0:T(8,128)(2,1)} %get-tuple-element.221), channel_id=1, source_target_pairs={{0,4},{1,5},{2,6},{3,7},{4,0},{5,1},{6,2},{7,3},{8,12},{9,13},{10,... | collective-permute-start | bytes 147464 | tf_op jit(solution)/shard_map/ppermute | solution.py:1011
  369.8 17.6 %collective-permute-start.63 = (bf16[2,16,768]{2,1,0:T(8,128)(2,1)S(1)}, bf16[2,16,768]{2,1,0:T(8,128)(2,1)S(1)}, u32[]{:S(2)}, u32[]{:S(2)}) collective-permute-start(bf16[2,16,768]{2,1,0:T(8,128)(2,1)S(1)} %get-tuple-element.370), channel_id=1, source_target_pairs={{1,0},{2,1},{3,2},{4,3},{5,4},{6,5},{7,6},{0,7},{9,8},{10,9},{11,1... | collective-permute-start | bytes 147464 | tf_op jit(solution)/shard_map/ppermute | solution.py:1129
  396.4 16.9 %collective-permute-start.61 = (bf16[3,64,128]{2,1,0:T(8,128)(2,1)}, bf16[3,64,128]{2,1,0:T(8,128)(2,1)S(1)}, u32[]{:S(2)}, u32[]{:S(2)}) collective-permute-start(bf16[3,64,128]{2,1,0:T(8,128)(2,1)} %owner_last.2), channel_id=1, source_target_pairs={{0,4},{1,5},{2,6},{3,7},{4,0},{5,1},{6,2},{7,3},{8,12},{9,13},{10,... | collective-permute-start | bytes 147464 | tf_op jit(solution)/shard_map/ppermute | solution.py:1011
  489.9 89.9 %collective-permute-start.49 = (bf16[256,768]{1,0:T(8,128)(2,1)S(1)}, bf16[256,768]{1,0:T(8,128)(2,1)S(1)}, u32[]{:S(2)}, u32[]{:S(2)}) collective-permute-start(bf16[256,768]{1,0:T(8,128)(2,1)S(1)} %get-tuple-element.375), channel_id=1, source_target_pairs={{0,8},{1,9},{2,10},{3,11},{4,12},{5,13},{6,14},{7,15},{8,0},{9,1},... | collective-permute-start | bytes 1179656 | tf_op jit(solution)/shard_map/ppermute | solution.py:1011
  491.9 9.8 %collective-permute-start.67 = (bf16[3,64,128]{2,1,0:T(8,128)(2,1)S(1)}, bf16[3,64,128]{2,1,0:T(8,128)(2,1)S(1)}, u32[]{:S(2)}, u32[]{:S(2)}) collective-permute-start(bf16[3,64,128]{2,1,0:T(8,128)(2,1)S(1)} %get-tuple-element.394), channel_id=1, source_target_pairs={{0,4},{1,5},{2,6},{3,7},{4,0},{5,1},{6,2},{7,3},{8,12},{9,13},{10,... | collective-permute-start | bytes 147464 | tf_op jit(solution)/shard_map/ppermute | solution.py:1011
  505.0 14.3 %collective-permute-start.70 = (bf16[3,64,128]{2,1,0:T(8,128)(2,1)}, bf16[3,64,128]{2,1,0:T(8,128)(2,1)S(1)}, u32[]{:S(2)}, u32[]{:S(2)}) collective-permute-start(bf16[3,64,128]{2,1,0:T(8,128)(2,1)} %get-tuple-element.253), channel_id=1, source_target_pairs={{0,4},{1,5},{2,6},{3,7},{4,0},{5,1},{6,2},{7,3},{8,12},{9,13},{10,... | collective-permute-start | bytes 147464 | tf_op jit(solution)/shard_map/ppermute | solution.py:1011
  520.3 18.6 %collective-permute-start.79 = (bf16[2,16,768]{2,1,0:T(8,128)(2,1)S(1)}, bf16[2,16,768]{2,1,0:T(8,128)(2,1)S(1)}, u32[]{:S(2)}, u32[]{:S(2)}) collective-permute-start(bf16[2,16,768]{2,1,0:T(8,128)(2,1)S(1)} %get-tuple-element.368), channel_id=1, source_target_pairs={{1,0},{2,1},{3,2},{4,3},{5,4},{6,5},{7,6},{0,7},{9,8},{10,9},{11,1... | collective-permute-start | bytes 147464 | tf_op jit(solution)/shard_map/ppermute | solution.py:1129
  547.7 17.1 %collective-permute-start.77 = (bf16[3,64,128]{2,1,0:T(8,128)(2,1)}, bf16[3,64,128]{2,1,0:T(8,128)(2,1)S(1)}, u32[]{:S(2)}, u32[]{:S(2)}) collective-permute-start(bf16[3,64,128]{2,1,0:T(8,128)(2,1)} %owner_last.3), channel_id=1, source_target_pairs={{0,4},{1,5},{2,6},{3,7},{4,0},{5,1},{6,2},{7,3},{8,12},{9,13},{10,... | collective-permute-start | bytes 147464 | tf_op jit(solution)/shard_map/ppermute | solution.py:1011
  571.5 19.4 %collective-permute-start.80 = (bf16[6,64,128]{2,1,0:T(8,128)(2,1)S(1)}, bf16[6,64,128]{2,1,0:T(8,128)(2,1)S(1)}, u32[]{:S(2)}, u32[]{:S(2)}) collective-permute-start(bf16[6,64,128]{2,1,0:T(8,128)(2,1)S(1)} %pad_maximum_fusion.37), channel_id=1, source_target_pairs={{0,2},{1,3},{2,0},{3,1},{4,6},{5,7},{6,4},{7,5},{8,10},{9,11},{10,... | collective-permute-start | bytes 294920 | tf_op jit(solution)/shard_map/ppermute | solution.py:1011
  579.8 9.0 %collective-permute-start.101 = (f32[10,768]{1,0:T(8,128)S(1)}, f32[10,768]{1,0:T(8,128)S(1)}, u32[]{:S(2)}, u32[]{:S(2)}) collective-permute-start(f32[10,768]{1,0:T(8,128)S(1)} %add.431), channel_id=1, source_target_pairs={{0,8},{1,9},{2,10},{3,11},{4,12},{5,13},{6,14},{7,15},{8,0},{9,1},... | collective-permute-start | bytes 92168 | tf_op jit(solution)/shard_map/ppermute | solution.py:1011
  613.3 13.8 %collective-permute-start.85 = (bf16[1,2,2,2,24,768]{5,4,1,2,3,0:T(8,128)(2,1)S(1)}, bf16[1,2,2,2,24,768]{5,4,1,2,3,0:T(8,128)(2,1)S(1)}, u32[]{:S(2)}, u32[]{:S(2)}) collective-permute-start(bf16[1,2,2,2,24,768]{5,4,1,2,3,0:T(8,128)(2,1)S(1)} %dynamic-slice_bitcast_fusion.9), channel_id=1, source_target_pairs={{0,16},{16,0},{1,17},{17,1},{2,18},{18,2},{3,19},{19,3},{4,20},{20... | collective-permute-start | bytes 884744 | tf_op jit(solution)/shard_map/ppermute | solution.py:1011
  615.4 16.2 %collective-permute-start.89 = (bf16[1,2,2,2,24,768]{5,4,2,1,3,0:T(8,128)(2,1)S(1)}, bf16[1,2,2,2,24,768]{5,4,2,1,3,0:T(8,128)(2,1)S(1)}, u32[]{:S(2)}, u32[]{:S(2)}) collective-permute-start(bf16[1,2,2,2,24,768]{5,4,2,1,3,0:T(8,128)(2,1)S(1)} %dynamic-slice_bitcast_fusion.8), channel_id=1, source_target_pairs={{0,2},{1,3},{2,0},{3,1},{4,6},{5,7},{6,4},{7,5},{8,10},{9,11},{10,... | collective-permute-start | bytes 884744 | tf_op jit(solution)/shard_map/ppermute | solution.py:1011
  617.2 21.6 %collective-permute-start.93 = (bf16[1,2,2,2,24,768]{5,4,2,3,1,0:T(8,128)(2,1)S(1)}, bf16[1,2,2,2,24,768]{5,4,2,3,1,0:T(8,128)(2,1)S(1)}, u32[]{:S(2)}, u32[]{:S(2)}) collective-permute-start(bf16[1,2,2,2,24,768]{5,4,2,3,1,0:T(8,128)(2,1)S(1)} %dynamic-slice_bitcast_fusion.7), channel_id=1, source_target_pairs={{0,4},{1,5},{2,6},{3,7},{4,0},{5,1},{6,2},{7,3},{8,12},{9,13},{10,... | collective-permute-start | bytes 884744 | tf_op jit(solution)/shard_map/ppermute | solution.py:1011
  617.2 45.3 %collective-permute-start.97 = (bf16[256,768]{1,0:T(8,128)(2,1)S(1)}, bf16[256,768]{1,0:T(8,128)(2,1)S(1)}, u32[]{:S(2)}, u32[]{:S(2)}) collective-permute-start(bf16[256,768]{1,0:T(8,128)(2,1)S(1)} %fusion.39), channel_id=1, source_target_pairs={{0,8},{1,9},{2,10},{3,11},{4,12},{5,13},{6,14},{7,15},{8,0},{9,1},... | collective-permute-start | bytes 1179656 | tf_op jit(solution)/shard_map/ppermute | solution.py:1011
  627.3 13.7 %collective-permute-start.86 = (bf16[1,2,2,24,768]{4,3,1,2,0:T(8,128)(2,1)S(1)}, bf16[1,2,2,24,768]{4,3,1,2,0:T(8,128)(2,1)S(1)}, u32[]{:S(2)}, u32[]{:S(2)}) collective-permute-start(bf16[1,2,2,24,768]{4,3,1,2,0:T(8,128)(2,1)S(1)} %dynamic-slice_bitcast_fusion.12), channel_id=1, source_target_pairs={{0,2},{1,3},{2,0},{3,1},{4,6},{5,7},{6,4},{7,5},{8,10},{9,11},{10,... | collective-permute-start | bytes 442376 | tf_op jit(solution)/shard_map/ppermute | solution.py:1011
  631.7 18.2 %collective-permute-start.90 = (bf16[1,2,2,24,768]{4,3,2,1,0:T(8,128)(2,1)S(1)}, bf16[1,2,2,24,768]{4,3,2,1,0:T(8,128)(2,1)S(1)}, u32[]{:S(2)}, u32[]{:S(2)}) collective-permute-start(bf16[1,2,2,24,768]{4,3,2,1,0:T(8,128)(2,1)S(1)} %dynamic-slice_bitcast_fusion.11), channel_id=1, source_target_pairs={{0,4},{1,5},{2,6},{3,7},{4,0},{5,1},{6,2},{7,3},{8,12},{9,13},{10,... | collective-permute-start | bytes 442376 | tf_op jit(solution)/shard_map/ppermute | solution.py:1011
  638.8 13.7 %collective-permute-start.94 = (bf16[1,2,2,24,768]{4,3,1,2,0:T(8,128)(2,1)S(1)}, bf16[1,2,2,24,768]{4,3,1,2,0:T(8,128)(2,1)S(1)}, u32[]{:S(2)}, u32[]{:S(2)}) collective-permute-start(bf16[1,2,2,24,768]{4,3,1,2,0:T(8,128)(2,1)S(1)} %dynamic-slice_bitcast_fusion.10), channel_id=1, source_target_pairs={{0,16},{16,0},{1,17},{17,1},{2,18},{18,2},{3,19},{19,3},{4,20},{20... | collective-permute-start | bytes 442376 | tf_op jit(solution)/shard_map/ppermute | solution.py:1011
  641.1 13.3 %collective-permute-start.87 = (bf16[1,2,24,768]{3,2,1,0:T(8,128)(2,1)S(1)}, bf16[1,2,24,768]{3,2,1,0:T(8,128)(2,1)S(1)}, u32[]{:S(2)}, u32[]{:S(2)}) collective-permute-start(bf16[1,2,24,768]{3,2,1,0:T(8,128)(2,1)S(1)} %dynamic-slice_bitcast_fusion.15), channel_id=1, source_target_pairs={{0,4},{1,5},{2,6},{3,7},{4,0},{5,1},{6,2},{7,3},{8,12},{9,13},{10,... | collective-permute-start | bytes 221192 | tf_op jit(solution)/shard_map/ppermute | solution.py:1011
  (191 other events, 1213.0 us)
Sparse Core Ops, SparseCore 0:
  53.9 106.2 all-gather.2
  163.7 107.7 all-gather.4
  339.7 146.2 reduce-scatter.4
  491.9 183.5 reduce-scatter.2

commit v4 on v3

--- a/solution.py
+++ b/solution.py
@@ -20,6 +20,7 @@
 WINDOW = 40
 TAPS = 40
 CHUNK = 128
+LARGE = 2 * 10**6
 
 negative = -1e30
 epsilon = 1e-05
@@ -107,6 +108,8 @@
 
 
 def in_hbm(array):
+    if array.size * array.dtype.itemsize < LARGE:
+        return array
     return pltpu.with_memory_space_constraint(array, pltpu.HBM)
 
 
@@ -535,7 +538,7 @@
         grad_weights = nt(grad, mixed)
         inner = jnp.sum(weights * grad_weights, axis=1, keepdims=True)
         grad_scores = (weights * (grad_weights - inner) * score_scale).astype(bf16)
-        dq_ref[:, columns] = nn(grad_scores, key_marks)
+        dq_ref[:, columns] = nn(grad_scores, key_marks).astype(bf16)
         grad_keys = tn(grad_scores, qk)
         grad_mixed = tn(weights_low, grad)
         if not side:
@@ -558,7 +561,7 @@
         ],
         [lanes(rows, 2 * WIDE), whole(marks.shape)],
         (
-            jax.ShapeDtypeStruct((rows, HEADS * WIDE), f32),
+            jax.ShapeDtypeStruct((rows, HEADS * WIDE), bf16),
             jax.ShapeDtypeStruct(marks.shape, bf16),
         ),
         (qk, grad, weights, marks, mixed),
@@ -567,51 +570,64 @@
 
 
 def conv_back_kernel(
-    bound_ref, scalar_ref, v_ref, low_ref, high_ref, grad_ref, grad_low_ref, grad_high_ref,
-    dv_ref, dtaps_ref, pad_ref, acc_ref,
+    bound_ref, scalar_ref, grad_ref, grad_low_ref, grad_high_ref, dv_ref, pad_ref, acc_ref
 ):
-    batches = low_ref.shape[0]
-    length = v_ref.shape[0] // batches
-    dtaps_ref[KCONV:] = jnp.zeros((TAPS - KCONV, WIDE), f32)
+    segments = grad_low_ref.shape[0]
+    length = grad_ref.shape[0] // segments
     taps = tap_rows(scalar_ref, True)
-    for batch in range(batches):
-        rows = slice(batch * length, (batch + 1) * length)
-        bound = bound_ref[batch]
-        grad = grad_ref[rows].astype(f32)
-        fill_padded(pad_ref, grad_low_ref[batch], grad, grad_high_ref[batch])
-        convolve(pad_ref, taps, bound, acc_ref)
+    for segment in range(segments):
+        rows = slice(segment * length, (segment + 1) * length)
+        fill_padded(pad_ref, grad_low_ref[segment], grad_ref[rows], grad_high_ref[segment])
+        convolve(pad_ref, taps, bound_ref[segment], acc_ref)
         dv_ref[rows] = acc_ref[...]
-        fill_padded(pad_ref, low_ref[batch], v_ref[rows], high_ref[batch])
-        acc_ref[...] = grad
-        for offset, row in enumerate(taps_gradient(acc_ref, pad_ref, bound, length)):
-            if batch:
-                row = row + dtaps_ref[offset : offset + 1]
-            dtaps_ref[offset : offset + 1] = row
-
-
-def conv_back(bounds, v, low, high, grad, grad_low, grad_high, taps):
-    batches = low.shape[0]
-    rows = v.shape[0]
-    length = rows // batches
+
+
+def conv_back(bounds, taps, grad, grad_low, grad_high):
+    segments = grad_low.shape[0]
+    rows = grad.shape[0]
+    length = rows // segments
+    halo = lanes3(segments, HALO, WIDE)
     return over_pairs(
         conv_back_kernel,
         "conv_back",
         (bounds, taps),
-        [
-            lanes(rows, WIDE),
-            lanes3(batches, HALO, WIDE),
-            lanes3(batches, HALO, WIDE),
-            lanes(rows, WIDE),
-            lanes3(batches, HALO, WIDE),
-            lanes3(batches, HALO, WIDE),
-        ],
-        [lanes(rows, WIDE), lanes(TAPS, WIDE)],
-        (
-            jax.ShapeDtypeStruct((rows, HEADS * HD), f32),
-            jax.ShapeDtypeStruct((TAPS, HEADS * HD), f32),
-        ),
-        (v, low, high, grad, grad_low, grad_high),
-        10**10,
+        [lanes(rows, WIDE), halo, halo],
+        lanes(rows, WIDE),
+        jax.ShapeDtypeStruct((rows, HEADS * HD), f32),
+        (grad, grad_low, grad_high),
+        5 * 10**9,
+        [pltpu.VMEM((length + 2 * HALO, WIDE), f32), pltpu.VMEM((length, WIDE), f32)],
+    )
+
+
+def taps_back_kernel(bound_ref, v_ref, low_ref, high_ref, grad_ref, dtaps_ref, pad_ref, acc_ref):
+    segments = low_ref.shape[0]
+    length = v_ref.shape[0] // segments
+    dtaps_ref[KCONV:] = jnp.zeros((TAPS - KCONV, WIDE), f32)
+    for segment in range(segments):
+        rows = slice(segment * length, (segment + 1) * length)
+        fill_padded(pad_ref, low_ref[segment], v_ref[rows], high_ref[segment])
+        acc_ref[...] = grad_ref[rows].astype(f32)
+        for offset, row in enumerate(taps_gradient(acc_ref, pad_ref, bound_ref[segment], length)):
+            if segment:
+                row = row + dtaps_ref[offset : offset + 1]
+            dtaps_ref[offset : offset + 1] = row
+
+
+def taps_back(bounds, v, low, high, grad):
+    segments = low.shape[0]
+    rows = v.shape[0]
+    length = rows // segments
+    halo = lanes3(segments, HALO, WIDE)
+    return over_pairs(
+        taps_back_kernel,
+        "taps_back",
+        (bounds,),
+        [lanes(rows, WIDE), halo, halo, lanes(rows, WIDE)],
+        lanes(TAPS, WIDE),
+        jax.ShapeDtypeStruct((TAPS, HEADS * HD), f32),
+        (v, low, high, grad),
+        5 * 10**9,
         [pltpu.VMEM((length + 2 * HALO, WIDE), f32), pltpu.VMEM((length, WIDE), f32)],
     )
 
@@ -737,7 +753,7 @@
         grad_marks = half_values(grads, side, lane)
         grad_probs = nt(grad_marks, values)
         grad_scores = (probs * (grad_probs - inner) * score_scale).astype(bf16)
-        dqk_ref[:, columns] = dq_ref[:, columns] + tn(grad_scores, query_marks)
+        dqk_ref[:, columns] = (dq_ref[:, columns].astype(f32) + tn(grad_scores, query_marks)).astype(bf16)
         grad_values = grad_values + tn(probs.astype(bf16), grad_marks)
         part = nn(grad_scores, qk)
         for doc in range(DOCS):
@@ -767,7 +783,7 @@
         ],
         [lanes(rows, 2 * WIDE), lanes(rows, WIDE), whole(part_shape)],
         (
-            jax.ShapeDtypeStruct((rows, HEADS * WIDE), f32),
+            jax.ShapeDtypeStruct((rows, HEADS * WIDE), bf16),
             jax.ShapeDtypeStruct((rows, HEADS * HD), f32),
             jax.ShapeDtypeStruct(part_shape, bf16),
         ),
@@ -783,7 +799,7 @@
     pair = pl.program_id(0)
     onehot = (iota((ids_ref.shape[0], SLOTS), 1) == ids_ref[...]).astype(f32).astype(bf16)
     marks = [read_marks(marks_ref, place_ref, 2 * pair + side).astype(bf16) for side in range(2)]
-    dqk = (dqk_in_ref[...] + nn(onehot, jnp.concatenate(marks, axis=1))).astype(bf16)
+    dqk = (dqk_in_ref[...].astype(f32) + nn(onehot, jnp.concatenate(marks, axis=1))).astype(bf16)
     dv = (dv_in_ref[...] + dconv_ref[...]).astype(bf16)
     dqk_ref[...] = dqk
     dv_ref[...] = dv
@@ -1002,6 +1018,53 @@
     )
 
 
+def final_kernel(folds, width, *refs):
+    late_refs, early_refs = refs[:3], refs[3:5]
+    fold_ref, query_ref, key_ref, value_ref, out_ref, up_ref, down_ref = refs[5:]
+    rows = value_ref.shape[1]
+    left = iota((rows, WIDE), 1) < HD
+    for layer in range(2):
+        base = layer * width
+        for pair in range(PAIRS):
+            ref = late_refs[pair // (PAIRS // 2)]
+            at = base + (pair % (PAIRS // 2)) * 2 * WIDE
+            first = ref[:, at : at + WIDE].astype(f32)
+            second = ref[:, at + WIDE : at + 2 * WIDE].astype(f32)
+            columns = slice(pair * WIDE, (pair + 1) * WIDE)
+            query_ref[layer, :, columns] = jnp.where(left, first, pltpu.roll(second, HD, 1))
+            key_ref[layer, :, columns] = jnp.where(left, pltpu.roll(first, HD, 1), second)
+        value_ref[layer] = late_refs[2][:, base : base + width].astype(f32)
+        early = early_refs[layer]
+        hidden_units = folds * width
+        out_ref[layer] = early[:, 2 * hidden_units :].astype(f32)
+        for block in range(width // WIDE):
+            parts = [
+                early[:, s * width + block * WIDE : s * width + (block + 1) * WIDE]
+                for s in range(folds)
+            ]
+            size = folds * WIDE
+            up_ref[layer, :, block * size : (block + 1) * size] = nt(
+                jnp.concatenate(parts, axis=1), fold_ref[...]
+            )
+        for s in range(folds):
+            down_ref[layer, :, s * width : (s + 1) * width] = early[
+                :, hidden_units + s * width : hidden_units + (s + 1) * width
+            ].astype(f32)
+
+
+def final_layout(late, early, fold, shard, width, hidden_units):
+    square = jax.ShapeDtypeStruct((2, shard, width), f32)
+    wide = jax.ShapeDtypeStruct((2, shard, hidden_units), f32)
+    outs = small_call(
+        functools.partial(final_kernel, hidden_units // width, width),
+        "final_layout",
+        (square, square, square, square, wide, wide),
+        (*late, *early, fold),
+    )
+    down = outs[5].reshape(2, shard * (hidden_units // width), width)
+    return [*outs[:5], down]
+
+
 def bits_of(axis):
     return lax.axis_size(axis).bit_length() - 1
 
@@ -1050,13 +1113,6 @@
             gathered, beside = lax.optimization_barrier((gathered, beside))
         gathered = jnp.concatenate([gathered, flip(gathered, "sp", 1 << bit)], axis=0)
     return gathered if beside is None else (gathered, beside)
-
-
-def all_sum(value):
-    for axis in ("sp", "dp"):
-        for bit in range(bits_of(axis)):
-            value = value + flip(value, axis, 1 << bit)
-    return value
 
 
 class Shares:
@@ -1084,8 +1140,19 @@
         part.values = self.values[..., first:last]
         return part
 
+    def join(self, *others):
+        self.values = jnp.concatenate([self.values] + [other.values for other in others], axis=-1)
+
     def result(self):
-        return jnp.concatenate(list(self.values), axis=-1)
+        return self.values[0]
+
+
+def late_parts(hidden_low, dqk, dv, width):
+    qk = tn(hidden_low, dqk).astype(bf16)
+    parts = [
+        Shares(part) for part in (qk[:, :width], qk[:, width:], tn(hidden_low, dv).astype(bf16))
+    ]
+    return [part.halve(("sp", 0)) for part in parts]
 
 
 def turn_order(turn):
@@ -1275,10 +1342,10 @@
         else:
             qk, v, sums = project(place, row_ids, start_hidden, start, room, 0)
         low, high = halo_of(v, segments)
-        marks, swapped = owner_marks(to_owners(sums, each), inverse)
-        swapped, v_conv = lax.optimization_barrier((swapped, v))
-        conv = conv_forward(local_bound, v_conv, low, high, taps[layer])
-        all_marks, conv = from_owners(swapped, conv)
+        conv = conv_forward(local_bound, v, low, high, taps[layer])
+        parts, conv = lax.optimization_barrier((to_owners(sums, each), conv))
+        marks, swapped = owner_marks(parts, inverse)
+        all_marks = from_owners(swapped)
         pseudo, mark_kernel, steps = owner_pseudo(marks)
         partial = key_partial(place, row_ids, qk, v, all_marks)
         near = join_pair(partial, flip(partial[room // 2 :], "sp", 1))
@@ -1303,11 +1370,10 @@
 
     cotangent_other, hidden_low = lax.optimization_barrier((cotangent_other, hidden_low))
     grad = in_order(cotangent_keep, cotangent_other, top).reshape(rows, width).astype(f32)
-    keep, send, mask, top = swap_rows(hidden_low.reshape(segments, length, width))
-    output = in_order(keep, flip(send, "sp", mask), top)[:, None]
+    output_keep, output_send, mask, top = swap_rows(hidden_low.reshape(segments, length, width))
     early_shares = [None] * layers
-    late_shares = [None] * layers
-    waiting = []
+    late_gradients = None
+    late_done = []
     small = [None] * layers
     for layer in reversed(range(layers)):
         (hidden_low, qk, v, low, high, marks, pseudo, mark_kernel, steps, all_marks, values,
@@ -1321,7 +1387,7 @@
             (task_grads, (normed_low, expanded_grad, activated_low, dense_grad, branch, projected_grad))
         )
         normed_low, expanded_grad, activated_low, dense_grad, branch, projected_grad = held
-        waiting += [tn(normed_low, expanded_grad)]
+        waiting = [tn(normed_low, expanded_grad)]
         waiting += [
             tn(activated_low[:, s * width : (s + 1) * width], dense_grad) for s in range(folds)
         ]
@@ -1332,63 +1398,71 @@
             scatter_dimension=0,
             tiled=True,
         )
-        late = shares.shape[1] - (2 * hidden_units + width)
-        if late:
-            late_shares[layer + 1] = shares[:, :late]
-        early_shares[layer] = shares[:, late:]
+        early_shares[layer] = shares
         total, payload = owner_back(to_owners(task_grads, each), pseudo, values)
         own_grads = newton_back(marks, mark_kernel, steps, values, total)
+        if layer == layers - 1:
+            payload, output_send = lax.optimization_barrier((payload, output_send))
+            output_other = flip(output_send, "sp", mask)
         all_grads, own_grads = from_owners(payload, own_grads)
+        if late_gradients is not None:
+            parts = late_parts(*late_gradients, width)
+            all_grads, values = lax.optimization_barrier((all_grads, [part.values for part in parts]))
+            for part, value in zip(parts, values):
+                part.values = value
+            late_done.append(parts)
+            late_gradients = None
         dqk, dv, query_part = key_back(
             place, row_ids, qk, v, all_marks, all_mixed, all_grads, dq
         )
-        query_part, conv_grad_in = lax.optimization_barrier((query_part, branch_grad))
-        dconv, dtaps = conv_back(
-            local_bound, v, low, high, conv_grad_in, grad_low, grad_high, taps[layer]
-        )
-        last = owner_last(to_owners(query_part, each), own_grads, inverse)
-        mark_grads, (dconv, dtaps) = from_owners(last, (dconv, dtaps))
+        if layer == layers - 1:
+            query_part, output_other = lax.optimization_barrier((query_part, output_other))
+            output = in_order(output_keep, output_other, top)[:, None]
+        query_part, held = lax.optimization_barrier((query_part, branch_grad))
+        dconv = conv_back(local_bound, taps[layer], held, grad_low, grad_high)
+        parts, dconv = lax.optimization_barrier((to_owners(query_part, each), dconv))
+        last = owner_last(parts, own_grads, inverse)
+        last, held = lax.optimization_barrier((last, held))
+        dtaps = taps_back(local_bound, v, low, high, held)
+        mark_grads, dtaps = from_owners(last, dtaps)
         dqk, dv, grad = spread(
             place, col_ids, mark_grads, dqk, dv, dconv, grad_first,
             tails[(layer - 1) % layers], place_of_heads,
         )
-        waiting = [tn(hidden_low, dqk), tn(hidden_low, dv)]
+        late_gradients = (hidden_low, dqk, dv)
         conv_grad = dtaps[:KCONV].reshape(KCONV, HEADS, HD).sum(axis=-1).T
         small[layer] = (conv_grad, scales[:2], scales[2:])
-    final = [
-        Shares(part.astype(bf16)) for part in (waiting[0][:, :width], waiting[0][:, width:], waiting[1])
-    ]
-    for turn, part in enumerate(final):
-        part.halve(turn_order(turn)[0])
-    keep, send, mask, top = swap_rows(grad.reshape(segments, length, width))
-    values, send = lax.optimization_barrier(([part.values for part in final], send.astype(bf16)))
-    other = flip(send, "sp", mask)
-    for turn, part in enumerate(final):
-        part.values = values[turn]
-        part.halve(*turn_order(turn)[1:])
-    last, other = lax.optimization_barrier(([part.result() for part in final], other))
-    late_shares[0] = jnp.concatenate(last, axis=1)
-    grad_tokens = in_order(keep, other.astype(f32), top)[:, None]
     conv_rows = jnp.stack([small[layer][0] for layer in range(layers)]).reshape(-1)
     conv_rows = jnp.pad(conv_rows, (0, -conv_rows.shape[0] % width)).reshape(-1, width)
     scales = [small[layer][k] for k in (1, 2) for layer in range(layers)]
-    packed = all_sum(jnp.concatenate(scales + [conv_rows], axis=0))
+    packed = jnp.concatenate(scales + [conv_rows], axis=0)
+    final = late_parts(*late_gradients, width)
+    orders = [turn_order(turn) for turn in range(3)]
+    keep, send, mask, top = swap_rows(grad.reshape(segments, length, width))
+    other = send.astype(bf16)
+    for number in range(len(orders[0])):
+        values, packed, other = lax.optimization_barrier(
+            ([part.values for part in final], packed, other)
+        )
+        axis, bit = orders[0][number]
+        packed = packed + flip(packed, axis, 1 << bit)
+        if number == 1:
+            other = flip(other, "sp", mask)
+        if number == 2:
+            waiting_other, other = other, packed[:1]
+        for turn, (part, value, order) in enumerate(zip(final, values, orders)):
+            part.values = value
+            if number:
+                part.halve(order[number])
+            else:
+                part.join(*[parts[turn] for parts in reversed(late_done)])
+    last, other = lax.optimization_barrier(([part.result() for part in final], waiting_other))
+    grad_tokens = in_order(keep, other.astype(f32), top)[:, None]
     gain_sum = packed[: 2 * layers].reshape(layers, 2, width)
     bias_sum = packed[2 * layers : 4 * layers].reshape(layers, 2, width)
     conv_sum = packed[4 * layers :].reshape(-1)[: layers * HEADS * KCONV]
     conv_sum = conv_sum.reshape(layers, HEADS, KCONV)
-    results = [[] for _ in range(6)]
-    for layer in range(layers):
-        late, early = late_shares[layer], early_shares[layer]
-        pair = late[:, : 2 * width].astype(f32).reshape(shard, HEADS, 2, HD)
-        results[0].append(pair[:, :, 0].reshape(shard, width))
-        results[1].append(pair[:, :, 1].reshape(shard, width))
-        results[2].append(late[:, 2 * width :].astype(f32))
-        results[3].append(early[:, 2 * hidden_units :].astype(f32))
-        results[4].append(unfolded(early[:, :hidden_units], fold, folds))
-        down_grad = early[:, hidden_units : 2 * hidden_units].astype(f32)
-        results[5].append(down_grad.reshape(shard * folds, width))
-    grads = [jnp.stack(parts) for parts in results]
+    grads = final_layout(last, early_shares, fold, shard, width, hidden_units)
     return (
         output,
         grad_tokens,

time: 702 us -> 684 us (0.974)
  Pallas kernels: 276 us -> 254 us
  local copies, waits for them, and re-layouts: 72.9 us -> 93.2 us
    pallas_call x18 -> x20, Pallas kernels: 153 us -> 127 us  [over_pairs(): pl.pallas_call(body, grid_spec=pltpu.PrefetchScalarGridSpec(num_scalar_pr...]
    unnamed x247 -> x362, local copies, waits for them, and re-layouts: 38 us -> 51.1 us
    reduce_scatter x2, waiting for transfers between devices: 7.38 us -> 0.01 us  [local(): lax.psum_scatter(jnp.concatenate([part.astype(bf16) for part in waiting],...]
    ppermute x95 -> x98, starting transfers between devices: 101 us -> 94.3 us  [flip(): return lax.ppermute(value, axis, [(i, i ^ mask) for i in range(count)])]
    ppermute x95 -> x98, waiting for transfers between devices: 124 us -> 130 us  [flip(): return lax.ppermute(value, axis, [(i, i ^ mask) for i in range(count)])]
    pallas_call x12 -> x13, Pallas kernels: 51.3 us -> 55.8 us  [small_call(): pl.pallas_call(body, out_shape=out_shape, scratch_shapes=scratch, cost_es...]
  transfers between devices with their start and end apart: 107 -> 110, of which waited for: 58 -> 45; matrix products, arithmetic and copies ran while one was open for 12% -> 14% of each run, Pallas kernels for 36% -> 33%
where the time goes in v4:
time: 684 us; the launch traced here: 674 us
  Pallas kernels  254 us (37%)
  waiting for transfers between devices  134 us (20%)
  starting transfers between devices  105 us (15%)
  local copies, waits for them, and re-layouts  93.2 us (14%)
  matrix products  36 us (5%)
  other arithmetic  34.9 us (5%)
  between operations  17 us (2%)
    ppermute x98, waiting for transfers between devices, flip(): return lax.ppermute(value, axis, [(i, i ^ mask) for i in range(count)])  130 us
    pallas_call x20, Pallas kernels, over_pairs(): pl.pallas_call(body, grid_spec=pltpu.PrefetchScalarGridSpec(num_scalar_pr...  127 us
    ppermute x98, starting transfers between devices, flip(): return lax.ppermute(value, axis, [(i, i ^ mask) for i in range(count)])  94.3 us
    pallas_call x4, Pallas kernels, dense_call(): pl.pallas_call(body, grid=(folds,), in_specs=in_specs, out_specs=out_spec...  64.8 us
    pallas_call x13, Pallas kernels, small_call(): pl.pallas_call(body, out_shape=out_shape, scratch_shapes=scratch, cost_es...  55.8 us
    unnamed x362, local copies, waits for them, and re-layouts  51.1 us
    dot_general x16, matrix products, tn(): lax.dot_general(left, right, (((0,), (0,)), ((), ())), preferred_element_...  33.1 us
  transfers between devices with their start and end apart: 110, of which 45 were waited for; matrix products, arithmetic and copies ran while one was open for 14% of the time, Pallas kernels for 33%

profile of v4, /device:TPU:0, one launch (start us, length us, event | category | flops | bytes accessed | tf_op | source)
XLA Modules:
  0.0 674.2 jit_solution(10315462111403444723)
XLA Ops:
  45.2 5.1 collective-permute-done.10
  71.8 7.8 %project.2 = (bf16[512,1536]{1,0:T(8,128)(2,1)S(1)}, bf16[512,768]{1,0:T(8,128)(2,1)S(1)}, f32[24,64,128]{2,1,0:T(8,128)S(1)}) custom-call(s32[24]{0:T(128)S(1)} %fusion.71.place_ref, s32[1,512]{1,0:T(1,128)S(1)} %fusion.68.ids_ref, bf16[3,512,768]{2,1,0:T(8,128)(2,1)} %pad_maximum_fusion.1.hidden_qk_ref.hidden_v_ref, ...), custom_call_target="tpu_custom_call" | custom-call | flops 1811939328 | bytes 14944256 | tf_op jit(solution)/shard_map/project/pallas_call | solution.py:122
  89.4 7.0 %conv_forward.2.conv_ref = f32[512,768]{1,0:T(8,128)S(1)} custom-call(s32[2]{0:T(128)S(1)} %broadcast_subtract_fusion.bound_ref, f32[396]{0:T(512)S(1)} %reshape_squeeze.13.scalar_ref, bf16[512,768]{1,0:T(8,128)(2,1)S(1)} %get-tuple-element.213.v_ref, bf16[2,16,768]{2,1,0:T(8,128)(2,1)S(1)} %pad_select_fusion.7.low_ref, ...), custom_call_target="tpu_custom_call" | custom-call | flops 5000000000 | bytes 2457600 | tf_op jit(solution)/shard_map/conv_forward/pallas_call | solution.py:122
  100.8 5.0 collective-permute-done.22
  114.2 5.5 key_partial.2.mine_ref
  129.7 6.9 %owner_pseudo.2 = (f32[3,64,64]{2,1,0:T(8,128)}, f32[3,64,64]{2,1,0:T(8,128)}, f32[6,3,4,64,64]{4,3,2,1,0:T(8,128)}) custom-call(f32[3,64,128]{2,1,0:T(8,128)} %get-tuple-element.220.marks_ref), custom_call_target="tpu_custom_call" | custom-call | flops 5000000000 | bytes 1000000 | tf_op jit(solution)/shard_map/owner_pseudo/pallas_call | solution.py:284
  161.5 14.0 %dense_forward.2 = (f32[512,768]{1,0:T(8,128)S(1)}, f32[512,128]{1,0:T(8,128)S(1)}, bf16[512,768]{1,0:T(8,128)(2,1)S(1)}, f32[512,3072]{1,0:T(8,128)}, bf16[512,...) custom-call(f32[512,768]{1,0:T(8,128)S(1)} %convert_element_type.493, ...), custom_call_target="tpu_custom_call" | custom-call | flops 5435817984 | bytes 30000000 | tf_op jit(solution)/shard_map/dense_forward/pallas_call | solution.py:899
  177.1 7.4 %project.3 = (bf16[512,1536]{1,0:T(8,128)(2,1)S(1)}, bf16[512,768]{1,0:T(8,128)(2,1)S(1)}, f32[24,64,128]{2,1,0:T(8,128)S(1)}) custom-call(s32[24]{0:T(128)S(1)} %fusion.71.place_ref, s32[1,512]{1,0:T(1,128)S(1)} %fusion.68.ids_ref, bf16[1,512,768]{2,1,0:T(8,128)(2,1)S(1)} %bitcast.235, bf16[1,512,768]{2,1,0:T(8,128)(2,1)S(1)} %bitcast.236, ...), custom_call_target="tpu_custom_call" | custom-call | flops 1811939328 | bytes 33032192 | tf_op jit(solution)/shard_map/project/pallas_call | solution.py:122
  200.1 7.0 %conv_forward.3.conv_ref = f32[512,768]{1,0:T(8,128)S(1)} custom-call(s32[2]{0:T(128)S(1)} %copy-done.101, f32[396]{0:T(512)S(1)} %copy-done.96, bf16[512,768]{1,0:T(8,128)(2,1)S(1)} %copy-done.20, bf16[2,16,768]{2,1,0:T(8,128)(2,1)S(1)} %pad_select_fusion.5.low_ref, bf16[2,16,768]{2,1,0:T(8,128)(2,1)S(1)} %pad_select_fusion.4.high_ref), custom_call_target="tpu_custom_call" | custom-call | flops 5000000000 | bytes 2457600 | tf_op jit(solution)/shard_map/conv_forward/pallas_call | solution.py:122
  223.9 5.5 key_partial.3.mine_ref
  240.3 6.9 %owner_pseudo.3 = (f32[3,64,64]{2,1,0:T(8,128)}, f32[3,64,64]{2,1,0:T(8,128)}, f32[6,3,4,64,64]{4,3,2,1,0:T(8,128)}) custom-call(f32[3,64,128]{2,1,0:T(8,128)} %get-tuple-element.241.marks_ref), custom_call_target="tpu_custom_call" | custom-call | flops 5000000000 | bytes 1000000 | tf_op jit(solution)/shard_map/owner_pseudo/pallas_call | solution.py:284
  276.1 14.2 %dense_forward.3 = (f32[512,768]{1,0:T(8,128)S(1)}, f32[512,128]{1,0:T(8,128)S(1)}, bf16[512,768]{1,0:T(8,128)(2,1)S(1)}, f32[512,3072]{1,0:T(8,128)}, bf16[512,...) custom-call(f32[512,768]{1,0:T(8,128)S(1)} %copy-done.44, ...), custom_call_target="tpu_custom_call" | custom-call | flops 5435817984 | bytes 30000000 | tf_op jit(solution)/shard_map/dense_forward/pallas_call | solution.py:899
  292.6 18.4 %dense_backward.2 = (bf16[512,768]{1,0:T(8,128)(2,1)S(1)}, bf16[512,3072]{1,0:T(8,128)(2,1)}, f32[512,768]{1,0:T(8,128)S(1)}, bf16[512,768]{1,0:T(8,128)(2,1)S(1...) custom-call(f32[512,768]{1,0:T(8,128)S(1)} %bitcast_convert_fusion.grad_ref, ...), custom_call_target="tpu_custom_call" | custom-call | flops 5435817984 | bytes 30000000 | tf_op jit(solution)/shard_map/dense_backward/pallas_call | solution.py:899
  311.0 6.4 token_back.2
  346.7 10.4 %newton_back.2.refs_4_ = f32[3,64,128]{2,1,0:T(8,128)} custom-call(f32[3,64,128]{2,1,0:T(8,128)} %get-tuple-element.241.marks_ref, f32[3,64,64]{2,1,0:T(8,128)} %get-tuple-element.268.kernel_ref, f32[6,3,4,64,64]{4,3,2,1,0:T(8,128)} %get-tuple-element.269.steps_ref, f32[3,64,128]{2,1,0:T(8,128)} %get-tuple-element.265.refs_5_.values_ref, ...), custom_call_target="tpu_custom_call" | custom-call | flops 10000000000 | bytes 1000000 | tf_op jit(solution)/shard_map/newton_back/pallas_call | solution.py:284
  370.7 6.6 key_back.2
  378.5 7.2 %collective-permute-done.56 = bf16[256,768]{1,0:T(8,128)(2,1)S(1)} collective-permute-done((bf16[256,768]{1,0:T(8,128)(2,1)}, bf16[256,768]{1,0:T(8,128)(2,1)S(1)}, u32[]{:S(2)}, u32[]{:S(2)}) %collective-permute-start.56) | collective-permute-done | bytes 393248 | tf_op jit(solution)/shard_map/ppermute | solution.py:1074
  391.2 7.0 %conv_back.2.dconv_ref = f32[512,768]{1,0:T(8,128)S(1)} custom-call(s32[2]{0:T(128)S(1)} %copy-done.102, f32[396]{0:T(512)S(1)} %copy-done.97, bf16[512,768]{1,0:T(8,128)(2,1)S(1)} %copy-done.69, bf16[2,16,768]{2,1,0:T(8,128)(2,1)S(1)} %pad_select_fusion.3.grad_low_ref, bf16[2,16,768]{2,1,0:T(8,128)(2,1)S(1)} %pad_select_fusion.2.grad_high_ref), custom_call_target="tpu_custom_call" | custom-call | flops 5000000000 | bytes 2457600 | tf_op jit(solution)/shard_map/conv_back/pallas_call | solution.py:122
  404.7 8.0 %taps_back.2 = f32[40,768]{1,0:T(8,128)S(1)} custom-call(s32[2]{0:T(128)S(1)} %copy-done.103, bf16[512,768]{1,0:T(8,128)(2,1)S(1)} %copy-done.23, bf16[2,16,768]{2,1,0:T(8,128)(2,1)S(1)} %copy-done.88, bf16[2,16,768]{2,1,0:T(8,128)(2,1)S(1)} %copy-done.90, bf16[512,768]{1,0:T(8,128)(2,1)S(1)} %copy-done.70), custom_call_target="tpu_custom_call" | custom-call | flops 5000000000 | bytes 1794048 | tf_op jit(solution)/shard_map/taps_back/pallas_call | solution.py:122
  414.6 5.5 collective-permute-done.64
  427.3 8.7 %spread.2 = (bf16[512,1536]{1,0:T(8,128)(2,1)S(1)}, bf16[512,768]{1,0:T(8,128)(2,1)S(1)}, f32[512,768]{1,0:T(8,128)S(1)}) custom-call(s32[24]{0:T(128)S(1)} %fusion.71.place_ref, s32[512,1]{1,0:T(8,128)S(1)} %copy-done.34, bf16[24,64,128]{2,1,0:T(8,128)(2,1)S(1)} %pad_maximum_fusion.10.marks_ref, bf16[512,1536]{1,0:T(8,128)(2,1)S(1)} %copy-done.46, ...), custom_call_target="tpu_custom_call" | custom-call | flops 2415919104 | bytes 38930432 | tf_op jit(solution)/shard_map/spread/pallas_call | solution.py:122
  436.1 18.3 %dense_backward.3 = (bf16[512,768]{1,0:T(8,128)(2,1)S(1)}, bf16[512,3072]{1,0:T(8,128)(2,1)}, f32[512,768]{1,0:T(8,128)S(1)}, bf16[512,768]{1,0:T(8,128)(2,1)S(1...) custom-call(f32[512,768]{1,0:T(8,128)S(1)} %get-tuple-element.291.grad_ref, f32[512,768]{1,0:T(8,128)S(1)} %copy-done.36, ...), custom_call_target="tpu_custom_call" | custom-call | flops 5435817984 | bytes 30000000 | tf_op jit(solution)/shard_map/dense_backward/pallas_call | solution.py:899
  454.4 6.6 token_back.3
  499.5 10.6 %newton_back.3.refs_4_ = f32[3,64,128]{2,1,0:T(8,128)} custom-call(f32[3,64,128]{2,1,0:T(8,128)} %get-tuple-element.220.marks_ref, f32[3,64,64]{2,1,0:T(8,128)} %get-tuple-element.307.kernel_ref, f32[6,3,4,64,64]{4,3,2,1,0:T(8,128)} %get-tuple-element.308.steps_ref, f32[3,64,128]{2,1,0:T(8,128)} %get-tuple-element.305.refs_5_.values_ref, ...), custom_call_target="tpu_custom_call" | custom-call | flops 10000000000 | bytes 1000000 | tf_op jit(solution)/shard_map/newton_back/pallas_call | solution.py:284
  521.4 6.7 key_back.3
  533.8 7.0 %conv_back.3.dconv_ref = f32[512,768]{1,0:T(8,128)S(1)} custom-call(s32[2]{0:T(128)S(1)} %copy-done.104, f32[396]{0:T(512)S(1)} %copy-done.95, bf16[512,768]{1,0:T(8,128)(2,1)S(1)} %copy-done.66, bf16[2,16,768]{2,1,0:T(8,128)(2,1)S(1)} %pad_select_fusion.1.grad_low_ref, bf16[2,16,768]{2,1,0:T(8,128)(2,1)S(1)} %pad_select_fusion.grad_high_ref), custom_call_target="tpu_custom_call" | custom-call | flops 5000000000 | bytes 2457600 | tf_op jit(solution)/shard_map/conv_back/pallas_call | solution.py:122
  544.8 8.0 %taps_back.3 = f32[40,768]{1,0:T(8,128)S(1)} custom-call(s32[2]{0:T(128)S(1)} %copy-done.104, bf16[512,768]{1,0:T(8,128)(2,1)S(1)} %copy-done.18, bf16[2,16,768]{2,1,0:T(8,128)(2,1)S(1)} %copy-done.84, bf16[2,16,768]{2,1,0:T(8,128)(2,1)S(1)} %copy-done.86, bf16[512,768]{1,0:T(8,128)(2,1)S(1)} %copy-done.67), custom_call_target="tpu_custom_call" | custom-call | flops 5000000000 | bytes 1794048 | tf_op jit(solution)/shard_map/taps_back/pallas_call | solution.py:122
  554.7 5.3 collective-permute-done.83
  565.9 8.8 %spread.3 = (bf16[512,1536]{1,0:T(8,128)(2,1)S(1)}, bf16[512,768]{1,0:T(8,128)(2,1)S(1)}, f32[512,768]{1,0:T(8,128)S(1)}) custom-call(s32[24]{0:T(128)S(1)} %fusion.71.place_ref, s32[512,1]{1,0:T(8,128)S(1)} %copy-done.34, bf16[24,64,128]{2,1,0:T(8,128)(2,1)S(1)} %pad_maximum_fusion.12.marks_ref, bf16[512,1536]{1,0:T(8,128)(2,1)S(1)} %copy-done.52, ...), custom_call_target="tpu_custom_call" | custom-call | flops 2415919104 | bytes 38930432 | tf_op jit(solution)/shard_map/spread/pallas_call | solution.py:122
  589.4 12.7 %collective-permute-done.92 = f32[10,768]{1,0:T(8,128)S(1)} collective-permute-done((f32[10,768]{1,0:T(8,128)S(1)}, f32[10,768]{1,0:T(8,128)S(1)}, u32[]{:S(2)}, u32[]{:S(2)}) %collective-permute-start.92) | collective-permute-done | bytes 30752 | tf_op jit(solution)/shard_map/ppermute | solution.py:1074
  602.5 19.7 %collective-permute-done.91 = bf16[1,2,2,2,24,1536]{5,4,2,3,1,0:T(8,128)(2,1)S(1)} collective-permute-done((bf16[1,2,2,2,24,1536]{5,4,2,3,1,0:T(8,128)(2,1)S(1)}, bf16[1,2,2,2,24,1536]{5,4,2,3,1,0:T(8,128)(2,1)S(1)}, u32[]{:S(2)}, u32[]{:S(2)}) %collective-permute-start.91) | collective-permute-done | bytes 589856 | tf_op jit(solution)/shard_map/ppermute | solution.py:1074
  642.3 4.5 collective-permute-done.101
  (832 shorter events, 378.4 us)
Async XLA Ops:
  7.2 152.5 %all-gather.3.cloned.1.call-start = ((), (), s32[]{:S(2)}) async-start(), calls=%async_computation.2 | async-start | bytes 14598144 | tf_op jit(solution)/shard_map/all_gather | solution.py:1328
  17.5 23.7 %collective-permute-start.9 = (bf16[256,768]{1,0:T(8,128)(2,1)}, bf16[256,768]{1,0:T(8,128)(2,1)S(1)}, u32[]{:S(2)}, u32[]{:S(2)}) collective-permute-start(bf16[256,768]{1,0:T(8,128)(2,1)} %get-tuple-element.460), channel_id=1, source_target_pairs={{0,8},{1,9},{2,10},{3,11},{4,12},{5,13},{6,14},{7,15},{8,0},{9,1},... | collective-permute-start | bytes 1179656 | tf_op jit(solution)/shard_map/ppermute | solution.py:1074
  29.3 10.9 %collective-permute-start.7 = (bf16[96,768]{1,0:T(8,128)(2,1)S(1)}, bf16[96,768]{1,0:T(8,128)(2,1)S(1)}, u32[]{:S(2)}, u32[]{:S(2)}) collective-permute-start(bf16[96,768]{1,0:T(8,128)(2,1)S(1)} %pad_maximum_fusion.27), channel_id=1, source_target_pairs={{0,4},{1,5},{2,6},{3,7},{4,0},{5,1},{6,2},{7,3},{8,12},{9,13},{10,... | collective-permute-start | bytes 442376 | tf_op jit(solution)/shard_map/ppermute | solution.py:1074
  54.0 218.2 %all-gather.5.cloned.1.call-start = ((), (), s32[]{:S(2)}) async-start(), calls=%async_computation.3 | async-start | bytes 14598144 | tf_op jit(solution)/shard_map/all_gather | solution.py:1328
  57.6 603.1 %reduce-scatter.5.cloned.1.call-start = ((), (), s32[]{:S(2)}) async-start(), calls=%async_computation.5 | async-start | bytes 10948608 | tf_op jit(solution)/shard_map/reduce_scatter | solution.py:1395
  85.9 11.7 %collective-permute-start.17 = (bf16[3,64,128]{2,1,0:T(8,128)(2,1)S(1)}, bf16[3,64,128]{2,1,0:T(8,128)(2,1)S(1)}, u32[]{:S(2)}, u32[]{:S(2)}) collective-permute-start(bf16[3,64,128]{2,1,0:T(8,128)(2,1)S(1)} %get-tuple-element.487), channel_id=1, source_target_pairs={{0,4},{1,5},{2,6},{3,7},{4,0},{5,1},{6,2},{7,3},{8,12},{9,13},{10,... | collective-permute-start | bytes 147464 | tf_op jit(solution)/shard_map/ppermute | solution.py:1074
  86.7 10.9 %collective-permute-start.18 = (bf16[3,64,128]{2,1,0:T(8,128)(2,1)S(1)}, bf16[3,64,128]{2,1,0:T(8,128)(2,1)S(1)}, u32[]{:S(2)}, u32[]{:S(2)}) collective-permute-start(bf16[3,64,128]{2,1,0:T(8,128)(2,1)S(1)} %get-tuple-element.486), channel_id=1, source_target_pairs={{0,2},{1,3},{2,0},{3,1},{4,6},{5,7},{6,4},{7,5},{8,10},{9,11},{10,... | collective-permute-start | bytes 147464 | tf_op jit(solution)/shard_map/ppermute | solution.py:1074
  86.7 10.9 %collective-permute-start.19 = (bf16[3,64,128]{2,1,0:T(8,128)(2,1)S(1)}, bf16[3,64,128]{2,1,0:T(8,128)(2,1)S(1)}, u32[]{:S(2)}, u32[]{:S(2)}) collective-permute-start(bf16[3,64,128]{2,1,0:T(8,128)(2,1)S(1)} %get-tuple-element.485), channel_id=1, source_target_pairs={{0,6},{1,7},{2,4},{3,5},{4,2},{5,3},{6,0},{7,1},{8,14},{9,15},{10,... | collective-permute-start | bytes 147464 | tf_op jit(solution)/shard_map/ppermute | solution.py:1074
  195.8 12.5 %collective-permute-start.34 = (bf16[3,64,128]{2,1,0:T(8,128)(2,1)S(1)}, bf16[3,64,128]{2,1,0:T(8,128)(2,1)S(1)}, u32[]{:S(2)}, u32[]{:S(2)}) collective-permute-start(bf16[3,64,128]{2,1,0:T(8,128)(2,1)S(1)} %get-tuple-element.479), channel_id=1, source_target_pairs={{0,4},{1,5},{2,6},{3,7},{4,0},{5,1},{6,2},{7,3},{8,12},{9,13},{10,... | collective-permute-start | bytes 147464 | tf_op jit(solution)/shard_map/ppermute | solution.py:1074
  238.9 10.9 %collective-permute-start.45 = (bf16[3,64,128]{2,1,0:T(8,128)(2,1)}, bf16[3,64,128]{2,1,0:T(8,128)(2,1)}, u32[]{:S(2)}, u32[]{:S(2)}) collective-permute-start(bf16[3,64,128]{2,1,0:T(8,128)(2,1)} %get-tuple-element.473), channel_id=1, source_target_pairs={{0,6},{1,7},{2,4},{3,5},{4,2},{5,3},{6,0},{7,1},{8,14},{9,15},{10,... | collective-permute-start | bytes 147464 | tf_op jit(solution)/shard_map/ppermute | solution.py:1074
  260.8 29.5 %collective-permute-start.32 = (bf16[256,768]{1,0:T(8,128)(2,1)}, bf16[256,768]{1,0:T(8,128)(2,1)}, u32[]{:S(2)}, u32[]{:S(2)}) collective-permute-start(bf16[256,768]{1,0:T(8,128)(2,1)} %get-tuple-element.230), channel_id=1, source_target_pairs={{0,8},{1,9},{2,10},{3,11},{4,12},{5,13},{6,14},{7,15},{8,0},{9,1},... | collective-permute-start | bytes 1179656 | tf_op jit(solution)/shard_map/ppermute | solution.py:1074
  332.4 328.3 %reduce-scatter.3.cloned.1.call-start = ((), (), s32[]{:S(2)}) async-start(), calls=%async_computation.4 | async-start | bytes 10948608 | tf_op jit(solution)/shard_map/reduce_scatter | solution.py:1395
  344.8 12.2 %collective-permute-start.53 = (bf16[3,64,128]{2,1,0:T(8,128)(2,1)}, bf16[3,64,128]{2,1,0:T(8,128)(2,1)}, u32[]{:S(2)}, u32[]{:S(2)}) collective-permute-start(bf16[3,64,128]{2,1,0:T(8,128)(2,1)} %get-tuple-element.267), channel_id=1, source_target_pairs={{0,4},{1,5},{2,6},{3,7},{4,0},{5,1},{6,2},{7,3},{8,12},{9,13},{10,... | collective-permute-start | bytes 147464 | tf_op jit(solution)/shard_map/ppermute | solution.py:1074
  365.2 20.5 %collective-permute-start.56 = (bf16[256,768]{1,0:T(8,128)(2,1)}, bf16[256,768]{1,0:T(8,128)(2,1)S(1)}, u32[]{:S(2)}, u32[]{:S(2)}) collective-permute-start(bf16[256,768]{1,0:T(8,128)(2,1)} %get-tuple-element.274), channel_id=1, source_target_pairs={{0,8},{1,9},{2,10},{3,11},{4,12},{5,13},{6,14},{7,15},{8,0},{9,1},... | collective-permute-start | bytes 1179656 | tf_op jit(solution)/shard_map/ppermute | solution.py:1074
  387.7 11.8 %collective-permute-start.58 = (bf16[3,32,128]{2,1,0:T(8,128)(2,1)S(1)}, bf16[3,32,128]{2,1,0:T(8,128)(2,1)S(1)}, u32[]{:S(2)}, u32[]{:S(2)}) collective-permute-start(bf16[3,32,128]{2,1,0:T(8,128)(2,1)S(1)} %get-tuple-element.495), channel_id=1, source_target_pairs={{0,4},{1,5},{2,6},{3,7},{4,0},{5,1},{6,2},{7,3},{8,12},{9,13},{10,... | collective-permute-start | bytes 73736 | tf_op jit(solution)/shard_map/ppermute | solution.py:1074
  387.7 11.8 %collective-permute-start.59 = (bf16[3,32,128]{2,1,0:T(8,128)(2,1)S(1)}, bf16[3,32,128]{2,1,0:T(8,128)(2,1)S(1)}, u32[]{:S(2)}, u32[]{:S(2)}) collective-permute-start(bf16[3,32,128]{2,1,0:T(8,128)(2,1)S(1)} %get-tuple-element.494), channel_id=1, source_target_pairs={{0,2},{1,3},{2,0},{3,1},{4,6},{5,7},{6,4},{7,5},{8,10},{9,11},{10,... | collective-permute-start | bytes 73736 | tf_op jit(solution)/shard_map/ppermute | solution.py:1074
  388.1 11.4 %collective-permute-start.60 = (bf16[3,32,128]{2,1,0:T(8,128)(2,1)S(1)}, bf16[3,32,128]{2,1,0:T(8,128)(2,1)S(1)}, u32[]{:S(2)}, u32[]{:S(2)}) collective-permute-start(bf16[3,32,128]{2,1,0:T(8,128)(2,1)S(1)} %get-tuple-element.493), channel_id=1, source_target_pairs={{0,6},{1,7},{2,4},{3,5},{4,2},{5,3},{6,0},{7,1},{8,14},{9,15},{10,... | collective-permute-start | bytes 73736 | tf_op jit(solution)/shard_map/ppermute | solution.py:1074
  402.4 10.9 %collective-permute-start.63 = (bf16[3,64,128]{2,1,0:T(8,128)(2,1)}, bf16[3,64,128]{2,1,0:T(8,128)(2,1)S(1)}, u32[]{:S(2)}, u32[]{:S(2)}) collective-permute-start(bf16[3,64,128]{2,1,0:T(8,128)(2,1)} %owner_last.2), channel_id=1, source_target_pairs={{0,4},{1,5},{2,6},{3,7},{4,0},{5,1},{6,2},{7,3},{8,12},{9,13},{10,... | collective-permute-start | bytes 147464 | tf_op jit(solution)/shard_map/ppermute | solution.py:1074
  462.2 24.2 %collective-permute-start.66 = (bf16[12,64,128]{2,1,0:T(8,128)(2,1)S(1)}, bf16[12,64,128]{2,1,0:T(8,128)(2,1)S(1)}, u32[]{:S(2)}, u32[]{:S(2)}) collective-permute-start(bf16[12,64,128]{2,1,0:T(8,128)(2,1)S(1)} %slice.412), channel_id=1, source_target_pairs={{0,1},{1,0},{2,3},{3,2},{4,5},{5,4},{6,7},{7,6},{8,9},{9,8},{10,11... | collective-permute-start | bytes 589832 | tf_op jit(solution)/shard_map/ppermute | solution.py:1074
  467.3 47.6 %collective-permute-start.73 = (bf16[1,2,2,2,2,24,768]{6,5,2,3,4,1,0:T(8,128)(2,1)}, bf16[1,2,2,2,2,24,768]{6,5,2,3,4,1,0:T(8,128)(2,1)}, u32[]{:S(2)}, u32[]{:S(2)}) collective-permute-start(bf16[1,2,2,2,2,24,768]{6,5,2,3,4,1,0:T(8,128)(2,1)} %bitcast.229), channel_id=1, source_target_pairs={{0,1},{1,0},{2,3},{3,2},{4,5},{5,4},{6,7},{7,6},{8,9},{9,8},{10,11... | collective-permute-start | bytes 1769480 | tf_op jit(solution)/shard_map/ppermute | solution.py:1074
  468.0 25.3 %collective-permute-start.80 = (bf16[2,16,768]{2,1,0:T(8,128)(2,1)}, bf16[2,16,768]{2,1,0:T(8,128)(2,1)S(1)}, u32[]{:S(2)}, u32[]{:S(2)}) collective-permute-start(bf16[2,16,768]{2,1,0:T(8,128)(2,1)} %get-tuple-element.448), channel_id=1, source_target_pairs={{0,1},{1,2},{2,3},{3,4},{4,5},{5,6},{6,7},{7,0},{8,9},{9,10},{10,1... | collective-permute-start | bytes 147464 | tf_op jit(solution)/shard_map/ppermute | solution.py:1195
  493.3 23.7 %collective-permute-start.74 = (bf16[1,2,2,2,2,24,768]{6,5,2,1,3,4,0:T(8,128)(2,1)}, bf16[1,2,2,2,2,24,768]{6,5,2,1,3,4,0:T(8,128)(2,1)}, u32[]{:S(2)}, u32[]{:S(2)}) collective-permute-start(bf16[1,2,2,2,2,24,768]{6,5,2,1,3,4,0:T(8,128)(2,1)} %bitcast.228), channel_id=1, source_target_pairs={{0,1},{1,0},{2,3},{3,2},{4,5},{5,4},{6,7},{7,6},{8,9},{9,8},{10,11... | collective-permute-start | bytes 1769480 | tf_op jit(solution)/shard_map/ppermute | solution.py:1074
  494.0 25.1 %collective-permute-start.75 = (bf16[1,2,2,2,2,24,768]{6,5,2,4,1,3,0:T(8,128)(2,1)}, bf16[1,2,2,2,2,24,768]{6,5,2,4,1,3,0:T(8,128)(2,1)}, u32[]{:S(2)}, u32[]{:S(2)}) collective-permute-start(bf16[1,2,2,2,2,24,768]{6,5,2,4,1,3,0:T(8,128)(2,1)} %bitcast.227), channel_id=1, source_target_pairs={{0,1},{1,0},{2,3},{3,2},{4,5},{5,4},{6,7},{7,6},{8,9},{9,8},{10,11... | collective-permute-start | bytes 1769480 | tf_op jit(solution)/shard_map/ppermute | solution.py:1074
  494.1 16.5 %collective-permute-start.81 = (bf16[2,16,768]{2,1,0:T(8,128)(2,1)}, bf16[2,16,768]{2,1,0:T(8,128)(2,1)S(1)}, u32[]{:S(2)}, u32[]{:S(2)}) collective-permute-start(bf16[2,16,768]{2,1,0:T(8,128)(2,1)} %get-tuple-element.447), channel_id=1, source_target_pairs={{1,0},{2,1},{3,2},{4,3},{5,4},{6,5},{7,6},{0,7},{9,8},{10,9},{11,1... | collective-permute-start | bytes 147464 | tf_op jit(solution)/shard_map/ppermute | solution.py:1196
  497.7 12.4 %collective-permute-start.70 = (bf16[3,64,128]{2,1,0:T(8,128)(2,1)}, bf16[3,64,128]{2,1,0:T(8,128)(2,1)S(1)}, u32[]{:S(2)}, u32[]{:S(2)}) collective-permute-start(bf16[3,64,128]{2,1,0:T(8,128)(2,1)} %get-tuple-element.306), channel_id=1, source_target_pairs={{0,4},{1,5},{2,6},{3,7},{4,0},{5,1},{6,2},{7,3},{8,12},{9,13},{10,... | collective-permute-start | bytes 147464 | tf_op jit(solution)/shard_map/ppermute | solution.py:1074
  530.3 11.7 %collective-permute-start.77 = (bf16[3,32,128]{2,1,0:T(8,128)(2,1)S(1)}, bf16[3,32,128]{2,1,0:T(8,128)(2,1)S(1)}, u32[]{:S(2)}, u32[]{:S(2)}) collective-permute-start(bf16[3,32,128]{2,1,0:T(8,128)(2,1)S(1)} %get-tuple-element.491), channel_id=1, source_target_pairs={{0,4},{1,5},{2,6},{3,7},{4,0},{5,1},{6,2},{7,3},{8,12},{9,13},{10,... | collective-permute-start | bytes 73736 | tf_op jit(solution)/shard_map/ppermute | solution.py:1074
  530.6 11.4 %collective-permute-start.78 = (bf16[3,32,128]{2,1,0:T(8,128)(2,1)S(1)}, bf16[3,32,128]{2,1,0:T(8,128)(2,1)S(1)}, u32[]{:S(2)}, u32[]{:S(2)}) collective-permute-start(bf16[3,32,128]{2,1,0:T(8,128)(2,1)S(1)} %get-tuple-element.490), channel_id=1, source_target_pairs={{0,2},{1,3},{2,0},{3,1},{4,6},{5,7},{6,4},{7,5},{8,10},{9,11},{10,... | collective-permute-start | bytes 73736 | tf_op jit(solution)/shard_map/ppermute | solution.py:1074
  582.7 19.4 %collective-permute-start.89 = (bf16[1,2,2,2,24,1536]{5,4,1,2,3,0:T(8,128)(2,1)S(1)}, bf16[1,2,2,2,24,1536]{5,4,1,2,3,0:T(8,128)(2,1)S(1)}, u32[]{:S(2)}, u32[]{:S(2)}) collective-permute-start(bf16[1,2,2,2,24,1536]{5,4,1,2,3,0:T(8,128)(2,1)S(1)} %dynamic-slice_bitcast_fusion.3), channel_id=1, source_target_pairs={{0,16},{16,0},{1,17},{17,1},{2,18},{18,2},{3,19},{19,3},{4,20},{20... | collective-permute-start | bytes 1769480 | tf_op jit(solution)/shard_map/ppermute | solution.py:1074
  583.4 18.9 %collective-permute-start.90 = (bf16[1,2,2,2,24,1536]{5,4,2,1,3,0:T(8,128)(2,1)S(1)}, bf16[1,2,2,2,24,1536]{5,4,2,1,3,0:T(8,128)(2,1)S(1)}, u32[]{:S(2)}, u32[]{:S(2)}) collective-permute-start(bf16[1,2,2,2,24,1536]{5,4,2,1,3,0:T(8,128)(2,1)S(1)} %dynamic-slice_bitcast_fusion.2), channel_id=1, source_target_pairs={{0,2},{1,3},{2,0},{3,1},{4,6},{5,7},{6,4},{7,5},{8,10},{9,11},{10,... | collective-permute-start | bytes 1769480 | tf_op jit(solution)/shard_map/ppermute | solution.py:1074
  584.6 17.5 %collective-permute-start.92 = (f32[10,768]{1,0:T(8,128)S(1)}, f32[10,768]{1,0:T(8,128)S(1)}, u32[]{:S(2)}, u32[]{:S(2)}) collective-permute-start(f32[10,768]{1,0:T(8,128)S(1)} %add.423), channel_id=1, source_target_pairs={{0,16},{16,0},{1,17},{17,1},{2,18},{18,2},{3,19},{19,3},{4,20},{20... | collective-permute-start | bytes 92168 | tf_op jit(solution)/shard_map/ppermute | solution.py:1074
  585.4 36.7 %collective-permute-start.91 = (bf16[1,2,2,2,24,1536]{5,4,2,3,1,0:T(8,128)(2,1)S(1)}, bf16[1,2,2,2,24,1536]{5,4,2,3,1,0:T(8,128)(2,1)S(1)}, u32[]{:S(2)}, u32[]{:S(2)}) collective-permute-start(bf16[1,2,2,2,24,1536]{5,4,2,3,1,0:T(8,128)(2,1)S(1)} %dynamic-slice_bitcast_fusion.1), channel_id=1, source_target_pairs={{0,4},{1,5},{2,6},{3,7},{4,0},{5,1},{6,2},{7,3},{8,12},{9,13},{10,... | collective-permute-start | bytes 1769480 | tf_op jit(solution)/shard_map/ppermute | solution.py:1074
  586.9 35.4 %collective-permute-start.93 = (bf16[256,768]{1,0:T(8,128)(2,1)S(1)}, bf16[256,768]{1,0:T(8,128)(2,1)S(1)}, u32[]{:S(2)}, u32[]{:S(2)}) collective-permute-start(bf16[256,768]{1,0:T(8,128)(2,1)S(1)} %fusion.44), channel_id=1, source_target_pairs={{0,8},{1,9},{2,10},{3,11},{4,12},{5,13},{6,14},{7,15},{8,0},{9,1},... | collective-permute-start | bytes 1179656 | tf_op jit(solution)/shard_map/ppermute | solution.py:1074
  (252 other events, 1780.5 us)
Sparse Core Ops, SparseCore 0:
  54.1 105.4 all-gather.2
  163.2 107.4 all-gather.4
  332.5 146.8 reduce-scatter.4
  493.4 151.4 reduce-scatter.2

commit v5 on v4

--- a/solution.py
+++ b/solution.py
@@ -20,6 +20,7 @@
 WINDOW = 40
 TAPS = 40
 CHUNK = 128
+CONV_BLOCK = 128
 LARGE = 2 * 10**6
 
 negative = -1e30
@@ -107,13 +108,13 @@
     return pl.BlockSpec((batches, rows, width), lambda p, *scalars: (0, 0, p))
 
 
-def in_hbm(array):
-    if array.size * array.dtype.itemsize < LARGE:
+def in_hbm(array, large=LARGE):
+    if array.size * array.dtype.itemsize < large:
         return array
     return pltpu.with_memory_space_constraint(array, pltpu.HBM)
 
 
-def over_pairs(body, name, scalars, in_specs, out_specs, out_shape, args, flops, scratch=()):
+def over_pairs(body, name, scalars, in_specs, out_specs, out_shape, args, flops, scratch=(), large=LARGE):
     moved = sum(a.size * a.dtype.itemsize for a in args)
     moved += sum(
         functools.reduce(lambda x, y: x * y, o.shape) * o.dtype.itemsize
@@ -132,7 +133,7 @@
         cost_estimate=pl.CostEstimate(flops=flops, bytes_accessed=moved, transcendentals=0),
         compiler_params=pltpu.CompilerParams(vmem_limit_bytes=16 * 1024 * 1024),
         name=name,
-    )(*scalars, *[in_hbm(a) for a in args])
+    )(*scalars, *[in_hbm(a, large) for a in args])
 
 
 def project_kernel(
@@ -221,11 +222,10 @@
     return first, second, column - first - second
 
 
-def join_kernel(mine_ref, other_ref, out_ref):
+def join_kernel(mine_ref, other_ref, *out_refs):
     lane = iota((LMK, WIDE), 1)
-    half = mine_ref.shape[0]
-
-    def one(task, carry):
+    each = out_refs[0].shape[0]
+    for task in range(other_ref.shape[0]):
         mine, other = mine_ref[task], other_ref[task]
         top_mine, top_other = mine[:, HD : HD + 1], other[:, HD : HD + 1]
         top = jnp.maximum(top_mine, top_other)
@@ -233,24 +233,18 @@
         parts = exact_three(top) + exact_three(joined[:, HD + 32 : HD + 33])
         for index, part in enumerate(parts):
             joined = jnp.where(lane == HD + index, part, joined)
-        out_ref[task] = joined.astype(bf16)
-        return carry
-
-    lax.fori_loop(0, half, one, 0, unroll=4)
-
-
-def join_pair(parts, other):
-    return pl.pallas_call(
+        out_refs[task // each][task % each] = joined.astype(bf16)
+
+
+def join_pair(parts, other, each):
+    shape = (each,) + other.shape[1:]
+    return small_call(
         join_kernel,
-        grid=(1,),
-        in_specs=[
-            pl.BlockSpec(other.shape, lambda g: (0, 0, 0)),
-            pl.BlockSpec(other.shape, lambda g: (0, 0, 0)),
-        ],
-        out_specs=pl.BlockSpec(other.shape, lambda g: (0, 0, 0)),
-        out_shape=jax.ShapeDtypeStruct(other.shape, bf16),
-        name="join_pair",
-    )(parts, other)
+        "join_pair",
+        [jax.ShapeDtypeStruct(shape, bf16)] * (other.shape[0] // each),
+        (parts, other),
+        flops=10**6,
+    )
 
 
 def identity():
@@ -400,7 +394,7 @@
 
 def convolve(pad_ref, taps, bound, out_ref):
     length = out_ref.shape[0]
-    block = 64
+    block = CONV_BLOCK
     for first in range(0, length, block):
         total = jnp.zeros((block, WIDE), f32)
         for offset in range(KCONV):
@@ -835,6 +829,7 @@
         ),
         (col_ids, marks, dqk, dv, dconv, grad_first, weight, weight),
         8 * rows * width * width,
+        large=10**6,
     )
 
 
@@ -906,7 +901,7 @@
         cost_estimate=pl.CostEstimate(flops=flops, bytes_accessed=3 * 10**7, transcendentals=0),
         compiler_params=pltpu.CompilerParams(vmem_limit_bytes=44 * 1024 * 1024),
         name=name,
-    )(*[in_hbm(a) for a in args])
+    )(*[in_hbm(a, 10**6) for a in args])
 
 
 def weight_specs(width, folds):
@@ -1089,14 +1084,15 @@
     return reverse_bits(relative, bits) * each + index % each
 
 
+def send_apart(parts):
+    bits = row_bits()
+    return [parts[0]] + [
+        flip(part, "sp", reverse_bits(index, bits)) for index, part in enumerate(parts) if index
+    ]
+
+
 def send_direct(near, each):
-    bits = row_bits()
-    parts = [near[:each]]
-    for index in range(1, near.shape[0] // each):
-        parts.append(
-            flip(near[index * each : (index + 1) * each], "sp", reverse_bits(index, bits))
-        )
-    return parts
+    return send_apart([near[at : at + each] for at in range(0, near.shape[0], each)])
 
 
 def to_owners(tasks, each):
@@ -1300,7 +1296,7 @@
             turns, held = lax.optimization_barrier(
                 (turns, (first[1:], out_weight, up_weight, down_weight))
             )
-            later_first = held[0] + [first[0]]
+            first[1:] = held[0]
             up_folded = folded(held[2].reshape(layers * shard, hidden_units), fold, folds)
             up_folded = up_folded.reshape(layers, shard, hidden_units)
             later_blocks = [
@@ -1309,8 +1305,8 @@
                         held[1][layer],
                         up_folded[layer],
                         held[3][layer].reshape(shard, hidden_units),
-                        later_first[layer],
-                    ],
+                    ]
+                    + ([first[layer + 1]] if layer + 1 < layers else []),
                     axis=1,
                 )
                 for layer in range(layers)
@@ -1348,8 +1344,8 @@
         all_marks = from_owners(swapped)
         pseudo, mark_kernel, steps = owner_pseudo(marks)
         partial = key_partial(place, row_ids, qk, v, all_marks)
-        near = join_pair(partial, flip(partial[room // 2 :], "sp", 1))
-        values, payload = owner_merge(send_direct(near, each), pseudo)
+        near = join_pair(partial, flip(partial[room // 2 :], "sp", 1), each)
+        values, payload = owner_merge(send_apart(near), pseudo)
         payload, qk_held = lax.optimization_barrier((payload, qk))
         token_weights = token_prep(place, col_ids, qk_held, all_marks)
         all_mixed, token_weights = from_owners(payload, token_weights)
@@ -1365,7 +1361,10 @@
         )
         hidden, hidden_low = next_hidden, next_low
         if layer == 0:
-            hidden_low, cotangent_send = lax.optimization_barrier((hidden_low, cotangent_send))
+            hidden_low, cotangent_send, first[0] = lax.optimization_barrier(
+                (hidden_low, cotangent_send, first[0])
+            )
+            first_heads = lax.all_gather(first[0], every, axis=0, tiled=True)
             cotangent_other = flip(cotangent_send, "sp", mask)
 
     cotangent_other, hidden_low = lax.optimization_barrier((cotangent_other, hidden_low))
@@ -1404,6 +1403,8 @@
         if layer == layers - 1:
             payload, output_send = lax.optimization_barrier((payload, output_send))
             output_other = flip(output_send, "sp", mask)
+        if late_gradients is not None:
+            payload, late_gradients = lax.optimization_barrier((payload, late_gradients))
         all_grads, own_grads = from_owners(payload, own_grads)
         if late_gradients is not None:
             parts = late_parts(*late_gradients, width)
@@ -1427,7 +1428,7 @@
         mark_grads, dtaps = from_owners(last, dtaps)
         dqk, dv, grad = spread(
             place, col_ids, mark_grads, dqk, dv, dconv, grad_first,
-            tails[(layer - 1) % layers], place_of_heads,
+            *((tails[layer - 1], place_of_heads) if layer else (first_heads, 0)),
         )
         late_gradients = (hidden_low, dqk, dv)
         conv_grad = dtaps[:KCONV].reshape(KCONV, HEADS, HD).sum(axis=-1).T
@@ -1436,27 +1437,23 @@
     conv_rows = jnp.pad(conv_rows, (0, -conv_rows.shape[0] % width)).reshape(-1, width)
     scales = [small[layer][k] for k in (1, 2) for layer in range(layers)]
     packed = jnp.concatenate(scales + [conv_rows], axis=0)
+    keep, send, mask, top = swap_rows(grad.reshape(segments, length, width))
+    other = flip(send.astype(bf16), "sp", mask)
     final = late_parts(*late_gradients, width)
     orders = [turn_order(turn) for turn in range(3)]
-    keep, send, mask, top = swap_rows(grad.reshape(segments, length, width))
-    other = send.astype(bf16)
     for number in range(len(orders[0])):
-        values, packed, other = lax.optimization_barrier(
-            ([part.values for part in final], packed, other)
-        )
+        values, packed = lax.optimization_barrier(([part.values for part in final], packed))
+        if number == 2:
+            values, other = lax.optimization_barrier((values, other))
         axis, bit = orders[0][number]
         packed = packed + flip(packed, axis, 1 << bit)
-        if number == 1:
-            other = flip(other, "sp", mask)
-        if number == 2:
-            waiting_other, other = other, packed[:1]
         for turn, (part, value, order) in enumerate(zip(final, values, orders)):
             part.values = value
             if number:
                 part.halve(order[number])
             else:
                 part.join(*[parts[turn] for parts in reversed(late_done)])
-    last, other = lax.optimization_barrier(([part.result() for part in final], waiting_other))
+    last = [part.result() for part in final]
     grad_tokens = in_order(keep, other.astype(f32), top)[:, None]
     gain_sum = packed[: 2 * layers].reshape(layers, 2, width)
     bias_sum = packed[2 * layers : 4 * layers].reshape(layers, 2, width)

time: 684 us -> 684 us (level)
  local copies, waits for them, and re-layouts: 93.2 us -> 74.1 us
  waiting for transfers between devices: 134 us -> 146 us
    unnamed x362 -> x342, local copies, waits for them, and re-layouts: 51.1 us -> 38.4 us
    pallas_call x13 -> x15, Pallas kernels: 55.8 us -> 61.8 us  [small_call(): pl.pallas_call(body, out_shape=out_shape, scratch_shapes=scratch, cost_es...]
  transfers between devices with their start and end apart: 110 -> 111, of which waited for: 45 -> 48; matrix products, arithmetic and copies ran while one was open for 14% -> 16% of each run, Pallas kernels for 33% -> 37%
where the time goes in v5:
time: 684 us; the launch traced here: 676 us
  Pallas kernels  258 us (38%)
  waiting for transfers between devices  146 us (21%)
  starting transfers between devices  103 us (15%)
  local copies, waits for them, and re-layouts  74.1 us (11%)
  other arithmetic  39.7 us (6%)
  matrix products  37.3 us (5%)
  between operations  17.1 us (3%)
    ppermute x98, waiting for transfers between devices, flip(): return lax.ppermute(value, axis, [(i, i ^ mask) for i in range(count)])  136 us
    pallas_call x20, Pallas kernels, over_pairs(): pl.pallas_call(body, grid_spec=pltpu.PrefetchScalarGridSpec(num_scalar_pr...  129 us
    ppermute x98, starting transfers between devices, flip(): return lax.ppermute(value, axis, [(i, i ^ mask) for i in range(count)])  96.1 us
    pallas_call x4, Pallas kernels, dense_call(): pl.pallas_call(body, grid=(folds,), in_specs=in_specs, out_specs=out_spec...  66.5 us
    pallas_call x15, Pallas kernels, small_call(): pl.pallas_call(body, out_shape=out_shape, scratch_shapes=scratch, cost_es...  61.8 us
    unnamed x342, local copies, waits for them, and re-layouts  38.4 us
    dot_general x16, matrix products, tn(): lax.dot_general(left, right, (((0,), (0,)), ((), ())), preferred_element_...  34.3 us
  transfers between devices with their start and end apart: 111, of which 48 were waited for; matrix products, arithmetic and copies ran while one was open for 16% of the time, Pallas kernels for 37%

profile of v5, /device:TPU:0, one launch (start us, length us, event | category | flops | bytes accessed | tf_op | source)
XLA Modules:
  0.0 675.7 jit_solution(7750718248466721799)
XLA Ops:
  17.2 16.9 %collective-permute-done.2 = bf16[24,768]{1,0:T(8,128)(2,1)S(1)} collective-permute-done((bf16[24,768]{1,0:T(8,128)(2,1)S(1)}, bf16[24,768]{1,0:T(8,128)(2,1)S(1)}, u32[]{:S(2)}, u32[]{:S(2)}) %collective-permute-start.2) | collective-permute-done | bytes 36896 | tf_op jit(solution)/shard_map/ppermute | solution.py:1069
  75.4 7.8 %project.2 = (bf16[512,1536]{1,0:T(8,128)(2,1)S(1)}, bf16[512,768]{1,0:T(8,128)(2,1)S(1)}, f32[24,64,128]{2,1,0:T(8,128)S(1)}) custom-call(s32[24]{0:T(128)S(1)} %fusion.71.place_ref, s32[1,512]{1,0:T(1,128)S(1)} %fusion.68.ids_ref, bf16[3,512,768]{2,1,0:T(8,128)(2,1)} %pad_maximum_fusion.1.hidden_qk_ref.hidden_v_ref, ...), custom_call_target="tpu_custom_call" | custom-call | flops 1811939328 | bytes 14944256 | tf_op jit(solution)/shard_map/project/pallas_call | solution.py:123
  93.0 7.0 %conv_forward.2.conv_ref = f32[512,768]{1,0:T(8,128)S(1)} custom-call(s32[2]{0:T(128)S(1)} %broadcast_subtract_fusion.bound_ref, f32[396]{0:T(512)S(1)} %reshape_squeeze.13.scalar_ref, bf16[512,768]{1,0:T(8,128)(2,1)S(1)} %get-tuple-element.223.v_ref, bf16[2,16,768]{2,1,0:T(8,128)(2,1)S(1)} %pad_select_fusion.7.low_ref, ...), custom_call_target="tpu_custom_call" | custom-call | flops 5000000000 | bytes 2457600 | tf_op jit(solution)/shard_map/conv_forward/pallas_call | solution.py:123
  105.6 6.0 collective-permute-done.22
  119.8 5.5 key_partial.2.mine_ref
  134.6 6.9 %owner_pseudo.2 = (f32[3,64,64]{2,1,0:T(8,128)}, f32[3,64,64]{2,1,0:T(8,128)}, f32[6,3,4,64,64]{4,3,2,1,0:T(8,128)}) custom-call(f32[3,64,128]{2,1,0:T(8,128)} %get-tuple-element.234.marks_ref), custom_call_target="tpu_custom_call" | custom-call | flops 5000000000 | bytes 1000000 | tf_op jit(solution)/shard_map/owner_pseudo/pallas_call | solution.py:278
  166.2 14.1 %dense_forward.2 = (f32[512,768]{1,0:T(8,128)S(1)}, f32[512,128]{1,0:T(8,128)S(1)}, bf16[512,768]{1,0:T(8,128)(2,1)S(1)}, f32[512,3072]{1,0:T(8,128)}, bf16[512,...) custom-call(f32[512,768]{1,0:T(8,128)} %convert_element_type.493.hid, ...), custom_call_target="tpu_custom_call" | custom-call | flops 5435817984 | bytes 30000000 | tf_op jit(solution)/shard_map/dense_forward/pallas_call | solution.py:894
  182.6 7.4 %project.3 = (bf16[512,1536]{1,0:T(8,128)(2,1)S(1)}, bf16[512,768]{1,0:T(8,128)(2,1)S(1)}, f32[24,64,128]{2,1,0:T(8,128)S(1)}) custom-call(s32[24]{0:T(128)S(1)} %fusion.71.place_ref, s32[1,512]{1,0:T(1,128)S(1)} %fusion.68.ids_ref, bf16[1,512,768]{2,1,0:T(8,128)(2,1)S(1)} %bitcast.233, bf16[1,512,768]{2,1,0:T(8,128)(2,1)S(1)} %bitcast.234, ...), custom_call_target="tpu_custom_call" | custom-call | flops 1811939328 | bytes 33032192 | tf_op jit(solution)/shard_map/project/pallas_call | solution.py:123
  206.5 7.0 %conv_forward.3.conv_ref = f32[512,768]{1,0:T(8,128)S(1)} custom-call(s32[2]{0:T(128)S(1)} %copy-done.97, f32[396]{0:T(512)S(1)} %copy-done.89, bf16[512,768]{1,0:T(8,128)(2,1)S(1)} %copy-done.20, bf16[2,16,768]{2,1,0:T(8,128)(2,1)S(1)} %pad_select_fusion.5.low_ref, bf16[2,16,768]{2,1,0:T(8,128)(2,1)S(1)} %pad_select_fusion.4.high_ref), custom_call_target="tpu_custom_call" | custom-call | flops 5000000000 | bytes 2457600 | tf_op jit(solution)/shard_map/conv_forward/pallas_call | solution.py:123
  219.4 4.8 collective-permute-done.39
  234.1 5.5 key_partial.3.mine_ref
  249.0 6.9 %owner_pseudo.3 = (f32[3,64,64]{2,1,0:T(8,128)}, f32[3,64,64]{2,1,0:T(8,128)}, f32[6,3,4,64,64]{4,3,2,1,0:T(8,128)}) custom-call(f32[3,64,128]{2,1,0:T(8,128)} %get-tuple-element.259.marks_ref), custom_call_target="tpu_custom_call" | custom-call | flops 5000000000 | bytes 1000000 | tf_op jit(solution)/shard_map/owner_pseudo/pallas_call | solution.py:278
  279.1 14.7 %dense_forward.3 = (f32[512,768]{1,0:T(8,128)S(1)}, f32[512,128]{1,0:T(8,128)S(1)}, bf16[512,768]{1,0:T(8,128)(2,1)S(1)}, f32[512,3072]{1,0:T(8,128)}, bf16[512,...) custom-call(f32[512,768]{1,0:T(8,128)} %copy-done.37, ...), custom_call_target="tpu_custom_call" | custom-call | flops 5435817984 | bytes 30000000 | tf_op jit(solution)/shard_map/dense_forward/pallas_call | solution.py:894
  297.1 19.0 %dense_backward.2 = (bf16[512,768]{1,0:T(8,128)(2,1)S(1)}, bf16[512,3072]{1,0:T(8,128)(2,1)S(1)}, f32[512,768]{1,0:T(8,128)S(1)}, bf16[512,768]{1,0:T(8,128)(2,1...) custom-call(f32[512,768]{1,0:T(8,128)} %bitcast_convert_fusion.grad_ref, f32[512,768]{1,0:T(8,128)} %copy-done.41, ...), custom_call_target="tpu_custom_call" | custom-call | flops 5435817984 | bytes 30000000 | tf_op jit(solution)/shard_map/dense_backward/pallas_call | solution.py:894
  316.2 6.4 token_back.2
  352.4 10.4 %newton_back.2.refs_4_ = f32[3,64,128]{2,1,0:T(8,128)} custom-call(f32[3,64,128]{2,1,0:T(8,128)} %get-tuple-element.259.marks_ref, f32[3,64,64]{2,1,0:T(8,128)} %get-tuple-element.286.kernel_ref, f32[6,3,4,64,64]{4,3,2,1,0:T(8,128)} %get-tuple-element.287.steps_ref, f32[3,64,128]{2,1,0:T(8,128)} %get-tuple-element.283.refs_5_.values_ref, ...), custom_call_target="tpu_custom_call" | custom-call | flops 10000000000 | bytes 1000000 | tf_op jit(solution)/shard_map/newton_back/pallas_call | solution.py:278
  376.3 6.6 key_back.2
  384.1 6.1 collective-permute-done.56
  395.8 7.0 %conv_back.2.dconv_ref = f32[512,768]{1,0:T(8,128)S(1)} custom-call(s32[2]{0:T(128)S(1)} %copy-done.98, f32[396]{0:T(512)S(1)} %copy-done.90, bf16[512,768]{1,0:T(8,128)(2,1)S(1)} %copy-done.60, bf16[2,16,768]{2,1,0:T(8,128)(2,1)S(1)} %pad_select_fusion.3.grad_low_ref, bf16[2,16,768]{2,1,0:T(8,128)(2,1)S(1)} %pad_select_fusion.2.grad_high_ref), custom_call_target="tpu_custom_call" | custom-call | flops 5000000000 | bytes 2457600 | tf_op jit(solution)/shard_map/conv_back/pallas_call | solution.py:123
  408.7 8.0 %taps_back.2 = f32[40,768]{1,0:T(8,128)S(1)} custom-call(s32[2]{0:T(128)S(1)} %copy-done.98, bf16[512,768]{1,0:T(8,128)(2,1)S(1)} %copy-done.23, bf16[2,16,768]{2,1,0:T(8,128)(2,1)S(1)} %copy-done.83, bf16[2,16,768]{2,1,0:T(8,128)(2,1)S(1)} %copy-done.81, bf16[512,768]{1,0:T(8,128)(2,1)S(1)} %copy-done.61), custom_call_target="tpu_custom_call" | custom-call | flops 5000000000 | bytes 1794048 | tf_op jit(solution)/shard_map/taps_back/pallas_call | solution.py:123
  423.9 9.8 %spread.2 = (bf16[512,1536]{1,0:T(8,128)(2,1)S(1)}, bf16[512,768]{1,0:T(8,128)(2,1)S(1)}, f32[512,768]{1,0:T(8,128)S(1)}) custom-call(s32[24]{0:T(128)S(1)} %fusion.71.place_ref, s32[512,1]{1,0:T(8,128)S(1)} %copy-done.33, bf16[24,64,128]{2,1,0:T(8,128)(2,1)S(1)} %pad_maximum_fusion.10.marks_ref, bf16[512,1536]{1,0:T(8,128)(2,1)} %copy-done.38, ...), custom_call_target="tpu_custom_call" | custom-call | flops 2415919104 | bytes 38930432 | tf_op jit(solution)/shard_map/spread/pallas_call | solution.py:123
  436.1 18.7 %dense_backward.3 = (bf16[512,768]{1,0:T(8,128)(2,1)S(1)}, bf16[512,3072]{1,0:T(8,128)(2,1)S(1)}, f32[512,768]{1,0:T(8,128)S(1)}, bf16[512,768]{1,0:T(8,128)(2,1...) custom-call(f32[512,768]{1,0:T(8,128)} %copy-done.43, f32[512,768]{1,0:T(8,128)} %copy-done.34, ...), custom_call_target="tpu_custom_call" | custom-call | flops 5435817984 | bytes 30000000 | tf_op jit(solution)/shard_map/dense_backward/pallas_call | solution.py:894
  454.9 6.4 token_back.3
  497.6 10.4 %newton_back.3.refs_4_ = f32[3,64,128]{2,1,0:T(8,128)} custom-call(f32[3,64,128]{2,1,0:T(8,128)} %get-tuple-element.234.marks_ref, f32[3,64,64]{2,1,0:T(8,128)} %get-tuple-element.328.kernel_ref, f32[6,3,4,64,64]{4,3,2,1,0:T(8,128)} %get-tuple-element.329.steps_ref, f32[3,64,128]{2,1,0:T(8,128)} %get-tuple-element.323.refs_5_.values_ref, ...), custom_call_target="tpu_custom_call" | custom-call | flops 10000000000 | bytes 1000000 | tf_op jit(solution)/shard_map/newton_back/pallas_call | solution.py:278
  510.8 4.4 collective-permute-done.71
  520.9 6.6 key_back.3
  533.1 7.3 %conv_back.3.dconv_ref = f32[512,768]{1,0:T(8,128)S(1)} custom-call(s32[2]{0:T(128)S(1)} %copy-done.98, f32[396]{0:T(512)S(1)} %copy-done.88, bf16[512,768]{1,0:T(8,128)(2,1)S(1)} %copy-done.57, bf16[2,16,768]{2,1,0:T(8,128)(2,1)S(1)} %pad_select_fusion.1.grad_low_ref, bf16[2,16,768]{2,1,0:T(8,128)(2,1)S(1)} %pad_select_fusion.grad_high_ref), custom_call_target="tpu_custom_call" | custom-call | flops 5000000000 | bytes 2457600 | tf_op jit(solution)/shard_map/conv_back/pallas_call | solution.py:123
  546.0 8.0 %taps_back.3 = f32[40,768]{1,0:T(8,128)S(1)} custom-call(s32[2]{0:T(128)S(1)} %copy-done.98, bf16[512,768]{1,0:T(8,128)(2,1)S(1)} %copy-done.18, bf16[2,16,768]{2,1,0:T(8,128)(2,1)S(1)} %copy-done.79, bf16[2,16,768]{2,1,0:T(8,128)(2,1)S(1)} %copy-done.77, bf16[512,768]{1,0:T(8,128)(2,1)S(1)} %copy-done.58), custom_call_target="tpu_custom_call" | custom-call | flops 5000000000 | bytes 1794048 | tf_op jit(solution)/shard_map/taps_back/pallas_call | solution.py:123
  560.3 9.7 %spread.3 = (bf16[512,1536]{1,0:T(8,128)(2,1)S(1)}, bf16[512,768]{1,0:T(8,128)(2,1)S(1)}, f32[512,768]{1,0:T(8,128)S(1)}) custom-call(s32[24]{0:T(128)S(1)} %fusion.71.place_ref, s32[512,1]{1,0:T(8,128)S(1)} %copy-done.33, bf16[24,64,128]{2,1,0:T(8,128)(2,1)S(1)} %pad_maximum_fusion.12.marks_ref, bf16[512,1536]{1,0:T(8,128)(2,1)} %copy-done.53, ...), custom_call_target="tpu_custom_call" | custom-call | flops 2415919104 | bytes 17696768 | tf_op jit(solution)/shard_map/spread/pallas_call | solution.py:123
  590.6 31.4 %collective-permute-done.91 = bf16[1,2,2,2,24,1536]{5,4,2,3,1,0:T(8,128)(2,1)S(1)} collective-permute-done((bf16[1,2,2,2,24,1536]{5,4,2,3,1,0:T(8,128)(2,1)S(1)}, bf16[1,2,2,2,24,1536]{5,4,2,3,1,0:T(8,128)(2,1)S(1)}, u32[]{:S(2)}, u32[]{:S(2)}) %collective-permute-start.91) | collective-permute-done | bytes 589856 | tf_op jit(solution)/shard_map/ppermute | solution.py:1069
  627.2 4.8 collective-permute-done.96
  662.3 4.4 final_layout.1
  (815 shorter events, 362.5 us)
Async XLA Ops:
  7.2 159.0 %all-gather.4.cloned.1.call-start = ((), (), s32[]{:S(2)}) async-start(), calls=%async_computation.2 | async-start | bytes 14598144 | tf_op jit(solution)/shard_map/all_gather | solution.py:1324
  8.5 41.3 %collective-permute-start.9 = (bf16[256,768]{1,0:T(8,128)(2,1)S(1)}, bf16[256,768]{1,0:T(8,128)(2,1)S(1)}, u32[]{:S(2)}, u32[]{:S(2)}) collective-permute-start(bf16[256,768]{1,0:T(8,128)(2,1)S(1)} %get-tuple-element.480), channel_id=1, source_target_pairs={{0,8},{1,9},{2,10},{3,11},{4,12},{5,13},{6,14},{7,15},{8,0},{9,1},... | collective-permute-start | bytes 1179656 | tf_op jit(solution)/shard_map/ppermute | solution.py:1069
  13.3 20.8 %collective-permute-start.2 = (bf16[24,768]{1,0:T(8,128)(2,1)S(1)}, bf16[24,768]{1,0:T(8,128)(2,1)S(1)}, u32[]{:S(2)}, u32[]{:S(2)}) collective-permute-start(bf16[24,768]{1,0:T(8,128)(2,1)S(1)} %get-tuple-element.517), channel_id=1, source_target_pairs={{0,8},{1,9},{2,10},{3,11},{4,12},{5,13},{6,14},{7,15},{8,0},{9,1},... | collective-permute-start | bytes 110600 | tf_op jit(solution)/shard_map/ppermute | solution.py:1069
  13.4 22.2 %collective-permute-start = (bf16[24,768]{1,0:T(8,128)(2,1)S(1)}, bf16[24,768]{1,0:T(8,128)(2,1)S(1)}, u32[]{:S(2)}, u32[]{:S(2)}) collective-permute-start(bf16[24,768]{1,0:T(8,128)(2,1)S(1)} %get-tuple-element.518), channel_id=1, source_target_pairs={{0,8},{1,9},{2,10},{3,11},{4,12},{5,13},{6,14},{7,15},{8,0},{9,1},... | collective-permute-start | bytes 110600 | tf_op jit(solution)/shard_map/ppermute | solution.py:1069
  16.3 19.4 %collective-permute-start.4 = (bf16[24,768]{1,0:T(8,128)(2,1)S(1)}, bf16[24,768]{1,0:T(8,128)(2,1)S(1)}, u32[]{:S(2)}, u32[]{:S(2)}) collective-permute-start(bf16[24,768]{1,0:T(8,128)(2,1)S(1)} %get-tuple-element.516), channel_id=1, source_target_pairs={{0,8},{1,9},{2,10},{3,11},{4,12},{5,13},{6,14},{7,15},{8,0},{9,1},... | collective-permute-start | bytes 110600 | tf_op jit(solution)/shard_map/ppermute | solution.py:1069
  60.1 217.2 %all-gather.6.cloned.1.call-start = ((), (), s32[]{:S(2)}) async-start(), calls=%async_computation.3 | async-start | bytes 10948608 | tf_op jit(solution)/shard_map/all_gather | solution.py:1324
  61.2 499.1 %all-gather.8.cloned.1.call-start = ((), (), s32[]{:S(2)}) async-start(), calls=%async_computation.4 | async-start | bytes 3649536 | tf_op jit(solution)/shard_map/all_gather | solution.py:1367
  89.5 11.7 %collective-permute-start.17 = (bf16[3,64,128]{2,1,0:T(8,128)(2,1)S(1)}, bf16[3,64,128]{2,1,0:T(8,128)(2,1)S(1)}, u32[]{:S(2)}, u32[]{:S(2)}) collective-permute-start(bf16[3,64,128]{2,1,0:T(8,128)(2,1)S(1)} %get-tuple-element.499), channel_id=1, source_target_pairs={{0,4},{1,5},{2,6},{3,7},{4,0},{5,1},{6,2},{7,3},{8,12},{9,13},{10,... | collective-permute-start | bytes 147464 | tf_op jit(solution)/shard_map/ppermute | solution.py:1069
  131.9 11.8 %collective-permute-start.28 = (bf16[3,64,128]{2,1,0:T(8,128)(2,1)}, bf16[3,64,128]{2,1,0:T(8,128)(2,1)S(1)}, u32[]{:S(2)}, u32[]{:S(2)}) collective-permute-start(bf16[3,64,128]{2,1,0:T(8,128)(2,1)} %get-tuple-element.233), channel_id=1, source_target_pairs={{0,6},{1,7},{2,4},{3,5},{4,2},{5,3},{6,0},{7,1},{8,14},{9,15},{10,... | collective-permute-start | bytes 147464 | tf_op jit(solution)/shard_map/ppermute | solution.py:1069
  197.7 464.6 %reduce-scatter.5.cloned.1.call-start = ((), (), s32[]{:S(2)}) async-start(), calls=%async_computation.6 | async-start | bytes 10948608 | tf_op jit(solution)/shard_map/reduce_scatter | solution.py:1394
  202.2 12.6 %collective-permute-start.34 = (bf16[3,64,128]{2,1,0:T(8,128)(2,1)S(1)}, bf16[3,64,128]{2,1,0:T(8,128)(2,1)S(1)}, u32[]{:S(2)}, u32[]{:S(2)}) collective-permute-start(bf16[3,64,128]{2,1,0:T(8,128)(2,1)S(1)} %get-tuple-element.495), channel_id=1, source_target_pairs={{0,4},{1,5},{2,6},{3,7},{4,0},{5,1},{6,2},{7,3},{8,12},{9,13},{10,... | collective-permute-start | bytes 147464 | tf_op jit(solution)/shard_map/ppermute | solution.py:1069
  203.9 10.9 %collective-permute-start.35 = (bf16[3,64,128]{2,1,0:T(8,128)(2,1)S(1)}, bf16[3,64,128]{2,1,0:T(8,128)(2,1)S(1)}, u32[]{:S(2)}, u32[]{:S(2)}) collective-permute-start(bf16[3,64,128]{2,1,0:T(8,128)(2,1)S(1)} %get-tuple-element.494), channel_id=1, source_target_pairs={{0,2},{1,3},{2,0},{3,1},{4,6},{5,7},{6,4},{7,5},{8,10},{9,11},{10,... | collective-permute-start | bytes 147464 | tf_op jit(solution)/shard_map/ppermute | solution.py:1069
  266.8 27.1 %collective-permute-start.32 = (bf16[256,768]{1,0:T(8,128)(2,1)}, bf16[256,768]{1,0:T(8,128)(2,1)}, u32[]{:S(2)}, u32[]{:S(2)}) collective-permute-start(bf16[256,768]{1,0:T(8,128)(2,1)} %get-tuple-element.244), channel_id=1, source_target_pairs={{0,8},{1,9},{2,10},{3,11},{4,12},{5,13},{6,14},{7,15},{8,0},{9,1},... | collective-permute-start | bytes 1179656 | tf_op jit(solution)/shard_map/ppermute | solution.py:1069
  337.4 324.9 %reduce-scatter.3.cloned.1.call-start = ((), (), s32[]{:S(2)}) async-start(), calls=%async_computation.5 | async-start | bytes 10948608 | tf_op jit(solution)/shard_map/reduce_scatter | solution.py:1394
  370.3 20.0 %collective-permute-start.56 = (bf16[256,768]{1,0:T(8,128)(2,1)}, bf16[256,768]{1,0:T(8,128)(2,1)S(1)}, u32[]{:S(2)}, u32[]{:S(2)}) collective-permute-start(bf16[256,768]{1,0:T(8,128)(2,1)} %get-tuple-element.292), channel_id=1, source_target_pairs={{0,8},{1,9},{2,10},{3,11},{4,12},{5,13},{6,14},{7,15},{8,0},{9,1},... | collective-permute-start | bytes 1179656 | tf_op jit(solution)/shard_map/ppermute | solution.py:1069
  392.3 11.8 %collective-permute-start.58 = (bf16[3,32,128]{2,1,0:T(8,128)(2,1)S(1)}, bf16[3,32,128]{2,1,0:T(8,128)(2,1)S(1)}, u32[]{:S(2)}, u32[]{:S(2)}) collective-permute-start(bf16[3,32,128]{2,1,0:T(8,128)(2,1)S(1)} %get-tuple-element.507), channel_id=1, source_target_pairs={{0,4},{1,5},{2,6},{3,7},{4,0},{5,1},{6,2},{7,3},{8,12},{9,13},{10,... | collective-permute-start | bytes 73736 | tf_op jit(solution)/shard_map/ppermute | solution.py:1069
  392.3 11.8 %collective-permute-start.59 = (bf16[3,32,128]{2,1,0:T(8,128)(2,1)S(1)}, bf16[3,32,128]{2,1,0:T(8,128)(2,1)S(1)}, u32[]{:S(2)}, u32[]{:S(2)}) collective-permute-start(bf16[3,32,128]{2,1,0:T(8,128)(2,1)S(1)} %get-tuple-element.506), channel_id=1, source_target_pairs={{0,2},{1,3},{2,0},{3,1},{4,6},{5,7},{6,4},{7,5},{8,10},{9,11},{10,... | collective-permute-start | bytes 73736 | tf_op jit(solution)/shard_map/ppermute | solution.py:1069
  393.5 10.6 %collective-permute-start.60 = (bf16[3,32,128]{2,1,0:T(8,128)(2,1)S(1)}, bf16[3,32,128]{2,1,0:T(8,128)(2,1)S(1)}, u32[]{:S(2)}, u32[]{:S(2)}) collective-permute-start(bf16[3,32,128]{2,1,0:T(8,128)(2,1)S(1)} %get-tuple-element.505), channel_id=1, source_target_pairs={{0,6},{1,7},{2,4},{3,5},{4,2},{5,3},{6,0},{7,1},{8,14},{9,15},{10,... | collective-permute-start | bytes 73736 | tf_op jit(solution)/shard_map/ppermute | solution.py:1069
  463.1 22.6 %collective-permute-start.81 = (bf16[2,16,768]{2,1,0:T(8,128)(2,1)}, bf16[2,16,768]{2,1,0:T(8,128)(2,1)S(1)}, u32[]{:S(2)}, u32[]{:S(2)}) collective-permute-start(bf16[2,16,768]{2,1,0:T(8,128)(2,1)} %get-tuple-element.467), channel_id=1, source_target_pairs={{1,0},{2,1},{3,2},{4,3},{5,4},{6,5},{7,6},{0,7},{9,8},{10,9},{11,1... | collective-permute-start | bytes 147464 | tf_op jit(solution)/shard_map/ppermute | solution.py:1192
  467.3 48.0 %collective-permute-start.80 = (bf16[2,16,768]{2,1,0:T(8,128)(2,1)}, bf16[2,16,768]{2,1,0:T(8,128)(2,1)S(1)}, u32[]{:S(2)}, u32[]{:S(2)}) collective-permute-start(bf16[2,16,768]{2,1,0:T(8,128)(2,1)} %get-tuple-element.468), channel_id=1, source_target_pairs={{0,1},{1,2},{2,3},{3,4},{4,5},{5,6},{6,7},{7,0},{8,9},{9,10},{10,1... | collective-permute-start | bytes 147464 | tf_op jit(solution)/shard_map/ppermute | solution.py:1191
  467.6 11.9 %collective-permute-start.66 = (bf16[12,64,128]{2,1,0:T(8,128)(2,1)S(1)}, bf16[12,64,128]{2,1,0:T(8,128)(2,1)S(1)}, u32[]{:S(2)}, u32[]{:S(2)}) collective-permute-start(bf16[12,64,128]{2,1,0:T(8,128)(2,1)S(1)} %slice.379), channel_id=1, source_target_pairs={{0,1},{1,0},{2,3},{3,2},{4,5},{5,4},{6,7},{7,6},{8,9},{9,8},{10,11... | collective-permute-start | bytes 589832 | tf_op jit(solution)/shard_map/ppermute | solution.py:1069
  494.8 22.0 %collective-permute-start.75 = (bf16[1,2,2,2,2,24,768]{6,5,2,4,1,3,0:T(8,128)(2,1)}, bf16[1,2,2,2,2,24,768]{6,5,2,4,1,3,0:T(8,128)(2,1)}, u32[]{:S(2)}, u32[]{:S(2)}) collective-permute-start(bf16[1,2,2,2,2,24,768]{6,5,2,4,1,3,0:T(8,128)(2,1)} %bitcast.225), channel_id=1, source_target_pairs={{0,1},{1,0},{2,3},{3,2},{4,5},{5,4},{6,7},{7,6},{8,9},{9,8},{10,11... | collective-permute-start | bytes 1769480 | tf_op jit(solution)/shard_map/ppermute | solution.py:1069
  497.6 12.3 %collective-permute-start.70 = (bf16[3,64,128]{2,1,0:T(8,128)(2,1)S(1)}, bf16[3,64,128]{2,1,0:T(8,128)(2,1)S(1)}, u32[]{:S(2)}, u32[]{:S(2)}) collective-permute-start(bf16[3,64,128]{2,1,0:T(8,128)(2,1)S(1)} %copy-done.126), channel_id=1, source_target_pairs={{0,4},{1,5},{2,6},{3,7},{4,0},{5,1},{6,2},{7,3},{8,12},{9,13},{10,... | collective-permute-start | bytes 147464 | tf_op jit(solution)/shard_map/ppermute | solution.py:1069
  529.6 12.0 %collective-permute-start.77 = (bf16[3,32,128]{2,1,0:T(8,128)(2,1)S(1)}, bf16[3,32,128]{2,1,0:T(8,128)(2,1)S(1)}, u32[]{:S(2)}, u32[]{:S(2)}) collective-permute-start(bf16[3,32,128]{2,1,0:T(8,128)(2,1)S(1)} %get-tuple-element.503), channel_id=1, source_target_pairs={{0,4},{1,5},{2,6},{3,7},{4,0},{5,1},{6,2},{7,3},{8,12},{9,13},{10,... | collective-permute-start | bytes 73736 | tf_op jit(solution)/shard_map/ppermute | solution.py:1069
  577.8 45.1 %collective-permute-start.93 = (bf16[256,768]{1,0:T(8,128)(2,1)S(1)}, bf16[256,768]{1,0:T(8,128)(2,1)S(1)}, u32[]{:S(2)}, u32[]{:S(2)}) collective-permute-start(bf16[256,768]{1,0:T(8,128)(2,1)S(1)} %fusion.44), channel_id=1, source_target_pairs={{0,8},{1,9},{2,10},{3,11},{4,12},{5,13},{6,14},{7,15},{8,0},{9,1},... | collective-permute-start | bytes 1179656 | tf_op jit(solution)/shard_map/ppermute | solution.py:1069
  584.3 37.7 %collective-permute-start.91 = (bf16[1,2,2,2,24,1536]{5,4,2,3,1,0:T(8,128)(2,1)S(1)}, bf16[1,2,2,2,24,1536]{5,4,2,3,1,0:T(8,128)(2,1)S(1)}, u32[]{:S(2)}, u32[]{:S(2)}) collective-permute-start(bf16[1,2,2,2,24,1536]{5,4,2,3,1,0:T(8,128)(2,1)S(1)} %dynamic-slice_bitcast_fusion.1), channel_id=1, source_target_pairs={{0,4},{1,5},{2,6},{3,7},{4,0},{5,1},{6,2},{7,3},{8,12},{9,13},{10,... | collective-permute-start | bytes 1769480 | tf_op jit(solution)/shard_map/ppermute | solution.py:1069
  586.7 35.5 %collective-permute-start.90 = (bf16[1,2,2,2,24,1536]{5,4,2,1,3,0:T(8,128)(2,1)S(1)}, bf16[1,2,2,2,24,1536]{5,4,2,1,3,0:T(8,128)(2,1)S(1)}, u32[]{:S(2)}, u32[]{:S(2)}) collective-permute-start(bf16[1,2,2,2,24,1536]{5,4,2,1,3,0:T(8,128)(2,1)S(1)} %dynamic-slice_bitcast_fusion.2), channel_id=1, source_target_pairs={{0,2},{1,3},{2,0},{3,1},{4,6},{5,7},{6,4},{7,5},{8,10},{9,11},{10,... | collective-permute-start | bytes 1769480 | tf_op jit(solution)/shard_map/ppermute | solution.py:1069
  586.9 35.4 %collective-permute-start.89 = (bf16[1,2,2,2,24,1536]{5,4,1,2,3,0:T(8,128)(2,1)S(1)}, bf16[1,2,2,2,24,1536]{5,4,1,2,3,0:T(8,128)(2,1)S(1)}, u32[]{:S(2)}, u32[]{:S(2)}) collective-permute-start(bf16[1,2,2,2,24,1536]{5,4,1,2,3,0:T(8,128)(2,1)S(1)} %dynamic-slice_bitcast_fusion.3), channel_id=1, source_target_pairs={{0,16},{16,0},{1,17},{17,1},{2,18},{18,2},{3,19},{19,3},{4,20},{20... | collective-permute-start | bytes 1769480 | tf_op jit(solution)/shard_map/ppermute | solution.py:1069
  623.4 10.6 %collective-permute-start.95 = (bf16[1,2,2,24,1536]{4,3,2,1,0:T(8,128)(2,1)S(1)}, bf16[1,2,2,24,1536]{4,3,2,1,0:T(8,128)(2,1)S(1)}, u32[]{:S(2)}, u32[]{:S(2)}) collective-permute-start(bf16[1,2,2,24,1536]{4,3,2,1,0:T(8,128)(2,1)S(1)} %dynamic-slice_bitcast_fusion.11), channel_id=1, source_target_pairs={{0,4},{1,5},{2,6},{3,7},{4,0},{5,1},{6,2},{7,3},{8,12},{9,13},{10,... | collective-permute-start | bytes 884744 | tf_op jit(solution)/shard_map/ppermute | solution.py:1069
  623.5 10.7 %collective-permute-start.94 = (bf16[1,2,2,24,1536]{4,3,1,2,0:T(8,128)(2,1)S(1)}, bf16[1,2,2,24,1536]{4,3,1,2,0:T(8,128)(2,1)S(1)}, u32[]{:S(2)}, u32[]{:S(2)}) collective-permute-start(bf16[1,2,2,24,1536]{4,3,1,2,0:T(8,128)(2,1)S(1)} %dynamic-slice_bitcast_fusion.12), channel_id=1, source_target_pairs={{0,2},{1,3},{2,0},{3,1},{4,6},{5,7},{6,4},{7,5},{8,10},{9,11},{10,... | collective-permute-start | bytes 884744 | tf_op jit(solution)/shard_map/ppermute | solution.py:1069
  648.8 11.5 %collective-permute-start.104 = (bf16[1,24,1536]{2,1,0:T(8,128)(2,1)S(1)}, bf16[1,24,1536]{2,1,0:T(8,128)(2,1)S(1)}, u32[]{:S(2)}, u32[]{:S(2)}) collective-permute-start(bf16[1,24,1536]{2,1,0:T(8,128)(2,1)S(1)} %dynamic-slice_bitcast_fusion.16), channel_id=1, source_target_pairs={{0,8},{1,9},{2,10},{3,11},{4,12},{5,13},{6,14},{7,15},{8,0},{9,1},... | collective-permute-start | bytes 221192 | tf_op jit(solution)/shard_map/ppermute | solution.py:1069
  650.1 10.9 %collective-permute-start.103 = (bf16[1,24,1536]{2,1,0:T(8,128)(2,1)S(1)}, bf16[1,24,1536]{2,1,0:T(8,128)(2,1)S(1)}, u32[]{:S(2)}, u32[]{:S(2)}) collective-permute-start(bf16[1,24,1536]{2,1,0:T(8,128)(2,1)S(1)} %dynamic-slice_bitcast_fusion.17), channel_id=1, source_target_pairs={{0,8},{1,9},{2,10},{3,11},{4,12},{5,13},{6,14},{7,15},{8,0},{9,1},... | collective-permute-start | bytes 221192 | tf_op jit(solution)/shard_map/ppermute | solution.py:1069
  (246 other events, 1833.0 us)
Sparse Core Ops, SparseCore 0:
  60.2 105.9 all-gather.3
  169.1 90.3 all-gather.5
  263.0 66.7 all-gather.7
  337.6 147.1 reduce-scatter.4
  490.7 151.2 reduce-scatter.2

commit v6 on v5

--- a/solution.py
+++ b/solution.py
@@ -1313,7 +1313,7 @@
             ]
         if number == 3:
             turns, token_rows = lax.optimization_barrier((turns, token_rows))
-        if number == len(orders[0]) - 1:
+        if number == len(orders[0]) - 2:
             turns, later_blocks[0] = lax.optimization_barrier((turns, later_blocks[0]))
         turns = [
             jnp.concatenate([turn, flip(turn, order[number][0], 1 << order[number][1])], axis=0)

time: 684 us -> 685 us (level)
    unnamed x342 -> x338, local copies, waits for them, and re-layouts: 38.4 us -> 38.3 us
  transfers between devices with their start and end apart: 111 -> 111, of which waited for: 48 -> 45; matrix products, arithmetic and copies ran while one was open for 16% -> 16% of each run, Pallas kernels for 37% -> 37%
where the time goes in v6:
time: 685 us; the launch traced here: 677 us
  Pallas kernels  258 us (38%)
  waiting for transfers between devices  149 us (22%)
  starting transfers between devices  105 us (15%)
  local copies, waits for them, and re-layouts  73 us (11%)
  matrix products  37.6 us (5%)
  other arithmetic  36.9 us (5%)
  between operations  17.2 us (3%)
    ppermute x98, waiting for transfers between devices, flip(): return lax.ppermute(value, axis, [(i, i ^ mask) for i in range(count)])  139 us
    pallas_call x20, Pallas kernels, over_pairs(): pl.pallas_call(body, grid_spec=pltpu.PrefetchScalarGridSpec(num_scalar_pr...  129 us
    ppermute x98, starting transfers between devices, flip(): return lax.ppermute(value, axis, [(i, i ^ mask) for i in range(count)])  98.8 us
    pallas_call x4, Pallas kernels, dense_call(): pl.pallas_call(body, grid=(folds,), in_specs=in_specs, out_specs=out_spec...  66.9 us
    pallas_call x15, Pallas kernels, small_call(): pl.pallas_call(body, out_shape=out_shape, scratch_shapes=scratch, cost_es...  61.6 us
    unnamed x338, local copies, waits for them, and re-layouts  38.3 us
    dot_general x16, matrix products, tn(): lax.dot_general(left, right, (((0,), (0,)), ((), ())), preferred_element_...  34.7 us
  transfers between devices with their start and end apart: 111, of which 45 were waited for; matrix products, arithmetic and copies ran while one was open for 16% of the time, Pallas kernels for 37%

profile of v6, /device:TPU:0, one launch (start us, length us, event | category | flops | bytes accessed | tf_op | source)
XLA Modules:
  0.0 676.5 jit_solution(7326148860277660510)
XLA Ops:
  17.9 17.1 %collective-permute-done.2 = bf16[24,768]{1,0:T(8,128)(2,1)S(1)} collective-permute-done((bf16[24,768]{1,0:T(8,128)(2,1)S(1)}, bf16[24,768]{1,0:T(8,128)(2,1)S(1)}, u32[]{:S(2)}, u32[]{:S(2)}) %collective-permute-start.2) | collective-permute-done | bytes 36896 | tf_op jit(solution)/shard_map/ppermute | solution.py:1069
  60.1 5.9 collective-permute-done.10
  76.1 7.8 %project.2 = (bf16[512,1536]{1,0:T(8,128)(2,1)S(1)}, bf16[512,768]{1,0:T(8,128)(2,1)S(1)}, f32[24,64,128]{2,1,0:T(8,128)S(1)}) custom-call(s32[24]{0:T(128)S(1)} %fusion.71.place_ref, s32[1,512]{1,0:T(1,128)S(1)} %fusion.68.ids_ref, bf16[3,512,768]{2,1,0:T(8,128)(2,1)} %pad_maximum_fusion.1.hidden_qk_ref.hidden_v_ref, ...), custom_call_target="tpu_custom_call" | custom-call | flops 1811939328 | bytes 14944256 | tf_op jit(solution)/shard_map/project/pallas_call | solution.py:123
  87.5 4.5 collective-permute-done.20
  96.3 7.0 %conv_forward.2.conv_ref = f32[512,768]{1,0:T(8,128)S(1)} custom-call(s32[2]{0:T(128)S(1)} %broadcast_subtract_fusion.bound_ref, f32[396]{0:T(512)S(1)} %reshape_squeeze.13.scalar_ref, bf16[512,768]{1,0:T(8,128)(2,1)S(1)} %get-tuple-element.223.v_ref, bf16[2,16,768]{2,1,0:T(8,128)(2,1)S(1)} %pad_select_fusion.7.low_ref, ...), custom_call_target="tpu_custom_call" | custom-call | flops 5000000000 | bytes 2457600 | tf_op jit(solution)/shard_map/conv_forward/pallas_call | solution.py:123
  113.0 5.8 collective-permute-done.23
  121.3 5.5 key_partial.2.mine_ref
  136.0 6.9 %owner_pseudo.2 = (f32[3,64,64]{2,1,0:T(8,128)}, f32[3,64,64]{2,1,0:T(8,128)}, f32[6,3,4,64,64]{4,3,2,1,0:T(8,128)}) custom-call(f32[3,64,128]{2,1,0:T(8,128)} %get-tuple-element.234.marks_ref), custom_call_target="tpu_custom_call" | custom-call | flops 5000000000 | bytes 1000000 | tf_op jit(solution)/shard_map/owner_pseudo/pallas_call | solution.py:278
  162.6 14.4 %dense_forward.2 = (f32[512,768]{1,0:T(8,128)S(1)}, f32[512,128]{1,0:T(8,128)S(1)}, bf16[512,768]{1,0:T(8,128)(2,1)S(1)}, f32[512,3072]{1,0:T(8,128)}, bf16[512,...) custom-call(f32[512,768]{1,0:T(8,128)} %convert_element_type.493.hid, ...), custom_call_target="tpu_custom_call" | custom-call | flops 5435817984 | bytes 30000000 | tf_op jit(solution)/shard_map/dense_forward/pallas_call | solution.py:894
  179.3 7.4 %project.3 = (bf16[512,1536]{1,0:T(8,128)(2,1)S(1)}, bf16[512,768]{1,0:T(8,128)(2,1)S(1)}, f32[24,64,128]{2,1,0:T(8,128)S(1)}) custom-call(s32[24]{0:T(128)S(1)} %fusion.71.place_ref, s32[1,512]{1,0:T(1,128)S(1)} %fusion.68.ids_ref, bf16[1,512,768]{2,1,0:T(8,128)(2,1)S(1)} %bitcast.233, bf16[1,512,768]{2,1,0:T(8,128)(2,1)S(1)} %bitcast.234, ...), custom_call_target="tpu_custom_call" | custom-call | flops 1811939328 | bytes 33032192 | tf_op jit(solution)/shard_map/project/pallas_call | solution.py:123
  203.7 7.0 %conv_forward.3.conv_ref = f32[512,768]{1,0:T(8,128)S(1)} custom-call(s32[2]{0:T(128)S(1)} %copy-done.97, f32[396]{0:T(512)S(1)} %copy-done.89, bf16[512,768]{1,0:T(8,128)(2,1)S(1)} %copy-done.20, bf16[2,16,768]{2,1,0:T(8,128)(2,1)S(1)} %pad_select_fusion.5.low_ref, bf16[2,16,768]{2,1,0:T(8,128)(2,1)S(1)} %pad_select_fusion.4.high_ref), custom_call_target="tpu_custom_call" | custom-call | flops 5000000000 | bytes 2457600 | tf_op jit(solution)/shard_map/conv_forward/pallas_call | solution.py:123
  216.7 6.4 collective-permute-done.39
  227.3 4.7 collective-permute-done.40
  234.4 5.5 key_partial.3.mine_ref
  249.3 6.8 %owner_pseudo.3 = (f32[3,64,64]{2,1,0:T(8,128)}, f32[3,64,64]{2,1,0:T(8,128)}, f32[6,3,4,64,64]{4,3,2,1,0:T(8,128)}) custom-call(f32[3,64,128]{2,1,0:T(8,128)} %get-tuple-element.259.marks_ref), custom_call_target="tpu_custom_call" | custom-call | flops 5000000000 | bytes 1000000 | tf_op jit(solution)/shard_map/owner_pseudo/pallas_call | solution.py:278
  279.7 14.8 %dense_forward.3 = (f32[512,768]{1,0:T(8,128)S(1)}, f32[512,128]{1,0:T(8,128)S(1)}, bf16[512,768]{1,0:T(8,128)(2,1)S(1)}, f32[512,3072]{1,0:T(8,128)}, bf16[512,...) custom-call(f32[512,768]{1,0:T(8,128)} %copy-done.37, ...), custom_call_target="tpu_custom_call" | custom-call | flops 5435817984 | bytes 30000000 | tf_op jit(solution)/shard_map/dense_forward/pallas_call | solution.py:894
  297.7 19.0 %dense_backward.2 = (bf16[512,768]{1,0:T(8,128)(2,1)S(1)}, bf16[512,3072]{1,0:T(8,128)(2,1)S(1)}, f32[512,768]{1,0:T(8,128)S(1)}, bf16[512,768]{1,0:T(8,128)(2,1...) custom-call(f32[512,768]{1,0:T(8,128)} %bitcast_convert_fusion.grad_ref, f32[512,768]{1,0:T(8,128)} %copy-done.41, ...), custom_call_target="tpu_custom_call" | custom-call | flops 5435817984 | bytes 30000000 | tf_op jit(solution)/shard_map/dense_backward/pallas_call | solution.py:894
  316.8 6.4 token_back.2
  353.2 10.4 %newton_back.2.refs_4_ = f32[3,64,128]{2,1,0:T(8,128)} custom-call(f32[3,64,128]{2,1,0:T(8,128)} %get-tuple-element.259.marks_ref, f32[3,64,64]{2,1,0:T(8,128)} %get-tuple-element.286.kernel_ref, f32[6,3,4,64,64]{4,3,2,1,0:T(8,128)} %get-tuple-element.287.steps_ref, f32[3,64,128]{2,1,0:T(8,128)} %get-tuple-element.283.refs_5_.values_ref, ...), custom_call_target="tpu_custom_call" | custom-call | flops 10000000000 | bytes 1000000 | tf_op jit(solution)/shard_map/newton_back/pallas_call | solution.py:278
  377.9 6.7 key_back.2
  385.7 4.9 collective-permute-done.56
  396.2 7.0 %conv_back.2.dconv_ref = f32[512,768]{1,0:T(8,128)S(1)} custom-call(s32[2]{0:T(128)S(1)} %copy-done.98, f32[396]{0:T(512)S(1)} %copy-done.90, bf16[512,768]{1,0:T(8,128)(2,1)S(1)} %copy-done.60, bf16[2,16,768]{2,1,0:T(8,128)(2,1)S(1)} %pad_select_fusion.3.grad_low_ref, bf16[2,16,768]{2,1,0:T(8,128)(2,1)S(1)} %pad_select_fusion.2.grad_high_ref), custom_call_target="tpu_custom_call" | custom-call | flops 5000000000 | bytes 2457600 | tf_op jit(solution)/shard_map/conv_back/pallas_call | solution.py:123
  409.2 8.0 %taps_back.2 = f32[40,768]{1,0:T(8,128)S(1)} custom-call(s32[2]{0:T(128)S(1)} %copy-done.98, bf16[512,768]{1,0:T(8,128)(2,1)S(1)} %copy-done.23, bf16[2,16,768]{2,1,0:T(8,128)(2,1)S(1)} %copy-done.83, bf16[2,16,768]{2,1,0:T(8,128)(2,1)S(1)} %copy-done.81, bf16[512,768]{1,0:T(8,128)(2,1)S(1)} %copy-done.61), custom_call_target="tpu_custom_call" | custom-call | flops 5000000000 | bytes 1794048 | tf_op jit(solution)/shard_map/taps_back/pallas_call | solution.py:123
  425.6 9.7 %spread.2 = (bf16[512,1536]{1,0:T(8,128)(2,1)S(1)}, bf16[512,768]{1,0:T(8,128)(2,1)S(1)}, f32[512,768]{1,0:T(8,128)S(1)}) custom-call(s32[24]{0:T(128)S(1)} %fusion.71.place_ref, s32[512,1]{1,0:T(8,128)S(1)} %copy-done.33, bf16[24,64,128]{2,1,0:T(8,128)(2,1)S(1)} %pad_maximum_fusion.10.marks_ref, bf16[512,1536]{1,0:T(8,128)(2,1)} %copy-done.38, ...), custom_call_target="tpu_custom_call" | custom-call | flops 2415919104 | bytes 38930432 | tf_op jit(solution)/shard_map/spread/pallas_call | solution.py:123
  437.7 18.7 %dense_backward.3 = (bf16[512,768]{1,0:T(8,128)(2,1)S(1)}, bf16[512,3072]{1,0:T(8,128)(2,1)S(1)}, f32[512,768]{1,0:T(8,128)S(1)}, bf16[512,768]{1,0:T(8,128)(2,1...) custom-call(f32[512,768]{1,0:T(8,128)} %copy-done.43, f32[512,768]{1,0:T(8,128)} %copy-done.34, ...), custom_call_target="tpu_custom_call" | custom-call | flops 5435817984 | bytes 30000000 | tf_op jit(solution)/shard_map/dense_backward/pallas_call | solution.py:894
  456.4 6.4 token_back.3
  499.2 10.4 %newton_back.3.refs_4_ = f32[3,64,128]{2,1,0:T(8,128)} custom-call(f32[3,64,128]{2,1,0:T(8,128)} %get-tuple-element.234.marks_ref, f32[3,64,64]{2,1,0:T(8,128)} %get-tuple-element.328.kernel_ref, f32[6,3,4,64,64]{4,3,2,1,0:T(8,128)} %get-tuple-element.329.steps_ref, f32[3,64,128]{2,1,0:T(8,128)} %get-tuple-element.323.refs_5_.values_ref, ...), custom_call_target="tpu_custom_call" | custom-call | flops 10000000000 | bytes 1000000 | tf_op jit(solution)/shard_map/newton_back/pallas_call | solution.py:278
  522.1 6.6 key_back.3
  534.3 7.3 %conv_back.3.dconv_ref = f32[512,768]{1,0:T(8,128)S(1)} custom-call(s32[2]{0:T(128)S(1)} %copy-done.98, f32[396]{0:T(512)S(1)} %copy-done.88, bf16[512,768]{1,0:T(8,128)(2,1)S(1)} %copy-done.57, bf16[2,16,768]{2,1,0:T(8,128)(2,1)S(1)} %pad_select_fusion.1.grad_low_ref, bf16[2,16,768]{2,1,0:T(8,128)(2,1)S(1)} %pad_select_fusion.grad_high_ref), custom_call_target="tpu_custom_call" | custom-call | flops 5000000000 | bytes 2457600 | tf_op jit(solution)/shard_map/conv_back/pallas_call | solution.py:123
  546.9 8.0 %taps_back.3 = f32[40,768]{1,0:T(8,128)S(1)} custom-call(s32[2]{0:T(128)S(1)} %copy-done.98, bf16[512,768]{1,0:T(8,128)(2,1)S(1)} %copy-done.18, bf16[2,16,768]{2,1,0:T(8,128)(2,1)S(1)} %copy-done.79, bf16[2,16,768]{2,1,0:T(8,128)(2,1)S(1)} %copy-done.77, bf16[512,768]{1,0:T(8,128)(2,1)S(1)} %copy-done.58), custom_call_target="tpu_custom_call" | custom-call | flops 5000000000 | bytes 1794048 | tf_op jit(solution)/shard_map/taps_back/pallas_call | solution.py:123
  561.2 9.7 %spread.3 = (bf16[512,1536]{1,0:T(8,128)(2,1)S(1)}, bf16[512,768]{1,0:T(8,128)(2,1)S(1)}, f32[512,768]{1,0:T(8,128)S(1)}) custom-call(s32[24]{0:T(128)S(1)} %fusion.71.place_ref, s32[512,1]{1,0:T(8,128)S(1)} %copy-done.33, bf16[24,64,128]{2,1,0:T(8,128)(2,1)S(1)} %pad_maximum_fusion.12.marks_ref, bf16[512,1536]{1,0:T(8,128)(2,1)} %copy-done.53, ...), custom_call_target="tpu_custom_call" | custom-call | flops 2415919104 | bytes 17696768 | tf_op jit(solution)/shard_map/spread/pallas_call | solution.py:123
  593.2 29.9 %collective-permute-done.91 = bf16[1,2,2,2,24,1536]{5,4,2,3,1,0:T(8,128)(2,1)S(1)} collective-permute-done((bf16[1,2,2,2,24,1536]{5,4,2,3,1,0:T(8,128)(2,1)S(1)}, bf16[1,2,2,2,24,1536]{5,4,2,3,1,0:T(8,128)(2,1)S(1)}, u32[]{:S(2)}, u32[]{:S(2)}) %collective-permute-start.91) | collective-permute-done | bytes 589856 | tf_op jit(solution)/shard_map/ppermute | solution.py:1069
  (811 shorter events, 362.5 us)
Async XLA Ops:
  7.2 155.3 %all-gather.4.cloned.1.call-start = ((), (), s32[]{:S(2)}) async-start(), calls=%async_computation.2 | async-start | bytes 14598144 | tf_op jit(solution)/shard_map/all_gather | solution.py:1324
  9.2 40.4 %collective-permute-start.9 = (bf16[256,768]{1,0:T(8,128)(2,1)}, bf16[256,768]{1,0:T(8,128)(2,1)S(1)}, u32[]{:S(2)}, u32[]{:S(2)}) collective-permute-start(bf16[256,768]{1,0:T(8,128)(2,1)} %get-tuple-element.480), channel_id=1, source_target_pairs={{0,8},{1,9},{2,10},{3,11},{4,12},{5,13},{6,14},{7,15},{8,0},{9,1},... | collective-permute-start | bytes 1179656 | tf_op jit(solution)/shard_map/ppermute | solution.py:1069
  14.0 21.0 %collective-permute-start.2 = (bf16[24,768]{1,0:T(8,128)(2,1)S(1)}, bf16[24,768]{1,0:T(8,128)(2,1)S(1)}, u32[]{:S(2)}, u32[]{:S(2)}) collective-permute-start(bf16[24,768]{1,0:T(8,128)(2,1)S(1)} %get-tuple-element.517), channel_id=1, source_target_pairs={{0,8},{1,9},{2,10},{3,11},{4,12},{5,13},{6,14},{7,15},{8,0},{9,1},... | collective-permute-start | bytes 110600 | tf_op jit(solution)/shard_map/ppermute | solution.py:1069
  14.1 22.5 %collective-permute-start = (bf16[24,768]{1,0:T(8,128)(2,1)S(1)}, bf16[24,768]{1,0:T(8,128)(2,1)S(1)}, u32[]{:S(2)}, u32[]{:S(2)}) collective-permute-start(bf16[24,768]{1,0:T(8,128)(2,1)S(1)} %get-tuple-element.518), channel_id=1, source_target_pairs={{0,8},{1,9},{2,10},{3,11},{4,12},{5,13},{6,14},{7,15},{8,0},{9,1},... | collective-permute-start | bytes 110600 | tf_op jit(solution)/shard_map/ppermute | solution.py:1069
  17.0 19.6 %collective-permute-start.4 = (bf16[24,768]{1,0:T(8,128)(2,1)S(1)}, bf16[24,768]{1,0:T(8,128)(2,1)S(1)}, u32[]{:S(2)}, u32[]{:S(2)}) collective-permute-start(bf16[24,768]{1,0:T(8,128)(2,1)S(1)} %get-tuple-element.516), channel_id=1, source_target_pairs={{0,8},{1,9},{2,10},{3,11},{4,12},{5,13},{6,14},{7,15},{8,0},{9,1},... | collective-permute-start | bytes 110600 | tf_op jit(solution)/shard_map/ppermute | solution.py:1069
  49.8 228.0 %all-gather.6.cloned.1.call-start = ((), (), s32[]{:S(2)}) async-start(), calls=%async_computation.3 | async-start | bytes 10948608 | tf_op jit(solution)/shard_map/all_gather | solution.py:1324
  50.9 510.3 %all-gather.8.cloned.1.call-start = ((), (), s32[]{:S(2)}) async-start(), calls=%async_computation.4 | async-start | bytes 3649536 | tf_op jit(solution)/shard_map/all_gather | solution.py:1367
  58.4 12.9 %collective-permute-start.14 = (bf16[192,768]{1,0:T(8,128)(2,1)S(1)}, bf16[192,768]{1,0:T(8,128)(2,1)S(1)}, u32[]{:S(2)}, u32[]{:S(2)}) collective-permute-start(bf16[192,768]{1,0:T(8,128)(2,1)S(1)} %pad_maximum_fusion.16), channel_id=1, source_target_pairs={{0,4},{1,5},{2,6},{3,7},{4,0},{5,1},{6,2},{7,3},{8,12},{9,13},{10,... | collective-permute-start | bytes 884744 | tf_op jit(solution)/shard_map/ppermute | solution.py:1069
  92.8 11.7 %collective-permute-start.17 = (bf16[3,64,128]{2,1,0:T(8,128)(2,1)S(1)}, bf16[3,64,128]{2,1,0:T(8,128)(2,1)S(1)}, u32[]{:S(2)}, u32[]{:S(2)}) collective-permute-start(bf16[3,64,128]{2,1,0:T(8,128)(2,1)S(1)} %get-tuple-element.499), channel_id=1, source_target_pairs={{0,4},{1,5},{2,6},{3,7},{4,0},{5,1},{6,2},{7,3},{8,12},{9,13},{10,... | collective-permute-start | bytes 147464 | tf_op jit(solution)/shard_map/ppermute | solution.py:1069
  93.4 11.1 %collective-permute-start.18 = (bf16[3,64,128]{2,1,0:T(8,128)(2,1)S(1)}, bf16[3,64,128]{2,1,0:T(8,128)(2,1)S(1)}, u32[]{:S(2)}, u32[]{:S(2)}) collective-permute-start(bf16[3,64,128]{2,1,0:T(8,128)(2,1)S(1)} %get-tuple-element.498), channel_id=1, source_target_pairs={{0,2},{1,3},{2,0},{3,1},{4,6},{5,7},{6,4},{7,5},{8,10},{9,11},{10,... | collective-permute-start | bytes 147464 | tf_op jit(solution)/shard_map/ppermute | solution.py:1069
  93.4 11.1 %collective-permute-start.19 = (bf16[3,64,128]{2,1,0:T(8,128)(2,1)S(1)}, bf16[3,64,128]{2,1,0:T(8,128)(2,1)S(1)}, u32[]{:S(2)}, u32[]{:S(2)}) collective-permute-start(bf16[3,64,128]{2,1,0:T(8,128)(2,1)S(1)} %get-tuple-element.497), channel_id=1, source_target_pairs={{0,6},{1,7},{2,4},{3,5},{4,2},{5,3},{6,0},{7,1},{8,14},{9,15},{10,... | collective-permute-start | bytes 147464 | tf_op jit(solution)/shard_map/ppermute | solution.py:1069
  194.2 468.9 %reduce-scatter.5.cloned.1.call-start = ((), (), s32[]{:S(2)}) async-start(), calls=%async_computation.6 | async-start | bytes 10948608 | tf_op jit(solution)/shard_map/reduce_scatter | solution.py:1394
  199.5 12.4 %collective-permute-start.34 = (bf16[3,64,128]{2,1,0:T(8,128)(2,1)S(1)}, bf16[3,64,128]{2,1,0:T(8,128)(2,1)S(1)}, u32[]{:S(2)}, u32[]{:S(2)}) collective-permute-start(bf16[3,64,128]{2,1,0:T(8,128)(2,1)S(1)} %get-tuple-element.495), channel_id=1, source_target_pairs={{0,4},{1,5},{2,6},{3,7},{4,0},{5,1},{6,2},{7,3},{8,12},{9,13},{10,... | collective-permute-start | bytes 147464 | tf_op jit(solution)/shard_map/ppermute | solution.py:1069
  201.2 10.7 %collective-permute-start.35 = (bf16[3,64,128]{2,1,0:T(8,128)(2,1)S(1)}, bf16[3,64,128]{2,1,0:T(8,128)(2,1)S(1)}, u32[]{:S(2)}, u32[]{:S(2)}) collective-permute-start(bf16[3,64,128]{2,1,0:T(8,128)(2,1)S(1)} %get-tuple-element.494), channel_id=1, source_target_pairs={{0,2},{1,3},{2,0},{3,1},{4,6},{5,7},{6,4},{7,5},{8,10},{9,11},{10,... | collective-permute-start | bytes 147464 | tf_op jit(solution)/shard_map/ppermute | solution.py:1069
  201.4 10.6 %collective-permute-start.36 = (bf16[3,64,128]{2,1,0:T(8,128)(2,1)S(1)}, bf16[3,64,128]{2,1,0:T(8,128)(2,1)S(1)}, u32[]{:S(2)}, u32[]{:S(2)}) collective-permute-start(bf16[3,64,128]{2,1,0:T(8,128)(2,1)S(1)} %get-tuple-element.493), channel_id=1, source_target_pairs={{0,6},{1,7},{2,4},{3,5},{4,2},{5,3},{6,0},{7,1},{8,14},{9,15},{10,... | collective-permute-start | bytes 147464 | tf_op jit(solution)/shard_map/ppermute | solution.py:1069
  266.9 27.6 %collective-permute-start.32 = (bf16[256,768]{1,0:T(8,128)(2,1)}, bf16[256,768]{1,0:T(8,128)(2,1)}, u32[]{:S(2)}, u32[]{:S(2)}) collective-permute-start(bf16[256,768]{1,0:T(8,128)(2,1)} %get-tuple-element.244), channel_id=1, source_target_pairs={{0,8},{1,9},{2,10},{3,11},{4,12},{5,13},{6,14},{7,15},{8,0},{9,1},... | collective-permute-start | bytes 1179656 | tf_op jit(solution)/shard_map/ppermute | solution.py:1069
  338.2 324.9 %reduce-scatter.3.cloned.1.call-start = ((), (), s32[]{:S(2)}) async-start(), calls=%async_computation.5 | async-start | bytes 10948608 | tf_op jit(solution)/shard_map/reduce_scatter | solution.py:1394
  352.8 10.8 %collective-permute-start.53 = (bf16[3,64,128]{2,1,0:T(8,128)(2,1)}, bf16[3,64,128]{2,1,0:T(8,128)(2,1)}, u32[]{:S(2)}, u32[]{:S(2)}) collective-permute-start(bf16[3,64,128]{2,1,0:T(8,128)(2,1)} %get-tuple-element.285), channel_id=1, source_target_pairs={{0,4},{1,5},{2,6},{3,7},{4,0},{5,1},{6,2},{7,3},{8,12},{9,13},{10,... | collective-permute-start | bytes 147464 | tf_op jit(solution)/shard_map/ppermute | solution.py:1069
  371.1 19.6 %collective-permute-start.56 = (bf16[256,768]{1,0:T(8,128)(2,1)}, bf16[256,768]{1,0:T(8,128)(2,1)S(1)}, u32[]{:S(2)}, u32[]{:S(2)}) collective-permute-start(bf16[256,768]{1,0:T(8,128)(2,1)} %get-tuple-element.292), channel_id=1, source_target_pairs={{0,8},{1,9},{2,10},{3,11},{4,12},{5,13},{6,14},{7,15},{8,0},{9,1},... | collective-permute-start | bytes 1179656 | tf_op jit(solution)/shard_map/ppermute | solution.py:1069
  392.7 11.8 %collective-permute-start.58 = (bf16[3,32,128]{2,1,0:T(8,128)(2,1)S(1)}, bf16[3,32,128]{2,1,0:T(8,128)(2,1)S(1)}, u32[]{:S(2)}, u32[]{:S(2)}) collective-permute-start(bf16[3,32,128]{2,1,0:T(8,128)(2,1)S(1)} %get-tuple-element.507), channel_id=1, source_target_pairs={{0,4},{1,5},{2,6},{3,7},{4,0},{5,1},{6,2},{7,3},{8,12},{9,13},{10,... | collective-permute-start | bytes 73736 | tf_op jit(solution)/shard_map/ppermute | solution.py:1069
  392.7 11.8 %collective-permute-start.59 = (bf16[3,32,128]{2,1,0:T(8,128)(2,1)S(1)}, bf16[3,32,128]{2,1,0:T(8,128)(2,1)S(1)}, u32[]{:S(2)}, u32[]{:S(2)}) collective-permute-start(bf16[3,32,128]{2,1,0:T(8,128)(2,1)S(1)} %get-tuple-element.506), channel_id=1, source_target_pairs={{0,2},{1,3},{2,0},{3,1},{4,6},{5,7},{6,4},{7,5},{8,10},{9,11},{10,... | collective-permute-start | bytes 73736 | tf_op jit(solution)/shard_map/ppermute | solution.py:1069
  464.6 22.1 %collective-permute-start.81 = (bf16[2,16,768]{2,1,0:T(8,128)(2,1)}, bf16[2,16,768]{2,1,0:T(8,128)(2,1)S(1)}, u32[]{:S(2)}, u32[]{:S(2)}) collective-permute-start(bf16[2,16,768]{2,1,0:T(8,128)(2,1)} %get-tuple-element.467), channel_id=1, source_target_pairs={{1,0},{2,1},{3,2},{4,3},{5,4},{6,5},{7,6},{0,7},{9,8},{10,9},{11,1... | collective-permute-start | bytes 147464 | tf_op jit(solution)/shard_map/ppermute | solution.py:1192
  468.1 48.4 %collective-permute-start.80 = (bf16[2,16,768]{2,1,0:T(8,128)(2,1)}, bf16[2,16,768]{2,1,0:T(8,128)(2,1)S(1)}, u32[]{:S(2)}, u32[]{:S(2)}) collective-permute-start(bf16[2,16,768]{2,1,0:T(8,128)(2,1)} %get-tuple-element.468), channel_id=1, source_target_pairs={{0,1},{1,2},{2,3},{3,4},{4,5},{5,6},{6,7},{7,0},{8,9},{9,10},{10,1... | collective-permute-start | bytes 147464 | tf_op jit(solution)/shard_map/ppermute | solution.py:1191
  468.4 12.1 %collective-permute-start.66 = (bf16[12,64,128]{2,1,0:T(8,128)(2,1)S(1)}, bf16[12,64,128]{2,1,0:T(8,128)(2,1)S(1)}, u32[]{:S(2)}, u32[]{:S(2)}) collective-permute-start(bf16[12,64,128]{2,1,0:T(8,128)(2,1)S(1)} %slice.379), channel_id=1, source_target_pairs={{0,1},{1,0},{2,3},{3,2},{4,5},{5,4},{6,7},{7,6},{8,9},{9,8},{10,11... | collective-permute-start | bytes 589832 | tf_op jit(solution)/shard_map/ppermute | solution.py:1069
  495.8 22.2 %collective-permute-start.75 = (bf16[1,2,2,2,2,24,768]{6,5,2,4,1,3,0:T(8,128)(2,1)}, bf16[1,2,2,2,2,24,768]{6,5,2,4,1,3,0:T(8,128)(2,1)}, u32[]{:S(2)}, u32[]{:S(2)}) collective-permute-start(bf16[1,2,2,2,2,24,768]{6,5,2,4,1,3,0:T(8,128)(2,1)} %bitcast.225), channel_id=1, source_target_pairs={{0,1},{1,0},{2,3},{3,2},{4,5},{5,4},{6,7},{7,6},{8,9},{9,8},{10,11... | collective-permute-start | bytes 1769480 | tf_op jit(solution)/shard_map/ppermute | solution.py:1069
  498.6 12.8 %collective-permute-start.70 = (bf16[3,64,128]{2,1,0:T(8,128)(2,1)S(1)}, bf16[3,64,128]{2,1,0:T(8,128)(2,1)S(1)}, u32[]{:S(2)}, u32[]{:S(2)}) collective-permute-start(bf16[3,64,128]{2,1,0:T(8,128)(2,1)S(1)} %copy-done.124), channel_id=1, source_target_pairs={{0,4},{1,5},{2,6},{3,7},{4,0},{5,1},{6,2},{7,3},{8,12},{9,13},{10,... | collective-permute-start | bytes 147464 | tf_op jit(solution)/shard_map/ppermute | solution.py:1069
  530.8 12.0 %collective-permute-start.77 = (bf16[3,32,128]{2,1,0:T(8,128)(2,1)S(1)}, bf16[3,32,128]{2,1,0:T(8,128)(2,1)S(1)}, u32[]{:S(2)}, u32[]{:S(2)}) collective-permute-start(bf16[3,32,128]{2,1,0:T(8,128)(2,1)S(1)} %get-tuple-element.503), channel_id=1, source_target_pairs={{0,4},{1,5},{2,6},{3,7},{4,0},{5,1},{6,2},{7,3},{8,12},{9,13},{10,... | collective-permute-start | bytes 73736 | tf_op jit(solution)/shard_map/ppermute | solution.py:1069
  578.7 45.2 %collective-permute-start.93 = (bf16[256,768]{1,0:T(8,128)(2,1)S(1)}, bf16[256,768]{1,0:T(8,128)(2,1)S(1)}, u32[]{:S(2)}, u32[]{:S(2)}) collective-permute-start(bf16[256,768]{1,0:T(8,128)(2,1)S(1)} %fusion.44), channel_id=1, source_target_pairs={{0,8},{1,9},{2,10},{3,11},{4,12},{5,13},{6,14},{7,15},{8,0},{9,1},... | collective-permute-start | bytes 1179656 | tf_op jit(solution)/shard_map/ppermute | solution.py:1069
  586.5 36.7 %collective-permute-start.91 = (bf16[1,2,2,2,24,1536]{5,4,2,3,1,0:T(8,128)(2,1)S(1)}, bf16[1,2,2,2,24,1536]{5,4,2,3,1,0:T(8,128)(2,1)S(1)}, u32[]{:S(2)}, u32[]{:S(2)}) collective-permute-start(bf16[1,2,2,2,24,1536]{5,4,2,3,1,0:T(8,128)(2,1)S(1)} %dynamic-slice_bitcast_fusion.1), channel_id=1, source_target_pairs={{0,4},{1,5},{2,6},{3,7},{4,0},{5,1},{6,2},{7,3},{8,12},{9,13},{10,... | collective-permute-start | bytes 1769480 | tf_op jit(solution)/shard_map/ppermute | solution.py:1069
  588.6 34.7 %collective-permute-start.90 = (bf16[1,2,2,2,24,1536]{5,4,2,1,3,0:T(8,128)(2,1)S(1)}, bf16[1,2,2,2,24,1536]{5,4,2,1,3,0:T(8,128)(2,1)S(1)}, u32[]{:S(2)}, u32[]{:S(2)}) collective-permute-start(bf16[1,2,2,2,24,1536]{5,4,2,1,3,0:T(8,128)(2,1)S(1)} %dynamic-slice_bitcast_fusion.2), channel_id=1, source_target_pairs={{0,2},{1,3},{2,0},{3,1},{4,6},{5,7},{6,4},{7,5},{8,10},{9,11},{10,... | collective-permute-start | bytes 1769480 | tf_op jit(solution)/shard_map/ppermute | solution.py:1069
  589.1 34.4 %collective-permute-start.89 = (bf16[1,2,2,2,24,1536]{5,4,1,2,3,0:T(8,128)(2,1)S(1)}, bf16[1,2,2,2,24,1536]{5,4,1,2,3,0:T(8,128)(2,1)S(1)}, u32[]{:S(2)}, u32[]{:S(2)}) collective-permute-start(bf16[1,2,2,2,24,1536]{5,4,1,2,3,0:T(8,128)(2,1)S(1)} %dynamic-slice_bitcast_fusion.3), channel_id=1, source_target_pairs={{0,16},{16,0},{1,17},{17,1},{2,18},{18,2},{3,19},{19,3},{4,20},{20... | collective-permute-start | bytes 1769480 | tf_op jit(solution)/shard_map/ppermute | solution.py:1069
  648.4 12.8 %collective-permute-start.104 = (bf16[1,24,1536]{2,1,0:T(8,128)(2,1)S(1)}, bf16[1,24,1536]{2,1,0:T(8,128)(2,1)S(1)}, u32[]{:S(2)}, u32[]{:S(2)}) collective-permute-start(bf16[1,24,1536]{2,1,0:T(8,128)(2,1)S(1)} %dynamic-slice_bitcast_fusion.16), channel_id=1, source_target_pairs={{0,8},{1,9},{2,10},{3,11},{4,12},{5,13},{6,14},{7,15},{8,0},{9,1},... | collective-permute-start | bytes 221192 | tf_op jit(solution)/shard_map/ppermute | solution.py:1069
  (244 other events, 1874.0 us)
Sparse Core Ops, SparseCore 0:
  49.9 110.1 all-gather.3
  163.0 92.1 all-gather.5
  258.7 67.6 all-gather.7
  338.3 147.3 reduce-scatter.4
  491.6 151.7 reduce-scatter.2
